TPU v7x, 512 devices: a whole 4x8x8 slice. The times are simulated.
512 devices in a mesh: batch: 32 (over z, y_hi), weight: 16 (over x, y_lo, core).
Axes of the slice: x: 4, y: 8 (y_hi: 4, y_lo: 2; y = y_hi * 2 + y_lo), z: 8, core: 2. Of those that a mesh axis runs over, the one named last changes fastest.
Arguments:
- tokens: bfloat16 [16384, 8192], P(('batch', 'weight')), may hold values from -6 to 6
- segment_ids: int32 [16384], P('batch'), may hold values from 0 to 511, never falling along the last dimension, each value on 1 to 64 neighbouring positions
- norm_gain: float32 [8192], replicated, may hold values from 0.1 to 1.9
- query_weight: bfloat16 [8192, 8192], P('batch', 'weight'), may hold values from -0.0625 to 0.0625
- key_weight: bfloat16 [8192, 1024], P('batch'), may hold values from -0.0625 to 0.0625
- value_weight: bfloat16 [8192, 1024], P('batch'), may hold values from -0.0625 to 0.0625
Outputs:
- attended: bfloat16 [16384, 8192], P('batch', 'weight')
Inputs may be any that keep to these rules, and one draw needn't show every extreme that they name: `segment_ids`: segment ids never fall along the tokens; each id covers 1 to 64 consecutive tokens, one of them exactly 64.
All inputs are finite; a program needn't handle non-finite values.
Results may differ from a plain program's by a relative error of at most 0.0079.
Values may be sent and summed in bfloat16 or wider, within the bound.
No kernel may reach another device: no remote copies, remote signals or barrier semaphores. Data moves between devices by JAX's collectives and lax.ppermute only.
A program may use at most 64 MiB of HBM per device.

v0:
```python
import math

import jax
import jax.numpy as jnp
from jax import lax
from jax.sharding import PartitionSpec as P

HEADS = 64
KV_HEADS = 8
HEAD_DIM = 128


ROPE_BASE = 500000.0
EPSILON = 1e-05


def positions_in_segment(seg_ids):
    places = jnp.arange(seg_ids.shape[0], dtype=jnp.int32)
    earlier = jnp.concatenate([seg_ids[:1] - 1, seg_ids[:-1]])
    starts = jnp.where(seg_ids != earlier, places, 0)
    leading = lax.cummax(starts, axis=0)
    return places - leading


def rotate(vectors, positions):
    half_dim = vectors.shape[-1] // 2
    ratios = jnp.arange(half_dim, dtype=jnp.float32) * (2.0 / vectors.shape[-1])
    frequency = jnp.exp(-math.log(ROPE_BASE) * ratios)
    angles = positions.astype(jnp.float32)[:, None] * frequency[None, :]
    cosine = jnp.cos(angles)[:, None, :]
    sine_part = jnp.sin(angles)[:, None, :]
    front_half = vectors[..., :half_dim]
    back_half = vectors[..., half_dim:]
    return jnp.concatenate(
        [front_half * cosine - back_half * sine_part, back_half * cosine + front_half * sine_part],
        axis=-1,
    )


def attend(grouped, rotated_keys, value_rows, seg_ids):
    scores = jnp.einsum(
        "ingd,jnd->ngij", grouped, rotated_keys, preferred_element_type=jnp.float32
    ) * grouped.shape[-1] ** (-0.5)
    places = jnp.arange(seg_ids.shape[0], dtype=jnp.int32)
    allowed = (seg_ids[:, None] == seg_ids[None, :]) & (places[None, :] <= places[:, None])
    weights = jnp.where(allowed, jnp.exp(scores), 0.0)
    probabilities = (weights / jnp.sum(weights, axis=-1, keepdims=True)).astype(jnp.bfloat16)
    mixed = jnp.einsum(
        "ngij,jnd->ingd", probabilities, value_rows, preferred_element_type=jnp.float32
    )
    return mixed.astype(jnp.bfloat16)


def per_device(tokens, segment_ids, norm_gain, query_weight, key_weight, value_weight):
    head_dim = HEAD_DIM
    query_cols = query_weight.shape[1]
    heads_dev = query_cols // head_dim
    group_size = HEADS // KV_HEADS
    local_kv = max(1, heads_dev // group_size)
    first_kv = lax.axis_index("weight") * heads_dev // group_size
    key_width = local_kv * head_dim
    key_block = lax.dynamic_slice_in_dim(key_weight, first_kv * head_dim, key_width, 1)
    value_block = lax.dynamic_slice_in_dim(value_weight, first_kv * head_dim, key_width, 1)
    values = tokens.astype(jnp.float32)
    inverse_rms = lax.rsqrt(jnp.mean(values * values, axis=1, keepdims=True) + EPSILON)
    normed = (values * inverse_rms * norm_gain[None, :]).astype(jnp.bfloat16)
    local_weights = jnp.concatenate([query_weight, key_block, value_block], axis=1)
    full_weights = lax.all_gather(local_weights, "batch", axis=0, tiled=True)
    projected = jnp.dot(
        lax.all_gather(normed, "weight", axis=0, tiled=True),
        full_weights,
        preferred_element_type=jnp.float32,
    )
    query_part = projected[:, :query_cols]
    key_rows = projected[:, query_cols : query_cols + key_width].astype(jnp.bfloat16)
    value_rows = projected[:, query_cols + key_width :].astype(jnp.bfloat16)
    pack_rows = projected.shape[0]
    positions = positions_in_segment(segment_ids)
    queries = rotate(query_part.reshape(pack_rows, heads_dev, head_dim), positions).astype(
        jnp.bfloat16
    )
    rotated_keys = rotate(
        key_rows.astype(jnp.float32).reshape(pack_rows, local_kv, head_dim), positions
    ).astype(jnp.bfloat16)
    grouped = queries.reshape(pack_rows, local_kv, heads_dev // local_kv, head_dim)
    attended = attend(
        grouped, rotated_keys, value_rows.reshape(pack_rows, local_kv, head_dim), segment_ids
    )
    return attended.reshape(pack_rows, query_cols)


def solution(mesh):
    placed = (
        P(("batch", "weight"), None),
        P("batch"),
        P(),
        P("batch", "weight"),
        P("batch", None),
        P("batch", None),
    )
    return jax.shard_map(
        per_device, mesh=mesh, in_specs=placed, out_specs=P("batch", "weight"), check_vma=False
    )
```

profile of v0, /device:TPU:7, one launch (start us, length us, event | category | flops | bytes accessed | tf_op | source)
XLA Modules:
  0.0 284.0 jit_solution(18422892970738844618)
XLA Ops:
  6.5 0.0 all-gather.3.cloned.1.call-start
  6.5 1.2 fusion.7
  7.8 2.0 fusion.9
  9.8 0.0 all-gather.3.cloned.1.call-update
  9.9 0.0 all-gather.5.cloned.1.call-start
  9.9 0.9 constant_dynamic-slice_fusion
  10.8 1.7 pad_maximum_fusion
  12.6 0.0 all-gather.5.cloned.1.call-update
  12.6 1.3 slice.39
  14.5 0.8 select_bitcast_fusion
  15.3 0.3 reduce-window.9
  15.7 0.1 slice.41
  15.8 0.1 slice_reduce_fusion
  15.9 0.1 fusion.28
  16.0 1.0 fusion.10
  16.9 1.0 multiply_cosine_fusion
  17.9 54.5 %all-gather.3.cloned.1.call-done = bf16[512,8192]{1,0:T(8,128)(2,1)} async-done(((bf16[32,8192]{1,0:T(8,128)(2,1)}), bf16[512,8192]{1,0:T(8,128)(2,1)}) %all-gather.3.cloned.1.call-update) | async-done | bytes 8388624 | tf_op jit(solution)/shard_map/all_gather | solution.py:70
  72.4 183.2 %all-gather.5.cloned.1.call-done = bf16[8192,768]{1,0:T(8,128)(2,1)} async-done(((bf16[256,768]{1,0:T(8,128)(2,1)}), bf16[8192,768]{1,0:T(8,128)(2,1)}) %all-gather.5.cloned.1.call-update) | async-done | bytes 12582928 | tf_op jit(solution)/shard_map/all_gather | solution.py:68
  255.5 13.4 %fusion.33 = (bf16[512,768]{1,0:T(8,128)(2,1)}, f32[512,768]{1,0:T(8,128)S(1)}) fusion(bf16[512,8192]{1,0:T(8,128)(2,1)} %all-gather.3.cloned.1.call-done, bf16[8192,768]{1,0:T(8,128)(2,1)} %all-gather.5.cloned.1.call-done), kind=kOutput, calls=%fused_computation.54 | convolution fusion | flops 6442844160 | bytes 23330816 | tf_op jit(solution)/shard_map/dot_general | solution.py:69
  269.0 0.1 slice.51
  269.1 0.4 reshape.192
  269.5 0.6 fusion.32
  270.1 0.9 fusion.23
  271.0 1.2 fusion.27
  272.2 0.3 subtract_convert_fusion
  272.5 1.5 fusion
  274.0 2.2 fusion.4
  276.2 1.0 copy.16
  (3 shorter events, 0.1 us)
Async XLA Ops:
  6.5 65.8 %all-gather.3.cloned.1.call-start = ((), (), s32[]{:S(2)}) async-start(), calls=%async_computation | async-start | bytes 8912896 | tf_op jit(solution)/shard_map/all_gather | solution.py:70
  9.9 245.7 %all-gather.5.cloned.1.call-start = ((), (), s32[]{:S(2)}) async-start(), calls=%async_computation.1 | async-start | bytes 12976128 | tf_op jit(solution)/shard_map/all_gather | solution.py:68
Sparse Core Ops, SparseCore 0:
  10.0 62.3 all-gather.2
  75.5 179.9 all-gather.4
where the time goes:
time: 285 us; the launch traced here: 284 us
  waiting for transfers between devices  238 us (84%)
  matrix products  17.1 us (6%)
  between operations  14.2 us (5%)
  other arithmetic  10.7 us (4%)
  local copies, waits for them, and re-layouts  4.42 us (2%)
    all_gather x1, waiting for transfers between devices, per_device(): full_weights = lax.all_gather(local_weights, 'batch', axis=0, tiled=True)  183 us
    all_gather x1, waiting for transfers between devices, per_device(): lax.all_gather(normed, 'weight', axis=0, tiled=True)  54.5 us
    dot_general x1, matrix products, per_device(): jnp.dot(lax.all_gather(normed, 'weight', axis=0, tiled=True), full_weight...  13.4 us
  transfers between devices with their start and end apart: 2, of which 2 were waited for; matrix products, arithmetic and copies ran while one was open for 3% of the time, Pallas kernels for 0%

commit v1 on v0

--- a/solution.py
+++ b/solution.py
@@ -3,6 +3,7 @@
 import jax
 import jax.numpy as jnp
 from jax import lax
+from jax.sharding import Mesh
 from jax.sharding import PartitionSpec as P
 
 HEADS = 64
@@ -12,6 +13,8 @@
 
 ROPE_BASE = 500000.0
 EPSILON = 1e-05
+
+Z, YH, WC, CORE = "z", "yh", "wc", "core"
 
 
 def positions_in_segment(seg_ids):
@@ -56,25 +59,32 @@
     query_cols = query_weight.shape[1]
     heads_dev = query_cols // head_dim
     group_size = HEADS // KV_HEADS
-    local_kv = max(1, heads_dev // group_size)
-    first_kv = lax.axis_index("weight") * heads_dev // group_size
-    key_width = local_kv * head_dim
-    key_block = lax.dynamic_slice_in_dim(key_weight, first_kv * head_dim, key_width, 1)
-    value_block = lax.dynamic_slice_in_dim(value_weight, first_kv * head_dim, key_width, 1)
+    core = lax.axis_index(CORE)
+    n_core = lax.psum(1, CORE)
+    first_kv = (lax.axis_index(WC) * n_core + core) * heads_dev // group_size
+    key_block = lax.dynamic_slice_in_dim(key_weight, first_kv * head_dim, head_dim, 1)
+    value_block = lax.dynamic_slice_in_dim(value_weight, first_kv * head_dim, head_dim, 1)
+    kv_block = jnp.where(core == 0, key_block, value_block)
     values = tokens.astype(jnp.float32)
     inverse_rms = lax.rsqrt(jnp.mean(values * values, axis=1, keepdims=True) + EPSILON)
     normed = (values * inverse_rms * norm_gain[None, :]).astype(jnp.bfloat16)
-    local_weights = jnp.concatenate([query_weight, key_block, value_block], axis=1)
-    full_weights = lax.all_gather(local_weights, "batch", axis=0, tiled=True)
+    local_weights = jnp.concatenate([query_weight, kv_block], axis=1)
+    full_weights = lax.all_gather(
+        lax.all_gather(local_weights, YH, axis=0, tiled=True), Z, axis=0, tiled=True
+    )
+    gathered = lax.all_gather(lax.all_gather(normed, WC, axis=0), CORE, axis=0)
+    pack_rows = gathered.shape[0] * gathered.shape[1] * gathered.shape[2]
     projected = jnp.dot(
-        lax.all_gather(normed, "weight", axis=0, tiled=True),
-        full_weights,
-        preferred_element_type=jnp.float32,
+        gathered.reshape(pack_rows, -1), full_weights, preferred_element_type=jnp.float32
     )
+    projected = projected.reshape(gathered.shape[0], gathered.shape[1], gathered.shape[2], -1)
+    projected = jnp.swapaxes(projected, 0, 1).reshape(pack_rows, -1)
     query_part = projected[:, :query_cols]
-    key_rows = projected[:, query_cols : query_cols + key_width].astype(jnp.bfloat16)
-    value_rows = projected[:, query_cols + key_width :].astype(jnp.bfloat16)
-    pack_rows = projected.shape[0]
+    own_rows = projected[:, query_cols:].astype(jnp.bfloat16)
+    other_rows = lax.ppermute(own_rows, CORE, perm=[(0, 1), (1, 0)])
+    key_rows = jnp.where(core == 0, own_rows, other_rows)
+    value_rows = jnp.where(core == 0, other_rows, own_rows)
+    local_kv = 1
     positions = positions_in_segment(segment_ids)
     queries = rotate(query_part.reshape(pack_rows, heads_dev, head_dim), positions).astype(
         jnp.bfloat16
@@ -89,15 +99,24 @@
     return attended.reshape(pack_rows, query_cols)
 
 
+def split_mesh(mesh):
+    n_batch, n_weight = mesh.devices.shape
+    yh = n_batch // 8 if n_batch % 8 == 0 else 1
+    devices = mesh.devices.reshape(n_batch // yh, yh, n_weight // 2, 2)
+    return Mesh(devices, (Z, YH, WC, CORE))
+
+
 def solution(mesh):
+    fine = split_mesh(mesh)
+    batch, weight = (Z, YH), (WC, CORE)
     placed = (
-        P(("batch", "weight"), None),
-        P("batch"),
+        P(batch + weight, None),
+        P(batch),
         P(),
-        P("batch", "weight"),
-        P("batch", None),
-        P("batch", None),
+        P(batch, weight),
+        P(batch, None),
+        P(batch, None),
     )
     return jax.shard_map(
-        per_device, mesh=mesh, in_specs=placed, out_specs=P("batch", "weight"), check_vma=False
+        per_device, mesh=fine, in_specs=placed, out_specs=P(batch, weight), check_vma=False
     )

time: 285 us -> 339 us (1.19)
  waiting for transfers between devices: 238 us -> 286 us
    all_gather x2 -> x4, waiting for transfers between devices: 238 us -> 286 us  [the longest x2 121 us: per_device(): gathered = lax.all_gather(lax.all_gather(normed, WC, axis=0), CORE, axis=0)]
  transfers between devices with their start and end apart: 2 -> 5, of which waited for: 2 -> 4; matrix products, arithmetic and copies ran while one was open for 3% -> 2% of each run, Pallas kernels for 0% -> 0%
where the time goes in v1:
time: 339 us; the launch traced here: 337 us
  waiting for transfers between devices  286 us (84%)
  matrix products  18.2 us (5%)
  between operations  13.9 us (4%)
  other arithmetic  11.7 us (3%)
  local copies, waits for them, and re-layouts  4.85 us (1%)
    all_gather x2, waiting for transfers between devices, per_device(): gathered = lax.all_gather(lax.all_gather(normed, WC, axis=0), CORE, axis=0)  121 us
    all_gather x1, waiting for transfers between devices, per_device(): lax.all_gather(lax.all_gather(local_weights, YH, axis=0, tiled=True), Z,...  120 us
    all_gather x1, waiting for transfers between devices, per_device(): lax.all_gather(local_weights, YH, axis=0, tiled=True)  44.3 us
    dot_general x1, matrix products, per_device(): jnp.dot(gathered.reshape(pack_rows, -1), full_weights, preferred_element_...  15.4 us
  transfers between devices with their start and end apart: 5, of which 4 were waited for; matrix products, arithmetic and copies ran while one was open for 2% of the time, Pallas kernels for 0%

profile of v1, /device:TPU:7, one launch (start us, length us, event | category | flops | bytes accessed | tf_op | source)
XLA Modules:
  0.0 337.4 jit_solution(9586149501234721951)
XLA Ops:
  6.5 0.0 all-gather.11.cloned.1.call-start
  6.5 1.2 fusion.12
  7.8 0.0 copy-start.1
  7.8 2.0 fusion.14
  9.8 0.0 all-gather.11.cloned.1.call-update
  9.9 0.0 all-gather.7.cloned.1.call-start
  9.9 0.9 dynamic-slice_select_fusion
  10.8 1.7 pad_maximum_fusion
  12.5 0.0 all-gather.7.cloned.1.call-update
  12.6 0.0 all-gather.13.cloned.1.call-start
  12.6 97.1 %all-gather.11.cloned.1.call-done = bf16[256,8192]{1,0:T(8,128)(2,1)} async-done(((bf16[32,8192]{1,0:T(8,128)(2,1)}), bf16[256,8192]{1,0:T(8,128)(2,1)}) %all-gather.11.cloned.1.call-update) | async-done | bytes 4194320 | tf_op jit(solution)/shard_map/all_gather | solution.py:75
  109.7 0.0 all-gather.13.cloned.1.call-update
  109.7 0.0 all-gather.9.cloned.1.call-start
  109.7 44.3 %all-gather.7.cloned.1.call-done = bf16[1024,640]{1,0:T(8,128)(2,1)} async-done(((bf16[256,640]{1,0:T(8,128)(2,1)}), bf16[1024,640]{1,0:T(8,128)(2,1)}) %all-gather.7.cloned.1.call-update) | async-done | bytes 1310736 | tf_op jit(solution)/shard_map/all_gather | solution.py:73
  154.1 0.0 all-gather.9.cloned.1.call-update
  154.1 0.0 copy-done.1
  154.1 0.5 slice.34
  155.3 0.1 select_bitcast_fusion
  155.3 0.3 reduce-window.9
  155.6 0.1 slice.36
  155.8 0.1 slice_reduce_fusion
  155.9 0.1 fusion.35
  156.0 0.9 fusion.15
  156.9 1.8 multiply_cosine_fusion
  158.7 24.3 %all-gather.13.cloned.1.call-done = bf16[16,32,8192]{2,1,0:T(8,128)(2,1)} async-done(((bf16[8,32,8192]{2,1,0:T(8,128)(2,1)}), bf16[16,32,8192]{2,1,0:T(8,128)(2,1)}) %all-gather.13.cloned.1.call-update) | async-done | bytes 8388624 | tf_op jit(solution)/shard_map/all_gather | solution.py:75
  183.0 120.1 %all-gather.9.cloned.1.call-done = bf16[8192,640]{1,0:T(8,128)(2,1)} async-done(((bf16[1024,640]{1,0:T(8,128)(2,1)}), bf16[8192,640]{1,0:T(8,128)(2,1)}) %all-gather.9.cloned.1.call-update) | async-done | bytes 10485776 | tf_op jit(solution)/shard_map/all_gather | solution.py:72
  303.1 15.4 %fusion.6 = f32[8,2,32,640]{3,2,0,1:T(8,128)S(1)} fusion(bf16[2,8,32,8192]{3,2,1,0:T(8,128)(2,1)} %bitcast.67, bf16[8192,640]{1,0:T(8,128)(2,1)} %all-gather.9.cloned.1.call-done), kind=kOutput, calls=%fused_computation.8 | convolution fusion | flops 5368709120 | bytes 20185088 | tf_op jit(solution)/shard_map/dot_general | solution.py:77
  318.5 0.1 copy.17
  318.6 0.1 slice.45
  318.8 0.3 copy.18
  319.1 0.9 fusion.39
  320.0 0.3 copy.29
  320.3 1.4 copy.28
  321.7 0.0 copy-start
  321.7 2.7 collective-permute-start
  324.5 1.3 subtract_convert_fusion
  325.8 0.0 collective-permute-done
  325.8 1.2 fusion.33
  327.0 0.0 copy-done
  327.0 1.4 fusion.2
  328.5 1.3 fusion.9
  329.8 1.0 copy.23
  (5 shorter events, 0.1 us)
Async XLA Ops:
  6.5 103.1 %all-gather.11.cloned.1.call-start = ((), (), s32[]{:S(2)}) async-start(), calls=%async_computation.2 | async-start | bytes 4718592 | tf_op jit(solution)/shard_map/all_gather | solution.py:75
  7.8 146.3 %copy-start.1 = (s32[512]{0:T(512)S(1)}, s32[512]{0:T(512)}, u32[]{:S(2)}) copy-start(s32[512]{0:T(512)} %param.7) | copy-start | bytes 6148
  9.9 144.2 %all-gather.7.cloned.1.call-start = ((), (), s32[]{:S(2)}) async-start(), calls=%async_computation | async-start | bytes 1638400 | tf_op jit(solution)/shard_map/all_gather | solution.py:73
  12.6 170.5 %all-gather.13.cloned.1.call-start = ((), (), s32[]{:S(2)}) async-start(), calls=%async_computation.3 | async-start | bytes 12582912 | tf_op jit(solution)/shard_map/all_gather | solution.py:75
  109.7 193.4 %all-gather.9.cloned.1.call-start = ((), (), s32[]{:S(2)}) async-start(), calls=%async_computation.1 | async-start | bytes 11796480 | tf_op jit(solution)/shard_map/all_gather | solution.py:72
  321.7 5.3 %copy-start = (pred[512,512]{0,1:T(8,128)(4,1)S(1)}, pred[512,512]{0,1:T(8,128)(4,1)}, u32[]{:S(2)}) copy-start(pred[512,512]{0,1:T(8,128)(4,1)} %fusion.15) | copy-start | bytes 786436
  321.7 4.0 %collective-permute-start = (bf16[512,128]{1,0:T(8,128)(2,1)S(1)}, bf16[512,128]{1,0:T(8,128)(2,1)S(1)}, u32[]{:S(2)}, u32[]{:S(2)}) collective-permute-start(bf16[512,128]{1,0:T(8,128)(2,1)S(1)} %slice.62), channel_id=1, source_target_pairs={{0,1},{1,0},{2,3},{3,2},{4,5},{5,4},{6,7},{7,6},{8,9},{9,8},{10,11... | collective-permute-start | bytes 393224 | tf_op jit(solution)/shard_map/ppermute | solution.py:84
Sparse Core Ops, SparseCore 0:
  10.0 99.6 all-gather.10
  111.8 42.2 all-gather.6
  156.2 26.8 all-gather.12
  185.0 118.0 all-gather.8

commit v2 on v0

--- a/solution.py
+++ b/solution.py
@@ -12,6 +12,8 @@
 
 ROPE_BASE = 500000.0
 EPSILON = 1e-05
+
+CHIP_CYCLE = (0, 2, 4, 6, 7, 5, 3, 1)
 
 
 def positions_in_segment(seg_ids):
@@ -51,30 +53,68 @@
     return mixed.astype(jnp.bfloat16)
 
 
+def device_cycle():
+    cycle = []
+    for i, chip in enumerate(CHIP_CYCLE):
+        cores = (0, 1) if i % 2 == 0 else (1, 0)
+        cycle += [chip * 2 + c for c in cores]
+    return cycle
+
+
+def ring_gather(block, n):
+    cycle = device_cycle()
+    where_in = [0] * n
+    for q, w in enumerate(cycle):
+        where_in[w] = q
+    to_prev = [(cycle[q], cycle[(q - 1) % n]) for q in range(n)]
+    to_next = [(cycle[q], cycle[(q + 1) % n]) for q in range(n)]
+    right, left = [], []
+    from_right, from_left = block, block
+    for step in range(1, n // 2 + 1):
+        if step < n // 2:
+            from_right = lax.ppermute(from_right, "weight", perm=to_prev)
+            right.append(from_right)
+        from_left = lax.ppermute(from_left, "weight", perm=to_next)
+        left.append(from_left)
+    slots = jnp.stack([block] + right + left)
+    me = jnp.asarray(where_in, jnp.int32)[lax.axis_index("weight")]
+    distance = (jnp.asarray(where_in, jnp.int32) - me) % n
+    slot_of = jnp.where(distance < n // 2, distance, n + n // 2 - 1 - distance)
+    return slots, slot_of
+
+
 def per_device(tokens, segment_ids, norm_gain, query_weight, key_weight, value_weight):
     head_dim = HEAD_DIM
     query_cols = query_weight.shape[1]
     heads_dev = query_cols // head_dim
     group_size = HEADS // KV_HEADS
-    local_kv = max(1, heads_dev // group_size)
-    first_kv = lax.axis_index("weight") * heads_dev // group_size
-    key_width = local_kv * head_dim
-    key_block = lax.dynamic_slice_in_dim(key_weight, first_kv * head_dim, key_width, 1)
-    value_block = lax.dynamic_slice_in_dim(value_weight, first_kv * head_dim, key_width, 1)
+    n_weight = lax.psum(1, "weight")
+    me = lax.axis_index("weight")
+    core = me % 2
+    first_kv = me * heads_dev // group_size
+    key_block = lax.dynamic_slice_in_dim(key_weight, first_kv * head_dim, head_dim, 1)
+    value_block = lax.dynamic_slice_in_dim(value_weight, first_kv * head_dim, head_dim, 1)
+    kv_block = jnp.where(core == 0, key_block, value_block)
     values = tokens.astype(jnp.float32)
     inverse_rms = lax.rsqrt(jnp.mean(values * values, axis=1, keepdims=True) + EPSILON)
     normed = (values * inverse_rms * norm_gain[None, :]).astype(jnp.bfloat16)
-    local_weights = jnp.concatenate([query_weight, key_block, value_block], axis=1)
+    local_weights = jnp.concatenate([query_weight, kv_block], axis=1)
     full_weights = lax.all_gather(local_weights, "batch", axis=0, tiled=True)
+    slots, slot_of = ring_gather(normed, n_weight)
+    block_rows = normed.shape[0]
+    pack_rows = n_weight * block_rows
     projected = jnp.dot(
-        lax.all_gather(normed, "weight", axis=0, tiled=True),
-        full_weights,
-        preferred_element_type=jnp.float32,
+        slots.reshape(pack_rows, -1), full_weights, preferred_element_type=jnp.float32
     )
+    projected = jnp.take(projected.reshape(n_weight, block_rows, -1), slot_of, axis=0)
+    projected = projected.reshape(pack_rows, -1)
     query_part = projected[:, :query_cols]
-    key_rows = projected[:, query_cols : query_cols + key_width].astype(jnp.bfloat16)
-    value_rows = projected[:, query_cols + key_width :].astype(jnp.bfloat16)
-    pack_rows = projected.shape[0]
+    own_rows = projected[:, query_cols:].astype(jnp.bfloat16)
+    partner = [(w, w ^ 1) for w in range(n_weight)]
+    other_rows = lax.ppermute(own_rows, "weight", perm=partner)
+    key_rows = jnp.where(core == 0, own_rows, other_rows)
+    value_rows = jnp.where(core == 0, other_rows, own_rows)
+    local_kv = 1
     positions = positions_in_segment(segment_ids)
     queries = rotate(query_part.reshape(pack_rows, heads_dev, head_dim), positions).astype(
         jnp.bfloat16

time: 285 us -> 236 us (0.83)
  waiting for transfers between devices: 238 us -> 29.4 us
  starting transfers between devices: 0.04 us -> 138 us
  local copies, waits for them, and re-layouts: 4.42 us -> 20.3 us
  other arithmetic: 10.7 us -> 14.7 us
    all_gather x1, waiting for transfers between devices: 183 us -> 26 us  [per_device(): full_weights = lax.all_gather(local_weights, 'batch', axis=0, tiled=True)]
    ppermute x0 -> x16, starting transfers between devices: none -> 138 us  [the longest x8 116 us: ring_gather(): from_left = lax.ppermute(from_left, 'weight', perm=to_next)]
    all_gather x1 -> x0, waiting for transfers between devices: 54.5 us -> none  [per_device(): lax.all_gather(normed, 'weight', axis=0, tiled=True)]
    unnamed x0 -> x18, local copies, waits for them, and re-layouts: none -> 13.5 us
    ppermute x0 -> x16, waiting for transfers between devices: none -> 3.38 us  [the longest x7 2.67 us: ring_gather(): from_right = lax.ppermute(from_right, 'weight', perm=to_prev)]
  transfers between devices with their start and end apart: 2 -> 17, of which waited for: 2 -> 3; matrix products, arithmetic and copies ran while one was open for 3% -> 11% of each run, Pallas kernels for 0% -> 0%
where the time goes in v2:
time: 236 us; the launch traced here: 235 us
  starting transfers between devices  138 us (58%)
  waiting for transfers between devices  29.4 us (12%)
  local copies, waits for them, and re-layouts  20.3 us (9%)
  matrix products  18.3 us (8%)
  other arithmetic  14.7 us (6%)
  between operations  14.4 us (6%)
    ppermute x8, starting transfers between devices, ring_gather(): from_left = lax.ppermute(from_left, 'weight', perm=to_next)  116 us
    all_gather x1, waiting for transfers between devices, per_device(): full_weights = lax.all_gather(local_weights, 'batch', axis=0, tiled=True)  26 us
    ppermute x7, starting transfers between devices, ring_gather(): from_right = lax.ppermute(from_right, 'weight', perm=to_prev)  18.4 us
    dot_general x1, matrix products, per_device(): jnp.dot(slots.reshape(pack_rows, -1), full_weights, preferred_element_typ...  14.5 us
    unnamed x18, local copies, waits for them, and re-layouts  13.5 us
  transfers between devices with their start and end apart: 17, of which 3 were waited for; matrix products, arithmetic and copies ran while one was open for 11% of the time, Pallas kernels for 0%

profile of v2, /device:TPU:7, one launch (start us, length us, event | category | flops | bytes accessed | tf_op | source)
XLA Modules:
  0.0 234.7 jit_solution(5840181406514222191)
XLA Ops:
  6.5 1.2 fusion.9
  7.8 2.1 bitcast_dynamic-update-slice_fusion.15
  9.9 2.4 %collective-permute-start = (bf16[32,8192]{1,0:T(8,128)(2,1)S(1)}, bf16[32,8192]{1,0:T(8,128)(2,1)S(1)}, u32[]{:S(2)}, u32[]{:S(2)}) collective-permute-start(bf16[32,8192]{1,0:T(8,128)(2,1)S(1)} %get-tuple-element.8), channel_id=1, source_target_pairs={{0,2},{1,0},{5,1},{4,5},{8,4},{9,8},{13,9},{12,13},{14,12},{15,14}... | collective-permute-start | bytes 1572872 | tf_op jit(solution)/shard_map/ppermute | solution.py:75
  12.3 2.0 collective-permute-start.7
  14.4 0.9 dynamic-slice_select_fusion
  15.3 1.7 pad_maximum_fusion
  17.0 1.3 dynamic_slice.9
  18.3 1.3 compare_and_fusion
  19.7 1.3 slice.34
  21.6 0.8 select_bitcast_fusion
  23.2 1.7 fusion.12
  24.9 1.8 multiply_cosine_fusion
  26.7 3.2 %collective-permute-start.1 = (bf16[32,8192]{1,0:T(8,128)(2,1)S(1)}, bf16[32,8192]{1,0:T(8,128)(2,1)S(1)}, u32[]{:S(2)}, u32[]{:S(2)}) collective-permute-start(bf16[32,8192]{1,0:T(8,128)(2,1)S(1)} %collective-permute-done), channel_id=1, source_target_pairs={{0,2},{1,0},{5,1},{4,5},{8,4},{9,8},{13,9},{12,13},{14,12},{15,14}... | collective-permute-start | bytes 1572872 | tf_op jit(solution)/shard_map/ppermute | solution.py:75
  30.0 2.6 %collective-permute-start.8 = (bf16[32,8192]{1,0:T(8,128)(2,1)S(1)}, bf16[32,8192]{1,0:T(8,128)(2,1)S(1)}, u32[]{:S(2)}, u32[]{:S(2)}) collective-permute-start(bf16[32,8192]{1,0:T(8,128)(2,1)S(1)} %collective-permute-done.7), channel_id=1, source_target_pairs={{0,1},{1,5},{5,4},{4,8},{8,9},{9,13},{13,12},{12,14},{14,15},{15,1... | collective-permute-start | bytes 1572872 | tf_op jit(solution)/shard_map/ppermute | solution.py:77
  33.4 2.6 %collective-permute-done.1 = bf16[32,8192]{1,0:T(8,128)(2,1)S(1)} collective-permute-done((bf16[32,8192]{1,0:T(8,128)(2,1)S(1)}, bf16[32,8192]{1,0:T(8,128)(2,1)S(1)}, u32[]{:S(2)}, u32[]{:S(2)}) %collective-permute-start.1) | collective-permute-done | bytes 524320 | tf_op jit(solution)/shard_map/ppermute | solution.py:75
  36.1 4.1 %collective-permute-start.2 = (bf16[32,8192]{1,0:T(8,128)(2,1)S(1)}, bf16[32,8192]{1,0:T(8,128)(2,1)S(1)}, u32[]{:S(2)}, u32[]{:S(2)}) collective-permute-start(bf16[32,8192]{1,0:T(8,128)(2,1)S(1)} %collective-permute-done.1), channel_id=1, source_target_pairs={{0,2},{1,0},{5,1},{4,5},{8,4},{9,8},{13,9},{12,13},{14,12},{15,14}... | collective-permute-start | bytes 1572872 | tf_op jit(solution)/shard_map/ppermute | solution.py:75
  40.2 6.5 %collective-permute-start.9 = (bf16[32,8192]{1,0:T(8,128)(2,1)S(1)}, bf16[32,8192]{1,0:T(8,128)(2,1)S(1)}, u32[]{:S(2)}, u32[]{:S(2)}) collective-permute-start(bf16[32,8192]{1,0:T(8,128)(2,1)S(1)} %collective-permute-done.8), channel_id=1, source_target_pairs={{0,1},{1,5},{5,4},{4,8},{8,9},{9,13},{13,12},{12,14},{14,15},{15,1... | collective-permute-start | bytes 1572872 | tf_op jit(solution)/shard_map/ppermute | solution.py:77
  46.7 0.8 bitcast_dynamic-update-slice_fusion.13
  47.6 2.9 %collective-permute-start.3 = (bf16[32,8192]{1,0:T(8,128)(2,1)S(1)}, bf16[32,8192]{1,0:T(8,128)(2,1)S(1)}, u32[]{:S(2)}, u32[]{:S(2)}) collective-permute-start(bf16[32,8192]{1,0:T(8,128)(2,1)S(1)} %collective-permute-done.2), channel_id=1, source_target_pairs={{0,2},{1,0},{5,1},{4,5},{8,4},{9,8},{13,9},{12,13},{14,12},{15,14}... | collective-permute-start | bytes 1572872 | tf_op jit(solution)/shard_map/ppermute | solution.py:75
  50.5 10.9 %collective-permute-start.10 = (bf16[32,8192]{1,0:T(8,128)(2,1)S(1)}, bf16[32,8192]{1,0:T(8,128)(2,1)S(1)}, u32[]{:S(2)}, u32[]{:S(2)}) collective-permute-start(bf16[32,8192]{1,0:T(8,128)(2,1)S(1)} %collective-permute-done.9), channel_id=1, source_target_pairs={{0,1},{1,5},{5,4},{4,8},{8,9},{9,13},{13,12},{12,14},{14,15},{15,1... | collective-permute-start | bytes 1572872 | tf_op jit(solution)/shard_map/ppermute | solution.py:77
  61.4 0.8 bitcast_dynamic-update-slice_fusion.12
  62.2 1.9 collective-permute-start.4
  64.2 8.3 %collective-permute-start.11 = (bf16[32,8192]{1,0:T(8,128)(2,1)S(1)}, bf16[32,8192]{1,0:T(8,128)(2,1)S(1)}, u32[]{:S(2)}, u32[]{:S(2)}) collective-permute-start(bf16[32,8192]{1,0:T(8,128)(2,1)S(1)} %collective-permute-done.10), channel_id=1, source_target_pairs={{0,1},{1,5},{5,4},{4,8},{8,9},{9,13},{13,12},{12,14},{14,15},{15,1... | collective-permute-start | bytes 1572872 | tf_op jit(solution)/shard_map/ppermute | solution.py:77
  72.5 0.9 bitcast_dynamic-update-slice_fusion.11
  73.3 1.9 collective-permute-start.5
  75.2 8.3 %collective-permute-start.12 = (bf16[32,8192]{1,0:T(8,128)(2,1)S(1)}, bf16[32,8192]{1,0:T(8,128)(2,1)S(1)}, u32[]{:S(2)}, u32[]{:S(2)}) collective-permute-start(bf16[32,8192]{1,0:T(8,128)(2,1)S(1)} %collective-permute-done.11), channel_id=1, source_target_pairs={{0,1},{1,5},{5,4},{4,8},{8,9},{9,13},{13,12},{12,14},{14,15},{15,1... | collective-permute-start | bytes 1572872 | tf_op jit(solution)/shard_map/ppermute | solution.py:77
  83.5 0.9 bitcast_dynamic-update-slice_fusion.10
  84.4 1.9 collective-permute-start.6
  86.3 45.2 %collective-permute-start.13 = (bf16[32,8192]{1,0:T(8,128)(2,1)S(1)}, bf16[32,8192]{1,0:T(8,128)(2,1)S(1)}, u32[]{:S(2)}, u32[]{:S(2)}) collective-permute-start(bf16[32,8192]{1,0:T(8,128)(2,1)S(1)} %collective-permute-done.12), channel_id=1, source_target_pairs={{0,1},{1,5},{5,4},{4,8},{8,9},{9,13},{13,12},{12,14},{14,15},{15,1... | collective-permute-start | bytes 1572872 | tf_op jit(solution)/shard_map/ppermute | solution.py:77
  131.6 0.8 bitcast_dynamic-update-slice_fusion.9
  133.1 31.8 %collective-permute-start.14 = (bf16[32,8192]{1,0:T(8,128)(2,1)S(1)}, bf16[32,8192]{1,0:T(8,128)(2,1)S(1)}, u32[]{:S(2)}, u32[]{:S(2)}) collective-permute-start(bf16[32,8192]{1,0:T(8,128)(2,1)S(1)} %collective-permute-done.13), channel_id=1, source_target_pairs={{0,1},{1,5},{5,4},{4,8},{8,9},{9,13},{13,12},{12,14},{14,15},{15,1... | collective-permute-start | bytes 1572872 | tf_op jit(solution)/shard_map/ppermute | solution.py:77
  166.6 0.9 bitcast_dynamic-update-slice_fusion.6
  167.4 0.9 bitcast_dynamic-update-slice_fusion.5
  168.3 0.9 bitcast_dynamic-update-slice_fusion.4
  169.2 0.8 bitcast_dynamic-update-slice_fusion.3
  170.0 0.8 bitcast_dynamic-update-slice_fusion.2
  170.8 0.8 bitcast_dynamic-update-slice_fusion.1
  171.7 0.8 bitcast_dynamic-update-slice_fusion
  172.5 26.0 %all-gather.2.cloned.1.call-done = bf16[8192,640]{1,0:T(8,128)(2,1)} async-done(((bf16[256,640]{1,0:T(8,128)(2,1)}), bf16[8192,640]{1,0:T(8,128)(2,1)}) %all-gather.2.cloned.1.call-update) | async-done | bytes 10485776 | tf_op jit(solution)/shard_map/all_gather | solution.py:102
  198.5 14.5 %fusion = f32[16,32,640]{2,1,0:T(8,128)S(1)} fusion(bf16[16,32,8192]{2,1,0:T(8,128)(2,1)} %bitcast_dynamic-update-slice_fusion, bf16[8192,640]{1,0:T(8,128)(2,1)} %all-gather.2.cloned.1.call-done), kind=kOutput, calls=%fused_computation.1 | convolution fusion | flops 5368709120 | bytes 20185088 | tf_op jit(solution)/shard_map/dot_general | solution.py:106
  214.4 0.9 fusion.38
  215.6 1.4 copy.21
  217.0 3.5 %collective-permute-start.15 = (bf16[512,128]{1,0:T(8,128)(2,1)S(1)}, bf16[512,128]{1,0:T(8,128)(2,1)S(1)}, u32[]{:S(2)}, u32[]{:S(2)}) collective-permute-start(bf16[512,128]{1,0:T(8,128)(2,1)S(1)} %slice.64), channel_id=1, source_target_pairs={{0,1},{1,0},{2,3},{3,2},{4,5},{5,4},{6,7},{7,6},{8,9},{9,8},{10,11... | collective-permute-start | bytes 393224 | tf_op jit(solution)/shard_map/ppermute | solution.py:114
  220.5 1.3 subtract_convert_fusion
  221.8 1.2 fusion.30
  223.1 2.4 %fusion.2 = (f32[4,512]{1,0:T(4,128)S(1)}, f32[512,512,4]{1,0,2:T(8,128)S(1)}) fusion(pred[512,512]{0,1:T(8,128)(4,1)} %fusion.12, bf16[512,4,64]{2,0,1:T(8,128)(2,1)S(1)} %get-tuple-element.10, bf16[512,4,64]{2,0,1:T(8,128)(2,1)S(1)} %get-tuple-element.9, bf16[512,64]{1,0:T(8,128)(2,1)S(1)} %get-tuple-element.14, bf16[512,64]{1,0:T(8,128)(2,1)S(1)} %get-tuple-element.13), kind=kOutput, calls=%fused_computation.5 | convolution fusion | flops 272889856 | bytes 5120000 | tf_op jit(solution)/shard_map/ingd,jnd->ngij/dot_general | solution.py:43
  225.5 1.3 fusion.6
  226.8 1.0 copy.17
  (39 shorter events, 5.6 us)
Async XLA Ops:
  6.5 192.0 %all-gather.2.cloned.1.call-start = ((), (), s32[]{:S(2)}) async-start(), calls=%async_computation | async-start | bytes 10813440 | tf_op jit(solution)/shard_map/all_gather | solution.py:102
  9.9 16.9 %collective-permute-start = (bf16[32,8192]{1,0:T(8,128)(2,1)S(1)}, bf16[32,8192]{1,0:T(8,128)(2,1)S(1)}, u32[]{:S(2)}, u32[]{:S(2)}) collective-permute-start(bf16[32,8192]{1,0:T(8,128)(2,1)S(1)} %get-tuple-element.8), channel_id=1, source_target_pairs={{0,2},{1,0},{5,1},{4,5},{8,4},{9,8},{13,9},{12,13},{14,12},{15,14}... | collective-permute-start | bytes 1572872 | tf_op jit(solution)/shard_map/ppermute | solution.py:75
  12.3 17.6 %collective-permute-start.7 = (bf16[32,8192]{1,0:T(8,128)(2,1)S(1)}, bf16[32,8192]{1,0:T(8,128)(2,1)S(1)}, u32[]{:S(2)}, u32[]{:S(2)}) collective-permute-start(bf16[32,8192]{1,0:T(8,128)(2,1)S(1)} %get-tuple-element.8), channel_id=1, source_target_pairs={{0,1},{1,5},{5,4},{4,8},{8,9},{9,13},{13,12},{12,14},{14,15},{15,1... | collective-permute-start | bytes 1572872 | tf_op jit(solution)/shard_map/ppermute | solution.py:77
  26.7 9.3 %collective-permute-start.1 = (bf16[32,8192]{1,0:T(8,128)(2,1)S(1)}, bf16[32,8192]{1,0:T(8,128)(2,1)S(1)}, u32[]{:S(2)}, u32[]{:S(2)}) collective-permute-start(bf16[32,8192]{1,0:T(8,128)(2,1)S(1)} %collective-permute-done), channel_id=1, source_target_pairs={{0,2},{1,0},{5,1},{4,5},{8,4},{9,8},{13,9},{12,13},{14,12},{15,14}... | collective-permute-start | bytes 1572872 | tf_op jit(solution)/shard_map/ppermute | solution.py:75
  30.0 10.2 %collective-permute-start.8 = (bf16[32,8192]{1,0:T(8,128)(2,1)S(1)}, bf16[32,8192]{1,0:T(8,128)(2,1)S(1)}, u32[]{:S(2)}, u32[]{:S(2)}) collective-permute-start(bf16[32,8192]{1,0:T(8,128)(2,1)S(1)} %collective-permute-done.7), channel_id=1, source_target_pairs={{0,1},{1,5},{5,4},{4,8},{8,9},{9,13},{13,12},{12,14},{14,15},{15,1... | collective-permute-start | bytes 1572872 | tf_op jit(solution)/shard_map/ppermute | solution.py:77
  36.1 11.5 %collective-permute-start.2 = (bf16[32,8192]{1,0:T(8,128)(2,1)S(1)}, bf16[32,8192]{1,0:T(8,128)(2,1)S(1)}, u32[]{:S(2)}, u32[]{:S(2)}) collective-permute-start(bf16[32,8192]{1,0:T(8,128)(2,1)S(1)} %collective-permute-done.1), channel_id=1, source_target_pairs={{0,2},{1,0},{5,1},{4,5},{8,4},{9,8},{13,9},{12,13},{14,12},{15,14}... | collective-permute-start | bytes 1572872 | tf_op jit(solution)/shard_map/ppermute | solution.py:75
  40.2 10.3 %collective-permute-start.9 = (bf16[32,8192]{1,0:T(8,128)(2,1)S(1)}, bf16[32,8192]{1,0:T(8,128)(2,1)S(1)}, u32[]{:S(2)}, u32[]{:S(2)}) collective-permute-start(bf16[32,8192]{1,0:T(8,128)(2,1)S(1)} %collective-permute-done.8), channel_id=1, source_target_pairs={{0,1},{1,5},{5,4},{4,8},{8,9},{9,13},{13,12},{12,14},{14,15},{15,1... | collective-permute-start | bytes 1572872 | tf_op jit(solution)/shard_map/ppermute | solution.py:77
  47.6 14.7 %collective-permute-start.3 = (bf16[32,8192]{1,0:T(8,128)(2,1)S(1)}, bf16[32,8192]{1,0:T(8,128)(2,1)S(1)}, u32[]{:S(2)}, u32[]{:S(2)}) collective-permute-start(bf16[32,8192]{1,0:T(8,128)(2,1)S(1)} %collective-permute-done.2), channel_id=1, source_target_pairs={{0,2},{1,0},{5,1},{4,5},{8,4},{9,8},{13,9},{12,13},{14,12},{15,14}... | collective-permute-start | bytes 1572872 | tf_op jit(solution)/shard_map/ppermute | solution.py:75
  50.5 13.6 %collective-permute-start.10 = (bf16[32,8192]{1,0:T(8,128)(2,1)S(1)}, bf16[32,8192]{1,0:T(8,128)(2,1)S(1)}, u32[]{:S(2)}, u32[]{:S(2)}) collective-permute-start(bf16[32,8192]{1,0:T(8,128)(2,1)S(1)} %collective-permute-done.9), channel_id=1, source_target_pairs={{0,1},{1,5},{5,4},{4,8},{8,9},{9,13},{13,12},{12,14},{14,15},{15,1... | collective-permute-start | bytes 1572872 | tf_op jit(solution)/shard_map/ppermute | solution.py:77
  62.2 11.1 %collective-permute-start.4 = (bf16[32,8192]{1,0:T(8,128)(2,1)S(1)}, bf16[32,8192]{1,0:T(8,128)(2,1)S(1)}, u32[]{:S(2)}, u32[]{:S(2)}) collective-permute-start(bf16[32,8192]{1,0:T(8,128)(2,1)S(1)} %collective-permute-done.3), channel_id=1, source_target_pairs={{0,2},{1,0},{5,1},{4,5},{8,4},{9,8},{13,9},{12,13},{14,12},{15,14}... | collective-permute-start | bytes 1572872 | tf_op jit(solution)/shard_map/ppermute | solution.py:75
  64.2 11.1 %collective-permute-start.11 = (bf16[32,8192]{1,0:T(8,128)(2,1)S(1)}, bf16[32,8192]{1,0:T(8,128)(2,1)S(1)}, u32[]{:S(2)}, u32[]{:S(2)}) collective-permute-start(bf16[32,8192]{1,0:T(8,128)(2,1)S(1)} %collective-permute-done.10), channel_id=1, source_target_pairs={{0,1},{1,5},{5,4},{4,8},{8,9},{9,13},{13,12},{12,14},{14,15},{15,1... | collective-permute-start | bytes 1572872 | tf_op jit(solution)/shard_map/ppermute | solution.py:77
  73.3 11.1 %collective-permute-start.5 = (bf16[32,8192]{1,0:T(8,128)(2,1)S(1)}, bf16[32,8192]{1,0:T(8,128)(2,1)S(1)}, u32[]{:S(2)}, u32[]{:S(2)}) collective-permute-start(bf16[32,8192]{1,0:T(8,128)(2,1)S(1)} %collective-permute-done.4), channel_id=1, source_target_pairs={{0,2},{1,0},{5,1},{4,5},{8,4},{9,8},{13,9},{12,13},{14,12},{15,14}... | collective-permute-start | bytes 1572872 | tf_op jit(solution)/shard_map/ppermute | solution.py:75
  75.2 11.1 %collective-permute-start.12 = (bf16[32,8192]{1,0:T(8,128)(2,1)S(1)}, bf16[32,8192]{1,0:T(8,128)(2,1)S(1)}, u32[]{:S(2)}, u32[]{:S(2)}) collective-permute-start(bf16[32,8192]{1,0:T(8,128)(2,1)S(1)} %collective-permute-done.11), channel_id=1, source_target_pairs={{0,1},{1,5},{5,4},{4,8},{8,9},{9,13},{13,12},{12,14},{14,15},{15,1... | collective-permute-start | bytes 1572872 | tf_op jit(solution)/shard_map/ppermute | solution.py:77
  84.4 80.5 %collective-permute-start.6 = (bf16[32,8192]{1,0:T(8,128)(2,1)S(1)}, bf16[32,8192]{1,0:T(8,128)(2,1)S(1)}, u32[]{:S(2)}, u32[]{:S(2)}) collective-permute-start(bf16[32,8192]{1,0:T(8,128)(2,1)S(1)} %collective-permute-done.5), channel_id=1, source_target_pairs={{0,2},{1,0},{5,1},{4,5},{8,4},{9,8},{13,9},{12,13},{14,12},{15,14}... | collective-permute-start | bytes 1572872 | tf_op jit(solution)/shard_map/ppermute | solution.py:75
  86.3 46.8 %collective-permute-start.13 = (bf16[32,8192]{1,0:T(8,128)(2,1)S(1)}, bf16[32,8192]{1,0:T(8,128)(2,1)S(1)}, u32[]{:S(2)}, u32[]{:S(2)}) collective-permute-start(bf16[32,8192]{1,0:T(8,128)(2,1)S(1)} %collective-permute-done.12), channel_id=1, source_target_pairs={{0,1},{1,5},{5,4},{4,8},{8,9},{9,13},{13,12},{12,14},{14,15},{15,1... | collective-permute-start | bytes 1572872 | tf_op jit(solution)/shard_map/ppermute | solution.py:77
  133.1 38.6 %collective-permute-start.14 = (bf16[32,8192]{1,0:T(8,128)(2,1)S(1)}, bf16[32,8192]{1,0:T(8,128)(2,1)S(1)}, u32[]{:S(2)}, u32[]{:S(2)}) collective-permute-start(bf16[32,8192]{1,0:T(8,128)(2,1)S(1)} %collective-permute-done.13), channel_id=1, source_target_pairs={{0,1},{1,5},{5,4},{4,8},{8,9},{9,13},{13,12},{12,14},{14,15},{15,1... | collective-permute-start | bytes 1572872 | tf_op jit(solution)/shard_map/ppermute | solution.py:77
  217.0 8.5 %copy-start = (pred[512,512]{0,1:T(8,128)(4,1)S(1)}, pred[512,512]{0,1:T(8,128)(4,1)}, u32[]{:S(2)}) copy-start(pred[512,512]{0,1:T(8,128)(4,1)} %fusion.12) | copy-start | bytes 786436
  217.0 4.8 %collective-permute-start.15 = (bf16[512,128]{1,0:T(8,128)(2,1)S(1)}, bf16[512,128]{1,0:T(8,128)(2,1)S(1)}, u32[]{:S(2)}, u32[]{:S(2)}) collective-permute-start(bf16[512,128]{1,0:T(8,128)(2,1)S(1)} %slice.64), channel_id=1, source_target_pairs={{0,1},{1,0},{2,3},{3,2},{4,5},{5,4},{6,7},{7,6},{8,9},{9,8},{10,11... | collective-permute-start | bytes 393224 | tf_op jit(solution)/shard_map/ppermute | solution.py:114
Sparse Core Ops, SparseCore 0:
  17.1 181.3 all-gather.1

commit v3 on v0

--- a/solution.py
+++ b/solution.py
@@ -12,6 +12,8 @@
 
 ROPE_BASE = 500000.0
 EPSILON = 1e-05
+
+Z_CHIPS = 8
 
 
 def positions_in_segment(seg_ids):
@@ -51,30 +53,61 @@
     return mixed.astype(jnp.bfloat16)
 
 
+def ring_gather(block, axis, stride, count):
+    n = lax.psum(1, axis)
+    me = lax.axis_index(axis)
+    here = (me // stride) % count
+
+    def moved(step):
+        pairs = []
+        for src in range(n):
+            k = (src // stride) % count
+            pairs.append((src, src + (((k + step) % count) - k) * stride))
+        return pairs
+
+    out = jnp.zeros((count,) + block.shape, block.dtype)
+    out = lax.dynamic_update_index_in_dim(out, block, here, 0)
+    from_right, from_left = block, block
+    for step in range(1, count // 2 + 1):
+        if step < count - step:
+            from_right = lax.ppermute(from_right, axis, perm=moved(-1))
+            out = lax.dynamic_update_index_in_dim(out, from_right, (here + step) % count, 0)
+        from_left = lax.ppermute(from_left, axis, perm=moved(1))
+        out = lax.dynamic_update_index_in_dim(out, from_left, (here - step) % count, 0)
+    return out
+
+
 def per_device(tokens, segment_ids, norm_gain, query_weight, key_weight, value_weight):
     head_dim = HEAD_DIM
     query_cols = query_weight.shape[1]
     heads_dev = query_cols // head_dim
     group_size = HEADS // KV_HEADS
-    local_kv = max(1, heads_dev // group_size)
-    first_kv = lax.axis_index("weight") * heads_dev // group_size
-    key_width = local_kv * head_dim
-    key_block = lax.dynamic_slice_in_dim(key_weight, first_kv * head_dim, key_width, 1)
-    value_block = lax.dynamic_slice_in_dim(value_weight, first_kv * head_dim, key_width, 1)
+    n_weight = lax.psum(1, "weight")
+    me = lax.axis_index("weight")
+    core = me % 2
+    first_kv = me * heads_dev // group_size
+    key_block = lax.dynamic_slice_in_dim(key_weight, first_kv * head_dim, head_dim, 1)
+    value_block = lax.dynamic_slice_in_dim(value_weight, first_kv * head_dim, head_dim, 1)
+    kv_block = jnp.where(core == 0, key_block, value_block)
     values = tokens.astype(jnp.float32)
     inverse_rms = lax.rsqrt(jnp.mean(values * values, axis=1, keepdims=True) + EPSILON)
     normed = (values * inverse_rms * norm_gain[None, :]).astype(jnp.bfloat16)
-    local_weights = jnp.concatenate([query_weight, key_block, value_block], axis=1)
-    full_weights = lax.all_gather(local_weights, "batch", axis=0, tiled=True)
-    projected = jnp.dot(
-        lax.all_gather(normed, "weight", axis=0, tiled=True),
-        full_weights,
-        preferred_element_type=jnp.float32,
-    )
+    local_weights = jnp.concatenate([query_weight, kv_block], axis=1)
+    n_batch = lax.psum(1, "batch")
+    y_hi = n_batch // Z_CHIPS
+    near = ring_gather(local_weights, "batch", 1, y_hi)
+    near = near.reshape(-1, local_weights.shape[1])
+    full_weights = ring_gather(near, "batch", y_hi, Z_CHIPS).reshape(-1, near.shape[1])
+    gathered = lax.all_gather(normed, "weight", axis=0, tiled=True)
+    pack_rows = gathered.shape[0]
+    projected = jnp.dot(gathered, full_weights, preferred_element_type=jnp.float32)
     query_part = projected[:, :query_cols]
-    key_rows = projected[:, query_cols : query_cols + key_width].astype(jnp.bfloat16)
-    value_rows = projected[:, query_cols + key_width :].astype(jnp.bfloat16)
-    pack_rows = projected.shape[0]
+    own_rows = projected[:, query_cols:].astype(jnp.bfloat16)
+    partner = [(w, w ^ 1) for w in range(n_weight)]
+    other_rows = lax.ppermute(own_rows, "weight", perm=partner)
+    key_rows = jnp.where(core == 0, own_rows, other_rows)
+    value_rows = jnp.where(core == 0, other_rows, own_rows)
+    local_kv = 1
     positions = positions_in_segment(segment_ids)
     queries = rotate(query_part.reshape(pack_rows, heads_dev, head_dim), positions).astype(
         jnp.bfloat16

time: 285 us -> 229 us (0.80)
  waiting for transfers between devices: 238 us -> 110 us
  starting transfers between devices: 0.04 us -> 48.2 us
  local copies, waits for them, and re-layouts: 4.42 us -> 25 us
    all_gather x2 -> x1, waiting for transfers between devices: 238 us -> 0.01 us  [per_device(): gathered = lax.all_gather(normed, 'weight', axis=0, tiled=True)]
    ppermute x0 -> x11, waiting for transfers between devices: none -> 110 us  [the longest x6 105 us: ring_gather(): from_left = lax.ppermute(from_left, axis, perm=moved(1))]
    ppermute x0 -> x11, starting transfers between devices: none -> 48.2 us  [the longest x4 24.2 us: ring_gather(): from_right = lax.ppermute(from_right, axis, perm=moved(-1))]
    dynamic_update_slice x0 -> x11, local copies, waits for them, and re-layouts: none -> 16.2 us  [the longest x6 7.49 us: ring_gather(): lax.dynamic_update_index_in_dim(out, from_left, (here - step) % count, 0)]
    broadcast_in_dim x0 -> x2, local copies, waits for them, and re-layouts: none -> 4.89 us  [ring_gather(): out = jnp.zeros((count,) + block.shape, block.dtype)]
  transfers between devices with their start and end apart: 2 -> 12, of which waited for: 2 -> 7; matrix products, arithmetic and copies ran while one was open for 3% -> 13% of each run, Pallas kernels for 0% -> 0%
where the time goes in v3:
time: 229 us; the launch traced here: 226 us
  waiting for transfers between devices  110 us (48%)
  starting transfers between devices  48.2 us (21%)
  local copies, waits for them, and re-layouts  25 us (11%)
  matrix products  17.3 us (8%)
  between operations  14.6 us (6%)
  other arithmetic  10 us (4%)
    ppermute x6, waiting for transfers between devices, ring_gather(): from_left = lax.ppermute(from_left, axis, perm=moved(1))  105 us
    ppermute x4, starting transfers between devices, ring_gather(): from_right = lax.ppermute(from_right, axis, perm=moved(-1))  24.2 us
    ppermute x6, starting transfers between devices, ring_gather(): from_left = lax.ppermute(from_left, axis, perm=moved(1))  17.3 us
    dot_general x1, matrix products, per_device(): jnp.dot(gathered, full_weights, preferred_element_type=jnp.float32)  14.5 us
    dynamic_update_slice x6, local copies, waits for them, and re-layouts, ring_gather(): lax.dynamic_update_index_in_dim(out, from_left, (here - step) % count, 0)  7.49 us
    dynamic_update_slice x4, local copies, waits for them, and re-layouts, ring_gather(): lax.dynamic_update_index_in_dim(out, from_right, (here + step) % count, 0)  7.48 us
    ppermute x1, starting transfers between devices, per_device(): other_rows = lax.ppermute(own_rows, 'weight', perm=partner)  6.75 us
    ppermute x4, waiting for transfers between devices, ring_gather(): from_right = lax.ppermute(from_right, axis, perm=moved(-1))  5.44 us
  transfers between devices with their start and end apart: 12, of which 7 were waited for; matrix products, arithmetic and copies ran while one was open for 13% of the time, Pallas kernels for 0%

profile of v3, /device:TPU:7, one launch (start us, length us, event | category | flops | bytes accessed | tf_op | source)
XLA Modules:
  0.0 225.5 jit_solution(12782265324635948705)
XLA Ops:
  6.5 1.3 fusion.7
  7.8 2.0 fusion.9
  9.9 0.9 dynamic-slice_select_fusion
  10.8 1.0 pad_maximum_fusion
  11.8 4.2 %collective-permute-start.1 = (bf16[256,640]{1,0:T(8,128)(2,1)S(1)}, bf16[256,640]{1,0:T(8,128)(2,1)S(1)}, u32[]{:S(2)}, u32[]{:S(2)}) collective-permute-start(bf16[256,640]{1,0:T(8,128)(2,1)S(1)} %pad_maximum_fusion), channel_id=1, source_target_pairs={{0,16},{16,32},{32,48},{48,0},{64,80},{80,96},{96,112},{112,64},{1... | collective-permute-start | bytes 983048 | tf_op jit(solution)/shard_map/ppermute | solution.py:75
  16.0 3.6 %collective-permute-start = (bf16[256,640]{1,0:T(8,128)(2,1)S(1)}, bf16[256,640]{1,0:T(8,128)(2,1)S(1)}, u32[]{:S(2)}, u32[]{:S(2)}) collective-permute-start(bf16[256,640]{1,0:T(8,128)(2,1)S(1)} %pad_maximum_fusion), channel_id=1, source_target_pairs={{0,48},{16,0},{32,16},{48,32},{64,112},{80,64},{96,80},{112,96},{1... | collective-permute-start | bytes 983048 | tf_op jit(solution)/shard_map/ppermute | solution.py:73
  19.7 0.1 broadcast_in_dim.72
  19.9 8.2 %collective-permute-done.1 = bf16[256,640]{1,0:T(8,128)(2,1)S(1)} collective-permute-done((bf16[256,640]{1,0:T(8,128)(2,1)S(1)}, bf16[256,640]{1,0:T(8,128)(2,1)S(1)}, u32[]{:S(2)}, u32[]{:S(2)}) %collective-permute-start.1) | collective-permute-done | bytes 327712 | tf_op jit(solution)/shard_map/ppermute | solution.py:75
  28.1 3.1 %collective-permute-start.2 = (bf16[256,640]{1,0:T(8,128)(2,1)S(1)}, bf16[256,640]{1,0:T(8,128)(2,1)S(1)}, u32[]{:S(2)}, u32[]{:S(2)}) collective-permute-start(bf16[256,640]{1,0:T(8,128)(2,1)S(1)} %collective-permute-done.1), channel_id=1, source_target_pairs={{0,16},{16,32},{32,48},{48,0},{64,80},{80,96},{96,112},{112,64},{1... | collective-permute-start | bytes 983048 | tf_op jit(solution)/shard_map/ppermute | solution.py:75
  31.2 5.4 %collective-permute-done = bf16[256,640]{1,0:T(8,128)(2,1)S(1)} collective-permute-done((bf16[256,640]{1,0:T(8,128)(2,1)S(1)}, bf16[256,640]{1,0:T(8,128)(2,1)S(1)}, u32[]{:S(2)}, u32[]{:S(2)}) %collective-permute-start) | collective-permute-done | bytes 327712 | tf_op jit(solution)/shard_map/ppermute | solution.py:73
  36.7 17.9 %collective-permute-done.2 = bf16[256,640]{1,0:T(8,128)(2,1)S(1)} collective-permute-done((bf16[256,640]{1,0:T(8,128)(2,1)S(1)}, bf16[256,640]{1,0:T(8,128)(2,1)S(1)}, u32[]{:S(2)}, u32[]{:S(2)}) %collective-permute-start.2) | collective-permute-done | bytes 327712 | tf_op jit(solution)/shard_map/ppermute | solution.py:75
  54.6 4.3 %collective-permute-start.4 = (bf16[1024,640]{1,0:T(8,128)(2,1)S(1)}, bf16[1024,640]{1,0:T(8,128)(2,1)S(1)}, u32[]{:S(2)}, u32[]{:S(2)}) collective-permute-start(bf16[1024,640]{1,0:T(8,128)(2,1)S(1)} %bitcast.74), channel_id=1, source_target_pairs={{0,64},{16,80},{32,96},{48,112},{64,128},{80,144},{96,160},{112,17... | collective-permute-start | bytes 3932168 | tf_op jit(solution)/shard_map/ppermute | solution.py:75
  58.9 11.5 %collective-permute-start.3 = (bf16[1024,640]{1,0:T(8,128)(2,1)S(1)}, bf16[1024,640]{1,0:T(8,128)(2,1)}, u32[]{:S(2)}, u32[]{:S(2)}) collective-permute-start(bf16[1024,640]{1,0:T(8,128)(2,1)S(1)} %bitcast.75), channel_id=1, source_target_pairs={{0,448},{16,464},{32,480},{48,496},{64,0},{80,16},{96,32},{112,48}... | collective-permute-start | bytes 3932168 | tf_op jit(solution)/shard_map/ppermute | solution.py:73
  70.4 25.9 %collective-permute-done.4 = bf16[1024,640]{1,0:T(8,128)(2,1)S(1)} collective-permute-done((bf16[1024,640]{1,0:T(8,128)(2,1)S(1)}, bf16[1024,640]{1,0:T(8,128)(2,1)S(1)}, u32[]{:S(2)}, u32[]{:S(2)}) %collective-permute-start.4) | collective-permute-done | bytes 1310752 | tf_op jit(solution)/shard_map/ppermute | solution.py:75
  96.3 1.9 collective-permute-start.6
  98.2 4.6 %collective-permute-start.5 = (bf16[1024,640]{1,0:T(8,128)(2,1)}, bf16[1024,640]{1,0:T(8,128)(2,1)}, u32[]{:S(2)}, u32[]{:S(2)}) collective-permute-start(bf16[1024,640]{1,0:T(8,128)(2,1)} %collective-permute-done.3), channel_id=1, source_target_pairs={{0,448},{16,464},{32,480},{48,496},{64,0},{80,16},{96,32},{112,48}... | collective-permute-start | bytes 3932168 | tf_op jit(solution)/shard_map/ppermute | solution.py:73
  102.9 0.6 slice.34
  104.2 0.3 reduce-window.9
  104.7 23.2 %collective-permute-done.6 = bf16[1024,640]{1,0:T(8,128)(2,1)} collective-permute-done((bf16[1024,640]{1,0:T(8,128)(2,1)S(1)}, bf16[1024,640]{1,0:T(8,128)(2,1)}, u32[]{:S(2)}, u32[]{:S(2)}) %collective-permute-start.6) | collective-permute-done | bytes 1310752 | tf_op jit(solution)/shard_map/ppermute | solution.py:75
  127.9 1.9 collective-permute-start.8
  129.8 0.1 slice_reduce_fusion
  130.0 0.9 fusion.10
  130.9 1.8 multiply_cosine_fusion
  132.8 4.6 %collective-permute-start.7 = (bf16[1024,640]{1,0:T(8,128)(2,1)}, bf16[1024,640]{1,0:T(8,128)(2,1)}, u32[]{:S(2)}, u32[]{:S(2)}) collective-permute-start(bf16[1024,640]{1,0:T(8,128)(2,1)} %collective-permute-done.5), channel_id=1, source_target_pairs={{0,448},{16,464},{32,480},{48,496},{64,0},{80,16},{96,32},{112,48}... | collective-permute-start | bytes 3932168 | tf_op jit(solution)/shard_map/ppermute | solution.py:73
  137.4 4.8 %broadcast_in_dim.71 = bf16[8,1024,640]{2,1,0:T(8,128)(2,1)} broadcast(bf16[]{:T(256)} %constant.158.clone.1), dimensions={} | broadcast | bytes 10485762 | tf_op jit(solution)/shard_map/broadcast_in_dim | solution.py:68
  142.2 1.2 bitcast_dynamic-update-slice_fusion.7
  143.4 2.5 %bitcast_dynamic-update-slice_fusion.6 = bf16[8,1024,640]{2,1,0:T(8,128)(2,1)} fusion(bf16[8,1024,640]{2,1,0:T(8,128)(2,1)} %bitcast_dynamic-update-slice_fusion.7, s32[]{:T(128)S(6)} %select_n.151, bf16[1024,640]{1,0:T(8,128)(2,1)} %collective-permute-done.3), kind=kLoop, calls=%fused_computation.14 | loop fusion | bytes 2621444 | tf_op jit(solution)/shard_map/jit(dynamic_update_index_in_dim)/dynamic_update_slice | solution.py:74
  145.9 12.9 %collective-permute-done.8 = bf16[1024,640]{1,0:T(8,128)(2,1)} collective-permute-done((bf16[1024,640]{1,0:T(8,128)(2,1)}, bf16[1024,640]{1,0:T(8,128)(2,1)}, u32[]{:S(2)}, u32[]{:S(2)}) %collective-permute-start.8) | collective-permute-done | bytes 1310752 | tf_op jit(solution)/shard_map/ppermute | solution.py:75
  158.8 1.9 collective-permute-start.9
  160.7 1.2 bitcast_dynamic-update-slice_fusion.5
  161.8 2.5 %bitcast_dynamic-update-slice_fusion.4 = bf16[8,1024,640]{2,1,0:T(8,128)(2,1)} fusion(bf16[8,1024,640]{2,1,0:T(8,128)(2,1)} %bitcast_dynamic-update-slice_fusion.5, s32[]{:T(128)S(6)} %select_n.155, bf16[1024,640]{1,0:T(8,128)(2,1)} %collective-permute-done.5), kind=kLoop, calls=%fused_computation.12 | loop fusion | bytes 2621444 | tf_op jit(solution)/shard_map/jit(dynamic_update_index_in_dim)/dynamic_update_slice | solution.py:74
  164.3 2.6 %bitcast_dynamic-update-slice_fusion.3 = bf16[8,1024,640]{2,1,0:T(8,128)(2,1)} fusion(bf16[8,1024,640]{2,1,0:T(8,128)(2,1)} %bitcast_dynamic-update-slice_fusion.4, s32[]{:T(128)S(6)} %select_n.157, bf16[1024,640]{1,0:T(8,128)(2,1)} %collective-permute-done.6), kind=kLoop, calls=%fused_computation.11 | loop fusion | bytes 2621444 | tf_op jit(solution)/shard_map/jit(dynamic_update_index_in_dim)/dynamic_update_slice | solution.py:76
  166.9 2.5 %bitcast_dynamic-update-slice_fusion.2 = bf16[8,1024,640]{2,1,0:T(8,128)(2,1)} fusion(bf16[8,1024,640]{2,1,0:T(8,128)(2,1)} %bitcast_dynamic-update-slice_fusion.3, s32[]{:T(128)S(6)} %select_n.159, bf16[1024,640]{1,0:T(8,128)(2,1)} %collective-permute-done.7), kind=kLoop, calls=%fused_computation.10 | loop fusion | bytes 2621444 | tf_op jit(solution)/shard_map/jit(dynamic_update_index_in_dim)/dynamic_update_slice | solution.py:74
  169.3 2.5 %bitcast_dynamic-update-slice_fusion.1 = bf16[8,1024,640]{2,1,0:T(8,128)(2,1)} fusion(bf16[8,1024,640]{2,1,0:T(8,128)(2,1)} %bitcast_dynamic-update-slice_fusion.2, s32[]{:T(128)S(6)} %select_n.161, bf16[1024,640]{1,0:T(8,128)(2,1)} %collective-permute-done.8), kind=kLoop, calls=%fused_computation.9 | loop fusion | bytes 2621444 | tf_op jit(solution)/shard_map/jit(dynamic_update_index_in_dim)/dynamic_update_slice | solution.py:76
  171.8 16.8 %collective-permute-done.9 = bf16[1024,640]{1,0:T(8,128)(2,1)S(1)} collective-permute-done((bf16[1024,640]{1,0:T(8,128)(2,1)}, bf16[1024,640]{1,0:T(8,128)(2,1)S(1)}, u32[]{:S(2)}, u32[]{:S(2)}) %collective-permute-start.9) | collective-permute-done | bytes 1310752 | tf_op jit(solution)/shard_map/ppermute | solution.py:75
  188.6 1.2 bitcast_dynamic-update-slice_fusion
  189.8 14.5 %fusion.36 = f32[512,640]{1,0:T(8,128)S(1)} fusion(bf16[512,8192]{1,0:T(8,128)(2,1)} %all-gather.2.cloned.1.call-done, bf16[8192,640]{1,0:T(8,128)(2,1)} %bitcast.13), kind=kOutput, calls=%fused_computation.68 | convolution fusion | flops 5368709120 | bytes 20185088 | tf_op jit(solution)/shard_map/dot_general | solution.py:103
  204.4 0.7 slice.62
  205.0 0.1 slice.45
  205.2 6.7 %collective-permute-start.10 = (bf16[512,128]{1,0:T(8,128)(2,1)}, bf16[512,128]{1,0:T(8,128)(2,1)S(1)}, u32[]{:S(2)}, u32[]{:S(2)}) collective-permute-start(bf16[512,128]{1,0:T(8,128)(2,1)} %slice.62), channel_id=1, source_target_pairs={{0,1},{1,0},{2,3},{3,2},{4,5},{5,4},{6,7},{7,6},{8,9},{9,8},{10,11... | collective-permute-start | bytes 393224 | tf_op jit(solution)/shard_map/ppermute | solution.py:107
  211.9 0.4 reshape.201
  212.3 0.6 fusion.34
  212.9 0.3 copy-done
  213.3 0.3 subtract_convert_fusion
  213.6 1.2 fusion.28
  214.9 1.5 fusion
  216.4 1.3 fusion.4
  217.7 1.0 copy.16
  (27 shorter events, 0.6 us)
Async XLA Ops:
  6.5 13.3 %copy-start.2 = (bf16[256,512]{1,0:T(8,128)(2,1)S(1)}, bf16[256,512]{1,0:T(8,128)(2,1)}, u32[]{:S(2)}) copy-start(bf16[256,512]{1,0:T(8,128)(2,1)} %param.9) | copy-start | bytes 786436
  6.5 96.4 %copy-start.4 = (s32[512]{0:T(512)S(1)}, s32[512]{0:T(512)}, u32[]{:S(2)}) copy-start(s32[512]{0:T(512)} %param.7) | copy-start | bytes 6148
  6.5 183.3 %all-gather.2.cloned.1.call-start = ((), (), s32[]{:S(2)}) async-start(), calls=%async_computation | async-start | bytes 8912896 | tf_op jit(solution)/shard_map/all_gather | solution.py:101
  11.8 16.3 %collective-permute-start.1 = (bf16[256,640]{1,0:T(8,128)(2,1)S(1)}, bf16[256,640]{1,0:T(8,128)(2,1)S(1)}, u32[]{:S(2)}, u32[]{:S(2)}) collective-permute-start(bf16[256,640]{1,0:T(8,128)(2,1)S(1)} %pad_maximum_fusion), channel_id=1, source_target_pairs={{0,16},{16,32},{32,48},{48,0},{64,80},{80,96},{96,112},{112,64},{1... | collective-permute-start | bytes 983048 | tf_op jit(solution)/shard_map/ppermute | solution.py:75
  16.0 20.5 %collective-permute-start = (bf16[256,640]{1,0:T(8,128)(2,1)S(1)}, bf16[256,640]{1,0:T(8,128)(2,1)S(1)}, u32[]{:S(2)}, u32[]{:S(2)}) collective-permute-start(bf16[256,640]{1,0:T(8,128)(2,1)S(1)} %pad_maximum_fusion), channel_id=1, source_target_pairs={{0,48},{16,0},{32,16},{48,32},{64,112},{80,64},{96,80},{112,96},{1... | collective-permute-start | bytes 983048 | tf_op jit(solution)/shard_map/ppermute | solution.py:73
  28.1 26.5 %collective-permute-start.2 = (bf16[256,640]{1,0:T(8,128)(2,1)S(1)}, bf16[256,640]{1,0:T(8,128)(2,1)S(1)}, u32[]{:S(2)}, u32[]{:S(2)}) collective-permute-start(bf16[256,640]{1,0:T(8,128)(2,1)S(1)} %collective-permute-done.1), channel_id=1, source_target_pairs={{0,16},{16,32},{32,48},{48,0},{64,80},{80,96},{96,112},{112,64},{1... | collective-permute-start | bytes 983048 | tf_op jit(solution)/shard_map/ppermute | solution.py:75
  54.6 41.7 %collective-permute-start.4 = (bf16[1024,640]{1,0:T(8,128)(2,1)S(1)}, bf16[1024,640]{1,0:T(8,128)(2,1)S(1)}, u32[]{:S(2)}, u32[]{:S(2)}) collective-permute-start(bf16[1024,640]{1,0:T(8,128)(2,1)S(1)} %bitcast.74), channel_id=1, source_target_pairs={{0,64},{16,80},{32,96},{48,112},{64,128},{80,144},{96,160},{112,17... | collective-permute-start | bytes 3932168 | tf_op jit(solution)/shard_map/ppermute | solution.py:75
  58.9 39.3 %collective-permute-start.3 = (bf16[1024,640]{1,0:T(8,128)(2,1)S(1)}, bf16[1024,640]{1,0:T(8,128)(2,1)}, u32[]{:S(2)}, u32[]{:S(2)}) collective-permute-start(bf16[1024,640]{1,0:T(8,128)(2,1)S(1)} %bitcast.75), channel_id=1, source_target_pairs={{0,448},{16,464},{32,480},{48,496},{64,0},{80,16},{96,32},{112,48}... | collective-permute-start | bytes 3932168 | tf_op jit(solution)/shard_map/ppermute | solution.py:73
  96.3 31.6 %collective-permute-start.6 = (bf16[1024,640]{1,0:T(8,128)(2,1)S(1)}, bf16[1024,640]{1,0:T(8,128)(2,1)}, u32[]{:S(2)}, u32[]{:S(2)}) collective-permute-start(bf16[1024,640]{1,0:T(8,128)(2,1)S(1)} %collective-permute-done.4), channel_id=1, source_target_pairs={{0,64},{16,80},{32,96},{48,112},{64,128},{80,144},{96,160},{112,17... | collective-permute-start | bytes 3932168 | tf_op jit(solution)/shard_map/ppermute | solution.py:75
  98.2 34.5 %collective-permute-start.5 = (bf16[1024,640]{1,0:T(8,128)(2,1)}, bf16[1024,640]{1,0:T(8,128)(2,1)}, u32[]{:S(2)}, u32[]{:S(2)}) collective-permute-start(bf16[1024,640]{1,0:T(8,128)(2,1)} %collective-permute-done.3), channel_id=1, source_target_pairs={{0,448},{16,464},{32,480},{48,496},{64,0},{80,16},{96,32},{112,48}... | collective-permute-start | bytes 3932168 | tf_op jit(solution)/shard_map/ppermute | solution.py:73
  127.9 30.9 %collective-permute-start.8 = (bf16[1024,640]{1,0:T(8,128)(2,1)}, bf16[1024,640]{1,0:T(8,128)(2,1)}, u32[]{:S(2)}, u32[]{:S(2)}) collective-permute-start(bf16[1024,640]{1,0:T(8,128)(2,1)} %collective-permute-done.6), channel_id=1, source_target_pairs={{0,64},{16,80},{32,96},{48,112},{64,128},{80,144},{96,160},{112,17... | collective-permute-start | bytes 3932168 | tf_op jit(solution)/shard_map/ppermute | solution.py:75
  132.8 34.1 %collective-permute-start.7 = (bf16[1024,640]{1,0:T(8,128)(2,1)}, bf16[1024,640]{1,0:T(8,128)(2,1)}, u32[]{:S(2)}, u32[]{:S(2)}) collective-permute-start(bf16[1024,640]{1,0:T(8,128)(2,1)} %collective-permute-done.5), channel_id=1, source_target_pairs={{0,448},{16,464},{32,480},{48,496},{64,0},{80,16},{96,32},{112,48}... | collective-permute-start | bytes 3932168 | tf_op jit(solution)/shard_map/ppermute | solution.py:73
  158.8 29.8 %collective-permute-start.9 = (bf16[1024,640]{1,0:T(8,128)(2,1)}, bf16[1024,640]{1,0:T(8,128)(2,1)S(1)}, u32[]{:S(2)}, u32[]{:S(2)}) collective-permute-start(bf16[1024,640]{1,0:T(8,128)(2,1)} %collective-permute-done.8), channel_id=1, source_target_pairs={{0,64},{16,80},{32,96},{48,112},{64,128},{80,144},{96,160},{112,17... | collective-permute-start | bytes 3932168 | tf_op jit(solution)/shard_map/ppermute | solution.py:75
  205.2 8.4 %collective-permute-start.10 = (bf16[512,128]{1,0:T(8,128)(2,1)}, bf16[512,128]{1,0:T(8,128)(2,1)S(1)}, u32[]{:S(2)}, u32[]{:S(2)}) collective-permute-start(bf16[512,128]{1,0:T(8,128)(2,1)} %slice.62), channel_id=1, source_target_pairs={{0,1},{1,0},{2,3},{3,2},{4,5},{5,4},{6,7},{7,6},{8,9},{9,8},{10,11... | collective-permute-start | bytes 393224 | tf_op jit(solution)/shard_map/ppermute | solution.py:107
  212.3 1.0 copy-start
  212.3 1.0 copy-start.1
  212.3 2.6 %copy-start.3 = (pred[512,512]{0,1:T(8,128)(4,1)S(1)}, pred[512,512]{0,1:T(8,128)(4,1)}, u32[]{:S(2)}) copy-start(pred[512,512]{0,1:T(8,128)(4,1)} %fusion.10) | copy-start | bytes 786436
Sparse Core Ops, SparseCore 0:
  10.0 76.3 all-gather.1

commit v4 on v3

--- a/solution.py
+++ b/solution.py
@@ -92,17 +92,17 @@
     values = tokens.astype(jnp.float32)
     inverse_rms = lax.rsqrt(jnp.mean(values * values, axis=1, keepdims=True) + EPSILON)
     normed = (values * inverse_rms * norm_gain[None, :]).astype(jnp.bfloat16)
-    local_weights = jnp.concatenate([query_weight, kv_block], axis=1)
     n_batch = lax.psum(1, "batch")
     y_hi = n_batch // Z_CHIPS
-    near = ring_gather(local_weights, "batch", 1, y_hi)
-    near = near.reshape(-1, local_weights.shape[1])
-    full_weights = ring_gather(near, "batch", y_hi, Z_CHIPS).reshape(-1, near.shape[1])
+    near = ring_gather(query_weight, "batch", 1, y_hi).reshape(-1, query_cols)
+    query_full = ring_gather(near, "batch", y_hi, Z_CHIPS).reshape(-1, query_cols)
+    far = ring_gather(kv_block, "batch", y_hi, Z_CHIPS)
+    kv_full = ring_gather(far, "batch", 1, y_hi)
+    kv_full = jnp.swapaxes(kv_full, 0, 1).reshape(-1, head_dim)
     gathered = lax.all_gather(normed, "weight", axis=0, tiled=True)
     pack_rows = gathered.shape[0]
-    projected = jnp.dot(gathered, full_weights, preferred_element_type=jnp.float32)
-    query_part = projected[:, :query_cols]
-    own_rows = projected[:, query_cols:].astype(jnp.bfloat16)
+    query_part = jnp.dot(gathered, query_full, preferred_element_type=jnp.float32)
+    own_rows = jnp.dot(gathered, kv_full, preferred_element_type=jnp.float32).astype(jnp.bfloat16)
     partner = [(w, w ^ 1) for w in range(n_weight)]
     other_rows = lax.ppermute(own_rows, "weight", perm=partner)
     key_rows = jnp.where(core == 0, own_rows, other_rows)

time: 229 us -> 238 us (1.039)
  starting transfers between devices: 48.2 us -> 75.2 us
  waiting for transfers between devices: 110 us -> 84.5 us
  local copies, waits for them, and re-layouts: 25 us -> 34.5 us
    ppermute x6 -> x12, waiting for transfers between devices: 105 us -> 81.6 us  [ring_gather(): from_left = lax.ppermute(from_left, axis, perm=moved(1))]
    ppermute x4 -> x8, starting transfers between devices: 24.2 us -> 42.2 us  [ring_gather(): from_right = lax.ppermute(from_right, axis, perm=moved(-1))]
    dot_general x0 -> x1, local copies, waits for them, and re-layouts: none -> 11.3 us  [per_device(): jnp.dot(gathered, query_full, preferred_element_type=jnp.float32)]
    ppermute x6 -> x12, starting transfers between devices: 17.3 us -> 28.1 us  [ring_gather(): from_left = lax.ppermute(from_left, axis, perm=moved(1))]
    ppermute x4 -> x8, waiting for transfers between devices: 5.44 us -> 2.86 us  [ring_gather(): from_right = lax.ppermute(from_right, axis, perm=moved(-1))]
    dynamic_update_slice x4 -> x8, local copies, waits for them, and re-layouts: 7.48 us -> 5.19 us  [ring_gather(): lax.dynamic_update_index_in_dim(out, from_right, (here + step) % count, 0)]
    broadcast_in_dim x2 -> x4, local copies, waits for them, and re-layouts: 4.89 us -> 5.39 us  [ring_gather(): out = jnp.zeros((count,) + block.shape, block.dtype)]
    dynamic_update_slice x6 -> x12, local copies, waits for them, and re-layouts: 7.49 us -> 7.03 us  [ring_gather(): lax.dynamic_update_index_in_dim(out, from_left, (here - step) % count, 0)]
  transfers between devices with their start and end apart: 12 -> 22, of which waited for: 7 -> 8; matrix products, arithmetic and copies ran while one was open for 13% -> 20% of each run, Pallas kernels for 0% -> 0%
where the time goes in v4:
time: 238 us; the launch traced here: 235 us
  waiting for transfers between devices  84.5 us (36%)
  starting transfers between devices  75.2 us (32%)
  local copies, waits for them, and re-layouts  34.5 us (14%)
  matrix products  17.4 us (7%)
  between operations  14.6 us (6%)
  other arithmetic  9.03 us (4%)
    ppermute x12, waiting for transfers between devices, ring_gather(): from_left = lax.ppermute(from_left, axis, perm=moved(1))  81.6 us
    ppermute x8, starting transfers between devices, ring_gather(): from_right = lax.ppermute(from_right, axis, perm=moved(-1))  42.2 us
    ppermute x12, starting transfers between devices, ring_gather(): from_left = lax.ppermute(from_left, axis, perm=moved(1))  28.1 us
    dot_general x1, local copies, waits for them, and re-layouts, per_device(): jnp.dot(gathered, query_full, preferred_element_type=jnp.float32)  11.3 us
    dot_general x1, matrix products, per_device(): jnp.dot(gathered, query_full, preferred_element_type=jnp.float32)  8.43 us
    dynamic_update_slice x12, local copies, waits for them, and re-layouts, ring_gather(): lax.dynamic_update_index_in_dim(out, from_left, (here - step) % count, 0)  7.03 us
    dot_general x1, matrix products, per_device(): jnp.dot(gathered, kv_full, preferred_element_type=jnp.float32)  6.4 us
    broadcast_in_dim x4, local copies, waits for them, and re-layouts, ring_gather(): out = jnp.zeros((count,) + block.shape, block.dtype)  5.39 us
  transfers between devices with their start and end apart: 22, of which 8 were waited for; matrix products, arithmetic and copies ran while one was open for 20% of the time, Pallas kernels for 0%

profile of v4, /device:TPU:7, one launch (start us, length us, event | category | flops | bytes accessed | tf_op | source)
XLA Modules:
  0.0 235.2 jit_solution(11055179199546752467)
XLA Ops:
  6.5 1.2 fusion.9
  7.8 2.0 fusion.11
  9.9 5.9 %collective-permute-start.11 = (bf16[256,512]{1,0:T(8,128)(2,1)}, bf16[256,512]{1,0:T(8,128)(2,1)S(1)}, u32[]{:S(2)}, u32[]{:S(2)}) collective-permute-start(bf16[256,512]{1,0:T(8,128)(2,1)} %param.9), channel_id=1, source_target_pairs={{0,48},{16,0},{32,16},{48,32},{64,112},{80,64},{96,80},{112,96},{1... | collective-permute-start | bytes 786440 | tf_op jit(solution)/shard_map/ppermute | solution.py:73
  15.7 1.9 collective-permute-start.12
  18.6 1.5 bitcast_dynamic-update-slice_fusion.23
  20.2 10.7 %collective-permute-start = (bf16[256,128]{1,0:T(8,128)(2,1)S(1)}, bf16[256,128]{1,0:T(8,128)(2,1)S(1)}, u32[]{:S(2)}, u32[]{:S(2)}) collective-permute-start(bf16[256,128]{1,0:T(8,128)(2,1)S(1)} %get-tuple-element.6), channel_id=1, source_target_pairs={{0,448},{16,464},{32,480},{48,496},{64,0},{80,16},{96,32},{112,48}... | collective-permute-start | bytes 196616 | tf_op jit(solution)/shard_map/ppermute | solution.py:73
  30.8 1.9 collective-permute-start.1
  32.8 1.2 slice.26
  36.0 1.7 fusion.12
  38.9 4.6 %collective-permute-start.2 = (bf16[256,128]{1,0:T(8,128)(2,1)S(1)}, bf16[256,128]{1,0:T(8,128)(2,1)S(1)}, u32[]{:S(2)}, u32[]{:S(2)}) collective-permute-start(bf16[256,128]{1,0:T(8,128)(2,1)S(1)} %collective-permute-done), channel_id=1, source_target_pairs={{0,448},{16,464},{32,480},{48,496},{64,0},{80,16},{96,32},{112,48}... | collective-permute-start | bytes 196616 | tf_op jit(solution)/shard_map/ppermute | solution.py:73
  43.5 1.9 collective-permute-start.3
  46.1 3.8 %collective-permute-start.13 = (bf16[256,512]{1,0:T(8,128)(2,1)S(1)}, bf16[256,512]{1,0:T(8,128)(2,1)S(1)}, u32[]{:S(2)}, u32[]{:S(2)}) collective-permute-start(bf16[256,512]{1,0:T(8,128)(2,1)S(1)} %collective-permute-done.12), channel_id=1, source_target_pairs={{0,16},{16,32},{32,48},{48,0},{64,80},{80,96},{96,112},{112,64},{1... | collective-permute-start | bytes 786440 | tf_op jit(solution)/shard_map/ppermute | solution.py:75
  50.0 19.1 %collective-permute-done.13 = bf16[256,512]{1,0:T(8,128)(2,1)S(1)} collective-permute-done((bf16[256,512]{1,0:T(8,128)(2,1)S(1)}, bf16[256,512]{1,0:T(8,128)(2,1)S(1)}, u32[]{:S(2)}, u32[]{:S(2)}) %collective-permute-start.13) | collective-permute-done | bytes 262176 | tf_op jit(solution)/shard_map/ppermute | solution.py:75
  69.2 1.9 collective-permute-start.15
  71.8 4.6 %collective-permute-start.4 = (bf16[256,128]{1,0:T(8,128)(2,1)S(1)}, bf16[256,128]{1,0:T(8,128)(2,1)S(1)}, u32[]{:S(2)}, u32[]{:S(2)}) collective-permute-start(bf16[256,128]{1,0:T(8,128)(2,1)S(1)} %collective-permute-done.2), channel_id=1, source_target_pairs={{0,448},{16,464},{32,480},{48,496},{64,0},{80,16},{96,32},{112,48}... | collective-permute-start | bytes 196616 | tf_op jit(solution)/shard_map/ppermute | solution.py:73
  76.3 1.9 collective-permute-start.5
  78.9 4.6 %collective-permute-start.14 = (bf16[1024,512]{1,0:T(8,128)(2,1)S(1)}, bf16[1024,512]{1,0:T(8,128)(2,1)S(1)}, u32[]{:S(2)}, u32[]{:S(2)}) collective-permute-start(bf16[1024,512]{1,0:T(8,128)(2,1)S(1)} %bitcast.117), channel_id=1, source_target_pairs={{0,448},{16,464},{32,480},{48,496},{64,0},{80,16},{96,32},{112,48}... | collective-permute-start | bytes 3145736 | tf_op jit(solution)/shard_map/ppermute | solution.py:73
  84.1 12.5 %collective-permute-done.5 = bf16[256,128]{1,0:T(8,128)(2,1)S(1)} collective-permute-done((bf16[256,128]{1,0:T(8,128)(2,1)S(1)}, bf16[256,128]{1,0:T(8,128)(2,1)S(1)}, u32[]{:S(2)}, u32[]{:S(2)}) %collective-permute-start.5) | collective-permute-done | bytes 65568 | tf_op jit(solution)/shard_map/ppermute | solution.py:75
  96.6 1.9 collective-permute-start.6
  99.8 1.9 collective-permute-start.17
  101.7 1.1 collective-permute-done.6
  103.4 3.2 %collective-permute-start.8 = (bf16[8,256,128]{2,1,0:T(8,128)(2,1)}, bf16[8,256,128]{2,1,0:T(8,128)(2,1)S(1)}, u32[]{:S(2)}, u32[]{:S(2)}) collective-permute-start(bf16[8,256,128]{2,1,0:T(8,128)(2,1)} %bitcast_dynamic-update-slice_fusion.16), channel_id=1, source_target_pairs={{0,16},{16,32},{32,48},{48,0},{64,80},{80,96},{96,112},{112,64},{1... | collective-permute-start | bytes 1572872 | tf_op jit(solution)/shard_map/ppermute | solution.py:75
  106.6 4.2 %collective-permute-start.7 = (bf16[8,256,128]{2,1,0:T(8,128)(2,1)}, bf16[8,256,128]{2,1,0:T(8,128)(2,1)S(1)}, u32[]{:S(2)}, u32[]{:S(2)}) collective-permute-start(bf16[8,256,128]{2,1,0:T(8,128)(2,1)} %bitcast_dynamic-update-slice_fusion.16), channel_id=1, source_target_pairs={{0,48},{16,0},{32,16},{48,32},{64,112},{80,64},{96,80},{112,96},{1... | collective-permute-start | bytes 1572872 | tf_op jit(solution)/shard_map/ppermute | solution.py:73
  111.4 3.5 %collective-permute-start.16 = (bf16[1024,512]{1,0:T(8,128)(2,1)S(1)}, bf16[1024,512]{1,0:T(8,128)(2,1)S(1)}, u32[]{:S(2)}, u32[]{:S(2)}) collective-permute-start(bf16[1024,512]{1,0:T(8,128)(2,1)S(1)} %collective-permute-done.14), channel_id=1, source_target_pairs={{0,448},{16,464},{32,480},{48,496},{64,0},{80,16},{96,32},{112,48}... | collective-permute-start | bytes 3145736 | tf_op jit(solution)/shard_map/ppermute | solution.py:73
  115.4 1.1 bitcast_dynamic-update-slice_fusion.10
  116.5 13.8 %collective-permute-done.8 = bf16[8,256,128]{2,1,0:T(8,128)(2,1)S(1)} collective-permute-done((bf16[8,256,128]{2,1,0:T(8,128)(2,1)}, bf16[8,256,128]{2,1,0:T(8,128)(2,1)S(1)}, u32[]{:S(2)}, u32[]{:S(2)}) %collective-permute-start.8) | collective-permute-done | bytes 524320 | tf_op jit(solution)/shard_map/ppermute | solution.py:75
  130.3 3.4 %collective-permute-start.9 = (bf16[8,256,128]{2,1,0:T(8,128)(2,1)S(1)}, bf16[8,256,128]{2,1,0:T(8,128)(2,1)S(1)}, u32[]{:S(2)}, u32[]{:S(2)}) collective-permute-start(bf16[8,256,128]{2,1,0:T(8,128)(2,1)S(1)} %collective-permute-done.8), channel_id=1, source_target_pairs={{0,16},{16,32},{32,48},{48,0},{64,80},{80,96},{96,112},{112,64},{1... | collective-permute-start | bytes 1572872 | tf_op jit(solution)/shard_map/ppermute | solution.py:75
  133.7 4.0 %broadcast_in_dim.131 = bf16[8,1024,512]{2,1,0:T(8,128)(2,1)} broadcast(bf16[]{:T(256)} %constant.216.clone.1), dimensions={} | broadcast | bytes 8388610 | tf_op jit(solution)/shard_map/broadcast_in_dim | solution.py:68
  138.8 2.4 %collective-permute-start.19 = (bf16[1024,512]{1,0:T(8,128)(2,1)S(1)}, bf16[1024,512]{1,0:T(8,128)(2,1)S(1)}, u32[]{:S(2)}, u32[]{:S(2)}) collective-permute-start(bf16[1024,512]{1,0:T(8,128)(2,1)S(1)} %collective-permute-done.17), channel_id=1, source_target_pairs={{0,64},{16,80},{32,96},{48,112},{64,128},{80,144},{96,160},{112,17... | collective-permute-start | bytes 3145736 | tf_op jit(solution)/shard_map/ppermute | solution.py:75
  141.2 6.2 %collective-permute-done.9 = bf16[8,256,128]{2,1,0:T(8,128)(2,1)S(1)} collective-permute-done((bf16[8,256,128]{2,1,0:T(8,128)(2,1)S(1)}, bf16[8,256,128]{2,1,0:T(8,128)(2,1)S(1)}, u32[]{:S(2)}, u32[]{:S(2)}) %collective-permute-start.9) | collective-permute-done | bytes 524320 | tf_op jit(solution)/shard_map/ppermute | solution.py:75
  147.6 4.3 %collective-permute-start.18 = (bf16[1024,512]{1,0:T(8,128)(2,1)S(1)}, bf16[1024,512]{1,0:T(8,128)(2,1)S(1)}, u32[]{:S(2)}, u32[]{:S(2)}) collective-permute-start(bf16[1024,512]{1,0:T(8,128)(2,1)S(1)} %collective-permute-done.16), channel_id=1, source_target_pairs={{0,448},{16,464},{32,480},{48,496},{64,0},{80,16},{96,32},{112,48}... | collective-permute-start | bytes 3145736 | tf_op jit(solution)/shard_map/ppermute | solution.py:73
  151.9 1.1 bitcast_dynamic-update-slice_fusion.6
  152.9 1.1 bitcast_dynamic-update-slice_fusion.5
  154.0 11.9 %collective-permute-done.19 = bf16[1024,512]{1,0:T(8,128)(2,1)S(1)} collective-permute-done((bf16[1024,512]{1,0:T(8,128)(2,1)S(1)}, bf16[1024,512]{1,0:T(8,128)(2,1)S(1)}, u32[]{:S(2)}, u32[]{:S(2)}) %collective-permute-start.19) | collective-permute-done | bytes 1048608 | tf_op jit(solution)/shard_map/ppermute | solution.py:75
  166.0 1.9 collective-permute-start.20
  167.9 1.0 bitcast_dynamic-update-slice_fusion.4
  168.9 1.1 bitcast_dynamic-update-slice_fusion.3
  170.0 2.8 %collective-permute-done.18 = bf16[1024,512]{1,0:T(8,128)(2,1)S(1)} collective-permute-done((bf16[1024,512]{1,0:T(8,128)(2,1)S(1)}, bf16[1024,512]{1,0:T(8,128)(2,1)S(1)}, u32[]{:S(2)}, u32[]{:S(2)}) %collective-permute-start.18) | collective-permute-done | bytes 1048608 | tf_op jit(solution)/shard_map/ppermute | solution.py:73
  172.8 1.1 bitcast_dynamic-update-slice_fusion.2
  173.9 1.1 bitcast_dynamic-update-slice_fusion.1
  175.0 16.9 %collective-permute-done.20 = bf16[1024,512]{1,0:T(8,128)(2,1)S(1)} collective-permute-done((bf16[1024,512]{1,0:T(8,128)(2,1)S(1)}, bf16[1024,512]{1,0:T(8,128)(2,1)S(1)}, u32[]{:S(2)}, u32[]{:S(2)}) %collective-permute-start.20) | collective-permute-done | bytes 1048608 | tf_op jit(solution)/shard_map/ppermute | solution.py:75
  191.9 1.1 bitcast_dynamic-update-slice_fusion
  192.9 11.3 %copy.30 = bf16[512,8192]{1,0:T(8,128)(2,1)} copy(bf16[512,8192]{0,1:T(8,128)(2,1)} %bitcast.40) | data formatting | bytes 16777216 | tf_op jit(solution)/shard_map/dot_general | solution.py:104
  204.2 6.4 %convolution_convert_fusion = bf16[512,128]{0,1:T(8,128)(2,1)S(1)} fusion(bf16[512,8192]{1,0:T(8,128)(2,1)} %all-gather.2.cloned.1.call-done, bf16[8192,128]{1,0:T(8,128)(2,1)S(1)} %bitcast.115), kind=kOutput, calls=%fused_computation.11 | convolution fusion | flops 1073807360 | bytes 10616832 | tf_op jit(solution)/shard_map/dot_general | solution.py:105
  210.7 4.8 %collective-permute-start.10 = (bf16[512,128]{0,1:T(8,128)(2,1)S(1)}, bf16[512,128]{0,1:T(8,128)(2,1)S(1)}, u32[]{:S(2)}, u32[]{:S(2)}) collective-permute-start(bf16[512,128]{0,1:T(8,128)(2,1)S(1)} %convolution_convert_fusion), channel_id=1, source_target_pairs={{0,1},{1,0},{2,3},{3,2},{4,5},{5,4},{6,7},{7,6},{8,9},{9,8},{10,11... | collective-permute-start | bytes 393224 | tf_op jit(solution)/shard_map/ppermute | solution.py:107
  215.5 8.4 %fusion = f32[512,4,128]{0,2,1:T(8,128)S(1)} fusion(bf16[4,128,8192]{2,1,0:T(8,128)(2,1)} %bitcast.114, bf16[512,8192]{1,0:T(8,128)(2,1)S(1)} %copy-done), kind=kOutput, calls=%fused_computation | convolution fusion | flops 4294967296 | bytes 17825792 | tf_op jit(solution)/shard_map/dot_general | solution.py:104
  224.8 1.3 fusion.2
  226.0 1.3 fusion.6
  (51 shorter events, 12.0 us)
Async XLA Ops:
  6.5 197.7 %all-gather.2.cloned.1.call-start = ((), (), s32[]{:S(2)}) async-start(), calls=%async_computation | async-start | bytes 8912896 | tf_op jit(solution)/shard_map/all_gather | solution.py:102
  9.9 40.1 %collective-permute-start.11 = (bf16[256,512]{1,0:T(8,128)(2,1)}, bf16[256,512]{1,0:T(8,128)(2,1)S(1)}, u32[]{:S(2)}, u32[]{:S(2)}) collective-permute-start(bf16[256,512]{1,0:T(8,128)(2,1)} %param.9), channel_id=1, source_target_pairs={{0,48},{16,0},{32,16},{48,32},{64,112},{80,64},{96,80},{112,96},{1... | collective-permute-start | bytes 786440 | tf_op jit(solution)/shard_map/ppermute | solution.py:73
  15.7 30.3 %collective-permute-start.12 = (bf16[256,512]{1,0:T(8,128)(2,1)}, bf16[256,512]{1,0:T(8,128)(2,1)S(1)}, u32[]{:S(2)}, u32[]{:S(2)}) collective-permute-start(bf16[256,512]{1,0:T(8,128)(2,1)} %param.9), channel_id=1, source_target_pairs={{0,16},{16,32},{32,48},{48,0},{64,80},{80,96},{96,112},{112,64},{1... | collective-permute-start | bytes 786440 | tf_op jit(solution)/shard_map/ppermute | solution.py:75
  20.2 18.8 %collective-permute-start = (bf16[256,128]{1,0:T(8,128)(2,1)S(1)}, bf16[256,128]{1,0:T(8,128)(2,1)S(1)}, u32[]{:S(2)}, u32[]{:S(2)}) collective-permute-start(bf16[256,128]{1,0:T(8,128)(2,1)S(1)} %get-tuple-element.6), channel_id=1, source_target_pairs={{0,448},{16,464},{32,480},{48,496},{64,0},{80,16},{96,32},{112,48}... | collective-permute-start | bytes 196616 | tf_op jit(solution)/shard_map/ppermute | solution.py:73
  30.8 12.7 %collective-permute-start.1 = (bf16[256,128]{1,0:T(8,128)(2,1)S(1)}, bf16[256,128]{1,0:T(8,128)(2,1)S(1)}, u32[]{:S(2)}, u32[]{:S(2)}) collective-permute-start(bf16[256,128]{1,0:T(8,128)(2,1)S(1)} %get-tuple-element.6), channel_id=1, source_target_pairs={{0,64},{16,80},{32,96},{48,112},{64,128},{80,144},{96,160},{112,17... | collective-permute-start | bytes 196616 | tf_op jit(solution)/shard_map/ppermute | solution.py:75
  38.9 32.8 %collective-permute-start.2 = (bf16[256,128]{1,0:T(8,128)(2,1)S(1)}, bf16[256,128]{1,0:T(8,128)(2,1)S(1)}, u32[]{:S(2)}, u32[]{:S(2)}) collective-permute-start(bf16[256,128]{1,0:T(8,128)(2,1)S(1)} %collective-permute-done), channel_id=1, source_target_pairs={{0,448},{16,464},{32,480},{48,496},{64,0},{80,16},{96,32},{112,48}... | collective-permute-start | bytes 196616 | tf_op jit(solution)/shard_map/ppermute | solution.py:73
  43.5 32.8 %collective-permute-start.3 = (bf16[256,128]{1,0:T(8,128)(2,1)S(1)}, bf16[256,128]{1,0:T(8,128)(2,1)S(1)}, u32[]{:S(2)}, u32[]{:S(2)}) collective-permute-start(bf16[256,128]{1,0:T(8,128)(2,1)S(1)} %collective-permute-done.1), channel_id=1, source_target_pairs={{0,64},{16,80},{32,96},{48,112},{64,128},{80,144},{96,160},{112,17... | collective-permute-start | bytes 196616 | tf_op jit(solution)/shard_map/ppermute | solution.py:75
  46.1 23.1 %collective-permute-start.13 = (bf16[256,512]{1,0:T(8,128)(2,1)S(1)}, bf16[256,512]{1,0:T(8,128)(2,1)S(1)}, u32[]{:S(2)}, u32[]{:S(2)}) collective-permute-start(bf16[256,512]{1,0:T(8,128)(2,1)S(1)} %collective-permute-done.12), channel_id=1, source_target_pairs={{0,16},{16,32},{32,48},{48,0},{64,80},{80,96},{96,112},{112,64},{1... | collective-permute-start | bytes 786440 | tf_op jit(solution)/shard_map/ppermute | solution.py:75
  69.2 30.6 %collective-permute-start.15 = (bf16[1024,512]{1,0:T(8,128)(2,1)S(1)}, bf16[1024,512]{1,0:T(8,128)(2,1)S(1)}, u32[]{:S(2)}, u32[]{:S(2)}) collective-permute-start(bf16[1024,512]{1,0:T(8,128)(2,1)S(1)} %bitcast.116), channel_id=1, source_target_pairs={{0,64},{16,80},{32,96},{48,112},{64,128},{80,144},{96,160},{112,17... | collective-permute-start | bytes 3145736 | tf_op jit(solution)/shard_map/ppermute | solution.py:75
  71.8 26.7 %collective-permute-start.4 = (bf16[256,128]{1,0:T(8,128)(2,1)S(1)}, bf16[256,128]{1,0:T(8,128)(2,1)S(1)}, u32[]{:S(2)}, u32[]{:S(2)}) collective-permute-start(bf16[256,128]{1,0:T(8,128)(2,1)S(1)} %collective-permute-done.2), channel_id=1, source_target_pairs={{0,448},{16,464},{32,480},{48,496},{64,0},{80,16},{96,32},{112,48}... | collective-permute-start | bytes 196616 | tf_op jit(solution)/shard_map/ppermute | solution.py:73
  76.3 20.2 %collective-permute-start.5 = (bf16[256,128]{1,0:T(8,128)(2,1)S(1)}, bf16[256,128]{1,0:T(8,128)(2,1)S(1)}, u32[]{:S(2)}, u32[]{:S(2)}) collective-permute-start(bf16[256,128]{1,0:T(8,128)(2,1)S(1)} %collective-permute-done.3), channel_id=1, source_target_pairs={{0,64},{16,80},{32,96},{48,112},{64,128},{80,144},{96,160},{112,17... | collective-permute-start | bytes 196616 | tf_op jit(solution)/shard_map/ppermute | solution.py:75
  78.9 32.5 %collective-permute-start.14 = (bf16[1024,512]{1,0:T(8,128)(2,1)S(1)}, bf16[1024,512]{1,0:T(8,128)(2,1)S(1)}, u32[]{:S(2)}, u32[]{:S(2)}) collective-permute-start(bf16[1024,512]{1,0:T(8,128)(2,1)S(1)} %bitcast.117), channel_id=1, source_target_pairs={{0,448},{16,464},{32,480},{48,496},{64,0},{80,16},{96,32},{112,48}... | collective-permute-start | bytes 3145736 | tf_op jit(solution)/shard_map/ppermute | solution.py:73
  96.6 6.2 %collective-permute-start.6 = (bf16[256,128]{1,0:T(8,128)(2,1)S(1)}, bf16[256,128]{1,0:T(8,128)(2,1)S(1)}, u32[]{:S(2)}, u32[]{:S(2)}) collective-permute-start(bf16[256,128]{1,0:T(8,128)(2,1)S(1)} %collective-permute-done.5), channel_id=1, source_target_pairs={{0,64},{16,80},{32,96},{48,112},{64,128},{80,144},{96,160},{112,17... | collective-permute-start | bytes 196616 | tf_op jit(solution)/shard_map/ppermute | solution.py:75
  99.8 39.0 %collective-permute-start.17 = (bf16[1024,512]{1,0:T(8,128)(2,1)S(1)}, bf16[1024,512]{1,0:T(8,128)(2,1)S(1)}, u32[]{:S(2)}, u32[]{:S(2)}) collective-permute-start(bf16[1024,512]{1,0:T(8,128)(2,1)S(1)} %collective-permute-done.15), channel_id=1, source_target_pairs={{0,64},{16,80},{32,96},{48,112},{64,128},{80,144},{96,160},{112,17... | collective-permute-start | bytes 3145736 | tf_op jit(solution)/shard_map/ppermute | solution.py:75
  103.4 26.9 %collective-permute-start.8 = (bf16[8,256,128]{2,1,0:T(8,128)(2,1)}, bf16[8,256,128]{2,1,0:T(8,128)(2,1)S(1)}, u32[]{:S(2)}, u32[]{:S(2)}) collective-permute-start(bf16[8,256,128]{2,1,0:T(8,128)(2,1)} %bitcast_dynamic-update-slice_fusion.16), channel_id=1, source_target_pairs={{0,16},{16,32},{32,48},{48,0},{64,80},{80,96},{96,112},{112,64},{1... | collective-permute-start | bytes 1572872 | tf_op jit(solution)/shard_map/ppermute | solution.py:75
  106.6 32.0 %collective-permute-start.7 = (bf16[8,256,128]{2,1,0:T(8,128)(2,1)}, bf16[8,256,128]{2,1,0:T(8,128)(2,1)S(1)}, u32[]{:S(2)}, u32[]{:S(2)}) collective-permute-start(bf16[8,256,128]{2,1,0:T(8,128)(2,1)} %bitcast_dynamic-update-slice_fusion.16), channel_id=1, source_target_pairs={{0,48},{16,0},{32,16},{48,32},{64,112},{80,64},{96,80},{112,96},{1... | collective-permute-start | bytes 1572872 | tf_op jit(solution)/shard_map/ppermute | solution.py:73
  111.4 36.2 %collective-permute-start.16 = (bf16[1024,512]{1,0:T(8,128)(2,1)S(1)}, bf16[1024,512]{1,0:T(8,128)(2,1)S(1)}, u32[]{:S(2)}, u32[]{:S(2)}) collective-permute-start(bf16[1024,512]{1,0:T(8,128)(2,1)S(1)} %collective-permute-done.14), channel_id=1, source_target_pairs={{0,448},{16,464},{32,480},{48,496},{64,0},{80,16},{96,32},{112,48}... | collective-permute-start | bytes 3145736 | tf_op jit(solution)/shard_map/ppermute | solution.py:73
  130.3 17.2 %collective-permute-start.9 = (bf16[8,256,128]{2,1,0:T(8,128)(2,1)S(1)}, bf16[8,256,128]{2,1,0:T(8,128)(2,1)S(1)}, u32[]{:S(2)}, u32[]{:S(2)}) collective-permute-start(bf16[8,256,128]{2,1,0:T(8,128)(2,1)S(1)} %collective-permute-done.8), channel_id=1, source_target_pairs={{0,16},{16,32},{32,48},{48,0},{64,80},{80,96},{96,112},{112,64},{1... | collective-permute-start | bytes 1572872 | tf_op jit(solution)/shard_map/ppermute | solution.py:75
  138.8 27.2 %collective-permute-start.19 = (bf16[1024,512]{1,0:T(8,128)(2,1)S(1)}, bf16[1024,512]{1,0:T(8,128)(2,1)S(1)}, u32[]{:S(2)}, u32[]{:S(2)}) collective-permute-start(bf16[1024,512]{1,0:T(8,128)(2,1)S(1)} %collective-permute-done.17), channel_id=1, source_target_pairs={{0,64},{16,80},{32,96},{48,112},{64,128},{80,144},{96,160},{112,17... | collective-permute-start | bytes 3145736 | tf_op jit(solution)/shard_map/ppermute | solution.py:75
  147.6 25.3 %collective-permute-start.18 = (bf16[1024,512]{1,0:T(8,128)(2,1)S(1)}, bf16[1024,512]{1,0:T(8,128)(2,1)S(1)}, u32[]{:S(2)}, u32[]{:S(2)}) collective-permute-start(bf16[1024,512]{1,0:T(8,128)(2,1)S(1)} %collective-permute-done.16), channel_id=1, source_target_pairs={{0,448},{16,464},{32,480},{48,496},{64,0},{80,16},{96,32},{112,48}... | collective-permute-start | bytes 3145736 | tf_op jit(solution)/shard_map/ppermute | solution.py:73
  166.0 25.9 %collective-permute-start.20 = (bf16[1024,512]{1,0:T(8,128)(2,1)S(1)}, bf16[1024,512]{1,0:T(8,128)(2,1)S(1)}, u32[]{:S(2)}, u32[]{:S(2)}) collective-permute-start(bf16[1024,512]{1,0:T(8,128)(2,1)S(1)} %collective-permute-done.19), channel_id=1, source_target_pairs={{0,64},{16,80},{32,96},{48,112},{64,128},{80,144},{96,160},{112,17... | collective-permute-start | bytes 3145736 | tf_op jit(solution)/shard_map/ppermute | solution.py:75
  204.2 11.3 %copy-start = (bf16[512,8192]{1,0:T(8,128)(2,1)S(1)}, bf16[512,8192]{1,0:T(8,128)(2,1)}, u32[]{:S(2)}) copy-start(bf16[512,8192]{1,0:T(8,128)(2,1)} %all-gather.2.cloned.1.call-done) | copy-start | bytes 25165828
  210.7 13.5 %collective-permute-start.10 = (bf16[512,128]{0,1:T(8,128)(2,1)S(1)}, bf16[512,128]{0,1:T(8,128)(2,1)S(1)}, u32[]{:S(2)}, u32[]{:S(2)}) collective-permute-start(bf16[512,128]{0,1:T(8,128)(2,1)S(1)} %convolution_convert_fusion), channel_id=1, source_target_pairs={{0,1},{1,0},{2,3},{3,2},{4,5},{5,4},{6,7},{7,6},{8,9},{9,8},{10,11... | collective-permute-start | bytes 393224 | tf_op jit(solution)/shard_map/ppermute | solution.py:107
  215.5 9.2 %copy-start.1 = (pred[512,512]{0,1:T(8,128)(4,1)S(1)}, pred[512,512]{0,1:T(8,128)(4,1)}, u32[]{:S(2)}) copy-start(pred[512,512]{0,1:T(8,128)(4,1)} %fusion.12) | copy-start | bytes 786436
Sparse Core Ops, SparseCore 0:
  10.0 73.8 all-gather.1

commit v5 on v3

--- a/solution.py
+++ b/solution.py
@@ -77,6 +77,36 @@
     return out
 
 
+def ring_matmul(rows, block, axis, stride, count):
+    n = lax.psum(1, axis)
+    me = lax.axis_index(axis)
+    here = (me // stride) % count
+    depth = block.shape[0]
+
+    def moved(step):
+        pairs = []
+        for src in range(n):
+            k = (src // stride) % count
+            pairs.append((src, src + (((k + step) % count) - k) * stride))
+        return pairs
+
+    def product(part, owner):
+        lhs = lax.dynamic_slice_in_dim(rows, owner * depth, depth, 1)
+        return jnp.dot(lhs, part, preferred_element_type=jnp.float32)
+
+    total = product(block, here)
+    from_right, from_left = block, block
+    for step in range(1, count // 2 + 1):
+        if step == 2:
+            rows, from_right, from_left = lax.optimization_barrier((rows, from_right, from_left))
+        if step < count - step:
+            from_right = lax.ppermute(from_right, axis, perm=moved(-1))
+            total = total + product(from_right, (here + step) % count)
+        from_left = lax.ppermute(from_left, axis, perm=moved(1))
+        total = total + product(from_left, (here - step) % count)
+    return total
+
+
 def per_device(tokens, segment_ids, norm_gain, query_weight, key_weight, value_weight):
     head_dim = HEAD_DIM
     query_cols = query_weight.shape[1]
@@ -97,10 +127,9 @@
     y_hi = n_batch // Z_CHIPS
     near = ring_gather(local_weights, "batch", 1, y_hi)
     near = near.reshape(-1, local_weights.shape[1])
-    full_weights = ring_gather(near, "batch", y_hi, Z_CHIPS).reshape(-1, near.shape[1])
     gathered = lax.all_gather(normed, "weight", axis=0, tiled=True)
     pack_rows = gathered.shape[0]
-    projected = jnp.dot(gathered, full_weights, preferred_element_type=jnp.float32)
+    projected = ring_matmul(gathered, near, "batch", y_hi, Z_CHIPS)
     query_part = projected[:, :query_cols]
     own_rows = projected[:, query_cols:].astype(jnp.bfloat16)
     partner = [(w, w ^ 1) for w in range(n_weight)]

time: 229 us -> 216 us (0.943)
  the two profiles are of different devices: /device:TPU:7 before, /device:TPU:55 now
where the time goes in v5:
time: 216 us
  waiting for transfers between devices  127 us (59%)
  starting transfers between devices  44.3 us (21%)
  matrix products  16.8 us (8%)
  between operations  14.6 us (7%)
  other arithmetic  9.05 us (4%)
  local copies, waits for them, and re-layouts  4.12 us (2%)
    ppermute x4, waiting for transfers between devices, ring_matmul(): from_left = lax.ppermute(from_left, axis, perm=moved(1))  63.6 us
    ppermute x2, waiting for transfers between devices, ring_gather(): from_left = lax.ppermute(from_left, axis, perm=moved(1))  31.3 us
    ppermute x3, waiting for transfers between devices, ring_matmul(): from_right = lax.ppermute(from_right, axis, perm=moved(-1))  27.7 us
    ppermute x3, starting transfers between devices, ring_matmul(): from_right = lax.ppermute(from_right, axis, perm=moved(-1))  21 us
    dot_general x8, matrix products, product(): return jnp.dot(lhs, part, preferred_element_type=jnp.float32)  14 us
    ppermute x4, starting transfers between devices, ring_matmul(): from_left = lax.ppermute(from_left, axis, perm=moved(1))  7.65 us
    ppermute x1, starting transfers between devices, per_device(): other_rows = lax.ppermute(own_rows, 'weight', perm=partner)  6.41 us
    ppermute x2, starting transfers between devices, ring_gather(): from_left = lax.ppermute(from_left, axis, perm=moved(1))  5.06 us
  transfers between devices with their start and end apart: 12, of which 9 were waited for; matrix products, arithmetic and copies ran while one was open for 9% of the time, Pallas kernels for 0%

profile of v5, /device:TPU:55, one launch (start us, length us, event | category | flops | bytes accessed | tf_op | source)
XLA Modules:
  0.0 215.8 jit_solution(10953475496737112914)
XLA Ops:
  6.5 1.3 fusion.11
  7.8 2.0 fusion.13
  9.9 0.9 dynamic-slice_select_fusion
  10.9 1.9 collective-permute-start.1
  12.8 4.3 %collective-permute-start = (bf16[256,640]{1,0:T(8,128)(2,1)S(1)}, bf16[256,640]{1,0:T(8,128)(2,1)S(1)}, u32[]{:S(2)}, u32[]{:S(2)}) collective-permute-start(bf16[256,640]{1,0:T(8,128)(2,1)S(1)} %pad_maximum_fusion), channel_id=1, source_target_pairs={{0,48},{16,0},{32,16},{48,32},{64,112},{80,64},{96,80},{112,96},{1... | collective-permute-start | bytes 983048 | tf_op jit(solution)/shard_map/ppermute | solution.py:73
  17.2 0.1 broadcast_in_dim.43
  17.3 8.2 %collective-permute-done.1 = bf16[256,640]{1,0:T(8,128)(2,1)S(1)} collective-permute-done((bf16[256,640]{1,0:T(8,128)(2,1)S(1)}, bf16[256,640]{1,0:T(8,128)(2,1)S(1)}, u32[]{:S(2)}, u32[]{:S(2)}) %collective-permute-start.1) | collective-permute-done | bytes 327712 | tf_op jit(solution)/shard_map/ppermute | solution.py:75
  25.5 3.1 %collective-permute-start.2 = (bf16[256,640]{1,0:T(8,128)(2,1)S(1)}, bf16[256,640]{1,0:T(8,128)(2,1)S(1)}, u32[]{:S(2)}, u32[]{:S(2)}) collective-permute-start(bf16[256,640]{1,0:T(8,128)(2,1)S(1)} %collective-permute-done.1), channel_id=1, source_target_pairs={{0,16},{16,32},{32,48},{48,0},{64,80},{80,96},{96,112},{112,64},{1... | collective-permute-start | bytes 983048 | tf_op jit(solution)/shard_map/ppermute | solution.py:75
  28.7 4.2 %collective-permute-done = bf16[256,640]{1,0:T(8,128)(2,1)S(1)} collective-permute-done((bf16[256,640]{1,0:T(8,128)(2,1)S(1)}, bf16[256,640]{1,0:T(8,128)(2,1)S(1)}, u32[]{:S(2)}, u32[]{:S(2)}) %collective-permute-start) | collective-permute-done | bytes 327712 | tf_op jit(solution)/shard_map/ppermute | solution.py:73
  33.0 23.1 %collective-permute-done.2 = bf16[256,640]{1,0:T(8,128)(2,1)S(1)} collective-permute-done((bf16[256,640]{1,0:T(8,128)(2,1)S(1)}, bf16[256,640]{1,0:T(8,128)(2,1)S(1)}, u32[]{:S(2)}, u32[]{:S(2)}) %collective-permute-start.2) | collective-permute-done | bytes 327712 | tf_op jit(solution)/shard_map/ppermute | solution.py:75
  56.1 11.8 %collective-permute-start.3 = (bf16[1024,640]{1,0:T(8,128)(2,1)S(1)}, bf16[1024,640]{1,0:T(8,128)(2,1)S(1)}, u32[]{:S(2)}, u32[]{:S(2)}) collective-permute-start(bf16[1024,640]{1,0:T(8,128)(2,1)S(1)} %bitcast.62), channel_id=1, source_target_pairs={{0,448},{16,464},{32,480},{48,496},{64,0},{80,16},{96,32},{112,48}... | collective-permute-start | bytes 3932168 | tf_op jit(solution)/shard_map/ppermute | solution.py:103
  67.9 1.9 collective-permute-start.4
  69.8 25.8 %collective-permute-done.3 = bf16[1024,640]{1,0:T(8,128)(2,1)S(1)} collective-permute-done((bf16[1024,640]{1,0:T(8,128)(2,1)S(1)}, bf16[1024,640]{1,0:T(8,128)(2,1)S(1)}, u32[]{:S(2)}, u32[]{:S(2)}) %collective-permute-start.3) | collective-permute-done | bytes 1310752 | tf_op jit(solution)/shard_map/ppermute | solution.py:103
  95.6 5.1 %collective-permute-done.4 = bf16[1024,640]{1,0:T(8,128)(2,1)} collective-permute-done((bf16[1024,640]{1,0:T(8,128)(2,1)S(1)}, bf16[1024,640]{1,0:T(8,128)(2,1)}, u32[]{:S(2)}, u32[]{:S(2)}) %collective-permute-start.4) | collective-permute-done | bytes 1310752 | tf_op jit(solution)/shard_map/ppermute | solution.py:105
  100.8 1.9 collective-permute-start.6
  102.7 0.5 slice.34
  103.9 0.3 reduce-window.9
  104.3 0.1 slice_reduce_fusion
  104.5 4.6 %collective-permute-start.5 = (bf16[1024,640]{1,0:T(8,128)(2,1)S(1)}, bf16[1024,640]{1,0:T(8,128)(2,1)}, u32[]{:S(2)}, u32[]{:S(2)}) collective-permute-start(bf16[1024,640]{1,0:T(8,128)(2,1)S(1)} %collective-permute-done.3), channel_id=1, source_target_pairs={{0,448},{16,464},{32,480},{48,496},{64,0},{80,16},{96,32},{112,48}... | collective-permute-start | bytes 3932168 | tf_op jit(solution)/shard_map/ppermute | solution.py:103
  109.2 0.9 fusion.27
  110.1 22.7 %collective-permute-done.6 = bf16[1024,640]{1,0:T(8,128)(2,1)} collective-permute-done((bf16[1024,640]{1,0:T(8,128)(2,1)}, bf16[1024,640]{1,0:T(8,128)(2,1)}, u32[]{:S(2)}, u32[]{:S(2)}) %collective-permute-start.6) | collective-permute-done | bytes 1310752 | tf_op jit(solution)/shard_map/ppermute | solution.py:105
  132.9 1.9 collective-permute-start.8
  134.9 1.8 multiply_cosine_fusion
  136.7 2.3 %fusion.24 = f32[512,640]{1,0:T(8,128)S(1)} fusion(bf16[1024,640]{1,0:T(8,128)(2,1)S(1)} %collective-permute-done.3, bf16[512,8192]{1,0:T(8,128)(2,1)} %all-gather.2.cloned.1.call-done, s32[]{:T(128)S(6)} %select_n.150), kind=kOutput, calls=%fused_computation.32 | convolution fusion | flops 671088640 | bytes 3670020 | tf_op jit(solution)/shard_map/dot_general | solution.py:95
  139.0 3.0 %fusion.22 = f32[512,640]{1,0:T(8,128)S(1)} fusion(bf16[1024,640]{1,0:T(8,128)(2,1)} %collective-permute-done.4, bf16[512,8192]{1,0:T(8,128)(2,1)} %all-gather.2.cloned.1.call-done, s32[]{:T(128)S(6)} %select_n.152), kind=kOutput, calls=%fused_computation.30 | convolution fusion | flops 671088640 | bytes 3670020 | tf_op jit(solution)/shard_map/dot_general | solution.py:95
  142.0 4.6 %collective-permute-start.7 = (bf16[1024,640]{1,0:T(8,128)(2,1)}, bf16[1024,640]{1,0:T(8,128)(2,1)S(1)}, u32[]{:S(2)}, u32[]{:S(2)}) collective-permute-start(bf16[1024,640]{1,0:T(8,128)(2,1)} %collective-permute-done.5), channel_id=1, source_target_pairs={{0,448},{16,464},{32,480},{48,496},{64,0},{80,16},{96,32},{112,48}... | collective-permute-start | bytes 3932168 | tf_op jit(solution)/shard_map/ppermute | solution.py:103
  146.6 2.3 %fusion.20 = f32[512,640]{1,0:T(8,128)S(1)} fusion(bf16[1024,640]{1,0:T(8,128)(2,1)} %collective-permute-done.5, bf16[512,8192]{1,0:T(8,128)(2,1)S(1)} %copy-done, s32[]{:T(128)S(6)} %select_n.154), kind=kOutput, calls=%fused_computation.28 | convolution fusion | flops 671088640 | bytes 3670020 | tf_op jit(solution)/shard_map/dot_general | solution.py:95
  148.9 15.0 %collective-permute-done.8 = bf16[1024,640]{1,0:T(8,128)(2,1)S(1)} collective-permute-done((bf16[1024,640]{1,0:T(8,128)(2,1)}, bf16[1024,640]{1,0:T(8,128)(2,1)S(1)}, u32[]{:S(2)}, u32[]{:S(2)}) %collective-permute-start.8) | collective-permute-done | bytes 1310752 | tf_op jit(solution)/shard_map/ppermute | solution.py:105
  164.0 1.9 collective-permute-start.9
  165.9 2.3 %fusion.18 = f32[512,640]{1,0:T(8,128)S(1)} fusion(bf16[1024,640]{1,0:T(8,128)(2,1)} %collective-permute-done.6, bf16[512,8192]{1,0:T(8,128)(2,1)S(1)} %copy-done, s32[]{:T(128)S(6)} %select_n.156), kind=kOutput, calls=%fused_computation.26 | convolution fusion | flops 671088640 | bytes 3670020 | tf_op jit(solution)/shard_map/dot_general | solution.py:95
  168.2 1.1 fusion.7
  169.3 1.0 fusion.15
  170.3 1.9 collective-permute-done.7
  172.2 1.0 fusion.4
  173.2 20.7 %collective-permute-done.9 = bf16[1024,640]{1,0:T(8,128)(2,1)S(1)} collective-permute-done((bf16[1024,640]{1,0:T(8,128)(2,1)S(1)}, bf16[1024,640]{1,0:T(8,128)(2,1)S(1)}, u32[]{:S(2)}, u32[]{:S(2)}) %collective-permute-start.9) | collective-permute-done | bytes 1310752 | tf_op jit(solution)/shard_map/ppermute | solution.py:105
  193.9 1.0 convolution_add_fusion
  194.9 0.7 slice.62
  195.6 0.1 slice.45
  195.7 6.4 %collective-permute-start.10 = (bf16[512,128]{1,0:T(8,128)(2,1)}, bf16[512,128]{1,0:T(8,128)(2,1)S(1)}, u32[]{:S(2)}, u32[]{:S(2)}) collective-permute-start(bf16[512,128]{1,0:T(8,128)(2,1)} %slice.62), channel_id=1, source_target_pairs={{0,1},{1,0},{2,3},{3,2},{4,5},{5,4},{6,7},{7,6},{8,9},{9,8},{10,11... | collective-permute-start | bytes 393224 | tf_op jit(solution)/shard_map/ppermute | solution.py:136
  202.1 0.4 reshape.196
  202.5 0.6 fusion.59
  203.1 0.3 copy-done.1
  203.5 0.1 copy-done.2
  203.5 0.3 subtract_convert_fusion
  203.9 1.2 fusion.45
  205.1 1.5 fusion
  206.6 1.3 fusion.8
  207.9 1.0 copy.16
  (27 shorter events, 0.6 us)
Async XLA Ops:
  6.5 4.3 %copy-start.3 = (bf16[256,512]{1,0:T(8,128)(2,1)S(1)}, bf16[256,512]{1,0:T(8,128)(2,1)}, u32[]{:S(2)}) copy-start(bf16[256,512]{1,0:T(8,128)(2,1)} %param.9) | copy-start | bytes 786436
  6.5 94.2 %all-gather.2.cloned.1.call-start = ((), (), s32[]{:S(2)}) async-start(), calls=%async_computation | async-start | bytes 8912896 | tf_op jit(solution)/shard_map/all_gather | solution.py:130
  10.9 14.6 %collective-permute-start.1 = (bf16[256,640]{1,0:T(8,128)(2,1)S(1)}, bf16[256,640]{1,0:T(8,128)(2,1)S(1)}, u32[]{:S(2)}, u32[]{:S(2)}) collective-permute-start(bf16[256,640]{1,0:T(8,128)(2,1)S(1)} %pad_maximum_fusion), channel_id=1, source_target_pairs={{0,16},{16,32},{32,48},{48,0},{64,80},{80,96},{96,112},{112,64},{1... | collective-permute-start | bytes 983048 | tf_op jit(solution)/shard_map/ppermute | solution.py:75
  12.8 20.1 %collective-permute-start = (bf16[256,640]{1,0:T(8,128)(2,1)S(1)}, bf16[256,640]{1,0:T(8,128)(2,1)S(1)}, u32[]{:S(2)}, u32[]{:S(2)}) collective-permute-start(bf16[256,640]{1,0:T(8,128)(2,1)S(1)} %pad_maximum_fusion), channel_id=1, source_target_pairs={{0,48},{16,0},{32,16},{48,32},{64,112},{80,64},{96,80},{112,96},{1... | collective-permute-start | bytes 983048 | tf_op jit(solution)/shard_map/ppermute | solution.py:73
  17.3 85.4 %copy-start.5 = (s32[512]{0:T(512)S(1)}, s32[512]{0:T(512)}, u32[]{:S(2)}) copy-start(s32[512]{0:T(512)} %param.7) | copy-start | bytes 6148
  25.5 30.5 %collective-permute-start.2 = (bf16[256,640]{1,0:T(8,128)(2,1)S(1)}, bf16[256,640]{1,0:T(8,128)(2,1)S(1)}, u32[]{:S(2)}, u32[]{:S(2)}) collective-permute-start(bf16[256,640]{1,0:T(8,128)(2,1)S(1)} %collective-permute-done.1), channel_id=1, source_target_pairs={{0,16},{16,32},{32,48},{48,0},{64,80},{80,96},{96,112},{112,64},{1... | collective-permute-start | bytes 983048 | tf_op jit(solution)/shard_map/ppermute | solution.py:75
  56.1 39.6 %collective-permute-start.3 = (bf16[1024,640]{1,0:T(8,128)(2,1)S(1)}, bf16[1024,640]{1,0:T(8,128)(2,1)S(1)}, u32[]{:S(2)}, u32[]{:S(2)}) collective-permute-start(bf16[1024,640]{1,0:T(8,128)(2,1)S(1)} %bitcast.62), channel_id=1, source_target_pairs={{0,448},{16,464},{32,480},{48,496},{64,0},{80,16},{96,32},{112,48}... | collective-permute-start | bytes 3932168 | tf_op jit(solution)/shard_map/ppermute | solution.py:103
  67.9 32.9 %collective-permute-start.4 = (bf16[1024,640]{1,0:T(8,128)(2,1)S(1)}, bf16[1024,640]{1,0:T(8,128)(2,1)}, u32[]{:S(2)}, u32[]{:S(2)}) collective-permute-start(bf16[1024,640]{1,0:T(8,128)(2,1)S(1)} %bitcast.63), channel_id=1, source_target_pairs={{0,64},{16,80},{32,96},{48,112},{64,128},{80,144},{96,160},{112,17... | collective-permute-start | bytes 3932168 | tf_op jit(solution)/shard_map/ppermute | solution.py:105
  100.8 32.1 %collective-permute-start.6 = (bf16[1024,640]{1,0:T(8,128)(2,1)}, bf16[1024,640]{1,0:T(8,128)(2,1)}, u32[]{:S(2)}, u32[]{:S(2)}) collective-permute-start(bf16[1024,640]{1,0:T(8,128)(2,1)} %collective-permute-done.4), channel_id=1, source_target_pairs={{0,64},{16,80},{32,96},{48,112},{64,128},{80,144},{96,160},{112,17... | collective-permute-start | bytes 3932168 | tf_op jit(solution)/shard_map/ppermute | solution.py:105
  104.5 37.5 %collective-permute-start.5 = (bf16[1024,640]{1,0:T(8,128)(2,1)S(1)}, bf16[1024,640]{1,0:T(8,128)(2,1)}, u32[]{:S(2)}, u32[]{:S(2)}) collective-permute-start(bf16[1024,640]{1,0:T(8,128)(2,1)S(1)} %collective-permute-done.3), channel_id=1, source_target_pairs={{0,448},{16,464},{32,480},{48,496},{64,0},{80,16},{96,32},{112,48}... | collective-permute-start | bytes 3932168 | tf_op jit(solution)/shard_map/ppermute | solution.py:103
  132.9 31.1 %collective-permute-start.8 = (bf16[1024,640]{1,0:T(8,128)(2,1)}, bf16[1024,640]{1,0:T(8,128)(2,1)S(1)}, u32[]{:S(2)}, u32[]{:S(2)}) collective-permute-start(bf16[1024,640]{1,0:T(8,128)(2,1)} %collective-permute-done.6), channel_id=1, source_target_pairs={{0,64},{16,80},{32,96},{48,112},{64,128},{80,144},{96,160},{112,17... | collective-permute-start | bytes 3932168 | tf_op jit(solution)/shard_map/ppermute | solution.py:105
  136.7 9.9 %copy-start = (bf16[512,8192]{1,0:T(8,128)(2,1)S(1)}, bf16[512,8192]{1,0:T(8,128)(2,1)}, u32[]{:S(2)}) copy-start(bf16[512,8192]{1,0:T(8,128)(2,1)} %all-gather.2.cloned.1.call-done) | copy-start | bytes 25165828
  142.0 30.2 %collective-permute-start.7 = (bf16[1024,640]{1,0:T(8,128)(2,1)}, bf16[1024,640]{1,0:T(8,128)(2,1)S(1)}, u32[]{:S(2)}, u32[]{:S(2)}) collective-permute-start(bf16[1024,640]{1,0:T(8,128)(2,1)} %collective-permute-done.5), channel_id=1, source_target_pairs={{0,448},{16,464},{32,480},{48,496},{64,0},{80,16},{96,32},{112,48}... | collective-permute-start | bytes 3932168 | tf_op jit(solution)/shard_map/ppermute | solution.py:103
  164.0 30.0 %collective-permute-start.9 = (bf16[1024,640]{1,0:T(8,128)(2,1)S(1)}, bf16[1024,640]{1,0:T(8,128)(2,1)S(1)}, u32[]{:S(2)}, u32[]{:S(2)}) collective-permute-start(bf16[1024,640]{1,0:T(8,128)(2,1)S(1)} %collective-permute-done.8), channel_id=1, source_target_pairs={{0,64},{16,80},{32,96},{48,112},{64,128},{80,144},{96,160},{112,17... | collective-permute-start | bytes 3932168 | tf_op jit(solution)/shard_map/ppermute | solution.py:105
  195.7 8.1 %collective-permute-start.10 = (bf16[512,128]{1,0:T(8,128)(2,1)}, bf16[512,128]{1,0:T(8,128)(2,1)S(1)}, u32[]{:S(2)}, u32[]{:S(2)}) collective-permute-start(bf16[512,128]{1,0:T(8,128)(2,1)} %slice.62), channel_id=1, source_target_pairs={{0,1},{1,0},{2,3},{3,2},{4,5},{5,4},{6,7},{7,6},{8,9},{9,8},{10,11... | collective-permute-start | bytes 393224 | tf_op jit(solution)/shard_map/ppermute | solution.py:136
  202.5 1.0 copy-start.1
  202.5 1.0 copy-start.2
  203.8 1.3 copy-start.4
Sparse Core Ops, SparseCore 0:
  10.0 73.5 all-gather.1

commit v6 on v5

--- a/solution.py
+++ b/solution.py
@@ -122,16 +122,14 @@
     values = tokens.astype(jnp.float32)
     inverse_rms = lax.rsqrt(jnp.mean(values * values, axis=1, keepdims=True) + EPSILON)
     normed = (values * inverse_rms * norm_gain[None, :]).astype(jnp.bfloat16)
-    local_weights = jnp.concatenate([query_weight, kv_block], axis=1)
     n_batch = lax.psum(1, "batch")
     y_hi = n_batch // Z_CHIPS
-    near = ring_gather(local_weights, "batch", 1, y_hi)
-    near = near.reshape(-1, local_weights.shape[1])
+    near = ring_gather(query_weight, "batch", 1, y_hi).reshape(-1, query_cols)
+    kv_full = lax.all_gather(kv_block, "batch", axis=0, tiled=True)
     gathered = lax.all_gather(normed, "weight", axis=0, tiled=True)
     pack_rows = gathered.shape[0]
-    projected = ring_matmul(gathered, near, "batch", y_hi, Z_CHIPS)
-    query_part = projected[:, :query_cols]
-    own_rows = projected[:, query_cols:].astype(jnp.bfloat16)
+    query_part = ring_matmul(gathered, near, "batch", y_hi, Z_CHIPS)
+    own_rows = jnp.dot(gathered, kv_full, preferred_element_type=jnp.float32).astype(jnp.bfloat16)
     partner = [(w, w ^ 1) for w in range(n_weight)]
     other_rows = lax.ppermute(own_rows, "weight", perm=partner)
     key_rows = jnp.where(core == 0, own_rows, other_rows)

time: 216 us -> 253 us (1.17)
  the two profiles are of different devices: /device:TPU:55 before, /device:TPU:7 now
where the time goes in v6:
time: 253 us; the launch traced here: 251 us
  waiting for transfers between devices  162 us (64%)
  starting transfers between devices  42.6 us (17%)
  matrix products  20.5 us (8%)
  between operations  14.7 us (6%)
  other arithmetic  8.04 us (3%)
  local copies, waits for them, and re-layouts  3.67 us (1%)
    all_gather x1, waiting for transfers between devices, per_device(): kv_full = lax.all_gather(kv_block, 'batch', axis=0, tiled=True)  78.2 us
    ppermute x4, waiting for transfers between devices, ring_matmul(): from_left = lax.ppermute(from_left, axis, perm=moved(1))  41.2 us
    ppermute x2, waiting for transfers between devices, ring_gather(): from_left = lax.ppermute(from_left, axis, perm=moved(1))  21.4 us
    ppermute x3, starting transfers between devices, ring_matmul(): from_right = lax.ppermute(from_right, axis, perm=moved(-1))  19.7 us
    ppermute x3, waiting for transfers between devices, ring_matmul(): from_right = lax.ppermute(from_right, axis, perm=moved(-1))  16.2 us
    dot_general x8, matrix products, product(): return jnp.dot(lhs, part, preferred_element_type=jnp.float32)  9.85 us
    ppermute x4, starting transfers between devices, ring_matmul(): from_left = lax.ppermute(from_left, axis, perm=moved(1))  8.61 us
    dot_general x1, matrix products, per_device(): jnp.dot(gathered, kv_full, preferred_element_type=jnp.float32)  7 us
  transfers between devices with their start and end apart: 13, of which 8 were waited for; matrix products, arithmetic and copies ran while one was open for 9% of the time, Pallas kernels for 0%

profile of v6, /device:TPU:7, one launch (start us, length us, event | category | flops | bytes accessed | tf_op | source)
XLA Modules:
  0.0 251.3 jit_solution(16309729181224051123)
XLA Ops:
  6.5 1.3 fusion.11
  7.8 2.0 fusion.13
  9.9 1.5 dynamic-slice_select_fusion
  11.5 4.2 %collective-permute-start.2 = (bf16[256,512]{1,0:T(8,128)(2,1)}, bf16[256,512]{1,0:T(8,128)(2,1)S(1)}, u32[]{:S(2)}, u32[]{:S(2)}) collective-permute-start(bf16[256,512]{1,0:T(8,128)(2,1)} %param.9), channel_id=1, source_target_pairs={{0,16},{16,32},{32,48},{48,0},{64,80},{80,96},{96,112},{112,64},{1... | collective-permute-start | bytes 786440 | tf_op jit(solution)/shard_map/ppermute | solution.py:75
  15.7 3.6 %collective-permute-start.1 = (bf16[256,512]{1,0:T(8,128)(2,1)}, bf16[256,512]{1,0:T(8,128)(2,1)S(1)}, u32[]{:S(2)}, u32[]{:S(2)}) collective-permute-start(bf16[256,512]{1,0:T(8,128)(2,1)} %param.9), channel_id=1, source_target_pairs={{0,48},{16,0},{32,16},{48,32},{64,112},{80,64},{96,80},{112,96},{1... | collective-permute-start | bytes 786440 | tf_op jit(solution)/shard_map/ppermute | solution.py:73
  19.4 0.1 broadcast_in_dim.45
  19.5 1.0 bitcast_dynamic-update-slice_fusion.3
  20.5 6.1 %collective-permute-done.2 = bf16[256,512]{1,0:T(8,128)(2,1)S(1)} collective-permute-done((bf16[256,512]{1,0:T(8,128)(2,1)}, bf16[256,512]{1,0:T(8,128)(2,1)S(1)}, u32[]{:S(2)}, u32[]{:S(2)}) %collective-permute-start.2) | collective-permute-done | bytes 262176 | tf_op jit(solution)/shard_map/ppermute | solution.py:75
  26.6 2.2 collective-permute-start.3
  28.8 4.9 %collective-permute-done.1 = bf16[256,512]{1,0:T(8,128)(2,1)S(1)} collective-permute-done((bf16[256,512]{1,0:T(8,128)(2,1)}, bf16[256,512]{1,0:T(8,128)(2,1)S(1)}, u32[]{:S(2)}, u32[]{:S(2)}) %collective-permute-start.1) | collective-permute-done | bytes 262176 | tf_op jit(solution)/shard_map/ppermute | solution.py:73
  33.7 15.3 %collective-permute-done.3 = bf16[256,512]{1,0:T(8,128)(2,1)S(1)} collective-permute-done((bf16[256,512]{1,0:T(8,128)(2,1)S(1)}, bf16[256,512]{1,0:T(8,128)(2,1)S(1)}, u32[]{:S(2)}, u32[]{:S(2)}) %collective-permute-start.3) | collective-permute-done | bytes 262176 | tf_op jit(solution)/shard_map/ppermute | solution.py:75
  49.0 11.2 %collective-permute-start.4 = (bf16[1024,512]{1,0:T(8,128)(2,1)S(1)}, bf16[1024,512]{1,0:T(8,128)(2,1)S(1)}, u32[]{:S(2)}, u32[]{:S(2)}) collective-permute-start(bf16[1024,512]{1,0:T(8,128)(2,1)S(1)} %bitcast.66), channel_id=1, source_target_pairs={{0,448},{16,464},{32,480},{48,496},{64,0},{80,16},{96,32},{112,48}... | collective-permute-start | bytes 3145736 | tf_op jit(solution)/shard_map/ppermute | solution.py:103
  60.2 1.9 collective-permute-start.5
  62.3 0.6 slice.26
  63.5 0.1 select_bitcast_fusion
  63.6 0.3 reduce-window.9
  63.9 0.1 slice.28
  64.1 0.1 slice_reduce_fusion
  64.2 0.2 fusion.27
  64.4 16.2 %collective-permute-done.4 = bf16[1024,512]{1,0:T(8,128)(2,1)S(1)} collective-permute-done((bf16[1024,512]{1,0:T(8,128)(2,1)S(1)}, bf16[1024,512]{1,0:T(8,128)(2,1)S(1)}, u32[]{:S(2)}, u32[]{:S(2)}) %collective-permute-start.4) | collective-permute-done | bytes 1048608 | tf_op jit(solution)/shard_map/ppermute | solution.py:103
  80.6 5.2 %collective-permute-done.5 = bf16[1024,512]{1,0:T(8,128)(2,1)} collective-permute-done((bf16[1024,512]{1,0:T(8,128)(2,1)S(1)}, bf16[1024,512]{1,0:T(8,128)(2,1)}, u32[]{:S(2)}, u32[]{:S(2)}) %collective-permute-start.5) | collective-permute-done | bytes 1048608 | tf_op jit(solution)/shard_map/ppermute | solution.py:105
  85.7 1.9 collective-permute-start.7
  87.8 1.0 multiply_cosine_fusion
  88.8 4.7 %collective-permute-start.6 = (bf16[1024,512]{1,0:T(8,128)(2,1)}, bf16[1024,512]{1,0:T(8,128)(2,1)}, u32[]{:S(2)}, u32[]{:S(2)}) collective-permute-start(bf16[1024,512]{1,0:T(8,128)(2,1)} %copy-done.4), channel_id=1, source_target_pairs={{0,448},{16,464},{32,480},{48,496},{64,0},{80,16},{96,32},{112,48}... | collective-permute-start | bytes 3145736 | tf_op jit(solution)/shard_map/ppermute | solution.py:103
  93.5 78.2 %all-gather.5.cloned.1.call-done = bf16[8192,128]{1,0:T(8,128)(2,1)} async-done(((bf16[256,128]{1,0:T(8,128)(2,1)}), bf16[8192,128]{1,0:T(8,128)(2,1)}) %all-gather.5.cloned.1.call-update) | async-done | bytes 2097168 | tf_op jit(solution)/shard_map/all_gather | solution.py:128
  171.7 7.0 %convolution_convert_fusion = bf16[512,128]{0,1:T(8,128)(2,1)S(1)} fusion(bf16[512,8192]{1,0:T(8,128)(2,1)} %all-gather.3.cloned.1.call-done, bf16[8192,128]{1,0:T(8,128)(2,1)} %all-gather.5.cloned.1.call-done), kind=kOutput, calls=%fused_computation.16 | convolution fusion | flops 1073807360 | bytes 10616832 | tf_op jit(solution)/shard_map/dot_general | solution.py:132
  178.7 4.2 %collective-permute-start = (bf16[512,128]{0,1:T(8,128)(2,1)S(1)}, bf16[512,128]{0,1:T(8,128)(2,1)S(1)}, u32[]{:S(2)}, u32[]{:S(2)}) collective-permute-start(bf16[512,128]{0,1:T(8,128)(2,1)S(1)} %convolution_convert_fusion), channel_id=1, source_target_pairs={{0,1},{1,0},{2,3},{3,2},{4,5},{5,4},{6,7},{7,6},{8,9},{9,8},{10,11... | collective-permute-start | bytes 393224 | tf_op jit(solution)/shard_map/ppermute | solution.py:134
  182.9 2.7 %collective-permute-start.9 = (bf16[1024,512]{1,0:T(8,128)(2,1)}, bf16[1024,512]{1,0:T(8,128)(2,1)S(1)}, u32[]{:S(2)}, u32[]{:S(2)}) collective-permute-start(bf16[1024,512]{1,0:T(8,128)(2,1)} %collective-permute-done.7), channel_id=1, source_target_pairs={{0,64},{16,80},{32,96},{48,112},{64,128},{80,144},{96,160},{112,17... | collective-permute-start | bytes 3145736 | tf_op jit(solution)/shard_map/ppermute | solution.py:105
  185.6 0.8 fusion.24
  186.4 2.0 fusion.22
  188.4 1.2 fusion.46
  189.6 3.8 %collective-permute-start.8 = (bf16[1024,512]{1,0:T(8,128)(2,1)}, bf16[1024,512]{1,0:T(8,128)(2,1)S(1)}, u32[]{:S(2)}, u32[]{:S(2)}) collective-permute-start(bf16[1024,512]{1,0:T(8,128)(2,1)} %collective-permute-done.6), channel_id=1, source_target_pairs={{0,448},{16,464},{32,480},{48,496},{64,0},{80,16},{96,32},{112,48}... | collective-permute-start | bytes 3145736 | tf_op jit(solution)/shard_map/ppermute | solution.py:103
  193.4 2.0 fusion.20
  195.5 15.5 %collective-permute-done.9 = bf16[1024,512]{1,0:T(8,128)(2,1)S(1)} collective-permute-done((bf16[1024,512]{1,0:T(8,128)(2,1)}, bf16[1024,512]{1,0:T(8,128)(2,1)S(1)}, u32[]{:S(2)}, u32[]{:S(2)}) %collective-permute-start.9) | collective-permute-done | bytes 1048608 | tf_op jit(solution)/shard_map/ppermute | solution.py:105
  211.0 2.1 collective-permute-start.10
  213.1 2.0 fusion.18
  215.1 0.8 fusion.7
  215.9 0.8 fusion.15
  216.7 0.8 fusion.4
  217.5 20.5 %collective-permute-done.10 = bf16[1024,512]{1,0:T(8,128)(2,1)S(1)} collective-permute-done((bf16[1024,512]{1,0:T(8,128)(2,1)S(1)}, bf16[1024,512]{1,0:T(8,128)(2,1)S(1)}, u32[]{:S(2)}, u32[]{:S(2)}) %collective-permute-start.10) | collective-permute-done | bytes 1048608 | tf_op jit(solution)/shard_map/ppermute | solution.py:105
  238.0 0.7 convolution_add_fusion
  238.7 0.1 fusion.59
  238.8 0.3 copy.20
  239.2 0.3 copy.21
  239.5 0.3 subtract_convert_fusion
  239.8 2.3 fusion
  242.1 1.3 fusion.8
  243.5 1.0 copy.16
  (29 shorter events, 0.3 us)
Async XLA Ops:
  6.5 55.8 %copy-start.3 = (s32[512]{0:T(512)S(1)}, s32[512]{0:T(512)}, u32[]{:S(2)}) copy-start(s32[512]{0:T(512)} %param.7) | copy-start | bytes 6148
  6.5 79.2 %all-gather.3.cloned.1.call-start = ((), (), s32[]{:S(2)}) async-start(), calls=%async_computation | async-start | bytes 8912896 | tf_op jit(solution)/shard_map/all_gather | solution.py:129
  9.9 161.8 %all-gather.5.cloned.1.call-start = ((), (), s32[]{:S(2)}) async-start(), calls=%async_computation.1 | async-start | bytes 2162688 | tf_op jit(solution)/shard_map/all_gather | solution.py:128
  11.5 15.1 %collective-permute-start.2 = (bf16[256,512]{1,0:T(8,128)(2,1)}, bf16[256,512]{1,0:T(8,128)(2,1)S(1)}, u32[]{:S(2)}, u32[]{:S(2)}) collective-permute-start(bf16[256,512]{1,0:T(8,128)(2,1)} %param.9), channel_id=1, source_target_pairs={{0,16},{16,32},{32,48},{48,0},{64,80},{80,96},{96,112},{112,64},{1... | collective-permute-start | bytes 786440 | tf_op jit(solution)/shard_map/ppermute | solution.py:75
  15.7 17.9 %collective-permute-start.1 = (bf16[256,512]{1,0:T(8,128)(2,1)}, bf16[256,512]{1,0:T(8,128)(2,1)S(1)}, u32[]{:S(2)}, u32[]{:S(2)}) collective-permute-start(bf16[256,512]{1,0:T(8,128)(2,1)} %param.9), channel_id=1, source_target_pairs={{0,48},{16,0},{32,16},{48,32},{64,112},{80,64},{96,80},{112,96},{1... | collective-permute-start | bytes 786440 | tf_op jit(solution)/shard_map/ppermute | solution.py:73
  26.6 22.4 %collective-permute-start.3 = (bf16[256,512]{1,0:T(8,128)(2,1)S(1)}, bf16[256,512]{1,0:T(8,128)(2,1)S(1)}, u32[]{:S(2)}, u32[]{:S(2)}) collective-permute-start(bf16[256,512]{1,0:T(8,128)(2,1)S(1)} %collective-permute-done.2), channel_id=1, source_target_pairs={{0,16},{16,32},{32,48},{48,0},{64,80},{80,96},{96,112},{112,64},{1... | collective-permute-start | bytes 786440 | tf_op jit(solution)/shard_map/ppermute | solution.py:75
  49.0 31.6 %collective-permute-start.4 = (bf16[1024,512]{1,0:T(8,128)(2,1)S(1)}, bf16[1024,512]{1,0:T(8,128)(2,1)S(1)}, u32[]{:S(2)}, u32[]{:S(2)}) collective-permute-start(bf16[1024,512]{1,0:T(8,128)(2,1)S(1)} %bitcast.66), channel_id=1, source_target_pairs={{0,448},{16,464},{32,480},{48,496},{64,0},{80,16},{96,32},{112,48}... | collective-permute-start | bytes 3145736 | tf_op jit(solution)/shard_map/ppermute | solution.py:103
  60.2 25.5 %collective-permute-start.5 = (bf16[1024,512]{1,0:T(8,128)(2,1)S(1)}, bf16[1024,512]{1,0:T(8,128)(2,1)}, u32[]{:S(2)}, u32[]{:S(2)}) collective-permute-start(bf16[1024,512]{1,0:T(8,128)(2,1)S(1)} %bitcast.67), channel_id=1, source_target_pairs={{0,64},{16,80},{32,96},{48,112},{64,128},{80,144},{96,160},{112,17... | collective-permute-start | bytes 3145736 | tf_op jit(solution)/shard_map/ppermute | solution.py:105
  80.6 7.1 %copy-start.4 = (bf16[1024,512]{1,0:T(8,128)(2,1)}, bf16[1024,512]{1,0:T(8,128)(2,1)S(1)}, u32[]{:S(2)}) copy-start(bf16[1024,512]{1,0:T(8,128)(2,1)S(1)} %collective-permute-done.4) | copy-start | bytes 3145732
  85.7 97.1 %collective-permute-start.7 = (bf16[1024,512]{1,0:T(8,128)(2,1)}, bf16[1024,512]{1,0:T(8,128)(2,1)}, u32[]{:S(2)}, u32[]{:S(2)}) collective-permute-start(bf16[1024,512]{1,0:T(8,128)(2,1)} %collective-permute-done.5), channel_id=1, source_target_pairs={{0,64},{16,80},{32,96},{48,112},{64,128},{80,144},{96,160},{112,17... | collective-permute-start | bytes 3145736 | tf_op jit(solution)/shard_map/ppermute | solution.py:105
  88.7 96.8 %copy-start.5 = (bf16[1024,512]{1,0:T(8,128)(2,1)S(1)}, bf16[1024,512]{1,0:T(8,128)(2,1)}, u32[]{:S(2)}) copy-start(bf16[1024,512]{1,0:T(8,128)(2,1)} %copy-done.4) | copy-start | bytes 3145732
  88.8 100.9 %collective-permute-start.6 = (bf16[1024,512]{1,0:T(8,128)(2,1)}, bf16[1024,512]{1,0:T(8,128)(2,1)}, u32[]{:S(2)}, u32[]{:S(2)}) collective-permute-start(bf16[1024,512]{1,0:T(8,128)(2,1)} %copy-done.4), channel_id=1, source_target_pairs={{0,448},{16,464},{32,480},{48,496},{64,0},{80,16},{96,32},{112,48}... | collective-permute-start | bytes 3145736 | tf_op jit(solution)/shard_map/ppermute | solution.py:103
  171.7 13.9 %copy-start = (bf16[512,8192]{1,0:T(8,128)(2,1)S(1)}, bf16[512,8192]{1,0:T(8,128)(2,1)}, u32[]{:S(2)}) copy-start(bf16[512,8192]{1,0:T(8,128)(2,1)} %all-gather.3.cloned.1.call-done) | copy-start | bytes 25165828
  178.7 9.7 %collective-permute-start = (bf16[512,128]{0,1:T(8,128)(2,1)S(1)}, bf16[512,128]{0,1:T(8,128)(2,1)S(1)}, u32[]{:S(2)}, u32[]{:S(2)}) collective-permute-start(bf16[512,128]{0,1:T(8,128)(2,1)S(1)} %convolution_convert_fusion), channel_id=1, source_target_pairs={{0,1},{1,0},{2,3},{3,2},{4,5},{5,4},{6,7},{7,6},{8,9},{9,8},{10,11... | collective-permute-start | bytes 393224 | tf_op jit(solution)/shard_map/ppermute | solution.py:134
  182.9 28.1 %collective-permute-start.9 = (bf16[1024,512]{1,0:T(8,128)(2,1)}, bf16[1024,512]{1,0:T(8,128)(2,1)S(1)}, u32[]{:S(2)}, u32[]{:S(2)}) collective-permute-start(bf16[1024,512]{1,0:T(8,128)(2,1)} %collective-permute-done.7), channel_id=1, source_target_pairs={{0,64},{16,80},{32,96},{48,112},{64,128},{80,144},{96,160},{112,17... | collective-permute-start | bytes 3145736 | tf_op jit(solution)/shard_map/ppermute | solution.py:105
  188.4 7.1 %copy-start.1 = (bf16[512,128]{0,1:T(8,128)(2,1)}, bf16[512,128]{0,1:T(8,128)(2,1)S(1)}, u32[]{:S(2)}) copy-start(bf16[512,128]{0,1:T(8,128)(2,1)S(1)} %collective-permute-done) | copy-start | bytes 393220
  189.6 27.0 %collective-permute-start.8 = (bf16[1024,512]{1,0:T(8,128)(2,1)}, bf16[1024,512]{1,0:T(8,128)(2,1)S(1)}, u32[]{:S(2)}, u32[]{:S(2)}) collective-permute-start(bf16[1024,512]{1,0:T(8,128)(2,1)} %collective-permute-done.6), channel_id=1, source_target_pairs={{0,448},{16,464},{32,480},{48,496},{64,0},{80,16},{96,32},{112,48}... | collective-permute-start | bytes 3145736 | tf_op jit(solution)/shard_map/ppermute | solution.py:103
  211.0 27.0 %collective-permute-start.10 = (bf16[1024,512]{1,0:T(8,128)(2,1)S(1)}, bf16[1024,512]{1,0:T(8,128)(2,1)S(1)}, u32[]{:S(2)}, u32[]{:S(2)}) collective-permute-start(bf16[1024,512]{1,0:T(8,128)(2,1)S(1)} %collective-permute-done.9), channel_id=1, source_target_pairs={{0,64},{16,80},{32,96},{48,112},{64,128},{80,144},{96,160},{112,17... | collective-permute-start | bytes 3145736 | tf_op jit(solution)/shard_map/ppermute | solution.py:105
  239.5 2.6 %copy-start.2 = (bf16[512,128]{0,1:T(8,128)(2,1)S(1)}, bf16[512,128]{0,1:T(8,128)(2,1)}, u32[]{:S(2)}) copy-start(bf16[512,128]{0,1:T(8,128)(2,1)} %copy-done.1) | copy-start | bytes 393220
Sparse Core Ops, SparseCore 0:
  10.0 71.2 all-gather.2
  84.4 87.1 all-gather.4

commit v7 on v5

--- a/solution.py
+++ b/solution.py
@@ -125,11 +125,15 @@
     local_weights = jnp.concatenate([query_weight, kv_block], axis=1)
     n_batch = lax.psum(1, "batch")
     y_hi = n_batch // Z_CHIPS
-    near = ring_gather(local_weights, "batch", 1, y_hi)
-    near = near.reshape(-1, local_weights.shape[1])
+    split = (local_weights.shape[1] // 2 + 127) // 128 * 128
     gathered = lax.all_gather(normed, "weight", axis=0, tiled=True)
     pack_rows = gathered.shape[0]
-    projected = ring_matmul(gathered, near, "batch", y_hi, Z_CHIPS)
+    first, second = local_weights[:, :split], local_weights[:, split:]
+    near_first = ring_gather(first, "batch", 1, y_hi).reshape(-1, first.shape[1])
+    near_first, second = lax.optimization_barrier((near_first, second))
+    near_second = ring_gather(second, "batch", 1, y_hi).reshape(-1, second.shape[1])
+    parts = [ring_matmul(gathered, near, "batch", y_hi, Z_CHIPS) for near in (near_first, near_second)]
+    projected = jnp.concatenate(parts, axis=1)
     query_part = projected[:, :query_cols]
     own_rows = projected[:, query_cols:].astype(jnp.bfloat16)
     partner = [(w, w ^ 1) for w in range(n_weight)]

time: 216 us -> 219 us (1.014)
  the two profiles are of different devices: /device:TPU:55 before, /device:TPU:7 now
where the time goes in v7:
time: 219 us; the launch traced here: 215 us
  waiting for transfers between devices  90.8 us (41%)
  starting transfers between devices  74 us (34%)
  matrix products  17.8 us (8%)
  between operations  14.8 us (7%)
  other arithmetic  12.3 us (6%)
  local copies, waits for them, and re-layouts  5.33 us (2%)
    ppermute x8, waiting for transfers between devices, ring_matmul(): from_left = lax.ppermute(from_left, axis, perm=moved(1))  53.7 us
    ppermute x4, waiting for transfers between devices, ring_gather(): from_left = lax.ppermute(from_left, axis, perm=moved(1))  37 us
    ppermute x6, starting transfers between devices, ring_matmul(): from_right = lax.ppermute(from_right, axis, perm=moved(-1))  31.3 us
    ppermute x8, starting transfers between devices, ring_matmul(): from_left = lax.ppermute(from_left, axis, perm=moved(1))  17 us
    dot_general x16, matrix products, product(): return jnp.dot(lhs, part, preferred_element_type=jnp.float32)  14 us
    ppermute x4, starting transfers between devices, ring_gather(): from_left = lax.ppermute(from_left, axis, perm=moved(1))  10 us
    ppermute x1, starting transfers between devices, per_device(): other_rows = lax.ppermute(own_rows, 'weight', perm=partner)  7.93 us
    ppermute x2, starting transfers between devices, ring_gather(): from_right = lax.ppermute(from_right, axis, perm=moved(-1))  7.8 us
  transfers between devices with their start and end apart: 22, of which 7 were waited for; matrix products, arithmetic and copies ran while one was open for 11% of the time, Pallas kernels for 0%

profile of v7, /device:TPU:7, one launch (start us, length us, event | category | flops | bytes accessed | tf_op | source)
XLA Modules:
  0.0 215.1 jit_solution(15654437112029961480)
XLA Ops:
  6.5 1.2 fusion.14
  7.8 2.0 fusion.16
  9.9 0.9 slice.38
  10.8 5.9 %collective-permute-start = (bf16[256,384]{1,0:T(8,128)(2,1)S(1)}, bf16[256,384]{1,0:T(8,128)(2,1)S(1)}, u32[]{:S(2)}, u32[]{:S(2)}) collective-permute-start(bf16[256,384]{1,0:T(8,128)(2,1)S(1)} %slice.38), channel_id=1, source_target_pairs={{0,48},{16,0},{32,16},{48,32},{64,112},{80,64},{96,80},{112,96},{1... | collective-permute-start | bytes 589832 | tf_op jit(solution)/shard_map/ppermute | solution.py:73
  16.7 1.9 collective-permute-start.1
  18.7 1.2 slice.42
  20.5 0.8 select_bitcast_fusion
  21.9 0.9 dynamic-slice_select_fusion
  22.8 0.9 pad_maximum_fusion.1
  23.7 1.0 bitcast_dynamic-update-slice_fusion.3
  24.8 2.6 %collective-permute-done.1 = bf16[256,384]{1,0:T(8,128)(2,1)S(1)} collective-permute-done((bf16[256,384]{1,0:T(8,128)(2,1)S(1)}, bf16[256,384]{1,0:T(8,128)(2,1)S(1)}, u32[]{:S(2)}, u32[]{:S(2)}) %collective-permute-start.1) | collective-permute-done | bytes 196640 | tf_op jit(solution)/shard_map/ppermute | solution.py:75
  27.3 1.9 collective-permute-start.2
  29.4 16.0 %collective-permute-done.2 = bf16[256,384]{1,0:T(8,128)(2,1)S(1)} collective-permute-done((bf16[256,384]{1,0:T(8,128)(2,1)S(1)}, bf16[256,384]{1,0:T(8,128)(2,1)S(1)}, u32[]{:S(2)}, u32[]{:S(2)}) %collective-permute-start.2) | collective-permute-done | bytes 196640 | tf_op jit(solution)/shard_map/ppermute | solution.py:75
  45.4 10.8 %collective-permute-start.14 = (bf16[1024,384]{1,0:T(8,128)(2,1)S(1)}, bf16[1024,384]{1,0:T(8,128)(2,1)S(1)}, u32[]{:S(2)}, u32[]{:S(2)}) collective-permute-start(bf16[1024,384]{1,0:T(8,128)(2,1)S(1)} %bitcast.81), channel_id=1, source_target_pairs={{0,448},{16,464},{32,480},{48,496},{64,0},{80,16},{96,32},{112,48}... | collective-permute-start | bytes 2359304 | tf_op jit(solution)/shard_map/ppermute | solution.py:103
  56.2 1.9 collective-permute-start.15
  58.1 1.9 collective-permute-start.3
  60.1 4.3 %collective-permute-start.4 = (bf16[256,256]{1,0:T(8,128)(2,1)S(1)}, bf16[256,256]{1,0:T(8,128)(2,1)S(1)}, u32[]{:S(2)}, u32[]{:S(2)}) collective-permute-start(bf16[256,256]{1,0:T(8,128)(2,1)S(1)} %pad_maximum_fusion.1), channel_id=1, source_target_pairs={{0,16},{16,32},{32,48},{48,0},{64,80},{80,96},{96,112},{112,64},{1... | collective-permute-start | bytes 393224 | tf_op jit(solution)/shard_map/ppermute | solution.py:75
  64.4 9.8 %collective-permute-done.4 = bf16[256,256]{1,0:T(8,128)(2,1)S(1)} collective-permute-done((bf16[256,256]{1,0:T(8,128)(2,1)S(1)}, bf16[256,256]{1,0:T(8,128)(2,1)S(1)}, u32[]{:S(2)}, u32[]{:S(2)}) %collective-permute-start.4) | collective-permute-done | bytes 131104 | tf_op jit(solution)/shard_map/ppermute | solution.py:75
  74.2 1.9 collective-permute-start.5
  76.2 8.6 %collective-permute-done.5 = bf16[256,256]{1,0:T(8,128)(2,1)S(1)} collective-permute-done((bf16[256,256]{1,0:T(8,128)(2,1)S(1)}, bf16[256,256]{1,0:T(8,128)(2,1)S(1)}, u32[]{:S(2)}, u32[]{:S(2)}) %collective-permute-start.5) | collective-permute-done | bytes 131104 | tf_op jit(solution)/shard_map/ppermute | solution.py:75
  84.8 4.7 %collective-permute-start.6 = (bf16[1024,256]{1,0:T(8,128)(2,1)S(1)}, bf16[1024,256]{1,0:T(8,128)(2,1)}, u32[]{:S(2)}, u32[]{:S(2)}) collective-permute-start(bf16[1024,256]{1,0:T(8,128)(2,1)S(1)} %bitcast.84), channel_id=1, source_target_pairs={{0,448},{16,464},{32,480},{48,496},{64,0},{80,16},{96,32},{112,48}... | collective-permute-start | bytes 1572872 | tf_op jit(solution)/shard_map/ppermute | solution.py:103
  89.5 1.9 collective-permute-start.7
  91.6 1.7 fusion.33
  93.3 1.7 multiply_cosine_fusion
  95.0 4.8 %collective-permute-start.16 = (bf16[1024,384]{1,0:T(8,128)(2,1)S(1)}, bf16[1024,384]{1,0:T(8,128)(2,1)S(1)}, u32[]{:S(2)}, u32[]{:S(2)}) collective-permute-start(bf16[1024,384]{1,0:T(8,128)(2,1)S(1)} %collective-permute-done.14), channel_id=1, source_target_pairs={{0,448},{16,464},{32,480},{48,496},{64,0},{80,16},{96,32},{112,48}... | collective-permute-start | bytes 2359304 | tf_op jit(solution)/shard_map/ppermute | solution.py:103
  99.9 1.9 collective-permute-start.17
  101.8 4.6 %collective-permute-start.8 = (bf16[1024,256]{1,0:T(8,128)(2,1)}, bf16[1024,256]{1,0:T(8,128)(2,1)S(1)}, u32[]{:S(2)}, u32[]{:S(2)}) collective-permute-start(bf16[1024,256]{1,0:T(8,128)(2,1)} %collective-permute-done.6), channel_id=1, source_target_pairs={{0,448},{16,464},{32,480},{48,496},{64,0},{80,16},{96,32},{112,48}... | collective-permute-start | bytes 1572872 | tf_op jit(solution)/shard_map/ppermute | solution.py:103
  106.4 1.9 collective-permute-start.9
  108.4 1.8 fusion.40
  110.2 1.9 fusion.38
  112.1 1.9 fusion.35
  113.9 1.9 convolution_add_fusion.3
  115.8 14.1 %collective-permute-done.9 = bf16[1024,256]{1,0:T(8,128)(2,1)S(1)} collective-permute-done((bf16[1024,256]{1,0:T(8,128)(2,1)}, bf16[1024,256]{1,0:T(8,128)(2,1)S(1)}, u32[]{:S(2)}, u32[]{:S(2)}) %collective-permute-start.9) | collective-permute-done | bytes 524320 | tf_op jit(solution)/shard_map/ppermute | solution.py:105
  129.9 1.9 collective-permute-start.11
  131.8 4.6 %collective-permute-start.10 = (bf16[1024,256]{1,0:T(8,128)(2,1)S(1)}, bf16[1024,256]{1,0:T(8,128)(2,1)S(1)}, u32[]{:S(2)}, u32[]{:S(2)}) collective-permute-start(bf16[1024,256]{1,0:T(8,128)(2,1)S(1)} %collective-permute-done.8), channel_id=1, source_target_pairs={{0,448},{16,464},{32,480},{48,496},{64,0},{80,16},{96,32},{112,48}... | collective-permute-start | bytes 1572872 | tf_op jit(solution)/shard_map/ppermute | solution.py:103
  137.9 1.9 collective-permute-start.18
  140.4 3.4 %collective-permute-start.19 = (bf16[1024,384]{1,0:T(8,128)(2,1)S(1)}, bf16[1024,384]{1,0:T(8,128)(2,1)S(1)}, u32[]{:S(2)}, u32[]{:S(2)}) collective-permute-start(bf16[1024,384]{1,0:T(8,128)(2,1)S(1)} %collective-permute-done.17), channel_id=1, source_target_pairs={{0,64},{16,80},{32,96},{48,112},{64,128},{80,144},{96,160},{112,17... | collective-permute-start | bytes 2359304 | tf_op jit(solution)/shard_map/ppermute | solution.py:105
  144.4 0.6 fusion.5
  145.1 1.9 collective-permute-start.12
  148.0 22.0 %collective-permute-done.12 = bf16[1024,256]{1,0:T(8,128)(2,1)S(1)} collective-permute-done((bf16[1024,256]{1,0:T(8,128)(2,1)S(1)}, bf16[1024,256]{1,0:T(8,128)(2,1)S(1)}, u32[]{:S(2)}, u32[]{:S(2)}) %collective-permute-start.12) | collective-permute-done | bytes 524320 | tf_op jit(solution)/shard_map/ppermute | solution.py:105
  170.5 7.9 %collective-permute-start.13 = (bf16[512,128]{0,1:T(8,128)(2,1)S(1)}, bf16[512,128]{0,1:T(8,128)(2,1)S(1)}, u32[]{:S(2)}, u32[]{:S(2)}) collective-permute-start(bf16[512,128]{0,1:T(8,128)(2,1)S(1)} %slice.70), channel_id=1, source_target_pairs={{0,1},{1,0},{2,3},{3,2},{4,5},{5,4},{6,7},{7,6},{8,9},{9,8},{10,11... | collective-permute-start | bytes 393224 | tf_op jit(solution)/shard_map/ppermute | solution.py:140
  178.5 2.1 collective-permute-start.20
  181.9 1.2 fusion.61
  183.1 17.6 %collective-permute-done.20 = bf16[1024,384]{1,0:T(8,128)(2,1)S(1)} collective-permute-done((bf16[1024,384]{1,0:T(8,128)(2,1)S(1)}, bf16[1024,384]{1,0:T(8,128)(2,1)S(1)}, u32[]{:S(2)}, u32[]{:S(2)}) %collective-permute-start.20) | collective-permute-done | bytes 786464 | tf_op jit(solution)/shard_map/ppermute | solution.py:105
  202.2 1.3 subtract_convert_fusion
  203.5 2.5 %fusion = (f32[4,512]{1,0:T(4,128)S(1)}, f32[512,512,4]{1,0,2:T(8,128)S(1)}) fusion(pred[512,512]{0,1:T(8,128)(4,1)} %fusion.33, bf16[512,4,64]{2,0,1:T(8,128)(2,1)S(1)} %get-tuple-element.22, bf16[512,4,64]{2,0,1:T(8,128)(2,1)S(1)} %get-tuple-element.21, bf16[512,64]{0,1:T(8,128)(2,1)} %get-tuple-element.26, bf16[512,64]{0,1:T(8,128)(2,1)} %get-tuple-element.25), kind=kOutput, calls=%fused_computation.2 | convolution fusion | flops 272889856 | bytes 5120000 | tf_op jit(solution)/shard_map/ingd,jnd->ngij/dot_general | solution.py:43
  206.0 1.3 fusion.7
  207.3 1.0 copy.16
  (54 shorter events, 7.8 us)
Async XLA Ops:
  6.5 88.5 %all-gather.2.cloned.1.call-start = ((), (), s32[]{:S(2)}) async-start(), calls=%async_computation | async-start | bytes 8912896 | tf_op jit(solution)/shard_map/all_gather | solution.py:129
  10.8 18.5 %collective-permute-start = (bf16[256,384]{1,0:T(8,128)(2,1)S(1)}, bf16[256,384]{1,0:T(8,128)(2,1)S(1)}, u32[]{:S(2)}, u32[]{:S(2)}) collective-permute-start(bf16[256,384]{1,0:T(8,128)(2,1)S(1)} %slice.38), channel_id=1, source_target_pairs={{0,48},{16,0},{32,16},{48,32},{64,112},{80,64},{96,80},{112,96},{1... | collective-permute-start | bytes 589832 | tf_op jit(solution)/shard_map/ppermute | solution.py:73
  16.7 10.6 %collective-permute-start.1 = (bf16[256,384]{1,0:T(8,128)(2,1)S(1)}, bf16[256,384]{1,0:T(8,128)(2,1)S(1)}, u32[]{:S(2)}, u32[]{:S(2)}) collective-permute-start(bf16[256,384]{1,0:T(8,128)(2,1)S(1)} %slice.38), channel_id=1, source_target_pairs={{0,16},{16,32},{32,48},{48,0},{64,80},{80,96},{96,112},{112,64},{1... | collective-permute-start | bytes 589832 | tf_op jit(solution)/shard_map/ppermute | solution.py:75
  27.3 18.0 %collective-permute-start.2 = (bf16[256,384]{1,0:T(8,128)(2,1)S(1)}, bf16[256,384]{1,0:T(8,128)(2,1)S(1)}, u32[]{:S(2)}, u32[]{:S(2)}) collective-permute-start(bf16[256,384]{1,0:T(8,128)(2,1)S(1)} %collective-permute-done.1), channel_id=1, source_target_pairs={{0,16},{16,32},{32,48},{48,0},{64,80},{80,96},{96,112},{112,64},{1... | collective-permute-start | bytes 589832 | tf_op jit(solution)/shard_map/ppermute | solution.py:75
  45.4 49.6 %collective-permute-start.14 = (bf16[1024,384]{1,0:T(8,128)(2,1)S(1)}, bf16[1024,384]{1,0:T(8,128)(2,1)S(1)}, u32[]{:S(2)}, u32[]{:S(2)}) collective-permute-start(bf16[1024,384]{1,0:T(8,128)(2,1)S(1)} %bitcast.81), channel_id=1, source_target_pairs={{0,448},{16,464},{32,480},{48,496},{64,0},{80,16},{96,32},{112,48}... | collective-permute-start | bytes 2359304 | tf_op jit(solution)/shard_map/ppermute | solution.py:103
  56.2 38.8 %collective-permute-start.15 = (bf16[1024,384]{1,0:T(8,128)(2,1)S(1)}, bf16[1024,384]{1,0:T(8,128)(2,1)S(1)}, u32[]{:S(2)}, u32[]{:S(2)}) collective-permute-start(bf16[1024,384]{1,0:T(8,128)(2,1)S(1)} %bitcast.82), channel_id=1, source_target_pairs={{0,64},{16,80},{32,96},{48,112},{64,128},{80,144},{96,160},{112,17... | collective-permute-start | bytes 2359304 | tf_op jit(solution)/shard_map/ppermute | solution.py:105
  58.1 18.0 %collective-permute-start.3 = (bf16[256,256]{1,0:T(8,128)(2,1)S(1)}, bf16[256,256]{1,0:T(8,128)(2,1)S(1)}, u32[]{:S(2)}, u32[]{:S(2)}) collective-permute-start(bf16[256,256]{1,0:T(8,128)(2,1)S(1)} %pad_maximum_fusion.1), channel_id=1, source_target_pairs={{0,48},{16,0},{32,16},{48,32},{64,112},{80,64},{96,80},{112,96},{1... | collective-permute-start | bytes 393224 | tf_op jit(solution)/shard_map/ppermute | solution.py:73
  60.1 14.1 %collective-permute-start.4 = (bf16[256,256]{1,0:T(8,128)(2,1)S(1)}, bf16[256,256]{1,0:T(8,128)(2,1)S(1)}, u32[]{:S(2)}, u32[]{:S(2)}) collective-permute-start(bf16[256,256]{1,0:T(8,128)(2,1)S(1)} %pad_maximum_fusion.1), channel_id=1, source_target_pairs={{0,16},{16,32},{32,48},{48,0},{64,80},{80,96},{96,112},{112,64},{1... | collective-permute-start | bytes 393224 | tf_op jit(solution)/shard_map/ppermute | solution.py:75
  74.2 10.6 %collective-permute-start.5 = (bf16[256,256]{1,0:T(8,128)(2,1)S(1)}, bf16[256,256]{1,0:T(8,128)(2,1)S(1)}, u32[]{:S(2)}, u32[]{:S(2)}) collective-permute-start(bf16[256,256]{1,0:T(8,128)(2,1)S(1)} %collective-permute-done.4), channel_id=1, source_target_pairs={{0,16},{16,32},{32,48},{48,0},{64,80},{80,96},{96,112},{112,64},{1... | collective-permute-start | bytes 393224 | tf_op jit(solution)/shard_map/ppermute | solution.py:75
  84.8 17.0 %collective-permute-start.6 = (bf16[1024,256]{1,0:T(8,128)(2,1)S(1)}, bf16[1024,256]{1,0:T(8,128)(2,1)}, u32[]{:S(2)}, u32[]{:S(2)}) collective-permute-start(bf16[1024,256]{1,0:T(8,128)(2,1)S(1)} %bitcast.84), channel_id=1, source_target_pairs={{0,448},{16,464},{32,480},{48,496},{64,0},{80,16},{96,32},{112,48}... | collective-permute-start | bytes 1572872 | tf_op jit(solution)/shard_map/ppermute | solution.py:103
  89.5 12.4 %collective-permute-start.7 = (bf16[1024,256]{1,0:T(8,128)(2,1)S(1)}, bf16[1024,256]{1,0:T(8,128)(2,1)}, u32[]{:S(2)}, u32[]{:S(2)}) collective-permute-start(bf16[1024,256]{1,0:T(8,128)(2,1)S(1)} %bitcast.85), channel_id=1, source_target_pairs={{0,64},{16,80},{32,96},{48,112},{64,128},{80,144},{96,160},{112,17... | collective-permute-start | bytes 1572872 | tf_op jit(solution)/shard_map/ppermute | solution.py:105
  95.0 41.3 %copy-start = (bf16[512,8192]{1,0:T(8,128)(2,1)S(1)}, bf16[512,8192]{1,0:T(8,128)(2,1)}, u32[]{:S(2)}) copy-start(bf16[512,8192]{1,0:T(8,128)(2,1)} %all-gather.2.cloned.1.call-done) | copy-start | bytes 25165828
  95.0 42.8 %collective-permute-start.16 = (bf16[1024,384]{1,0:T(8,128)(2,1)S(1)}, bf16[1024,384]{1,0:T(8,128)(2,1)S(1)}, u32[]{:S(2)}, u32[]{:S(2)}) collective-permute-start(bf16[1024,384]{1,0:T(8,128)(2,1)S(1)} %collective-permute-done.14), channel_id=1, source_target_pairs={{0,448},{16,464},{32,480},{48,496},{64,0},{80,16},{96,32},{112,48}... | collective-permute-start | bytes 2359304 | tf_op jit(solution)/shard_map/ppermute | solution.py:103
  99.9 40.5 %collective-permute-start.17 = (bf16[1024,384]{1,0:T(8,128)(2,1)S(1)}, bf16[1024,384]{1,0:T(8,128)(2,1)S(1)}, u32[]{:S(2)}, u32[]{:S(2)}) collective-permute-start(bf16[1024,384]{1,0:T(8,128)(2,1)S(1)} %collective-permute-done.15), channel_id=1, source_target_pairs={{0,64},{16,80},{32,96},{48,112},{64,128},{80,144},{96,160},{112,17... | collective-permute-start | bytes 2359304 | tf_op jit(solution)/shard_map/ppermute | solution.py:105
  101.8 29.9 %collective-permute-start.8 = (bf16[1024,256]{1,0:T(8,128)(2,1)}, bf16[1024,256]{1,0:T(8,128)(2,1)S(1)}, u32[]{:S(2)}, u32[]{:S(2)}) collective-permute-start(bf16[1024,256]{1,0:T(8,128)(2,1)} %collective-permute-done.6), channel_id=1, source_target_pairs={{0,448},{16,464},{32,480},{48,496},{64,0},{80,16},{96,32},{112,48}... | collective-permute-start | bytes 1572872 | tf_op jit(solution)/shard_map/ppermute | solution.py:103
  106.4 23.4 %collective-permute-start.9 = (bf16[1024,256]{1,0:T(8,128)(2,1)}, bf16[1024,256]{1,0:T(8,128)(2,1)S(1)}, u32[]{:S(2)}, u32[]{:S(2)}) collective-permute-start(bf16[1024,256]{1,0:T(8,128)(2,1)} %collective-permute-done.7), channel_id=1, source_target_pairs={{0,64},{16,80},{32,96},{48,112},{64,128},{80,144},{96,160},{112,17... | collective-permute-start | bytes 1572872 | tf_op jit(solution)/shard_map/ppermute | solution.py:105
  129.9 15.2 %collective-permute-start.11 = (bf16[1024,256]{1,0:T(8,128)(2,1)S(1)}, bf16[1024,256]{1,0:T(8,128)(2,1)S(1)}, u32[]{:S(2)}, u32[]{:S(2)}) collective-permute-start(bf16[1024,256]{1,0:T(8,128)(2,1)S(1)} %collective-permute-done.9), channel_id=1, source_target_pairs={{0,64},{16,80},{32,96},{48,112},{64,128},{80,144},{96,160},{112,17... | collective-permute-start | bytes 1572872 | tf_op jit(solution)/shard_map/ppermute | solution.py:105
  131.8 15.7 %collective-permute-start.10 = (bf16[1024,256]{1,0:T(8,128)(2,1)S(1)}, bf16[1024,256]{1,0:T(8,128)(2,1)S(1)}, u32[]{:S(2)}, u32[]{:S(2)}) collective-permute-start(bf16[1024,256]{1,0:T(8,128)(2,1)S(1)} %collective-permute-done.8), channel_id=1, source_target_pairs={{0,448},{16,464},{32,480},{48,496},{64,0},{80,16},{96,32},{112,48}... | collective-permute-start | bytes 1572872 | tf_op jit(solution)/shard_map/ppermute | solution.py:103
  137.9 43.3 %collective-permute-start.18 = (bf16[1024,384]{1,0:T(8,128)(2,1)S(1)}, bf16[1024,384]{1,0:T(8,128)(2,1)S(1)}, u32[]{:S(2)}, u32[]{:S(2)}) collective-permute-start(bf16[1024,384]{1,0:T(8,128)(2,1)S(1)} %collective-permute-done.16), channel_id=1, source_target_pairs={{0,448},{16,464},{32,480},{48,496},{64,0},{80,16},{96,32},{112,48}... | collective-permute-start | bytes 2359304 | tf_op jit(solution)/shard_map/ppermute | solution.py:103
  140.4 38.0 %collective-permute-start.19 = (bf16[1024,384]{1,0:T(8,128)(2,1)S(1)}, bf16[1024,384]{1,0:T(8,128)(2,1)S(1)}, u32[]{:S(2)}, u32[]{:S(2)}) collective-permute-start(bf16[1024,384]{1,0:T(8,128)(2,1)S(1)} %collective-permute-done.17), channel_id=1, source_target_pairs={{0,64},{16,80},{32,96},{48,112},{64,128},{80,144},{96,160},{112,17... | collective-permute-start | bytes 2359304 | tf_op jit(solution)/shard_map/ppermute | solution.py:105
  145.1 24.9 %collective-permute-start.12 = (bf16[1024,256]{1,0:T(8,128)(2,1)S(1)}, bf16[1024,256]{1,0:T(8,128)(2,1)S(1)}, u32[]{:S(2)}, u32[]{:S(2)}) collective-permute-start(bf16[1024,256]{1,0:T(8,128)(2,1)S(1)} %collective-permute-done.11), channel_id=1, source_target_pairs={{0,64},{16,80},{32,96},{48,112},{64,128},{80,144},{96,160},{112,17... | collective-permute-start | bytes 1572872 | tf_op jit(solution)/shard_map/ppermute | solution.py:105
  170.5 11.3 %collective-permute-start.13 = (bf16[512,128]{0,1:T(8,128)(2,1)S(1)}, bf16[512,128]{0,1:T(8,128)(2,1)S(1)}, u32[]{:S(2)}, u32[]{:S(2)}) collective-permute-start(bf16[512,128]{0,1:T(8,128)(2,1)S(1)} %slice.70), channel_id=1, source_target_pairs={{0,1},{1,0},{2,3},{3,2},{4,5},{5,4},{6,7},{7,6},{8,9},{9,8},{10,11... | collective-permute-start | bytes 393224 | tf_op jit(solution)/shard_map/ppermute | solution.py:140
  178.5 22.3 %collective-permute-start.20 = (bf16[1024,384]{1,0:T(8,128)(2,1)S(1)}, bf16[1024,384]{1,0:T(8,128)(2,1)S(1)}, u32[]{:S(2)}, u32[]{:S(2)}) collective-permute-start(bf16[1024,384]{1,0:T(8,128)(2,1)S(1)} %collective-permute-done.19), channel_id=1, source_target_pairs={{0,64},{16,80},{32,96},{48,112},{64,128},{80,144},{96,160},{112,17... | collective-permute-start | bytes 2359304 | tf_op jit(solution)/shard_map/ppermute | solution.py:105
  202.2 3.8 %copy-start.1 = (pred[512,512]{0,1:T(8,128)(4,1)S(1)}, pred[512,512]{0,1:T(8,128)(4,1)}, u32[]{:S(2)}) copy-start(pred[512,512]{0,1:T(8,128)(4,1)} %fusion.33) | copy-start | bytes 786436
Sparse Core Ops, SparseCore 0:
  10.0 79.1 all-gather.1

commit v8 on v5

--- a/solution.py
+++ b/solution.py
@@ -1,8 +1,11 @@
+import functools
 import math
 
 import jax
 import jax.numpy as jnp
 from jax import lax
+from jax.experimental import pallas as pl
+from jax.experimental.pallas import tpu as pltpu
 from jax.sharding import PartitionSpec as P
 
 HEADS = 64
@@ -51,6 +54,67 @@
         "ngij,jnd->ingd", probabilities, value_rows, preferred_element_type=jnp.float32
     )
     return mixed.astype(jnp.bfloat16)
+
+
+def attention_kernel(heads, q_ref, k_ref, v_ref, cos_ref, sin_ref, row_seg_ref, col_seg_ref, o_ref):
+    half = HEAD_DIM // 2
+    cosine, sine = cos_ref[...], sin_ref[...]
+
+    def rope(x):
+        a, b = x[:, :half], x[:, half:]
+        return jnp.concatenate([a * cosine - b * sine, b * cosine + a * sine], axis=1)
+
+    keys = rope(k_ref[...].astype(jnp.float32)).astype(jnp.bfloat16)
+    values = v_ref[...]
+    rows = q_ref.shape[0]
+    places_i = lax.broadcasted_iota(jnp.int32, (rows, rows), 0)
+    places_j = lax.broadcasted_iota(jnp.int32, (rows, rows), 1)
+    allowed = (row_seg_ref[...] == col_seg_ref[...]) & (places_j <= places_i)
+    scale = HEAD_DIM ** (-0.5)
+    for h in range(heads):
+        cols = slice(h * HEAD_DIM, (h + 1) * HEAD_DIM)
+        query = rope(q_ref[:, cols]).astype(jnp.bfloat16)
+        scores = lax.dot_general(
+            query, keys, (((1,), (1,)), ((), ())), preferred_element_type=jnp.float32
+        ) * scale
+        weights = jnp.where(allowed, jnp.exp(scores), 0.0)
+        probabilities = (weights / jnp.sum(weights, axis=1, keepdims=True)).astype(jnp.bfloat16)
+        mixed = jnp.dot(probabilities, values, preferred_element_type=jnp.float32)
+        o_ref[:, cols] = mixed.astype(o_ref.dtype)
+
+
+def rope_tables(positions):
+    half_dim = HEAD_DIM // 2
+    ratios = jnp.arange(half_dim, dtype=jnp.float32) * (2.0 / HEAD_DIM)
+    frequency = jnp.exp(-math.log(ROPE_BASE) * ratios)
+    angles = positions.astype(jnp.float32)[:, None] * frequency[None, :]
+    return jnp.cos(angles), jnp.sin(angles)
+
+
+def attention_kernel_call(projected, cols, key_rows, value_rows, cosine, sine, seg_ids):
+    rows = projected.shape[0]
+    half_dim = HEAD_DIM // 2
+    vmem = pl.BlockSpec(memory_space=pltpu.VMEM)
+    heads = cols // HEAD_DIM
+    return pl.pallas_call(
+        functools.partial(attention_kernel, heads),
+        out_shape=jax.ShapeDtypeStruct((rows, cols), jnp.bfloat16),
+        in_specs=[vmem] * 7,
+        out_specs=vmem,
+        cost_estimate=pl.CostEstimate(
+            flops=4 * rows * rows * cols + 8 * rows * cols,
+            transcendentals=heads * rows * rows,
+            bytes_accessed=rows * cols * 6 + rows * HEAD_DIM * 4 + rows * half_dim * 8,
+        ),
+    )(
+        projected,
+        key_rows,
+        value_rows,
+        cosine,
+        sine,
+        seg_ids[:, None],
+        seg_ids[None, :],
+    )
 
 
 def ring_gather(block, axis, stride, count):
@@ -127,28 +191,19 @@
     y_hi = n_batch // Z_CHIPS
     near = ring_gather(local_weights, "batch", 1, y_hi)
     near = near.reshape(-1, local_weights.shape[1])
+    cosine, sine = rope_tables(positions_in_segment(segment_ids))
+    near, cosine, sine = lax.optimization_barrier((near, cosine, sine))
     gathered = lax.all_gather(normed, "weight", axis=0, tiled=True)
     pack_rows = gathered.shape[0]
     projected = ring_matmul(gathered, near, "batch", y_hi, Z_CHIPS)
-    query_part = projected[:, :query_cols]
     own_rows = projected[:, query_cols:].astype(jnp.bfloat16)
     partner = [(w, w ^ 1) for w in range(n_weight)]
     other_rows = lax.ppermute(own_rows, "weight", perm=partner)
     key_rows = jnp.where(core == 0, own_rows, other_rows)
     value_rows = jnp.where(core == 0, other_rows, own_rows)
-    local_kv = 1
-    positions = positions_in_segment(segment_ids)
-    queries = rotate(query_part.reshape(pack_rows, heads_dev, head_dim), positions).astype(
-        jnp.bfloat16
-    )
-    rotated_keys = rotate(
-        key_rows.astype(jnp.float32).reshape(pack_rows, local_kv, head_dim), positions
-    ).astype(jnp.bfloat16)
-    grouped = queries.reshape(pack_rows, local_kv, heads_dev // local_kv, head_dim)
-    attended = attend(
-        grouped, rotated_keys, value_rows.reshape(pack_rows, local_kv, head_dim), segment_ids
-    )
-    return attended.reshape(pack_rows, query_cols)
+    return attention_kernel_call(
+        projected, query_cols, key_rows, value_rows, cosine, sine, segment_ids
+    )
 
 
 def solution(mesh):

time: 216 us -> 217 us (level)
  the two profiles are of different devices: /device:TPU:55 before, /device:TPU:7 now
where the time goes in v8:
time: 217 us; the launch traced here: 214 us
  waiting for transfers between devices  110 us (51%)
  starting transfers between devices  56.5 us (26%)
  matrix products  15.9 us (7%)
  between operations  14.6 us (7%)
  Pallas kernels  8.27 us (4%)
  other arithmetic  7.34 us (3%)
    ppermute x4, waiting for transfers between devices, ring_matmul(): from_left = lax.ppermute(from_left, axis, perm=moved(1))  57.4 us
    ppermute x2, waiting for transfers between devices, ring_gather(): from_left = lax.ppermute(from_left, axis, perm=moved(1))  34.2 us
    ppermute x3, starting transfers between devices, ring_matmul(): from_right = lax.ppermute(from_right, axis, perm=moved(-1))  23.3 us
    ppermute x3, waiting for transfers between devices, ring_matmul(): from_right = lax.ppermute(from_right, axis, perm=moved(-1))  18.4 us
    ppermute x4, starting transfers between devices, ring_matmul(): from_left = lax.ppermute(from_left, axis, perm=moved(1))  16.9 us
    dot_general x8, matrix products, product(): return jnp.dot(lhs, part, preferred_element_type=jnp.float32)  15.9 us
    pallas_call x1, Pallas kernels, attention_kernel_call(): pl.pallas_call(functools.partial(attention_kernel, heads), out_shape=jax....  8.27 us
    ppermute x1, starting transfers between devices, per_device(): other_rows = lax.ppermute(own_rows, 'weight', perm=partner)  6.68 us
  transfers between devices with their start and end apart: 12, of which 7 were waited for; matrix products, arithmetic and copies ran while one was open for 9% of the time, Pallas kernels for 0%

profile of v8, /device:TPU:7, one launch (start us, length us, event | category | flops | bytes accessed | tf_op | source)
XLA Modules:
  0.0 214.4 jit_solution(9600720568622044751)
XLA Ops:
  6.5 1.3 fusion.3
  7.8 0.0 copy-start.3
  7.9 2.0 fusion.5
  9.9 0.0 all-gather.2.cloned.1.call-update
  9.9 0.9 dynamic-slice_select_fusion
  10.9 5.9 %collective-permute-start = (bf16[256,640]{1,0:T(8,128)(2,1)S(1)}, bf16[256,640]{1,0:T(8,128)(2,1)S(1)}, u32[]{:S(2)}, u32[]{:S(2)}) collective-permute-start(bf16[256,640]{1,0:T(8,128)(2,1)S(1)} %pad_maximum_fusion), channel_id=1, source_target_pairs={{0,48},{16,0},{32,16},{48,32},{64,112},{80,64},{96,80},{112,96},{1... | collective-permute-start | bytes 983048 | tf_op jit(solution)/shard_map/ppermute | solution.py:137
  16.8 1.9 collective-permute-start.1
  18.8 0.5 slice.17
  20.0 0.1 select_bitcast_fusion
  20.1 0.3 reduce-window.9
  20.4 0.1 slice.19
  20.5 0.1 slice_reduce_fusion
  20.6 0.1 broadcast_in_dim.30
  20.8 0.1 fusion.26
  20.8 1.8 multiply_sine_fusion
  22.7 9.1 %collective-permute-done.1 = bf16[256,640]{1,0:T(8,128)(2,1)S(1)} collective-permute-done((bf16[256,640]{1,0:T(8,128)(2,1)S(1)}, bf16[256,640]{1,0:T(8,128)(2,1)S(1)}, u32[]{:S(2)}, u32[]{:S(2)}) %collective-permute-start.1) | collective-permute-done | bytes 327712 | tf_op jit(solution)/shard_map/ppermute | solution.py:139
  31.7 1.9 collective-permute-start.2
  33.7 0.0 collective-permute-done
  33.8 25.1 %collective-permute-done.2 = bf16[256,640]{1,0:T(8,128)(2,1)S(1)} collective-permute-done((bf16[256,640]{1,0:T(8,128)(2,1)S(1)}, bf16[256,640]{1,0:T(8,128)(2,1)S(1)}, u32[]{:S(2)}, u32[]{:S(2)}) %collective-permute-start.2) | collective-permute-done | bytes 327712 | tf_op jit(solution)/shard_map/ppermute | solution.py:139
  58.9 10.6 %collective-permute-start.3 = (bf16[1024,640]{1,0:T(8,128)(2,1)S(1)}, bf16[1024,640]{1,0:T(8,128)(2,1)S(1)}, u32[]{:S(2)}, u32[]{:S(2)}) collective-permute-start(bf16[1024,640]{1,0:T(8,128)(2,1)S(1)} %bitcast.26), channel_id=1, source_target_pairs={{0,448},{16,464},{32,480},{48,496},{64,0},{80,16},{96,32},{112,48}... | collective-permute-start | bytes 3932168 | tf_op jit(solution)/shard_map/ppermute | solution.py:167
  69.5 1.9 collective-permute-start.4
  71.4 18.4 %collective-permute-done.3 = bf16[1024,640]{1,0:T(8,128)(2,1)S(1)} collective-permute-done((bf16[1024,640]{1,0:T(8,128)(2,1)S(1)}, bf16[1024,640]{1,0:T(8,128)(2,1)S(1)}, u32[]{:S(2)}, u32[]{:S(2)}) %collective-permute-start.3) | collective-permute-done | bytes 1310752 | tf_op jit(solution)/shard_map/ppermute | solution.py:167
  89.8 3.8 %collective-permute-done.4 = bf16[1024,640]{1,0:T(8,128)(2,1)} collective-permute-done((bf16[1024,640]{1,0:T(8,128)(2,1)S(1)}, bf16[1024,640]{1,0:T(8,128)(2,1)}, u32[]{:S(2)}, u32[]{:S(2)}) %collective-permute-start.4) | collective-permute-done | bytes 1310752 | tf_op jit(solution)/shard_map/ppermute | solution.py:169
  93.7 1.9 collective-permute-start.6
  95.6 6.2 %collective-permute-start.5 = (bf16[1024,640]{1,0:T(8,128)(2,1)S(1)}, bf16[1024,640]{1,0:T(8,128)(2,1)}, u32[]{:S(2)}, u32[]{:S(2)}) collective-permute-start(bf16[1024,640]{1,0:T(8,128)(2,1)S(1)} %collective-permute-done.3), channel_id=1, source_target_pairs={{0,448},{16,464},{32,480},{48,496},{64,0},{80,16},{96,32},{112,48}... | collective-permute-start | bytes 3932168 | tf_op jit(solution)/shard_map/ppermute | solution.py:167
  101.8 20.7 %collective-permute-done.6 = bf16[1024,640]{1,0:T(8,128)(2,1)} collective-permute-done((bf16[1024,640]{1,0:T(8,128)(2,1)}, bf16[1024,640]{1,0:T(8,128)(2,1)}, u32[]{:S(2)}, u32[]{:S(2)}) %collective-permute-start.6) | collective-permute-done | bytes 1310752 | tf_op jit(solution)/shard_map/ppermute | solution.py:169
  122.6 1.9 collective-permute-start.8
  124.6 0.0 copy-start.1
  124.7 2.4 %fusion.16 = f32[512,640]{1,0:T(8,128)S(1)} fusion(bf16[1024,640]{1,0:T(8,128)(2,1)S(1)} %bitcast.28, bf16[512,8192]{1,0:T(8,128)(2,1)} %all-gather.2.cloned.1.call-done, s32[]{:T(128)S(6)} %select_n.130), kind=kOutput, calls=%fused_computation.22 | convolution fusion | flops 671088640 | bytes 3670020 | tf_op jit(solution)/shard_map/dot_general | solution.py:159
  127.0 0.0 collective-permute-done.5
  127.0 6.4 %collective-permute-start.7 = (bf16[1024,640]{1,0:T(8,128)(2,1)}, bf16[1024,640]{1,0:T(8,128)(2,1)S(1)}, u32[]{:S(2)}, u32[]{:S(2)}) collective-permute-start(bf16[1024,640]{1,0:T(8,128)(2,1)} %collective-permute-done.5), channel_id=1, source_target_pairs={{0,448},{16,464},{32,480},{48,496},{64,0},{80,16},{96,32},{112,48}... | collective-permute-start | bytes 3932168 | tf_op jit(solution)/shard_map/ppermute | solution.py:167
  133.5 2.2 %convolution_add_fusion.3 = f32[512,640]{1,0:T(8,128)S(1)} fusion(f32[512,640]{1,0:T(8,128)S(1)} %fusion.16, bf16[1024,640]{1,0:T(8,128)(2,1)S(1)} %collective-permute-done.3, bf16[512,8192]{1,0:T(8,128)(2,1)} %all-gather.2.cloned.1.call-done, s32[]{:T(128)S(6)} %select_n.146), kind=kOutput, calls=%fused_computation.5 | convolution fusion | flops 671416320 | bytes 4980740 | tf_op jit(solution)/shard_map/dot_general | solution.py:159
  135.7 0.0 copy-done.1
  135.7 2.3 %fusion.12 = f32[512,640]{1,0:T(8,128)S(1)} fusion(bf16[1024,640]{1,0:T(8,128)(2,1)} %collective-permute-done.5, bf16[512,8192]{1,0:T(8,128)(2,1)S(1)} %copy-done.1, s32[]{:T(128)S(6)} %select_n.150), kind=kOutput, calls=%fused_computation.18 | convolution fusion | flops 671088640 | bytes 3670020 | tf_op jit(solution)/shard_map/dot_general | solution.py:159
  138.0 13.5 %collective-permute-done.8 = bf16[1024,640]{1,0:T(8,128)(2,1)} collective-permute-done((bf16[1024,640]{1,0:T(8,128)(2,1)}, bf16[1024,640]{1,0:T(8,128)(2,1)}, u32[]{:S(2)}, u32[]{:S(2)}) %collective-permute-start.8) | collective-permute-done | bytes 1310752 | tf_op jit(solution)/shard_map/ppermute | solution.py:169
  151.5 11.1 %collective-permute-start.9 = (bf16[1024,640]{1,0:T(8,128)(2,1)}, bf16[1024,640]{1,0:T(8,128)(2,1)S(1)}, u32[]{:S(2)}, u32[]{:S(2)}) collective-permute-start(bf16[1024,640]{1,0:T(8,128)(2,1)} %collective-permute-done.8), channel_id=1, source_target_pairs={{0,64},{16,80},{32,96},{48,112},{64,128},{80,144},{96,160},{112,17... | collective-permute-start | bytes 3932168 | tf_op jit(solution)/shard_map/ppermute | solution.py:169
  162.6 2.3 %fusion.10 = f32[512,640]{1,0:T(8,128)S(1)} fusion(bf16[1024,640]{1,0:T(8,128)(2,1)} %collective-permute-done.6, bf16[512,8192]{1,0:T(8,128)(2,1)S(1)} %copy-done.1, s32[]{:T(128)S(6)} %select_n.152), kind=kOutput, calls=%fused_computation.16 | convolution fusion | flops 671088640 | bytes 3670020 | tf_op jit(solution)/shard_map/dot_general | solution.py:159
  165.0 2.4 %fusion.2 = f32[512,640]{1,0:T(8,128)S(1)} fusion(f32[512,640]{1,0:T(8,128)S(1)} %fusion.10, f32[512,640]{1,0:T(8,128)S(1)} %fusion.12, f32[512,640]{1,0:T(8,128)S(1)} %convolution_add_fusion.3, bf16[1024,640]{1,0:T(8,128)(2,1)} %collective-permute-done.4, bf16[512,8192]{1,0:T(8,128)(2,1)S(1)} %copy-done.1, s32[]{:T(128)S(6)} %select_n.148), kind=kOutput, calls=%fused_computation.6 | convolution fusion | flops 672071680 | bytes 7602180 | tf_op jit(solution)/shard_map/dot_general | solution.py:159
  167.3 2.3 %fusion.7 = f32[512,640]{1,0:T(8,128)S(1)} fusion(bf16[1024,640]{1,0:T(8,128)(2,1)} %collective-permute-done.8, bf16[512,8192]{1,0:T(8,128)(2,1)S(1)} %copy-done.1, s32[]{:T(128)S(6)} %select_n.156), kind=kOutput, calls=%fused_computation.13 | convolution fusion | flops 671088640 | bytes 3670020 | tf_op jit(solution)/shard_map/dot_general | solution.py:159
  169.7 0.0 collective-permute-done.7
  169.7 1.0 fusion
  170.7 19.3 %collective-permute-done.9 = bf16[1024,640]{1,0:T(8,128)(2,1)S(1)} collective-permute-done((bf16[1024,640]{1,0:T(8,128)(2,1)}, bf16[1024,640]{1,0:T(8,128)(2,1)S(1)}, u32[]{:S(2)}, u32[]{:S(2)}) %collective-permute-start.9) | collective-permute-done | bytes 1310752 | tf_op jit(solution)/shard_map/ppermute | solution.py:169
  190.0 1.0 convolution_add_fusion.q_ref
  191.0 6.7 %collective-permute-start.10 = (bf16[512,128]{1,0:T(8,128)(2,1)S(1)}, bf16[512,128]{1,0:T(8,128)(2,1)S(1)}, u32[]{:S(2)}, u32[]{:S(2)}) collective-permute-start(bf16[512,128]{1,0:T(8,128)(2,1)S(1)} %slice.25), channel_id=1, source_target_pairs={{0,1},{1,0},{2,3},{3,2},{4,5},{5,4},{6,7},{7,6},{8,9},{9,8},{10,11... | collective-permute-start | bytes 393224 | tf_op jit(solution)/shard_map/ppermute | solution.py:201
  197.7 0.9 copy.7.row_seg_ref
  198.6 0.0 collective-permute-done.10
  198.6 0.7 broadcast_select_fusion
  199.3 8.3 %shard_map.64 = bf16[512,512]{1,0:T(8,128)(2,1)} custom-call(f32[512,640]{1,0:T(8,128)} %copy-done, bf16[512,128]{1,0:T(8,128)(2,1)} %get-tuple-element.18.k_ref, bf16[512,128]{1,0:T(8,128)(2,1)} %get-tuple-element.17.v_ref, f32[512,64]{1,0:T(8,128)} %get-tuple-element.15.cos_ref, f32[512,64]{1,0:T(8,128)} %get-tuple-element.16.sin_ref, ...), custom_call_target="tpu_custom_call" | custom-call | flops 538968064 | bytes 2097152 | tf_op jit(solution)/shard_map/pallas_call | solution.py:99
  (16 shorter events, 0.3 us)
Async XLA Ops:
  6.5 4.3 %copy-start.2 = (bf16[256,512]{1,0:T(8,128)(2,1)S(1)}, bf16[256,512]{1,0:T(8,128)(2,1)}, u32[]{:S(2)}) copy-start(bf16[256,512]{1,0:T(8,128)(2,1)} %param.9) | copy-start | bytes 786436
  6.5 87.1 %all-gather.2.cloned.1.call-start = ((), (), s32[]{:S(2)}) async-start(), calls=%async_computation | async-start | bytes 8912896 | tf_op jit(solution)/shard_map/all_gather | solution.py:196
  7.8 10.9 %copy-start.3 = (s32[512]{0:T(512)S(1)}, s32[512]{0:T(512)}, u32[]{:S(2)}) copy-start(s32[512]{0:T(512)} %param.7) | copy-start | bytes 6148
  10.9 22.8 %collective-permute-start = (bf16[256,640]{1,0:T(8,128)(2,1)S(1)}, bf16[256,640]{1,0:T(8,128)(2,1)S(1)}, u32[]{:S(2)}, u32[]{:S(2)}) collective-permute-start(bf16[256,640]{1,0:T(8,128)(2,1)S(1)} %pad_maximum_fusion), channel_id=1, source_target_pairs={{0,48},{16,0},{32,16},{48,32},{64,112},{80,64},{96,80},{112,96},{1... | collective-permute-start | bytes 983048 | tf_op jit(solution)/shard_map/ppermute | solution.py:137
  16.8 15.0 %collective-permute-start.1 = (bf16[256,640]{1,0:T(8,128)(2,1)S(1)}, bf16[256,640]{1,0:T(8,128)(2,1)S(1)}, u32[]{:S(2)}, u32[]{:S(2)}) collective-permute-start(bf16[256,640]{1,0:T(8,128)(2,1)S(1)} %pad_maximum_fusion), channel_id=1, source_target_pairs={{0,16},{16,32},{32,48},{48,0},{64,80},{80,96},{96,112},{112,64},{1... | collective-permute-start | bytes 983048 | tf_op jit(solution)/shard_map/ppermute | solution.py:139
  31.7 27.1 %collective-permute-start.2 = (bf16[256,640]{1,0:T(8,128)(2,1)S(1)}, bf16[256,640]{1,0:T(8,128)(2,1)S(1)}, u32[]{:S(2)}, u32[]{:S(2)}) collective-permute-start(bf16[256,640]{1,0:T(8,128)(2,1)S(1)} %collective-permute-done.1), channel_id=1, source_target_pairs={{0,16},{16,32},{32,48},{48,0},{64,80},{80,96},{96,112},{112,64},{1... | collective-permute-start | bytes 983048 | tf_op jit(solution)/shard_map/ppermute | solution.py:139
  58.9 30.9 %collective-permute-start.3 = (bf16[1024,640]{1,0:T(8,128)(2,1)S(1)}, bf16[1024,640]{1,0:T(8,128)(2,1)S(1)}, u32[]{:S(2)}, u32[]{:S(2)}) collective-permute-start(bf16[1024,640]{1,0:T(8,128)(2,1)S(1)} %bitcast.26), channel_id=1, source_target_pairs={{0,448},{16,464},{32,480},{48,496},{64,0},{80,16},{96,32},{112,48}... | collective-permute-start | bytes 3932168 | tf_op jit(solution)/shard_map/ppermute | solution.py:167
  69.5 24.2 %collective-permute-start.4 = (bf16[1024,640]{1,0:T(8,128)(2,1)S(1)}, bf16[1024,640]{1,0:T(8,128)(2,1)}, u32[]{:S(2)}, u32[]{:S(2)}) collective-permute-start(bf16[1024,640]{1,0:T(8,128)(2,1)S(1)} %bitcast.27), channel_id=1, source_target_pairs={{0,64},{16,80},{32,96},{48,112},{64,128},{80,144},{96,160},{112,17... | collective-permute-start | bytes 3932168 | tf_op jit(solution)/shard_map/ppermute | solution.py:169
  93.7 28.9 %collective-permute-start.6 = (bf16[1024,640]{1,0:T(8,128)(2,1)}, bf16[1024,640]{1,0:T(8,128)(2,1)}, u32[]{:S(2)}, u32[]{:S(2)}) collective-permute-start(bf16[1024,640]{1,0:T(8,128)(2,1)} %collective-permute-done.4), channel_id=1, source_target_pairs={{0,64},{16,80},{32,96},{48,112},{64,128},{80,144},{96,160},{112,17... | collective-permute-start | bytes 3932168 | tf_op jit(solution)/shard_map/ppermute | solution.py:169
  95.6 31.4 %collective-permute-start.5 = (bf16[1024,640]{1,0:T(8,128)(2,1)S(1)}, bf16[1024,640]{1,0:T(8,128)(2,1)}, u32[]{:S(2)}, u32[]{:S(2)}) collective-permute-start(bf16[1024,640]{1,0:T(8,128)(2,1)S(1)} %collective-permute-done.3), channel_id=1, source_target_pairs={{0,448},{16,464},{32,480},{48,496},{64,0},{80,16},{96,32},{112,48}... | collective-permute-start | bytes 3932168 | tf_op jit(solution)/shard_map/ppermute | solution.py:167
  122.6 29.0 %collective-permute-start.8 = (bf16[1024,640]{1,0:T(8,128)(2,1)}, bf16[1024,640]{1,0:T(8,128)(2,1)}, u32[]{:S(2)}, u32[]{:S(2)}) collective-permute-start(bf16[1024,640]{1,0:T(8,128)(2,1)} %collective-permute-done.6), channel_id=1, source_target_pairs={{0,64},{16,80},{32,96},{48,112},{64,128},{80,144},{96,160},{112,17... | collective-permute-start | bytes 3932168 | tf_op jit(solution)/shard_map/ppermute | solution.py:169
  124.6 11.1 %copy-start.1 = (bf16[512,8192]{1,0:T(8,128)(2,1)S(1)}, bf16[512,8192]{1,0:T(8,128)(2,1)}, u32[]{:S(2)}) copy-start(bf16[512,8192]{1,0:T(8,128)(2,1)} %all-gather.2.cloned.1.call-done) | copy-start | bytes 25165828
  127.0 42.6 %collective-permute-start.7 = (bf16[1024,640]{1,0:T(8,128)(2,1)}, bf16[1024,640]{1,0:T(8,128)(2,1)S(1)}, u32[]{:S(2)}, u32[]{:S(2)}) collective-permute-start(bf16[1024,640]{1,0:T(8,128)(2,1)} %collective-permute-done.5), channel_id=1, source_target_pairs={{0,448},{16,464},{32,480},{48,496},{64,0},{80,16},{96,32},{112,48}... | collective-permute-start | bytes 3932168 | tf_op jit(solution)/shard_map/ppermute | solution.py:167
  151.5 38.5 %collective-permute-start.9 = (bf16[1024,640]{1,0:T(8,128)(2,1)}, bf16[1024,640]{1,0:T(8,128)(2,1)S(1)}, u32[]{:S(2)}, u32[]{:S(2)}) collective-permute-start(bf16[1024,640]{1,0:T(8,128)(2,1)} %collective-permute-done.8), channel_id=1, source_target_pairs={{0,64},{16,80},{32,96},{48,112},{64,128},{80,144},{96,160},{112,17... | collective-permute-start | bytes 3932168 | tf_op jit(solution)/shard_map/ppermute | solution.py:169
  191.0 8.3 %copy-start = (f32[512,640]{1,0:T(8,128)}, f32[512,640]{1,0:T(8,128)S(1)}, u32[]{:S(2)}) copy-start(f32[512,640]{1,0:T(8,128)S(1)} %convolution_add_fusion.q_ref) | copy-start | bytes 3932164
  191.0 7.6 %collective-permute-start.10 = (bf16[512,128]{1,0:T(8,128)(2,1)S(1)}, bf16[512,128]{1,0:T(8,128)(2,1)S(1)}, u32[]{:S(2)}, u32[]{:S(2)}) collective-permute-start(bf16[512,128]{1,0:T(8,128)(2,1)S(1)} %slice.25), channel_id=1, source_target_pairs={{0,1},{1,0},{2,3},{3,2},{4,5},{5,4},{6,7},{7,6},{8,9},{9,8},{10,11... | collective-permute-start | bytes 393224 | tf_op jit(solution)/shard_map/ppermute | solution.py:201
Sparse Core Ops, SparseCore 0:
  10.0 78.1 all-gather.1

commit v9 on v8

--- a/solution.py
+++ b/solution.py
@@ -56,31 +56,42 @@
     return mixed.astype(jnp.bfloat16)
 
 
+ROW_TILE = 128
+SEGMENT_MOST = 64
+
+
 def attention_kernel(heads, q_ref, k_ref, v_ref, cos_ref, sin_ref, row_seg_ref, col_seg_ref, o_ref):
     half = HEAD_DIM // 2
-    cosine, sine = cos_ref[...], sin_ref[...]
-
-    def rope(x):
+
+    def rope(x, rows):
+        cosine, sine = cos_ref[rows, :], sin_ref[rows, :]
         a, b = x[:, :half], x[:, half:]
         return jnp.concatenate([a * cosine - b * sine, b * cosine + a * sine], axis=1)
 
-    keys = rope(k_ref[...].astype(jnp.float32)).astype(jnp.bfloat16)
-    values = v_ref[...]
-    rows = q_ref.shape[0]
-    places_i = lax.broadcasted_iota(jnp.int32, (rows, rows), 0)
-    places_j = lax.broadcasted_iota(jnp.int32, (rows, rows), 1)
-    allowed = (row_seg_ref[...] == col_seg_ref[...]) & (places_j <= places_i)
+    n_rows = q_ref.shape[0]
+    keys = rope(k_ref[...].astype(jnp.float32), slice(0, n_rows)).astype(jnp.bfloat16)
     scale = HEAD_DIM ** (-0.5)
-    for h in range(heads):
-        cols = slice(h * HEAD_DIM, (h + 1) * HEAD_DIM)
-        query = rope(q_ref[:, cols]).astype(jnp.bfloat16)
-        scores = lax.dot_general(
-            query, keys, (((1,), (1,)), ((), ())), preferred_element_type=jnp.float32
-        ) * scale
-        weights = jnp.where(allowed, jnp.exp(scores), 0.0)
-        probabilities = (weights / jnp.sum(weights, axis=1, keepdims=True)).astype(jnp.bfloat16)
-        mixed = jnp.dot(probabilities, values, preferred_element_type=jnp.float32)
-        o_ref[:, cols] = mixed.astype(o_ref.dtype)
+    reach = max(ROW_TILE, SEGMENT_MOST)
+    for r0 in range(0, n_rows, ROW_TILE):
+        c0 = max(0, r0 - reach)
+        c1 = r0 + ROW_TILE
+        rows = slice(r0, c1)
+        places_i = lax.broadcasted_iota(jnp.int32, (ROW_TILE, c1 - c0), 0) + r0
+        places_j = lax.broadcasted_iota(jnp.int32, (ROW_TILE, c1 - c0), 1) + c0
+        allowed = (row_seg_ref[rows, :] == col_seg_ref[:, c0:c1]) & (places_j <= places_i)
+        window_keys = keys[c0:c1]
+        window_values = v_ref[c0:c1, :]
+        for h in range(heads):
+            cols = slice(h * HEAD_DIM, (h + 1) * HEAD_DIM)
+            query = rope(q_ref[rows, cols], rows).astype(jnp.bfloat16)
+            scores = lax.dot_general(
+                query, window_keys, (((1,), (1,)), ((), ())), preferred_element_type=jnp.float32
+            ) * scale
+            weights = jnp.where(allowed, jnp.exp(scores), 0.0)
+            total = jnp.sum(weights, axis=1, keepdims=True)
+            probabilities = (weights / total).astype(jnp.bfloat16)
+            mixed = jnp.dot(probabilities, window_values, preferred_element_type=jnp.float32)
+            o_ref[rows, cols] = mixed.astype(o_ref.dtype)
 
 
 def rope_tables(positions):

time: 217 us -> 215 us (level)
  Pallas kernels: 8.27 us -> 5.98 us
    pallas_call x1, Pallas kernels: 8.27 us -> 5.98 us  [attention_kernel_call(): pl.pallas_call(functools.partial(attention_kernel, heads), out_shape=jax....]
where the time goes in v9:
time: 215 us; the launch traced here: 212 us
  waiting for transfers between devices  110 us (51%)
  starting transfers between devices  56.5 us (26%)
  matrix products  15.9 us (7%)
  between operations  14.6 us (7%)
  other arithmetic  7.34 us (3%)
  Pallas kernels  5.98 us (3%)
    ppermute x4, waiting for transfers between devices, ring_matmul(): from_left = lax.ppermute(from_left, axis, perm=moved(1))  57.4 us
    ppermute x2, waiting for transfers between devices, ring_gather(): from_left = lax.ppermute(from_left, axis, perm=moved(1))  34.2 us
    ppermute x3, starting transfers between devices, ring_matmul(): from_right = lax.ppermute(from_right, axis, perm=moved(-1))  23.3 us
    ppermute x3, waiting for transfers between devices, ring_matmul(): from_right = lax.ppermute(from_right, axis, perm=moved(-1))  18.4 us
    ppermute x4, starting transfers between devices, ring_matmul(): from_left = lax.ppermute(from_left, axis, perm=moved(1))  16.9 us
    dot_general x8, matrix products, product(): return jnp.dot(lhs, part, preferred_element_type=jnp.float32)  15.9 us
    ppermute x1, starting transfers between devices, per_device(): other_rows = lax.ppermute(own_rows, 'weight', perm=partner)  6.68 us
    pallas_call x1, Pallas kernels, attention_kernel_call(): pl.pallas_call(functools.partial(attention_kernel, heads), out_shape=jax....  5.98 us
  transfers between devices with their start and end apart: 12, of which 7 were waited for; matrix products, arithmetic and copies ran while one was open for 9% of the time, Pallas kernels for 0%

profile of v9, /device:TPU:7, one launch (start us, length us, event | category | flops | bytes accessed | tf_op | source)
XLA Modules:
  0.0 212.1 jit_solution(321770716027779397)
XLA Ops:
  6.5 1.3 fusion.3
  7.8 0.0 copy-start.3
  7.9 2.0 fusion.5
  9.9 0.0 all-gather.2.cloned.1.call-update
  9.9 0.9 dynamic-slice_select_fusion
  10.9 5.9 %collective-permute-start = (bf16[256,640]{1,0:T(8,128)(2,1)S(1)}, bf16[256,640]{1,0:T(8,128)(2,1)S(1)}, u32[]{:S(2)}, u32[]{:S(2)}) collective-permute-start(bf16[256,640]{1,0:T(8,128)(2,1)S(1)} %pad_maximum_fusion), channel_id=1, source_target_pairs={{0,48},{16,0},{32,16},{48,32},{64,112},{80,64},{96,80},{112,96},{1... | collective-permute-start | bytes 983048 | tf_op jit(solution)/shard_map/ppermute | solution.py:148
  16.8 1.9 collective-permute-start.1
  18.8 0.5 slice.17
  20.0 0.1 select_bitcast_fusion
  20.1 0.3 reduce-window.9
  20.4 0.1 slice.19
  20.5 0.1 slice_reduce_fusion
  20.6 0.1 broadcast_in_dim.30
  20.8 0.1 fusion.26
  20.8 1.8 multiply_sine_fusion
  22.7 9.1 %collective-permute-done.1 = bf16[256,640]{1,0:T(8,128)(2,1)S(1)} collective-permute-done((bf16[256,640]{1,0:T(8,128)(2,1)S(1)}, bf16[256,640]{1,0:T(8,128)(2,1)S(1)}, u32[]{:S(2)}, u32[]{:S(2)}) %collective-permute-start.1) | collective-permute-done | bytes 327712 | tf_op jit(solution)/shard_map/ppermute | solution.py:150
  31.7 1.9 collective-permute-start.2
  33.7 0.0 collective-permute-done
  33.8 25.1 %collective-permute-done.2 = bf16[256,640]{1,0:T(8,128)(2,1)S(1)} collective-permute-done((bf16[256,640]{1,0:T(8,128)(2,1)S(1)}, bf16[256,640]{1,0:T(8,128)(2,1)S(1)}, u32[]{:S(2)}, u32[]{:S(2)}) %collective-permute-start.2) | collective-permute-done | bytes 327712 | tf_op jit(solution)/shard_map/ppermute | solution.py:150
  58.9 10.6 %collective-permute-start.3 = (bf16[1024,640]{1,0:T(8,128)(2,1)S(1)}, bf16[1024,640]{1,0:T(8,128)(2,1)S(1)}, u32[]{:S(2)}, u32[]{:S(2)}) collective-permute-start(bf16[1024,640]{1,0:T(8,128)(2,1)S(1)} %bitcast.26), channel_id=1, source_target_pairs={{0,448},{16,464},{32,480},{48,496},{64,0},{80,16},{96,32},{112,48}... | collective-permute-start | bytes 3932168 | tf_op jit(solution)/shard_map/ppermute | solution.py:178
  69.5 1.9 collective-permute-start.4
  71.4 18.4 %collective-permute-done.3 = bf16[1024,640]{1,0:T(8,128)(2,1)S(1)} collective-permute-done((bf16[1024,640]{1,0:T(8,128)(2,1)S(1)}, bf16[1024,640]{1,0:T(8,128)(2,1)S(1)}, u32[]{:S(2)}, u32[]{:S(2)}) %collective-permute-start.3) | collective-permute-done | bytes 1310752 | tf_op jit(solution)/shard_map/ppermute | solution.py:178
  89.8 3.8 %collective-permute-done.4 = bf16[1024,640]{1,0:T(8,128)(2,1)} collective-permute-done((bf16[1024,640]{1,0:T(8,128)(2,1)S(1)}, bf16[1024,640]{1,0:T(8,128)(2,1)}, u32[]{:S(2)}, u32[]{:S(2)}) %collective-permute-start.4) | collective-permute-done | bytes 1310752 | tf_op jit(solution)/shard_map/ppermute | solution.py:180
  93.7 1.9 collective-permute-start.6
  95.6 6.2 %collective-permute-start.5 = (bf16[1024,640]{1,0:T(8,128)(2,1)S(1)}, bf16[1024,640]{1,0:T(8,128)(2,1)}, u32[]{:S(2)}, u32[]{:S(2)}) collective-permute-start(bf16[1024,640]{1,0:T(8,128)(2,1)S(1)} %collective-permute-done.3), channel_id=1, source_target_pairs={{0,448},{16,464},{32,480},{48,496},{64,0},{80,16},{96,32},{112,48}... | collective-permute-start | bytes 3932168 | tf_op jit(solution)/shard_map/ppermute | solution.py:178
  101.8 20.7 %collective-permute-done.6 = bf16[1024,640]{1,0:T(8,128)(2,1)} collective-permute-done((bf16[1024,640]{1,0:T(8,128)(2,1)}, bf16[1024,640]{1,0:T(8,128)(2,1)}, u32[]{:S(2)}, u32[]{:S(2)}) %collective-permute-start.6) | collective-permute-done | bytes 1310752 | tf_op jit(solution)/shard_map/ppermute | solution.py:180
  122.6 1.9 collective-permute-start.8
  124.6 0.0 copy-start.1
  124.7 2.4 %fusion.16 = f32[512,640]{1,0:T(8,128)S(1)} fusion(bf16[1024,640]{1,0:T(8,128)(2,1)S(1)} %bitcast.28, bf16[512,8192]{1,0:T(8,128)(2,1)} %all-gather.2.cloned.1.call-done, s32[]{:T(128)S(6)} %select_n.130), kind=kOutput, calls=%fused_computation.22 | convolution fusion | flops 671088640 | bytes 3670020 | tf_op jit(solution)/shard_map/dot_general | solution.py:170
  127.0 0.0 collective-permute-done.5
  127.0 6.4 %collective-permute-start.7 = (bf16[1024,640]{1,0:T(8,128)(2,1)}, bf16[1024,640]{1,0:T(8,128)(2,1)S(1)}, u32[]{:S(2)}, u32[]{:S(2)}) collective-permute-start(bf16[1024,640]{1,0:T(8,128)(2,1)} %collective-permute-done.5), channel_id=1, source_target_pairs={{0,448},{16,464},{32,480},{48,496},{64,0},{80,16},{96,32},{112,48}... | collective-permute-start | bytes 3932168 | tf_op jit(solution)/shard_map/ppermute | solution.py:178
  133.5 2.2 %convolution_add_fusion.3 = f32[512,640]{1,0:T(8,128)S(1)} fusion(f32[512,640]{1,0:T(8,128)S(1)} %fusion.16, bf16[1024,640]{1,0:T(8,128)(2,1)S(1)} %collective-permute-done.3, bf16[512,8192]{1,0:T(8,128)(2,1)} %all-gather.2.cloned.1.call-done, s32[]{:T(128)S(6)} %select_n.146), kind=kOutput, calls=%fused_computation.5 | convolution fusion | flops 671416320 | bytes 4980740 | tf_op jit(solution)/shard_map/dot_general | solution.py:170
  135.7 0.0 copy-done.1
  135.7 2.3 %fusion.12 = f32[512,640]{1,0:T(8,128)S(1)} fusion(bf16[1024,640]{1,0:T(8,128)(2,1)} %collective-permute-done.5, bf16[512,8192]{1,0:T(8,128)(2,1)S(1)} %copy-done.1, s32[]{:T(128)S(6)} %select_n.150), kind=kOutput, calls=%fused_computation.18 | convolution fusion | flops 671088640 | bytes 3670020 | tf_op jit(solution)/shard_map/dot_general | solution.py:170
  138.0 13.5 %collective-permute-done.8 = bf16[1024,640]{1,0:T(8,128)(2,1)} collective-permute-done((bf16[1024,640]{1,0:T(8,128)(2,1)}, bf16[1024,640]{1,0:T(8,128)(2,1)}, u32[]{:S(2)}, u32[]{:S(2)}) %collective-permute-start.8) | collective-permute-done | bytes 1310752 | tf_op jit(solution)/shard_map/ppermute | solution.py:180
  151.5 11.1 %collective-permute-start.9 = (bf16[1024,640]{1,0:T(8,128)(2,1)}, bf16[1024,640]{1,0:T(8,128)(2,1)S(1)}, u32[]{:S(2)}, u32[]{:S(2)}) collective-permute-start(bf16[1024,640]{1,0:T(8,128)(2,1)} %collective-permute-done.8), channel_id=1, source_target_pairs={{0,64},{16,80},{32,96},{48,112},{64,128},{80,144},{96,160},{112,17... | collective-permute-start | bytes 3932168 | tf_op jit(solution)/shard_map/ppermute | solution.py:180
  162.6 2.3 %fusion.10 = f32[512,640]{1,0:T(8,128)S(1)} fusion(bf16[1024,640]{1,0:T(8,128)(2,1)} %collective-permute-done.6, bf16[512,8192]{1,0:T(8,128)(2,1)S(1)} %copy-done.1, s32[]{:T(128)S(6)} %select_n.152), kind=kOutput, calls=%fused_computation.16 | convolution fusion | flops 671088640 | bytes 3670020 | tf_op jit(solution)/shard_map/dot_general | solution.py:170
  165.0 2.4 %fusion.2 = f32[512,640]{1,0:T(8,128)S(1)} fusion(f32[512,640]{1,0:T(8,128)S(1)} %fusion.10, f32[512,640]{1,0:T(8,128)S(1)} %fusion.12, f32[512,640]{1,0:T(8,128)S(1)} %convolution_add_fusion.3, bf16[1024,640]{1,0:T(8,128)(2,1)} %collective-permute-done.4, bf16[512,8192]{1,0:T(8,128)(2,1)S(1)} %copy-done.1, s32[]{:T(128)S(6)} %select_n.148), kind=kOutput, calls=%fused_computation.6 | convolution fusion | flops 672071680 | bytes 7602180 | tf_op jit(solution)/shard_map/dot_general | solution.py:170
  167.3 2.3 %fusion.7 = f32[512,640]{1,0:T(8,128)S(1)} fusion(bf16[1024,640]{1,0:T(8,128)(2,1)} %collective-permute-done.8, bf16[512,8192]{1,0:T(8,128)(2,1)S(1)} %copy-done.1, s32[]{:T(128)S(6)} %select_n.156), kind=kOutput, calls=%fused_computation.13 | convolution fusion | flops 671088640 | bytes 3670020 | tf_op jit(solution)/shard_map/dot_general | solution.py:170
  169.7 0.0 collective-permute-done.7
  169.7 1.0 fusion
  170.7 19.3 %collective-permute-done.9 = bf16[1024,640]{1,0:T(8,128)(2,1)S(1)} collective-permute-done((bf16[1024,640]{1,0:T(8,128)(2,1)}, bf16[1024,640]{1,0:T(8,128)(2,1)S(1)}, u32[]{:S(2)}, u32[]{:S(2)}) %collective-permute-start.9) | collective-permute-done | bytes 1310752 | tf_op jit(solution)/shard_map/ppermute | solution.py:180
  190.0 1.0 convolution_add_fusion.q_ref
  191.0 6.7 %collective-permute-start.10 = (bf16[512,128]{1,0:T(8,128)(2,1)S(1)}, bf16[512,128]{1,0:T(8,128)(2,1)S(1)}, u32[]{:S(2)}, u32[]{:S(2)}) collective-permute-start(bf16[512,128]{1,0:T(8,128)(2,1)S(1)} %slice.25), channel_id=1, source_target_pairs={{0,1},{1,0},{2,3},{3,2},{4,5},{5,4},{6,7},{7,6},{8,9},{9,8},{10,11... | collective-permute-start | bytes 393224 | tf_op jit(solution)/shard_map/ppermute | solution.py:212
  197.7 0.9 copy.7.row_seg_ref
  198.6 0.0 collective-permute-done.10
  198.6 0.7 broadcast_select_fusion
  199.3 6.0 %shard_map.64 = bf16[512,512]{1,0:T(8,128)(2,1)} custom-call(f32[512,640]{1,0:T(8,128)} %copy-done, bf16[512,128]{1,0:T(8,128)(2,1)} %get-tuple-element.18.k_ref, bf16[512,128]{1,0:T(8,128)(2,1)} %get-tuple-element.17.v_ref, f32[512,64]{1,0:T(8,128)} %get-tuple-element.15.cos_ref, f32[512,64]{1,0:T(8,128)} %get-tuple-element.16.sin_ref, ...), custom_call_target="tpu_custom_call" | custom-call | flops 538968064 | bytes 2097152 | tf_op jit(solution)/shard_map/pallas_call | solution.py:110
  (16 shorter events, 0.3 us)
Async XLA Ops:
  6.5 4.3 %copy-start.2 = (bf16[256,512]{1,0:T(8,128)(2,1)S(1)}, bf16[256,512]{1,0:T(8,128)(2,1)}, u32[]{:S(2)}) copy-start(bf16[256,512]{1,0:T(8,128)(2,1)} %param.9) | copy-start | bytes 786436
  6.5 87.1 %all-gather.2.cloned.1.call-start = ((), (), s32[]{:S(2)}) async-start(), calls=%async_computation | async-start | bytes 8912896 | tf_op jit(solution)/shard_map/all_gather | solution.py:207
  7.8 10.9 %copy-start.3 = (s32[512]{0:T(512)S(1)}, s32[512]{0:T(512)}, u32[]{:S(2)}) copy-start(s32[512]{0:T(512)} %param.7) | copy-start | bytes 6148
  10.9 22.8 %collective-permute-start = (bf16[256,640]{1,0:T(8,128)(2,1)S(1)}, bf16[256,640]{1,0:T(8,128)(2,1)S(1)}, u32[]{:S(2)}, u32[]{:S(2)}) collective-permute-start(bf16[256,640]{1,0:T(8,128)(2,1)S(1)} %pad_maximum_fusion), channel_id=1, source_target_pairs={{0,48},{16,0},{32,16},{48,32},{64,112},{80,64},{96,80},{112,96},{1... | collective-permute-start | bytes 983048 | tf_op jit(solution)/shard_map/ppermute | solution.py:148
  16.8 15.0 %collective-permute-start.1 = (bf16[256,640]{1,0:T(8,128)(2,1)S(1)}, bf16[256,640]{1,0:T(8,128)(2,1)S(1)}, u32[]{:S(2)}, u32[]{:S(2)}) collective-permute-start(bf16[256,640]{1,0:T(8,128)(2,1)S(1)} %pad_maximum_fusion), channel_id=1, source_target_pairs={{0,16},{16,32},{32,48},{48,0},{64,80},{80,96},{96,112},{112,64},{1... | collective-permute-start | bytes 983048 | tf_op jit(solution)/shard_map/ppermute | solution.py:150
  31.7 27.1 %collective-permute-start.2 = (bf16[256,640]{1,0:T(8,128)(2,1)S(1)}, bf16[256,640]{1,0:T(8,128)(2,1)S(1)}, u32[]{:S(2)}, u32[]{:S(2)}) collective-permute-start(bf16[256,640]{1,0:T(8,128)(2,1)S(1)} %collective-permute-done.1), channel_id=1, source_target_pairs={{0,16},{16,32},{32,48},{48,0},{64,80},{80,96},{96,112},{112,64},{1... | collective-permute-start | bytes 983048 | tf_op jit(solution)/shard_map/ppermute | solution.py:150
  58.9 30.9 %collective-permute-start.3 = (bf16[1024,640]{1,0:T(8,128)(2,1)S(1)}, bf16[1024,640]{1,0:T(8,128)(2,1)S(1)}, u32[]{:S(2)}, u32[]{:S(2)}) collective-permute-start(bf16[1024,640]{1,0:T(8,128)(2,1)S(1)} %bitcast.26), channel_id=1, source_target_pairs={{0,448},{16,464},{32,480},{48,496},{64,0},{80,16},{96,32},{112,48}... | collective-permute-start | bytes 3932168 | tf_op jit(solution)/shard_map/ppermute | solution.py:178
  69.5 24.2 %collective-permute-start.4 = (bf16[1024,640]{1,0:T(8,128)(2,1)S(1)}, bf16[1024,640]{1,0:T(8,128)(2,1)}, u32[]{:S(2)}, u32[]{:S(2)}) collective-permute-start(bf16[1024,640]{1,0:T(8,128)(2,1)S(1)} %bitcast.27), channel_id=1, source_target_pairs={{0,64},{16,80},{32,96},{48,112},{64,128},{80,144},{96,160},{112,17... | collective-permute-start | bytes 3932168 | tf_op jit(solution)/shard_map/ppermute | solution.py:180
  93.7 28.9 %collective-permute-start.6 = (bf16[1024,640]{1,0:T(8,128)(2,1)}, bf16[1024,640]{1,0:T(8,128)(2,1)}, u32[]{:S(2)}, u32[]{:S(2)}) collective-permute-start(bf16[1024,640]{1,0:T(8,128)(2,1)} %collective-permute-done.4), channel_id=1, source_target_pairs={{0,64},{16,80},{32,96},{48,112},{64,128},{80,144},{96,160},{112,17... | collective-permute-start | bytes 3932168 | tf_op jit(solution)/shard_map/ppermute | solution.py:180
  95.6 31.4 %collective-permute-start.5 = (bf16[1024,640]{1,0:T(8,128)(2,1)S(1)}, bf16[1024,640]{1,0:T(8,128)(2,1)}, u32[]{:S(2)}, u32[]{:S(2)}) collective-permute-start(bf16[1024,640]{1,0:T(8,128)(2,1)S(1)} %collective-permute-done.3), channel_id=1, source_target_pairs={{0,448},{16,464},{32,480},{48,496},{64,0},{80,16},{96,32},{112,48}... | collective-permute-start | bytes 3932168 | tf_op jit(solution)/shard_map/ppermute | solution.py:178
  122.6 29.0 %collective-permute-start.8 = (bf16[1024,640]{1,0:T(8,128)(2,1)}, bf16[1024,640]{1,0:T(8,128)(2,1)}, u32[]{:S(2)}, u32[]{:S(2)}) collective-permute-start(bf16[1024,640]{1,0:T(8,128)(2,1)} %collective-permute-done.6), channel_id=1, source_target_pairs={{0,64},{16,80},{32,96},{48,112},{64,128},{80,144},{96,160},{112,17... | collective-permute-start | bytes 3932168 | tf_op jit(solution)/shard_map/ppermute | solution.py:180
  124.6 11.1 %copy-start.1 = (bf16[512,8192]{1,0:T(8,128)(2,1)S(1)}, bf16[512,8192]{1,0:T(8,128)(2,1)}, u32[]{:S(2)}) copy-start(bf16[512,8192]{1,0:T(8,128)(2,1)} %all-gather.2.cloned.1.call-done) | copy-start | bytes 25165828
  127.0 42.6 %collective-permute-start.7 = (bf16[1024,640]{1,0:T(8,128)(2,1)}, bf16[1024,640]{1,0:T(8,128)(2,1)S(1)}, u32[]{:S(2)}, u32[]{:S(2)}) collective-permute-start(bf16[1024,640]{1,0:T(8,128)(2,1)} %collective-permute-done.5), channel_id=1, source_target_pairs={{0,448},{16,464},{32,480},{48,496},{64,0},{80,16},{96,32},{112,48}... | collective-permute-start | bytes 3932168 | tf_op jit(solution)/shard_map/ppermute | solution.py:178
  151.5 38.5 %collective-permute-start.9 = (bf16[1024,640]{1,0:T(8,128)(2,1)}, bf16[1024,640]{1,0:T(8,128)(2,1)S(1)}, u32[]{:S(2)}, u32[]{:S(2)}) collective-permute-start(bf16[1024,640]{1,0:T(8,128)(2,1)} %collective-permute-done.8), channel_id=1, source_target_pairs={{0,64},{16,80},{32,96},{48,112},{64,128},{80,144},{96,160},{112,17... | collective-permute-start | bytes 3932168 | tf_op jit(solution)/shard_map/ppermute | solution.py:180
  191.0 8.3 %copy-start = (f32[512,640]{1,0:T(8,128)}, f32[512,640]{1,0:T(8,128)S(1)}, u32[]{:S(2)}) copy-start(f32[512,640]{1,0:T(8,128)S(1)} %convolution_add_fusion.q_ref) | copy-start | bytes 3932164
  191.0 7.6 %collective-permute-start.10 = (bf16[512,128]{1,0:T(8,128)(2,1)S(1)}, bf16[512,128]{1,0:T(8,128)(2,1)S(1)}, u32[]{:S(2)}, u32[]{:S(2)}) collective-permute-start(bf16[512,128]{1,0:T(8,128)(2,1)S(1)} %slice.25), channel_id=1, source_target_pairs={{0,1},{1,0},{2,3},{3,2},{4,5},{5,4},{6,7},{7,6},{8,9},{9,8},{10,11... | collective-permute-start | bytes 393224 | tf_op jit(solution)/shard_map/ppermute | solution.py:212
Sparse Core Ops, SparseCore 0:
  10.0 78.1 all-gather.1

commit v10 on v9

--- a/solution.py
+++ b/solution.py
@@ -56,7 +56,7 @@
     return mixed.astype(jnp.bfloat16)
 
 
-ROW_TILE = 128
+ROW_TILE = 64
 SEGMENT_MOST = 64
 
 
@@ -79,19 +79,22 @@
         places_i = lax.broadcasted_iota(jnp.int32, (ROW_TILE, c1 - c0), 0) + r0
         places_j = lax.broadcasted_iota(jnp.int32, (ROW_TILE, c1 - c0), 1) + c0
         allowed = (row_seg_ref[rows, :] == col_seg_ref[:, c0:c1]) & (places_j <= places_i)
-        window_keys = keys[c0:c1]
-        window_values = v_ref[c0:c1, :]
+        allowed = jnp.concatenate([allowed] * heads, axis=0)
+        query = jnp.concatenate(
+            [rope(q_ref[rows, h * HEAD_DIM : (h + 1) * HEAD_DIM], rows) for h in range(heads)],
+            axis=0,
+        ).astype(jnp.bfloat16)
+        scores = lax.dot_general(
+            query, keys[c0:c1], (((1,), (1,)), ((), ())), preferred_element_type=jnp.float32
+        ) * scale
+        weights = jnp.where(allowed, jnp.exp(scores), 0.0)
+        total = jnp.sum(weights, axis=1, keepdims=True)
+        probabilities = (weights / total).astype(jnp.bfloat16)
+        mixed = jnp.dot(probabilities, v_ref[c0:c1, :], preferred_element_type=jnp.float32)
         for h in range(heads):
-            cols = slice(h * HEAD_DIM, (h + 1) * HEAD_DIM)
-            query = rope(q_ref[rows, cols], rows).astype(jnp.bfloat16)
-            scores = lax.dot_general(
-                query, window_keys, (((1,), (1,)), ((), ())), preferred_element_type=jnp.float32
-            ) * scale
-            weights = jnp.where(allowed, jnp.exp(scores), 0.0)
-            total = jnp.sum(weights, axis=1, keepdims=True)
-            probabilities = (weights / total).astype(jnp.bfloat16)
-            mixed = jnp.dot(probabilities, window_values, preferred_element_type=jnp.float32)
-            o_ref[rows, cols] = mixed.astype(o_ref.dtype)
+            o_ref[rows, h * HEAD_DIM : (h + 1) * HEAD_DIM] = mixed[
+                h * ROW_TILE : (h + 1) * ROW_TILE
+            ].astype(o_ref.dtype)
 
 
 def rope_tables(positions):
@@ -102,7 +105,7 @@
     return jnp.cos(angles), jnp.sin(angles)
 
 
-def attention_kernel_call(projected, cols, key_rows, value_rows, cosine, sine, seg_ids):
+def attention_kernel_call(projected, cols, key_rows, value_rows, cosine, sine, row_seg, col_seg):
     rows = projected.shape[0]
     half_dim = HEAD_DIM // 2
     vmem = pl.BlockSpec(memory_space=pltpu.VMEM)
@@ -123,8 +126,8 @@
         value_rows,
         cosine,
         sine,
-        seg_ids[:, None],
-        seg_ids[None, :],
+        row_seg,
+        col_seg,
     )
 
 
@@ -203,7 +206,10 @@
     near = ring_gather(local_weights, "batch", 1, y_hi)
     near = near.reshape(-1, local_weights.shape[1])
     cosine, sine = rope_tables(positions_in_segment(segment_ids))
-    near, cosine, sine = lax.optimization_barrier((near, cosine, sine))
+    row_seg, col_seg = segment_ids[:, None], segment_ids[None, :]
+    near, cosine, sine, row_seg, col_seg = lax.optimization_barrier(
+        (near, cosine, sine, row_seg, col_seg)
+    )
     gathered = lax.all_gather(normed, "weight", axis=0, tiled=True)
     pack_rows = gathered.shape[0]
     projected = ring_matmul(gathered, near, "batch", y_hi, Z_CHIPS)
@@ -213,7 +219,7 @@
     key_rows = jnp.where(core == 0, own_rows, other_rows)
     value_rows = jnp.where(core == 0, other_rows, own_rows)
     return attention_kernel_call(
-        projected, query_cols, key_rows, value_rows, cosine, sine, segment_ids
+        projected, query_cols, key_rows, value_rows, cosine, sine, row_seg, col_seg
     )
 
 

time: 215 us -> 215 us (level)
  no operation moved by 1% of the time
where the time goes in v10:
time: 215 us; the launch traced here: 212 us
  waiting for transfers between devices  110 us (51%)
  starting transfers between devices  56.5 us (26%)
  matrix products  15.9 us (7%)
  between operations  14.6 us (7%)
  other arithmetic  7.34 us (3%)
  Pallas kernels  6.07 us (3%)
    ppermute x4, waiting for transfers between devices, ring_matmul(): from_left = lax.ppermute(from_left, axis, perm=moved(1))  57.4 us
    ppermute x2, waiting for transfers between devices, ring_gather(): from_left = lax.ppermute(from_left, axis, perm=moved(1))  34.2 us
    ppermute x3, starting transfers between devices, ring_matmul(): from_right = lax.ppermute(from_right, axis, perm=moved(-1))  23.3 us
    ppermute x3, waiting for transfers between devices, ring_matmul(): from_right = lax.ppermute(from_right, axis, perm=moved(-1))  18.4 us
    ppermute x4, starting transfers between devices, ring_matmul(): from_left = lax.ppermute(from_left, axis, perm=moved(1))  16.9 us
    dot_general x8, matrix products, product(): return jnp.dot(lhs, part, preferred_element_type=jnp.float32)  15.9 us
    ppermute x1, starting transfers between devices, per_device(): other_rows = lax.ppermute(own_rows, 'weight', perm=partner)  6.68 us
    pallas_call x1, Pallas kernels, attention_kernel_call(): pl.pallas_call(functools.partial(attention_kernel, heads), out_shape=jax....  6.07 us
  transfers between devices with their start and end apart: 12, of which 7 were waited for; matrix products, arithmetic and copies ran while one was open for 9% of the time, Pallas kernels for 0%

profile of v10, /device:TPU:7, one launch (start us, length us, event | category | flops | bytes accessed | tf_op | source)
XLA Modules:
  0.0 212.2 jit_solution(5776164148350673986)
XLA Ops:
  6.5 1.3 fusion.3
  7.8 0.0 copy-start.3
  7.9 2.0 fusion.5
  9.9 0.0 all-gather.2.cloned.1.call-update
  9.9 0.9 dynamic-slice_select_fusion
  10.9 5.9 %collective-permute-start = (bf16[256,640]{1,0:T(8,128)(2,1)S(1)}, bf16[256,640]{1,0:T(8,128)(2,1)S(1)}, u32[]{:S(2)}, u32[]{:S(2)}) collective-permute-start(bf16[256,640]{1,0:T(8,128)(2,1)S(1)} %pad_maximum_fusion), channel_id=1, source_target_pairs={{0,48},{16,0},{32,16},{48,32},{64,112},{80,64},{96,80},{112,96},{1... | collective-permute-start | bytes 983048 | tf_op jit(solution)/shard_map/ppermute | solution.py:151
  16.8 1.9 collective-permute-start.1
  18.8 0.5 slice.17
  20.0 0.1 select_bitcast_fusion
  20.1 0.3 reduce-window.9
  20.4 0.1 slice.19
  20.5 0.1 slice_reduce_fusion
  20.6 0.1 broadcast_in_dim.30
  20.8 0.1 fusion.26
  20.8 1.8 multiply_sine_fusion
  22.7 9.1 %collective-permute-done.1 = bf16[256,640]{1,0:T(8,128)(2,1)S(1)} collective-permute-done((bf16[256,640]{1,0:T(8,128)(2,1)S(1)}, bf16[256,640]{1,0:T(8,128)(2,1)S(1)}, u32[]{:S(2)}, u32[]{:S(2)}) %collective-permute-start.1) | collective-permute-done | bytes 327712 | tf_op jit(solution)/shard_map/ppermute | solution.py:153
  31.7 1.9 collective-permute-start.2
  33.7 0.0 collective-permute-done
  33.8 25.1 %collective-permute-done.2 = bf16[256,640]{1,0:T(8,128)(2,1)S(1)} collective-permute-done((bf16[256,640]{1,0:T(8,128)(2,1)S(1)}, bf16[256,640]{1,0:T(8,128)(2,1)S(1)}, u32[]{:S(2)}, u32[]{:S(2)}) %collective-permute-start.2) | collective-permute-done | bytes 327712 | tf_op jit(solution)/shard_map/ppermute | solution.py:153
  58.9 10.6 %collective-permute-start.3 = (bf16[1024,640]{1,0:T(8,128)(2,1)S(1)}, bf16[1024,640]{1,0:T(8,128)(2,1)S(1)}, u32[]{:S(2)}, u32[]{:S(2)}) collective-permute-start(bf16[1024,640]{1,0:T(8,128)(2,1)S(1)} %bitcast.26), channel_id=1, source_target_pairs={{0,448},{16,464},{32,480},{48,496},{64,0},{80,16},{96,32},{112,48}... | collective-permute-start | bytes 3932168 | tf_op jit(solution)/shard_map/ppermute | solution.py:181
  69.5 1.9 collective-permute-start.4
  71.4 18.4 %collective-permute-done.3 = bf16[1024,640]{1,0:T(8,128)(2,1)S(1)} collective-permute-done((bf16[1024,640]{1,0:T(8,128)(2,1)S(1)}, bf16[1024,640]{1,0:T(8,128)(2,1)S(1)}, u32[]{:S(2)}, u32[]{:S(2)}) %collective-permute-start.3) | collective-permute-done | bytes 1310752 | tf_op jit(solution)/shard_map/ppermute | solution.py:181
  89.8 3.8 %collective-permute-done.4 = bf16[1024,640]{1,0:T(8,128)(2,1)} collective-permute-done((bf16[1024,640]{1,0:T(8,128)(2,1)S(1)}, bf16[1024,640]{1,0:T(8,128)(2,1)}, u32[]{:S(2)}, u32[]{:S(2)}) %collective-permute-start.4) | collective-permute-done | bytes 1310752 | tf_op jit(solution)/shard_map/ppermute | solution.py:183
  93.7 1.9 collective-permute-start.6
  95.6 6.2 %collective-permute-start.5 = (bf16[1024,640]{1,0:T(8,128)(2,1)S(1)}, bf16[1024,640]{1,0:T(8,128)(2,1)}, u32[]{:S(2)}, u32[]{:S(2)}) collective-permute-start(bf16[1024,640]{1,0:T(8,128)(2,1)S(1)} %collective-permute-done.3), channel_id=1, source_target_pairs={{0,448},{16,464},{32,480},{48,496},{64,0},{80,16},{96,32},{112,48}... | collective-permute-start | bytes 3932168 | tf_op jit(solution)/shard_map/ppermute | solution.py:181
  101.8 20.7 %collective-permute-done.6 = bf16[1024,640]{1,0:T(8,128)(2,1)} collective-permute-done((bf16[1024,640]{1,0:T(8,128)(2,1)}, bf16[1024,640]{1,0:T(8,128)(2,1)}, u32[]{:S(2)}, u32[]{:S(2)}) %collective-permute-start.6) | collective-permute-done | bytes 1310752 | tf_op jit(solution)/shard_map/ppermute | solution.py:183
  122.6 1.9 collective-permute-start.8
  124.6 0.0 copy-start.1
  124.7 2.4 %fusion.16 = f32[512,640]{1,0:T(8,128)S(1)} fusion(bf16[1024,640]{1,0:T(8,128)(2,1)S(1)} %bitcast.28, bf16[512,8192]{1,0:T(8,128)(2,1)} %all-gather.2.cloned.1.call-done, s32[]{:T(128)S(6)} %select_n.130), kind=kOutput, calls=%fused_computation.22 | convolution fusion | flops 671088640 | bytes 3670020 | tf_op jit(solution)/shard_map/dot_general | solution.py:173
  127.0 0.0 collective-permute-done.5
  127.0 6.4 %collective-permute-start.7 = (bf16[1024,640]{1,0:T(8,128)(2,1)}, bf16[1024,640]{1,0:T(8,128)(2,1)S(1)}, u32[]{:S(2)}, u32[]{:S(2)}) collective-permute-start(bf16[1024,640]{1,0:T(8,128)(2,1)} %collective-permute-done.5), channel_id=1, source_target_pairs={{0,448},{16,464},{32,480},{48,496},{64,0},{80,16},{96,32},{112,48}... | collective-permute-start | bytes 3932168 | tf_op jit(solution)/shard_map/ppermute | solution.py:181
  133.5 2.2 %convolution_add_fusion.3 = f32[512,640]{1,0:T(8,128)S(1)} fusion(f32[512,640]{1,0:T(8,128)S(1)} %fusion.16, bf16[1024,640]{1,0:T(8,128)(2,1)S(1)} %collective-permute-done.3, bf16[512,8192]{1,0:T(8,128)(2,1)} %all-gather.2.cloned.1.call-done, s32[]{:T(128)S(6)} %select_n.146), kind=kOutput, calls=%fused_computation.5 | convolution fusion | flops 671416320 | bytes 4980740 | tf_op jit(solution)/shard_map/dot_general | solution.py:173
  135.7 0.0 copy-done.1
  135.7 2.3 %fusion.12 = f32[512,640]{1,0:T(8,128)S(1)} fusion(bf16[1024,640]{1,0:T(8,128)(2,1)} %collective-permute-done.5, bf16[512,8192]{1,0:T(8,128)(2,1)S(1)} %copy-done.1, s32[]{:T(128)S(6)} %select_n.150), kind=kOutput, calls=%fused_computation.18 | convolution fusion | flops 671088640 | bytes 3670020 | tf_op jit(solution)/shard_map/dot_general | solution.py:173
  138.0 13.5 %collective-permute-done.8 = bf16[1024,640]{1,0:T(8,128)(2,1)} collective-permute-done((bf16[1024,640]{1,0:T(8,128)(2,1)}, bf16[1024,640]{1,0:T(8,128)(2,1)}, u32[]{:S(2)}, u32[]{:S(2)}) %collective-permute-start.8) | collective-permute-done | bytes 1310752 | tf_op jit(solution)/shard_map/ppermute | solution.py:183
  151.5 11.1 %collective-permute-start.9 = (bf16[1024,640]{1,0:T(8,128)(2,1)}, bf16[1024,640]{1,0:T(8,128)(2,1)S(1)}, u32[]{:S(2)}, u32[]{:S(2)}) collective-permute-start(bf16[1024,640]{1,0:T(8,128)(2,1)} %collective-permute-done.8), channel_id=1, source_target_pairs={{0,64},{16,80},{32,96},{48,112},{64,128},{80,144},{96,160},{112,17... | collective-permute-start | bytes 3932168 | tf_op jit(solution)/shard_map/ppermute | solution.py:183
  162.6 2.3 %fusion.10 = f32[512,640]{1,0:T(8,128)S(1)} fusion(bf16[1024,640]{1,0:T(8,128)(2,1)} %collective-permute-done.6, bf16[512,8192]{1,0:T(8,128)(2,1)S(1)} %copy-done.1, s32[]{:T(128)S(6)} %select_n.152), kind=kOutput, calls=%fused_computation.16 | convolution fusion | flops 671088640 | bytes 3670020 | tf_op jit(solution)/shard_map/dot_general | solution.py:173
  165.0 2.4 %fusion.2 = f32[512,640]{1,0:T(8,128)S(1)} fusion(f32[512,640]{1,0:T(8,128)S(1)} %fusion.10, f32[512,640]{1,0:T(8,128)S(1)} %fusion.12, f32[512,640]{1,0:T(8,128)S(1)} %convolution_add_fusion.3, bf16[1024,640]{1,0:T(8,128)(2,1)} %collective-permute-done.4, bf16[512,8192]{1,0:T(8,128)(2,1)S(1)} %copy-done.1, s32[]{:T(128)S(6)} %select_n.148), kind=kOutput, calls=%fused_computation.6 | convolution fusion | flops 672071680 | bytes 7602180 | tf_op jit(solution)/shard_map/dot_general | solution.py:173
  167.3 2.3 %fusion.7 = f32[512,640]{1,0:T(8,128)S(1)} fusion(bf16[1024,640]{1,0:T(8,128)(2,1)} %collective-permute-done.8, bf16[512,8192]{1,0:T(8,128)(2,1)S(1)} %copy-done.1, s32[]{:T(128)S(6)} %select_n.156), kind=kOutput, calls=%fused_computation.13 | convolution fusion | flops 671088640 | bytes 3670020 | tf_op jit(solution)/shard_map/dot_general | solution.py:173
  169.7 0.0 collective-permute-done.7
  169.7 1.0 fusion
  170.7 19.3 %collective-permute-done.9 = bf16[1024,640]{1,0:T(8,128)(2,1)S(1)} collective-permute-done((bf16[1024,640]{1,0:T(8,128)(2,1)}, bf16[1024,640]{1,0:T(8,128)(2,1)S(1)}, u32[]{:S(2)}, u32[]{:S(2)}) %collective-permute-start.9) | collective-permute-done | bytes 1310752 | tf_op jit(solution)/shard_map/ppermute | solution.py:183
  190.0 1.0 convolution_add_fusion.q_ref
  191.0 6.7 %collective-permute-start.10 = (bf16[512,128]{1,0:T(8,128)(2,1)S(1)}, bf16[512,128]{1,0:T(8,128)(2,1)S(1)}, u32[]{:S(2)}, u32[]{:S(2)}) collective-permute-start(bf16[512,128]{1,0:T(8,128)(2,1)S(1)} %slice.25), channel_id=1, source_target_pairs={{0,1},{1,0},{2,3},{3,2},{4,5},{5,4},{6,7},{7,6},{8,9},{9,8},{10,11... | collective-permute-start | bytes 393224 | tf_op jit(solution)/shard_map/ppermute | solution.py:218
  197.7 0.9 copy.7.row_seg_ref
  198.6 0.0 collective-permute-done.10
  198.6 0.7 broadcast_select_fusion
  199.3 6.1 %shard_map.64 = bf16[512,512]{1,0:T(8,128)(2,1)} custom-call(f32[512,640]{1,0:T(8,128)} %copy-done, bf16[512,128]{1,0:T(8,128)(2,1)} %get-tuple-element.22.k_ref, bf16[512,128]{1,0:T(8,128)(2,1)} %get-tuple-element.21.v_ref, f32[512,64]{1,0:T(8,128)} %get-tuple-element.17.cos_ref, f32[512,64]{1,0:T(8,128)} %get-tuple-element.18.sin_ref, ...), custom_call_target="tpu_custom_call" | custom-call | flops 538968064 | bytes 2097152 | tf_op jit(solution)/shard_map/pallas_call | solution.py:113
  (16 shorter events, 0.3 us)
Async XLA Ops:
  6.5 4.3 %copy-start.2 = (bf16[256,512]{1,0:T(8,128)(2,1)S(1)}, bf16[256,512]{1,0:T(8,128)(2,1)}, u32[]{:S(2)}) copy-start(bf16[256,512]{1,0:T(8,128)(2,1)} %param.9) | copy-start | bytes 786436
  6.5 87.1 %all-gather.2.cloned.1.call-start = ((), (), s32[]{:S(2)}) async-start(), calls=%async_computation | async-start | bytes 8912896 | tf_op jit(solution)/shard_map/all_gather | solution.py:213
  7.8 10.9 %copy-start.3 = (s32[512]{0:T(512)S(1)}, s32[512]{0:T(512)}, u32[]{:S(2)}) copy-start(s32[512]{0:T(512)} %param.7) | copy-start | bytes 6148
  10.9 22.8 %collective-permute-start = (bf16[256,640]{1,0:T(8,128)(2,1)S(1)}, bf16[256,640]{1,0:T(8,128)(2,1)S(1)}, u32[]{:S(2)}, u32[]{:S(2)}) collective-permute-start(bf16[256,640]{1,0:T(8,128)(2,1)S(1)} %pad_maximum_fusion), channel_id=1, source_target_pairs={{0,48},{16,0},{32,16},{48,32},{64,112},{80,64},{96,80},{112,96},{1... | collective-permute-start | bytes 983048 | tf_op jit(solution)/shard_map/ppermute | solution.py:151
  16.8 15.0 %collective-permute-start.1 = (bf16[256,640]{1,0:T(8,128)(2,1)S(1)}, bf16[256,640]{1,0:T(8,128)(2,1)S(1)}, u32[]{:S(2)}, u32[]{:S(2)}) collective-permute-start(bf16[256,640]{1,0:T(8,128)(2,1)S(1)} %pad_maximum_fusion), channel_id=1, source_target_pairs={{0,16},{16,32},{32,48},{48,0},{64,80},{80,96},{96,112},{112,64},{1... | collective-permute-start | bytes 983048 | tf_op jit(solution)/shard_map/ppermute | solution.py:153
  31.7 27.1 %collective-permute-start.2 = (bf16[256,640]{1,0:T(8,128)(2,1)S(1)}, bf16[256,640]{1,0:T(8,128)(2,1)S(1)}, u32[]{:S(2)}, u32[]{:S(2)}) collective-permute-start(bf16[256,640]{1,0:T(8,128)(2,1)S(1)} %collective-permute-done.1), channel_id=1, source_target_pairs={{0,16},{16,32},{32,48},{48,0},{64,80},{80,96},{96,112},{112,64},{1... | collective-permute-start | bytes 983048 | tf_op jit(solution)/shard_map/ppermute | solution.py:153
  58.9 30.9 %collective-permute-start.3 = (bf16[1024,640]{1,0:T(8,128)(2,1)S(1)}, bf16[1024,640]{1,0:T(8,128)(2,1)S(1)}, u32[]{:S(2)}, u32[]{:S(2)}) collective-permute-start(bf16[1024,640]{1,0:T(8,128)(2,1)S(1)} %bitcast.26), channel_id=1, source_target_pairs={{0,448},{16,464},{32,480},{48,496},{64,0},{80,16},{96,32},{112,48}... | collective-permute-start | bytes 3932168 | tf_op jit(solution)/shard_map/ppermute | solution.py:181
  69.5 24.2 %collective-permute-start.4 = (bf16[1024,640]{1,0:T(8,128)(2,1)S(1)}, bf16[1024,640]{1,0:T(8,128)(2,1)}, u32[]{:S(2)}, u32[]{:S(2)}) collective-permute-start(bf16[1024,640]{1,0:T(8,128)(2,1)S(1)} %bitcast.27), channel_id=1, source_target_pairs={{0,64},{16,80},{32,96},{48,112},{64,128},{80,144},{96,160},{112,17... | collective-permute-start | bytes 3932168 | tf_op jit(solution)/shard_map/ppermute | solution.py:183
  93.7 28.9 %collective-permute-start.6 = (bf16[1024,640]{1,0:T(8,128)(2,1)}, bf16[1024,640]{1,0:T(8,128)(2,1)}, u32[]{:S(2)}, u32[]{:S(2)}) collective-permute-start(bf16[1024,640]{1,0:T(8,128)(2,1)} %collective-permute-done.4), channel_id=1, source_target_pairs={{0,64},{16,80},{32,96},{48,112},{64,128},{80,144},{96,160},{112,17... | collective-permute-start | bytes 3932168 | tf_op jit(solution)/shard_map/ppermute | solution.py:183
  95.6 31.4 %collective-permute-start.5 = (bf16[1024,640]{1,0:T(8,128)(2,1)S(1)}, bf16[1024,640]{1,0:T(8,128)(2,1)}, u32[]{:S(2)}, u32[]{:S(2)}) collective-permute-start(bf16[1024,640]{1,0:T(8,128)(2,1)S(1)} %collective-permute-done.3), channel_id=1, source_target_pairs={{0,448},{16,464},{32,480},{48,496},{64,0},{80,16},{96,32},{112,48}... | collective-permute-start | bytes 3932168 | tf_op jit(solution)/shard_map/ppermute | solution.py:181
  122.6 29.0 %collective-permute-start.8 = (bf16[1024,640]{1,0:T(8,128)(2,1)}, bf16[1024,640]{1,0:T(8,128)(2,1)}, u32[]{:S(2)}, u32[]{:S(2)}) collective-permute-start(bf16[1024,640]{1,0:T(8,128)(2,1)} %collective-permute-done.6), channel_id=1, source_target_pairs={{0,64},{16,80},{32,96},{48,112},{64,128},{80,144},{96,160},{112,17... | collective-permute-start | bytes 3932168 | tf_op jit(solution)/shard_map/ppermute | solution.py:183
  124.6 11.1 %copy-start.1 = (bf16[512,8192]{1,0:T(8,128)(2,1)S(1)}, bf16[512,8192]{1,0:T(8,128)(2,1)}, u32[]{:S(2)}) copy-start(bf16[512,8192]{1,0:T(8,128)(2,1)} %all-gather.2.cloned.1.call-done) | copy-start | bytes 25165828
  127.0 42.6 %collective-permute-start.7 = (bf16[1024,640]{1,0:T(8,128)(2,1)}, bf16[1024,640]{1,0:T(8,128)(2,1)S(1)}, u32[]{:S(2)}, u32[]{:S(2)}) collective-permute-start(bf16[1024,640]{1,0:T(8,128)(2,1)} %collective-permute-done.5), channel_id=1, source_target_pairs={{0,448},{16,464},{32,480},{48,496},{64,0},{80,16},{96,32},{112,48}... | collective-permute-start | bytes 3932168 | tf_op jit(solution)/shard_map/ppermute | solution.py:181
  151.5 38.5 %collective-permute-start.9 = (bf16[1024,640]{1,0:T(8,128)(2,1)}, bf16[1024,640]{1,0:T(8,128)(2,1)S(1)}, u32[]{:S(2)}, u32[]{:S(2)}) collective-permute-start(bf16[1024,640]{1,0:T(8,128)(2,1)} %collective-permute-done.8), channel_id=1, source_target_pairs={{0,64},{16,80},{32,96},{48,112},{64,128},{80,144},{96,160},{112,17... | collective-permute-start | bytes 3932168 | tf_op jit(solution)/shard_map/ppermute | solution.py:183
  191.0 8.3 %copy-start = (f32[512,640]{1,0:T(8,128)}, f32[512,640]{1,0:T(8,128)S(1)}, u32[]{:S(2)}) copy-start(f32[512,640]{1,0:T(8,128)S(1)} %convolution_add_fusion.q_ref) | copy-start | bytes 3932164
  191.0 7.6 %collective-permute-start.10 = (bf16[512,128]{1,0:T(8,128)(2,1)S(1)}, bf16[512,128]{1,0:T(8,128)(2,1)S(1)}, u32[]{:S(2)}, u32[]{:S(2)}) collective-permute-start(bf16[512,128]{1,0:T(8,128)(2,1)S(1)} %slice.25), channel_id=1, source_target_pairs={{0,1},{1,0},{2,3},{3,2},{4,5},{5,4},{6,7},{7,6},{8,9},{9,8},{10,11... | collective-permute-start | bytes 393224 | tf_op jit(solution)/shard_map/ppermute | solution.py:218
Sparse Core Ops, SparseCore 0:
  10.0 78.1 all-gather.1

commit v11 on v10

--- a/solution.py
+++ b/solution.py
@@ -210,7 +210,9 @@
     near, cosine, sine, row_seg, col_seg = lax.optimization_barrier(
         (near, cosine, sine, row_seg, col_seg)
     )
-    gathered = lax.all_gather(normed, "weight", axis=0, tiled=True)
+    n_weight = lax.psum(1, "weight")
+    repeated = jnp.broadcast_to(normed[None], (n_weight,) + normed.shape)
+    gathered = lax.all_to_all(repeated, "weight", 0, 0, tiled=True).reshape(-1, normed.shape[1])
     pack_rows = gathered.shape[0]
     projected = ring_matmul(gathered, near, "batch", y_hi, Z_CHIPS)
     own_rows = projected[:, query_cols:].astype(jnp.bfloat16)

time: 215 us -> 294 us (1.37)
  waiting for transfers between devices: 110 us -> 195 us
  between operations: 14.6 us -> 1.16 us
  local copies, waits for them, and re-layouts: 1.86 us -> 6.06 us
  matrix products: 15.9 us -> 19.5 us
    ppermute x2, waiting for transfers between devices: 34.2 us -> 109 us  [ring_gather(): from_left = lax.ppermute(from_left, axis, perm=moved(1))]
    all_to_all x0 -> x1, starting transfers between devices: none -> 10.8 us  [per_device(): lax.all_to_all(repeated, 'weight', 0, 0, tiled=True)]
    ppermute x4, starting transfers between devices: 16.9 us -> 7.65 us  [ring_matmul(): from_left = lax.ppermute(from_left, axis, perm=moved(1))]
    ppermute x3, waiting for transfers between devices: 18.4 us -> 24.4 us  [ring_matmul(): from_right = lax.ppermute(from_right, axis, perm=moved(-1))]
    ppermute x2, starting transfers between devices: 3.83 us -> 9.26 us  [ring_gather(): from_left = lax.ppermute(from_left, axis, perm=moved(1))]
    ppermute x4, waiting for transfers between devices: 57.4 us -> 62 us  [ring_matmul(): from_left = lax.ppermute(from_left, axis, perm=moved(1))]
    broadcast_in_dim x0 -> x1, local copies, waits for them, and re-layouts: none -> 4.24 us  [per_device(): repeated = jnp.broadcast_to(normed[None], (n_weight,) + normed.shape)]
    ppermute x3, starting transfers between devices: 23.3 us -> 19.2 us  [ring_matmul(): from_right = lax.ppermute(from_right, axis, perm=moved(-1))]
  transfers between devices with their start and end apart: 12 -> 12, of which waited for: 7 -> 7; matrix products, arithmetic and copies ran while one was open for 9% -> 8% of each run, Pallas kernels for 0% -> 0%
where the time goes in v11:
time: 294 us; the launch traced here: 291 us
  waiting for transfers between devices  195 us (66%)
  starting transfers between devices  56.6 us (19%)
  matrix products  19.5 us (7%)
  other arithmetic  6.5 us (2%)
  Pallas kernels  6.07 us (2%)
  local copies, waits for them, and re-layouts  6.06 us (2%)
    ppermute x2, waiting for transfers between devices, ring_gather(): from_left = lax.ppermute(from_left, axis, perm=moved(1))  109 us
    ppermute x4, waiting for transfers between devices, ring_matmul(): from_left = lax.ppermute(from_left, axis, perm=moved(1))  62 us
    ppermute x3, waiting for transfers between devices, ring_matmul(): from_right = lax.ppermute(from_right, axis, perm=moved(-1))  24.4 us
    dot_general x8, matrix products, product(): return jnp.dot(lhs, part, preferred_element_type=jnp.float32)  19.5 us
    ppermute x3, starting transfers between devices, ring_matmul(): from_right = lax.ppermute(from_right, axis, perm=moved(-1))  19.2 us
    all_to_all x1, starting transfers between devices, per_device(): lax.all_to_all(repeated, 'weight', 0, 0, tiled=True)  10.8 us
    ppermute x2, starting transfers between devices, ring_gather(): from_left = lax.ppermute(from_left, axis, perm=moved(1))  9.26 us
    ppermute x1, starting transfers between devices, per_device(): other_rows = lax.ppermute(own_rows, 'weight', perm=partner)  7.82 us
  transfers between devices with their start and end apart: 12, of which 7 were waited for; matrix products, arithmetic and copies ran while one was open for 8% of the time, Pallas kernels for 0%

profile of v11, /device:TPU:7, one launch (start us, length us, event | category | flops | bytes accessed | tf_op | source)
XLA Modules:
  0.0 290.8 jit_solution(3402594805575509846)
XLA Ops:
  0.0 1.2 fusion.3
  1.3 1.2 fusion.5
  2.5 4.2 %broadcast_in_dim.36 = bf16[16,32,8192]{2,1,0:T(8,128)(2,1)} broadcast(bf16[32,8192]{1,0:T(8,128)(2,1)S(1)} %fusion.5), dimensions={1,2} | broadcast | bytes 8912896 | tf_op jit(solution)/shard_map/broadcast_in_dim | solution.py:214
  6.8 10.8 %all-to-all-start = ((bf16[16,32,8192]{2,1,0:T(8,128)(2,1)}), bf16[16,32,8192]{2,1,0:T(8,128)(2,1)}, u32[]{:S(2)}, u32[]{:S(2)}) async-start(bf16[16,32,8192]{2,1,0:T(8,128)(2,1)} %broadcast_in_dim.36), calls=%async_computation | async-start | bytes 16777216 | tf_op jit(solution)/shard_map/all_to_all | solution.py:215
  17.6 0.9 dynamic-slice_select_fusion
  18.5 0.0 copy-done.1
  18.5 1.9 collective-permute-start
  20.5 4.3 %collective-permute-start.1 = (bf16[256,640]{1,0:T(8,128)(2,1)S(1)}, bf16[256,640]{1,0:T(8,128)(2,1)S(1)}, u32[]{:S(2)}, u32[]{:S(2)}) collective-permute-start(bf16[256,640]{1,0:T(8,128)(2,1)S(1)} %pad_maximum_fusion), channel_id=1, source_target_pairs={{0,16},{16,32},{32,48},{48,0},{64,80},{80,96},{96,112},{112,64},{1... | collective-permute-start | bytes 983048 | tf_op jit(solution)/shard_map/ppermute | solution.py:153
  24.8 0.5 slice.17
  26.0 0.1 select_bitcast_fusion
  26.1 0.3 reduce-window.9
  26.4 0.1 slice.19
  26.5 0.1 slice_reduce_fusion
  26.6 0.1 broadcast_in_dim.37
  26.8 0.1 fusion.26
  26.9 1.8 multiply_sine_fusion
  28.7 101.3 %collective-permute-done.1 = bf16[256,640]{1,0:T(8,128)(2,1)S(1)} collective-permute-done((bf16[256,640]{1,0:T(8,128)(2,1)S(1)}, bf16[256,640]{1,0:T(8,128)(2,1)S(1)}, u32[]{:S(2)}, u32[]{:S(2)}) %collective-permute-start.1) | collective-permute-done | bytes 327712 | tf_op jit(solution)/shard_map/ppermute | solution.py:153
  130.0 5.0 %collective-permute-start.2 = (bf16[256,640]{1,0:T(8,128)(2,1)S(1)}, bf16[256,640]{1,0:T(8,128)(2,1)S(1)}, u32[]{:S(2)}, u32[]{:S(2)}) collective-permute-start(bf16[256,640]{1,0:T(8,128)(2,1)S(1)} %collective-permute-done.1), channel_id=1, source_target_pairs={{0,16},{16,32},{32,48},{48,0},{64,80},{80,96},{96,112},{112,64},{1... | collective-permute-start | bytes 983048 | tf_op jit(solution)/shard_map/ppermute | solution.py:153
  135.0 0.0 collective-permute-done
  135.1 7.2 %collective-permute-done.2 = bf16[256,640]{1,0:T(8,128)(2,1)S(1)} collective-permute-done((bf16[256,640]{1,0:T(8,128)(2,1)S(1)}, bf16[256,640]{1,0:T(8,128)(2,1)S(1)}, u32[]{:S(2)}, u32[]{:S(2)}) %collective-permute-start.2) | collective-permute-done | bytes 327712 | tf_op jit(solution)/shard_map/ppermute | solution.py:153
  142.3 10.0 %collective-permute-start.3 = (bf16[1024,640]{1,0:T(8,128)(2,1)S(1)}, bf16[1024,640]{1,0:T(8,128)(2,1)S(1)}, u32[]{:S(2)}, u32[]{:S(2)}) collective-permute-start(bf16[1024,640]{1,0:T(8,128)(2,1)S(1)} %bitcast.27), channel_id=1, source_target_pairs={{0,448},{16,464},{32,480},{48,496},{64,0},{80,16},{96,32},{112,48}... | collective-permute-start | bytes 3932168 | tf_op jit(solution)/shard_map/ppermute | solution.py:181
  152.4 1.9 collective-permute-start.4
  154.3 24.3 %collective-permute-done.3 = bf16[1024,640]{1,0:T(8,128)(2,1)S(1)} collective-permute-done((bf16[1024,640]{1,0:T(8,128)(2,1)S(1)}, bf16[1024,640]{1,0:T(8,128)(2,1)S(1)}, u32[]{:S(2)}, u32[]{:S(2)}) %collective-permute-start.3) | collective-permute-done | bytes 1310752 | tf_op jit(solution)/shard_map/ppermute | solution.py:181
  178.6 5.2 %collective-permute-done.4 = bf16[1024,640]{1,0:T(8,128)(2,1)} collective-permute-done((bf16[1024,640]{1,0:T(8,128)(2,1)S(1)}, bf16[1024,640]{1,0:T(8,128)(2,1)}, u32[]{:S(2)}, u32[]{:S(2)}) %collective-permute-start.4) | collective-permute-done | bytes 1310752 | tf_op jit(solution)/shard_map/ppermute | solution.py:183
  183.8 0.0 all-to-all-done
  183.8 1.9 collective-permute-start.6
  185.7 4.6 %collective-permute-start.5 = (bf16[1024,640]{1,0:T(8,128)(2,1)S(1)}, bf16[1024,640]{1,0:T(8,128)(2,1)}, u32[]{:S(2)}, u32[]{:S(2)}) collective-permute-start(bf16[1024,640]{1,0:T(8,128)(2,1)S(1)} %collective-permute-done.3), channel_id=1, source_target_pairs={{0,448},{16,464},{32,480},{48,496},{64,0},{80,16},{96,32},{112,48}... | collective-permute-start | bytes 3932168 | tf_op jit(solution)/shard_map/ppermute | solution.py:181
  190.3 24.2 %collective-permute-done.6 = bf16[1024,640]{1,0:T(8,128)(2,1)} collective-permute-done((bf16[1024,640]{1,0:T(8,128)(2,1)}, bf16[1024,640]{1,0:T(8,128)(2,1)}, u32[]{:S(2)}, u32[]{:S(2)}) %collective-permute-start.6) | collective-permute-done | bytes 1310752 | tf_op jit(solution)/shard_map/ppermute | solution.py:183
  214.5 1.9 collective-permute-start.8
  216.6 2.2 fusion.16
  218.8 0.0 collective-permute-done.5
  218.8 4.6 %collective-permute-start.7 = (bf16[1024,640]{1,0:T(8,128)(2,1)}, bf16[1024,640]{1,0:T(8,128)(2,1)S(1)}, u32[]{:S(2)}, u32[]{:S(2)}) collective-permute-start(bf16[1024,640]{1,0:T(8,128)(2,1)} %collective-permute-done.5), channel_id=1, source_target_pairs={{0,448},{16,464},{32,480},{48,496},{64,0},{80,16},{96,32},{112,48}... | collective-permute-start | bytes 3932168 | tf_op jit(solution)/shard_map/ppermute | solution.py:181
  223.4 2.2 convolution_add_fusion.3
  225.6 2.6 fusion.12
  228.3 16.0 %collective-permute-done.8 = bf16[1024,640]{1,0:T(8,128)(2,1)} collective-permute-done((bf16[1024,640]{1,0:T(8,128)(2,1)}, bf16[1024,640]{1,0:T(8,128)(2,1)}, u32[]{:S(2)}, u32[]{:S(2)}) %collective-permute-start.8) | collective-permute-done | bytes 1310752 | tf_op jit(solution)/shard_map/ppermute | solution.py:183
  244.3 1.9 collective-permute-start.9
  246.2 2.6 fusion.10
  248.8 2.7 fusion.2
  251.5 2.6 fusion.7
  254.2 0.0 collective-permute-done.7
  254.2 2.2 fusion
  256.4 16.6 %collective-permute-done.9 = bf16[1024,640]{1,0:T(8,128)(2,1)S(1)} collective-permute-done((bf16[1024,640]{1,0:T(8,128)(2,1)}, bf16[1024,640]{1,0:T(8,128)(2,1)S(1)}, u32[]{:S(2)}, u32[]{:S(2)}) %collective-permute-start.9) | collective-permute-done | bytes 1310752 | tf_op jit(solution)/shard_map/ppermute | solution.py:183
  273.0 2.2 convolution_add_fusion.q_ref
  275.3 7.8 %collective-permute-start.10 = (bf16[512,128]{1,0:T(8,128)(2,1)S(1)}, bf16[512,128]{1,0:T(8,128)(2,1)S(1)}, u32[]{:S(2)}, u32[]{:S(2)}) collective-permute-start(bf16[512,128]{1,0:T(8,128)(2,1)S(1)} %slice.25), channel_id=1, source_target_pairs={{0,1},{1,0},{2,3},{3,2},{4,5},{5,4},{6,7},{7,6},{8,9},{9,8},{10,11... | collective-permute-start | bytes 393224 | tf_op jit(solution)/shard_map/ppermute | solution.py:220
  283.1 0.9 copy.7.row_seg_ref
  284.0 0.0 collective-permute-done.10
  284.0 0.7 broadcast_select_fusion
  284.7 6.1 %shard_map.64 = bf16[512,512]{1,0:T(8,128)(2,1)} custom-call(f32[512,640]{1,0:T(8,128)} %copy-done, bf16[512,128]{1,0:T(8,128)(2,1)} %get-tuple-element.22.k_ref, bf16[512,128]{1,0:T(8,128)(2,1)} %get-tuple-element.21.v_ref, f32[512,64]{1,0:T(8,128)} %get-tuple-element.17.cos_ref, f32[512,64]{1,0:T(8,128)} %get-tuple-element.18.sin_ref, ...), custom_call_target="tpu_custom_call" | custom-call | flops 538968064 | bytes 2097152 | tf_op jit(solution)/shard_map/pallas_call | solution.py:113
  (14 shorter events, 0.3 us)
Async XLA Ops:
  6.7 11.7 %copy-start.1 = (bf16[256,512]{1,0:T(8,128)(2,1)S(1)}, bf16[256,512]{1,0:T(8,128)(2,1)}, u32[]{:S(2)}) copy-start(bf16[256,512]{1,0:T(8,128)(2,1)} %param.9) | copy-start | bytes 786436
  6.7 18.1 %copy-start.2 = (s32[512]{0:T(512)S(1)}, s32[512]{0:T(512)}, u32[]{:S(2)}) copy-start(s32[512]{0:T(512)} %param.7) | copy-start | bytes 6148
  6.8 177.0 %all-to-all-start = ((bf16[16,32,8192]{2,1,0:T(8,128)(2,1)}), bf16[16,32,8192]{2,1,0:T(8,128)(2,1)}, u32[]{:S(2)}, u32[]{:S(2)}) async-start(bf16[16,32,8192]{2,1,0:T(8,128)(2,1)} %broadcast_in_dim.36), calls=%async_computation | async-start | bytes 16777216 | tf_op jit(solution)/shard_map/all_to_all | solution.py:215
  18.5 116.4 %collective-permute-start = (bf16[256,640]{1,0:T(8,128)(2,1)S(1)}, bf16[256,640]{1,0:T(8,128)(2,1)S(1)}, u32[]{:S(2)}, u32[]{:S(2)}) collective-permute-start(bf16[256,640]{1,0:T(8,128)(2,1)S(1)} %pad_maximum_fusion), channel_id=1, source_target_pairs={{0,48},{16,0},{32,16},{48,32},{64,112},{80,64},{96,80},{112,96},{1... | collective-permute-start | bytes 983048 | tf_op jit(solution)/shard_map/ppermute | solution.py:151
  20.5 109.5 %collective-permute-start.1 = (bf16[256,640]{1,0:T(8,128)(2,1)S(1)}, bf16[256,640]{1,0:T(8,128)(2,1)S(1)}, u32[]{:S(2)}, u32[]{:S(2)}) collective-permute-start(bf16[256,640]{1,0:T(8,128)(2,1)S(1)} %pad_maximum_fusion), channel_id=1, source_target_pairs={{0,16},{16,32},{32,48},{48,0},{64,80},{80,96},{96,112},{112,64},{1... | collective-permute-start | bytes 983048 | tf_op jit(solution)/shard_map/ppermute | solution.py:153
  130.0 12.3 %collective-permute-start.2 = (bf16[256,640]{1,0:T(8,128)(2,1)S(1)}, bf16[256,640]{1,0:T(8,128)(2,1)S(1)}, u32[]{:S(2)}, u32[]{:S(2)}) collective-permute-start(bf16[256,640]{1,0:T(8,128)(2,1)S(1)} %collective-permute-done.1), channel_id=1, source_target_pairs={{0,16},{16,32},{32,48},{48,0},{64,80},{80,96},{96,112},{112,64},{1... | collective-permute-start | bytes 983048 | tf_op jit(solution)/shard_map/ppermute | solution.py:153
  142.3 36.3 %collective-permute-start.3 = (bf16[1024,640]{1,0:T(8,128)(2,1)S(1)}, bf16[1024,640]{1,0:T(8,128)(2,1)S(1)}, u32[]{:S(2)}, u32[]{:S(2)}) collective-permute-start(bf16[1024,640]{1,0:T(8,128)(2,1)S(1)} %bitcast.27), channel_id=1, source_target_pairs={{0,448},{16,464},{32,480},{48,496},{64,0},{80,16},{96,32},{112,48}... | collective-permute-start | bytes 3932168 | tf_op jit(solution)/shard_map/ppermute | solution.py:181
  152.4 31.4 %collective-permute-start.4 = (bf16[1024,640]{1,0:T(8,128)(2,1)S(1)}, bf16[1024,640]{1,0:T(8,128)(2,1)}, u32[]{:S(2)}, u32[]{:S(2)}) collective-permute-start(bf16[1024,640]{1,0:T(8,128)(2,1)S(1)} %bitcast.28), channel_id=1, source_target_pairs={{0,64},{16,80},{32,96},{48,112},{64,128},{80,144},{96,160},{112,17... | collective-permute-start | bytes 3932168 | tf_op jit(solution)/shard_map/ppermute | solution.py:183
  183.8 30.7 %collective-permute-start.6 = (bf16[1024,640]{1,0:T(8,128)(2,1)}, bf16[1024,640]{1,0:T(8,128)(2,1)}, u32[]{:S(2)}, u32[]{:S(2)}) collective-permute-start(bf16[1024,640]{1,0:T(8,128)(2,1)} %collective-permute-done.4), channel_id=1, source_target_pairs={{0,64},{16,80},{32,96},{48,112},{64,128},{80,144},{96,160},{112,17... | collective-permute-start | bytes 3932168 | tf_op jit(solution)/shard_map/ppermute | solution.py:183
  185.7 33.1 %collective-permute-start.5 = (bf16[1024,640]{1,0:T(8,128)(2,1)S(1)}, bf16[1024,640]{1,0:T(8,128)(2,1)}, u32[]{:S(2)}, u32[]{:S(2)}) collective-permute-start(bf16[1024,640]{1,0:T(8,128)(2,1)S(1)} %collective-permute-done.3), channel_id=1, source_target_pairs={{0,448},{16,464},{32,480},{48,496},{64,0},{80,16},{96,32},{112,48}... | collective-permute-start | bytes 3932168 | tf_op jit(solution)/shard_map/ppermute | solution.py:181
  214.5 29.8 %collective-permute-start.8 = (bf16[1024,640]{1,0:T(8,128)(2,1)}, bf16[1024,640]{1,0:T(8,128)(2,1)}, u32[]{:S(2)}, u32[]{:S(2)}) collective-permute-start(bf16[1024,640]{1,0:T(8,128)(2,1)} %collective-permute-done.6), channel_id=1, source_target_pairs={{0,64},{16,80},{32,96},{48,112},{64,128},{80,144},{96,160},{112,17... | collective-permute-start | bytes 3932168 | tf_op jit(solution)/shard_map/ppermute | solution.py:183
  218.8 35.4 %collective-permute-start.7 = (bf16[1024,640]{1,0:T(8,128)(2,1)}, bf16[1024,640]{1,0:T(8,128)(2,1)S(1)}, u32[]{:S(2)}, u32[]{:S(2)}) collective-permute-start(bf16[1024,640]{1,0:T(8,128)(2,1)} %collective-permute-done.5), channel_id=1, source_target_pairs={{0,448},{16,464},{32,480},{48,496},{64,0},{80,16},{96,32},{112,48}... | collective-permute-start | bytes 3932168 | tf_op jit(solution)/shard_map/ppermute | solution.py:181
  244.3 28.8 %collective-permute-start.9 = (bf16[1024,640]{1,0:T(8,128)(2,1)}, bf16[1024,640]{1,0:T(8,128)(2,1)S(1)}, u32[]{:S(2)}, u32[]{:S(2)}) collective-permute-start(bf16[1024,640]{1,0:T(8,128)(2,1)} %collective-permute-done.8), channel_id=1, source_target_pairs={{0,64},{16,80},{32,96},{48,112},{64,128},{80,144},{96,160},{112,17... | collective-permute-start | bytes 3932168 | tf_op jit(solution)/shard_map/ppermute | solution.py:183
  275.3 9.4 %copy-start = (f32[512,640]{1,0:T(8,128)}, f32[512,640]{1,0:T(8,128)S(1)}, u32[]{:S(2)}) copy-start(f32[512,640]{1,0:T(8,128)S(1)} %convolution_add_fusion.q_ref) | copy-start | bytes 3932164
  275.3 8.7 %collective-permute-start.10 = (bf16[512,128]{1,0:T(8,128)(2,1)S(1)}, bf16[512,128]{1,0:T(8,128)(2,1)S(1)}, u32[]{:S(2)}, u32[]{:S(2)}) collective-permute-start(bf16[512,128]{1,0:T(8,128)(2,1)S(1)} %slice.25), channel_id=1, source_target_pairs={{0,1},{1,0},{2,3},{3,2},{4,5},{5,4},{6,7},{7,6},{8,9},{9,8},{10,11... | collective-permute-start | bytes 393224 | tf_op jit(solution)/shard_map/ppermute | solution.py:220

commit v12 on v10

--- a/solution.py
+++ b/solution.py
@@ -150,9 +150,22 @@
         if step < count - step:
             from_right = lax.ppermute(from_right, axis, perm=moved(-1))
             out = lax.dynamic_update_index_in_dim(out, from_right, (here + step) % count, 0)
-        from_left = lax.ppermute(from_left, axis, perm=moved(1))
+            from_left = lax.ppermute(from_left, axis, perm=moved(1))
+        else:
+            cut = lane_cut(block.shape[-1])
+            from_left = jnp.concatenate(
+                [
+                    lax.ppermute(from_left[..., :cut], axis, perm=moved(1)),
+                    lax.ppermute(from_right[..., cut:], axis, perm=moved(-1)),
+                ],
+                axis=-1,
+            )
         out = lax.dynamic_update_index_in_dim(out, from_left, (here - step) % count, 0)
     return out
+
+
+def lane_cut(width):
+    return min(width, (width // 2 + 127) // 128 * 128)
 
 
 def ring_matmul(rows, block, axis, stride, count):
@@ -180,7 +193,16 @@
         if step < count - step:
             from_right = lax.ppermute(from_right, axis, perm=moved(-1))
             total = total + product(from_right, (here + step) % count)
-        from_left = lax.ppermute(from_left, axis, perm=moved(1))
+            from_left = lax.ppermute(from_left, axis, perm=moved(1))
+        else:
+            cut = lane_cut(block.shape[-1])
+            from_left = jnp.concatenate(
+                [
+                    lax.ppermute(from_left[..., :cut], axis, perm=moved(1)),
+                    lax.ppermute(from_right[..., cut:], axis, perm=moved(-1)),
+                ],
+                axis=-1,
+            )
         total = total + product(from_left, (here - step) % count)
     return total
 

time: 215 us -> 200 us (0.930)
  the two profiles are of different devices: /device:TPU:7 before, /device:TPU:63 now
where the time goes in v12:
time: 200 us
  waiting for transfers between devices  100 us (50%)
  starting transfers between devices  52.9 us (26%)
  matrix products  15.4 us (8%)
  between operations  14.6 us (7%)
  other arithmetic  7.41 us (4%)
  Pallas kernels  6.06 us (3%)
  local copies, waits for them, and re-layouts  3.14 us (2%)
    ppermute x3, waiting for transfers between devices, ring_matmul(): from_left = lax.ppermute(from_left, axis, perm=moved(1))  47.6 us
    ppermute x3, waiting for transfers between devices, ring_matmul(): from_right = lax.ppermute(from_right, axis, perm=moved(-1))  23.7 us
    ppermute x3, starting transfers between devices, ring_matmul(): from_right = lax.ppermute(from_right, axis, perm=moved(-1))  19.8 us
    dot_general x8, matrix products, product(): return jnp.dot(lhs, part, preferred_element_type=jnp.float32)  15.4 us
    ppermute x1, waiting for transfers between devices, ring_gather(): from_left = lax.ppermute(from_left, axis, perm=moved(1))  11 us
    ppermute x3, starting transfers between devices, ring_matmul(): from_left = lax.ppermute(from_left, axis, perm=moved(1))  7.82 us
    ppermute x1, waiting for transfers between devices, ring_gather(): lax.ppermute(from_right[..., cut:], axis, perm=moved(-1))  6.95 us
    pallas_call x1, Pallas kernels, attention_kernel_call(): pl.pallas_call(functools.partial(attention_kernel, heads), out_shape=jax....  6.06 us
  transfers between devices with their start and end apart: 14, of which 9 were waited for; matrix products, arithmetic and copies ran while one was open for 10% of the time, Pallas kernels for 0%

profile of v12, /device:TPU:63, one launch (start us, length us, event | category | flops | bytes accessed | tf_op | source)
XLA Modules:
  0.0 199.5 jit_solution(9148848021669281225)
XLA Ops:
  6.5 1.3 fusion.8
  7.8 0.0 copy-start.6
  7.9 2.0 %fusion.10 = bf16[32,8192]{1,0:T(8,128)(2,1)} fusion(bf16[32,8192]{1,0:T(8,128)(2,1)} %param.6, f32[8192]{0:T(1024)} %param.8, f32[32]{0:T(128)S(1)} %add_rsqrt_fusion), kind=kLoop, calls=%fused_computation.15 | loop fusion | flops 1048576 | bytes 1081472 | tf_op jit(solution)/shard_map/convert_element_type | solution.py:224
  9.9 0.0 all-gather.2.cloned.1.call-update
  9.9 0.9 dynamic-slice_select_fusion
  10.9 3.8 %collective-permute-start = (bf16[256,640]{1,0:T(8,128)(2,1)S(1)}, bf16[256,640]{1,0:T(8,128)(2,1)S(1)}, u32[]{:S(2)}, u32[]{:S(2)}) collective-permute-start(bf16[256,640]{1,0:T(8,128)(2,1)S(1)} %pad_maximum_fusion), channel_id=1, source_target_pairs={{0,48},{16,0},{32,16},{48,32},{64,112},{80,64},{96,80},{112,96},{1... | collective-permute-start | bytes 983048 | tf_op jit(solution)/shard_map/ppermute | solution.py:151
  14.7 3.6 %collective-permute-start.1 = (bf16[256,640]{1,0:T(8,128)(2,1)S(1)}, bf16[256,640]{1,0:T(8,128)(2,1)S(1)}, u32[]{:S(2)}, u32[]{:S(2)}) collective-permute-start(bf16[256,640]{1,0:T(8,128)(2,1)S(1)} %pad_maximum_fusion), channel_id=1, source_target_pairs={{0,16},{16,32},{32,48},{48,0},{64,80},{80,96},{96,112},{112,64},{1... | collective-permute-start | bytes 983048 | tf_op jit(solution)/shard_map/ppermute | solution.py:153
  18.4 0.6 slice.31
  19.6 0.1 select_bitcast_fusion
  19.7 0.3 reduce-window.9
  20.0 0.1 slice.33
  20.1 0.1 slice_reduce_fusion
  20.2 0.1 broadcast_in_dim.30
  20.4 0.1 fusion.32
  20.5 1.8 multiply_sine_fusion
  22.3 11.0 %collective-permute-done.1 = bf16[256,640]{1,0:T(8,128)(2,1)S(1)} collective-permute-done((bf16[256,640]{1,0:T(8,128)(2,1)S(1)}, bf16[256,640]{1,0:T(8,128)(2,1)S(1)}, u32[]{:S(2)}, u32[]{:S(2)}) %collective-permute-start.1) | collective-permute-done | bytes 327712 | tf_op jit(solution)/shard_map/ppermute | solution.py:153
  33.3 4.4 %collective-permute-start.2 = (bf16[256,384]{1,0:T(8,128)(2,1)S(1)}, bf16[256,384]{1,0:T(8,128)(2,1)S(1)}, u32[]{:S(2)}, u32[]{:S(2)}) collective-permute-start(bf16[256,384]{1,0:T(8,128)(2,1)S(1)} %slice.38), channel_id=1, source_target_pairs={{0,16},{16,32},{32,48},{48,0},{64,80},{80,96},{96,112},{112,64},{1... | collective-permute-start | bytes 589832 | tf_op jit(solution)/shard_map/ppermute | solution.py:158
  37.7 2.3 %collective-permute-start.3 = (bf16[256,256]{1,0:T(8,128)(2,1)S(1)}, bf16[256,256]{1,0:T(8,128)(2,1)S(1)}, u32[]{:S(2)}, u32[]{:S(2)}) collective-permute-start(bf16[256,256]{1,0:T(8,128)(2,1)S(1)} %slice.39), channel_id=1, source_target_pairs={{0,48},{16,0},{32,16},{48,32},{64,112},{80,64},{96,80},{112,96},{1... | collective-permute-start | bytes 393224 | tf_op jit(solution)/shard_map/ppermute | solution.py:159
  40.1 6.9 %collective-permute-done.3 = bf16[256,256]{1,0:T(8,128)(2,1)S(1)} collective-permute-done((bf16[256,256]{1,0:T(8,128)(2,1)S(1)}, bf16[256,256]{1,0:T(8,128)(2,1)S(1)}, u32[]{:S(2)}, u32[]{:S(2)}) %collective-permute-start.3) | collective-permute-done | bytes 131104 | tf_op jit(solution)/shard_map/ppermute | solution.py:159
  47.1 0.0 collective-permute-done.2
  47.1 6.7 %collective-permute-start.4 = (bf16[1024,640]{1,0:T(8,128)(2,1)S(1)}, bf16[1024,640]{1,0:T(8,128)(2,1)S(1)}, u32[]{:S(2)}, u32[]{:S(2)}) collective-permute-start(bf16[1024,640]{1,0:T(8,128)(2,1)S(1)} %bitcast.27), channel_id=1, source_target_pairs={{0,448},{16,464},{32,480},{48,496},{64,0},{80,16},{96,32},{112,48}... | collective-permute-start | bytes 3932168 | tf_op jit(solution)/shard_map/ppermute | solution.py:194
  53.8 1.9 collective-permute-start.5
  55.7 23.7 %collective-permute-done.4 = bf16[1024,640]{1,0:T(8,128)(2,1)S(1)} collective-permute-done((bf16[1024,640]{1,0:T(8,128)(2,1)S(1)}, bf16[1024,640]{1,0:T(8,128)(2,1)S(1)}, u32[]{:S(2)}, u32[]{:S(2)}) %collective-permute-start.4) | collective-permute-done | bytes 1310752 | tf_op jit(solution)/shard_map/ppermute | solution.py:194
  79.5 1.8 collective-permute-done.5
  81.3 2.6 %all-gather.2.cloned.1.call-done = bf16[512,8192]{1,0:T(8,128)(2,1)} async-done(((bf16[32,8192]{1,0:T(8,128)(2,1)}), bf16[512,8192]{1,0:T(8,128)(2,1)}) %all-gather.2.cloned.1.call-update) | async-done | bytes 8388624 | tf_op jit(solution)/shard_map/all_gather | solution.py:235
  83.9 4.0 %collective-permute-start.7 = (bf16[1024,640]{1,0:T(8,128)(2,1)S(1)}, bf16[1024,640]{1,0:T(8,128)(2,1)}, u32[]{:S(2)}, u32[]{:S(2)}) collective-permute-start(bf16[1024,640]{1,0:T(8,128)(2,1)S(1)} %collective-permute-done.5), channel_id=1, source_target_pairs={{0,64},{16,80},{32,96},{48,112},{64,128},{80,144},{96,160},{112,17... | collective-permute-start | bytes 3932168 | tf_op jit(solution)/shard_map/ppermute | solution.py:196
  87.9 8.6 %collective-permute-start.6 = (bf16[1024,640]{1,0:T(8,128)(2,1)S(1)}, bf16[1024,640]{1,0:T(8,128)(2,1)}, u32[]{:S(2)}, u32[]{:S(2)}) collective-permute-start(bf16[1024,640]{1,0:T(8,128)(2,1)S(1)} %collective-permute-done.4), channel_id=1, source_target_pairs={{0,448},{16,464},{32,480},{48,496},{64,0},{80,16},{96,32},{112,48}... | collective-permute-start | bytes 3932168 | tf_op jit(solution)/shard_map/ppermute | solution.py:194
  96.4 27.1 %collective-permute-done.7 = bf16[1024,640]{1,0:T(8,128)(2,1)} collective-permute-done((bf16[1024,640]{1,0:T(8,128)(2,1)S(1)}, bf16[1024,640]{1,0:T(8,128)(2,1)}, u32[]{:S(2)}, u32[]{:S(2)}) %collective-permute-start.7) | collective-permute-done | bytes 1310752 | tf_op jit(solution)/shard_map/ppermute | solution.py:196
  123.6 1.9 collective-permute-start.9
  125.5 4.6 %collective-permute-start.8 = (bf16[1024,640]{1,0:T(8,128)(2,1)}, bf16[1024,640]{1,0:T(8,128)(2,1)S(1)}, u32[]{:S(2)}, u32[]{:S(2)}) collective-permute-start(bf16[1024,640]{1,0:T(8,128)(2,1)} %collective-permute-done.6), channel_id=1, source_target_pairs={{0,448},{16,464},{32,480},{48,496},{64,0},{80,16},{96,32},{112,48}... | collective-permute-start | bytes 3932168 | tf_op jit(solution)/shard_map/ppermute | solution.py:194
  130.3 2.8 %fusion.21 = f32[512,640]{1,0:T(8,128)S(1)} fusion(bf16[1024,640]{1,0:T(8,128)(2,1)} %bitcast.29, bf16[512,8192]{1,0:T(8,128)(2,1)} %all-gather.2.cloned.1.call-done, s32[]{:T(128)S(6)} %select_n.130), kind=kOutput, calls=%fused_computation.26 | convolution fusion | flops 671088640 | bytes 3670020 | tf_op jit(solution)/shard_map/dot_general | solution.py:186
  133.1 2.5 %convolution_add_fusion.2 = f32[512,640]{1,0:T(8,128)S(1)} fusion(f32[512,640]{1,0:T(8,128)S(1)} %fusion.21, bf16[1024,640]{1,0:T(8,128)(2,1)S(1)} %collective-permute-done.4, bf16[512,8192]{1,0:T(8,128)(2,1)} %all-gather.2.cloned.1.call-done, s32[]{:T(128)S(6)} %select_n.146), kind=kOutput, calls=%fused_computation.4 | convolution fusion | flops 671416320 | bytes 4980740 | tf_op jit(solution)/shard_map/dot_general | solution.py:186
  135.6 2.3 %fusion.17 = f32[512,640]{1,0:T(8,128)S(1)} fusion(bf16[1024,640]{1,0:T(8,128)(2,1)} %collective-permute-done.6, bf16[512,8192]{1,0:T(8,128)(2,1)S(1)} %copy-done.4, s32[]{:T(128)S(6)} %select_n.150), kind=kOutput, calls=%fused_computation.22 | convolution fusion | flops 671088640 | bytes 3670020 | tf_op jit(solution)/shard_map/dot_general | solution.py:186
  137.9 18.6 %collective-permute-done.9 = bf16[1024,640]{1,0:T(8,128)(2,1)} collective-permute-done((bf16[1024,640]{1,0:T(8,128)(2,1)}, bf16[1024,640]{1,0:T(8,128)(2,1)}, u32[]{:S(2)}, u32[]{:S(2)}) %collective-permute-start.9) | collective-permute-done | bytes 1310752 | tf_op jit(solution)/shard_map/ppermute | solution.py:196
  156.5 1.2 slice.40
  157.8 1.9 collective-permute-start.10
  159.7 2.4 %fusion.15 = f32[512,640]{1,0:T(8,128)S(1)} fusion(bf16[1024,640]{1,0:T(8,128)(2,1)} %collective-permute-done.7, bf16[512,8192]{1,0:T(8,128)(2,1)S(1)} %copy-done.4, s32[]{:T(128)S(6)} %select_n.152), kind=kOutput, calls=%fused_computation.20 | convolution fusion | flops 671088640 | bytes 3670020 | tf_op jit(solution)/shard_map/dot_general | solution.py:186
  162.2 4.6 %collective-permute-start.11 = (bf16[1024,256]{1,0:T(8,128)(2,1)S(1)}, bf16[1024,256]{1,0:T(8,128)(2,1)S(1)}, u32[]{:S(2)}, u32[]{:S(2)}) collective-permute-start(bf16[1024,256]{1,0:T(8,128)(2,1)S(1)} %slice.41), channel_id=1, source_target_pairs={{0,448},{16,464},{32,480},{48,496},{64,0},{80,16},{96,32},{112,48}... | collective-permute-start | bytes 1572872 | tf_op jit(solution)/shard_map/ppermute | solution.py:202
  166.8 1.0 fusion.2
  167.8 2.3 %fusion.12 = f32[512,640]{1,0:T(8,128)S(1)} fusion(bf16[1024,640]{1,0:T(8,128)(2,1)} %collective-permute-done.9, bf16[512,8192]{1,0:T(8,128)(2,1)S(1)} %copy-done.4, s32[]{:T(128)S(6)} %select_n.156), kind=kOutput, calls=%fused_computation.17 | convolution fusion | flops 671088640 | bytes 3670020 | tf_op jit(solution)/shard_map/dot_general | solution.py:186
  170.1 5.9 %collective-permute-done.11 = bf16[1024,256]{1,0:T(8,128)(2,1)S(1)} collective-permute-done((bf16[1024,256]{1,0:T(8,128)(2,1)S(1)}, bf16[1024,256]{1,0:T(8,128)(2,1)S(1)}, u32[]{:S(2)}, u32[]{:S(2)}) %collective-permute-start.11) | collective-permute-done | bytes 524320 | tf_op jit(solution)/shard_map/ppermute | solution.py:202
  176.0 2.2 %collective-permute-done.10 = bf16[1024,384]{1,0:T(8,128)(2,1)S(1)} collective-permute-done((bf16[1024,384]{1,0:T(8,128)(2,1)S(1)}, bf16[1024,384]{1,0:T(8,128)(2,1)S(1)}, u32[]{:S(2)}, u32[]{:S(2)}) %collective-permute-start.10) | collective-permute-done | bytes 786464 | tf_op jit(solution)/shard_map/ppermute | solution.py:201
  178.3 1.0 fusion.4
  179.2 1.1 fusion.3.q_ref
  180.3 4.7 %collective-permute-start.12 = (bf16[512,128]{1,0:T(8,128)(2,1)S(1)}, bf16[512,128]{1,0:T(8,128)(2,1)S(1)}, u32[]{:S(2)}, u32[]{:S(2)}) collective-permute-start(bf16[512,128]{1,0:T(8,128)(2,1)S(1)} %slice.45), channel_id=1, source_target_pairs={{0,1},{1,0},{2,3},{3,2},{4,5},{5,4},{6,7},{7,6},{8,9},{9,8},{10,11... | collective-permute-start | bytes 393224 | tf_op jit(solution)/shard_map/ppermute | solution.py:240
  185.0 0.9 copy.7.row_seg_ref
  185.9 0.7 broadcast_select_fusion
  186.6 6.1 %shard_map.64 = bf16[512,512]{1,0:T(8,128)(2,1)} custom-call(f32[512,640]{1,0:T(8,128)} %copy-done, bf16[512,128]{1,0:T(8,128)(2,1)} %get-tuple-element.22.k_ref, bf16[512,128]{1,0:T(8,128)(2,1)} %get-tuple-element.21.v_ref, f32[512,64]{1,0:T(8,128)} %get-tuple-element.17.cos_ref, f32[512,64]{1,0:T(8,128)} %get-tuple-element.18.sin_ref, ...), custom_call_target="tpu_custom_call" | custom-call | flops 538968064 | bytes 2097152 | tf_op jit(solution)/shard_map/pallas_call | solution.py:113
  (30 shorter events, 0.4 us)
Async XLA Ops:
  6.5 4.3 %copy-start.5 = (bf16[256,512]{1,0:T(8,128)(2,1)S(1)}, bf16[256,512]{1,0:T(8,128)(2,1)}, u32[]{:S(2)}) copy-start(bf16[256,512]{1,0:T(8,128)(2,1)} %param.9) | copy-start | bytes 786436
  6.5 77.3 %all-gather.2.cloned.1.call-start = ((), (), s32[]{:S(2)}) async-start(), calls=%async_computation | async-start | bytes 8912896 | tf_op jit(solution)/shard_map/all_gather | solution.py:235
  7.8 10.5 %copy-start.6 = (s32[512]{0:T(512)S(1)}, s32[512]{0:T(512)}, u32[]{:S(2)}) copy-start(s32[512]{0:T(512)} %param.7) | copy-start | bytes 6148
  10.9 26.8 %collective-permute-start = (bf16[256,640]{1,0:T(8,128)(2,1)S(1)}, bf16[256,640]{1,0:T(8,128)(2,1)S(1)}, u32[]{:S(2)}, u32[]{:S(2)}) collective-permute-start(bf16[256,640]{1,0:T(8,128)(2,1)S(1)} %pad_maximum_fusion), channel_id=1, source_target_pairs={{0,48},{16,0},{32,16},{48,32},{64,112},{80,64},{96,80},{112,96},{1... | collective-permute-start | bytes 983048 | tf_op jit(solution)/shard_map/ppermute | solution.py:151
  14.7 18.6 %collective-permute-start.1 = (bf16[256,640]{1,0:T(8,128)(2,1)S(1)}, bf16[256,640]{1,0:T(8,128)(2,1)S(1)}, u32[]{:S(2)}, u32[]{:S(2)}) collective-permute-start(bf16[256,640]{1,0:T(8,128)(2,1)S(1)} %pad_maximum_fusion), channel_id=1, source_target_pairs={{0,16},{16,32},{32,48},{48,0},{64,80},{80,96},{96,112},{112,64},{1... | collective-permute-start | bytes 983048 | tf_op jit(solution)/shard_map/ppermute | solution.py:153
  33.3 13.8 %collective-permute-start.2 = (bf16[256,384]{1,0:T(8,128)(2,1)S(1)}, bf16[256,384]{1,0:T(8,128)(2,1)S(1)}, u32[]{:S(2)}, u32[]{:S(2)}) collective-permute-start(bf16[256,384]{1,0:T(8,128)(2,1)S(1)} %slice.38), channel_id=1, source_target_pairs={{0,16},{16,32},{32,48},{48,0},{64,80},{80,96},{96,112},{112,64},{1... | collective-permute-start | bytes 589832 | tf_op jit(solution)/shard_map/ppermute | solution.py:158
  37.7 9.4 %collective-permute-start.3 = (bf16[256,256]{1,0:T(8,128)(2,1)S(1)}, bf16[256,256]{1,0:T(8,128)(2,1)S(1)}, u32[]{:S(2)}, u32[]{:S(2)}) collective-permute-start(bf16[256,256]{1,0:T(8,128)(2,1)S(1)} %slice.39), channel_id=1, source_target_pairs={{0,48},{16,0},{32,16},{48,32},{64,112},{80,64},{96,80},{112,96},{1... | collective-permute-start | bytes 393224 | tf_op jit(solution)/shard_map/ppermute | solution.py:159
  47.1 32.3 %copy-start.1 = (bf16[4,256,640]{2,1,0:T(8,128)(2,1)}, bf16[4,256,640]{2,1,0:T(8,128)(2,1)S(1)}, u32[]{:S(2)}) copy-start(bf16[4,256,640]{2,1,0:T(8,128)(2,1)S(1)} %fusion.23) | copy-start | bytes 3932164
  47.1 32.3 %collective-permute-start.4 = (bf16[1024,640]{1,0:T(8,128)(2,1)S(1)}, bf16[1024,640]{1,0:T(8,128)(2,1)S(1)}, u32[]{:S(2)}, u32[]{:S(2)}) collective-permute-start(bf16[1024,640]{1,0:T(8,128)(2,1)S(1)} %bitcast.27), channel_id=1, source_target_pairs={{0,448},{16,464},{32,480},{48,496},{64,0},{80,16},{96,32},{112,48}... | collective-permute-start | bytes 3932168 | tf_op jit(solution)/shard_map/ppermute | solution.py:194
  53.8 27.4 %collective-permute-start.5 = (bf16[1024,640]{1,0:T(8,128)(2,1)S(1)}, bf16[1024,640]{1,0:T(8,128)(2,1)S(1)}, u32[]{:S(2)}, u32[]{:S(2)}) collective-permute-start(bf16[1024,640]{1,0:T(8,128)(2,1)S(1)} %bitcast.28), channel_id=1, source_target_pairs={{0,64},{16,80},{32,96},{48,112},{64,128},{80,144},{96,160},{112,17... | collective-permute-start | bytes 3932168 | tf_op jit(solution)/shard_map/ppermute | solution.py:196
  81.3 44.2 %copy-start.2 = (bf16[1024,640]{1,0:T(8,128)(2,1)}, bf16[1024,640]{1,0:T(8,128)(2,1)S(1)}, u32[]{:S(2)}) copy-start(bf16[1024,640]{1,0:T(8,128)(2,1)S(1)} %collective-permute-done.5) | copy-start | bytes 3932164
  83.9 39.7 %collective-permute-start.7 = (bf16[1024,640]{1,0:T(8,128)(2,1)S(1)}, bf16[1024,640]{1,0:T(8,128)(2,1)}, u32[]{:S(2)}, u32[]{:S(2)}) collective-permute-start(bf16[1024,640]{1,0:T(8,128)(2,1)S(1)} %collective-permute-done.5), channel_id=1, source_target_pairs={{0,64},{16,80},{32,96},{48,112},{64,128},{80,144},{96,160},{112,17... | collective-permute-start | bytes 3932168 | tf_op jit(solution)/shard_map/ppermute | solution.py:196
  87.9 37.7 %collective-permute-start.6 = (bf16[1024,640]{1,0:T(8,128)(2,1)S(1)}, bf16[1024,640]{1,0:T(8,128)(2,1)}, u32[]{:S(2)}, u32[]{:S(2)}) collective-permute-start(bf16[1024,640]{1,0:T(8,128)(2,1)S(1)} %collective-permute-done.4), channel_id=1, source_target_pairs={{0,448},{16,464},{32,480},{48,496},{64,0},{80,16},{96,32},{112,48}... | collective-permute-start | bytes 3932168 | tf_op jit(solution)/shard_map/ppermute | solution.py:194
  123.6 33.0 %collective-permute-start.9 = (bf16[1024,640]{1,0:T(8,128)(2,1)}, bf16[1024,640]{1,0:T(8,128)(2,1)}, u32[]{:S(2)}, u32[]{:S(2)}) collective-permute-start(bf16[1024,640]{1,0:T(8,128)(2,1)} %collective-permute-done.7), channel_id=1, source_target_pairs={{0,64},{16,80},{32,96},{48,112},{64,128},{80,144},{96,160},{112,17... | collective-permute-start | bytes 3932168 | tf_op jit(solution)/shard_map/ppermute | solution.py:196
  125.5 36.6 %collective-permute-start.8 = (bf16[1024,640]{1,0:T(8,128)(2,1)}, bf16[1024,640]{1,0:T(8,128)(2,1)S(1)}, u32[]{:S(2)}, u32[]{:S(2)}) collective-permute-start(bf16[1024,640]{1,0:T(8,128)(2,1)} %collective-permute-done.6), channel_id=1, source_target_pairs={{0,448},{16,464},{32,480},{48,496},{64,0},{80,16},{96,32},{112,48}... | collective-permute-start | bytes 3932168 | tf_op jit(solution)/shard_map/ppermute | solution.py:194
  130.3 5.3 %copy-start.4 = (bf16[512,8192]{1,0:T(8,128)(2,1)S(1)}, bf16[512,8192]{1,0:T(8,128)(2,1)}, u32[]{:S(2)}) copy-start(bf16[512,8192]{1,0:T(8,128)(2,1)} %all-gather.2.cloned.1.call-done) | copy-start | bytes 25165828
  157.8 20.5 %collective-permute-start.10 = (bf16[1024,384]{1,0:T(8,128)(2,1)S(1)}, bf16[1024,384]{1,0:T(8,128)(2,1)S(1)}, u32[]{:S(2)}, u32[]{:S(2)}) collective-permute-start(bf16[1024,384]{1,0:T(8,128)(2,1)S(1)} %slice.40), channel_id=1, source_target_pairs={{0,64},{16,80},{32,96},{48,112},{64,128},{80,144},{96,160},{112,17... | collective-permute-start | bytes 2359304 | tf_op jit(solution)/shard_map/ppermute | solution.py:201
  159.7 7.1 %copy-start.3 = (bf16[1024,640]{1,0:T(8,128)(2,1)S(1)}, bf16[1024,640]{1,0:T(8,128)(2,1)}, u32[]{:S(2)}) copy-start(bf16[1024,640]{1,0:T(8,128)(2,1)} %copy-done.2) | copy-start | bytes 3932164
  162.2 13.8 %collective-permute-start.11 = (bf16[1024,256]{1,0:T(8,128)(2,1)S(1)}, bf16[1024,256]{1,0:T(8,128)(2,1)S(1)}, u32[]{:S(2)}, u32[]{:S(2)}) collective-permute-start(bf16[1024,256]{1,0:T(8,128)(2,1)S(1)} %slice.41), channel_id=1, source_target_pairs={{0,448},{16,464},{32,480},{48,496},{64,0},{80,16},{96,32},{112,48}... | collective-permute-start | bytes 1572872 | tf_op jit(solution)/shard_map/ppermute | solution.py:202
  180.3 6.3 %copy-start = (f32[512,640]{1,0:T(8,128)}, f32[512,640]{1,0:T(8,128)S(1)}, u32[]{:S(2)}) copy-start(f32[512,640]{1,0:T(8,128)S(1)} %fusion.3.q_ref) | copy-start | bytes 3932164
  180.3 5.5 %collective-permute-start.12 = (bf16[512,128]{1,0:T(8,128)(2,1)S(1)}, bf16[512,128]{1,0:T(8,128)(2,1)S(1)}, u32[]{:S(2)}, u32[]{:S(2)}) collective-permute-start(bf16[512,128]{1,0:T(8,128)(2,1)S(1)} %slice.45), channel_id=1, source_target_pairs={{0,1},{1,0},{2,3},{3,2},{4,5},{5,4},{6,7},{7,6},{8,9},{9,8},{10,11... | collective-permute-start | bytes 393224 | tf_op jit(solution)/shard_map/ppermute | solution.py:240
Sparse Core Ops, SparseCore 0:
  10.0 73.7 all-gather.1

commit v13 on v12

--- a/solution.py
+++ b/solution.py
@@ -168,11 +168,11 @@
     return min(width, (width // 2 + 127) // 128 * 128)
 
 
-def ring_matmul(rows, block, axis, stride, count):
+def ring_matmul(rows, block, axis, stride, count, starts, wait_rows):
     n = lax.psum(1, axis)
     me = lax.axis_index(axis)
     here = (me // stride) % count
-    depth = block.shape[0]
+    depth = block.shape[1]
 
     def moved(step):
         pairs = []
@@ -182,13 +182,17 @@
         return pairs
 
     def product(part, owner):
-        lhs = lax.dynamic_slice_in_dim(rows, owner * depth, depth, 1)
-        return jnp.dot(lhs, part, preferred_element_type=jnp.float32)
+        result = None
+        for piece, start in enumerate(starts(owner)):
+            lhs = lax.dynamic_slice_in_dim(rows, start, depth, 1)
+            term = jnp.dot(lhs, part[piece], preferred_element_type=jnp.float32)
+            result = term if result is None else result + term
+        return result
 
     total = product(block, here)
     from_right, from_left = block, block
     for step in range(1, count // 2 + 1):
-        if step == 2:
+        if step == 2 and wait_rows:
             rows, from_right, from_left = lax.optimization_barrier((rows, from_right, from_left))
         if step < count - step:
             from_right = lax.ppermute(from_right, axis, perm=moved(-1))
@@ -225,16 +229,36 @@
     local_weights = jnp.concatenate([query_weight, kv_block], axis=1)
     n_batch = lax.psum(1, "batch")
     y_hi = n_batch // Z_CHIPS
+    shard = local_weights.shape[0]
+    yh = lax.axis_index("batch") % y_hi
     near = ring_gather(local_weights, "batch", 1, y_hi)
-    near = near.reshape(-1, local_weights.shape[1])
+    others = jnp.stack([near[(yh + r) % y_hi] for r in range(1, y_hi)])
     cosine, sine = rope_tables(positions_in_segment(segment_ids))
     row_seg, col_seg = segment_ids[:, None], segment_ids[None, :]
-    near, cosine, sine, row_seg, col_seg = lax.optimization_barrier(
-        (near, cosine, sine, row_seg, col_seg)
+    others, cosine, sine, row_seg, col_seg = lax.optimization_barrier(
+        (others, cosine, sine, row_seg, col_seg)
     )
     gathered = lax.all_gather(normed, "weight", axis=0, tiled=True)
     pack_rows = gathered.shape[0]
-    projected = ring_matmul(gathered, near, "batch", y_hi, Z_CHIPS)
+    own_part = ring_matmul(
+        gathered,
+        local_weights[None],
+        "batch",
+        y_hi,
+        Z_CHIPS,
+        lambda z: [(z * y_hi + yh) * shard],
+        False,
+    )
+    other_part = ring_matmul(
+        gathered,
+        others,
+        "batch",
+        y_hi,
+        Z_CHIPS,
+        lambda z: [(z * y_hi + (yh + r) % y_hi) * shard for r in range(1, y_hi)],
+        True,
+    )
+    projected = own_part + other_part
     own_rows = projected[:, query_cols:].astype(jnp.bfloat16)
     partner = [(w, w ^ 1) for w in range(n_weight)]
     other_rows = lax.ppermute(own_rows, "weight", perm=partner)

time: 200 us -> 197 us (0.985)
  the two profiles are of different devices: /device:TPU:63 before, /device:TPU:7 now
where the time goes in v13:
time: 197 us; the launch traced here: 195 us
  starting transfers between devices  86.3 us (44%)
  waiting for transfers between devices  49.4 us (25%)
  matrix products  24.3 us (12%)
  between operations  15.2 us (8%)
  other arithmetic  8.29 us (4%)
  Pallas kernels  6.07 us (3%)
  local copies, waits for them, and re-layouts  5.33 us (3%)
    ppermute x6, starting transfers between devices, ring_matmul(): from_right = lax.ppermute(from_right, axis, perm=moved(-1))  34.9 us
    dot_general x32, matrix products, product(): term = jnp.dot(lhs, part[piece], preferred_element_type=jnp.float32)  24.3 us
    ppermute x6, waiting for transfers between devices, ring_matmul(): from_right = lax.ppermute(from_right, axis, perm=moved(-1))  18.4 us
    ppermute x1, waiting for transfers between devices, ring_gather(): lax.ppermute(from_left[..., :cut], axis, perm=moved(1))  15.7 us
    ppermute x6, starting transfers between devices, ring_matmul(): from_left = lax.ppermute(from_left, axis, perm=moved(1))  11.5 us
    ppermute x1, starting transfers between devices, per_device(): other_rows = lax.ppermute(own_rows, 'weight', perm=partner)  11 us
    ppermute x6, waiting for transfers between devices, ring_matmul(): from_left = lax.ppermute(from_left, axis, perm=moved(1))  10.1 us
    ppermute x2, starting transfers between devices, ring_matmul(): lax.ppermute(from_right[..., cut:], axis, perm=moved(-1))  9.77 us
  transfers between devices with their start and end apart: 22, of which 6 were waited for; matrix products, arithmetic and copies ran while one was open for 16% of the time, Pallas kernels for 0%

profile of v13, /device:TPU:7, one launch (start us, length us, event | category | flops | bytes accessed | tf_op | source)
XLA Modules:
  0.0 194.9 jit_solution(4531561256789245926)
XLA Ops:
  6.5 1.3 fusion.18
  7.9 2.0 %fusion.20 = bf16[32,8192]{1,0:T(8,128)(2,1)} fusion(bf16[32,8192]{1,0:T(8,128)(2,1)} %param.6, f32[8192]{0:T(1024)} %param.8, f32[32]{0:T(128)S(1)} %add_rsqrt_fusion), kind=kLoop, calls=%fused_computation.35 | loop fusion | flops 1048576 | bytes 1081472 | tf_op jit(solution)/shard_map/convert_element_type | solution.py:228
  9.9 0.9 dynamic-slice_select_fusion
  10.9 0.8 fusion.121
  11.6 5.9 %collective-permute-start.8 = (bf16[256,640]{1,0:T(8,128)(2,1)S(1)}, bf16[256,640]{1,0:T(8,128)(2,1)S(1)}, u32[]{:S(2)}, u32[]{:S(2)}) collective-permute-start(bf16[256,640]{1,0:T(8,128)(2,1)S(1)} %get-tuple-element.25), channel_id=1, source_target_pairs={{0,48},{16,0},{32,16},{48,32},{64,112},{80,64},{96,80},{112,96},{1... | collective-permute-start | bytes 983048 | tf_op jit(solution)/shard_map/ppermute | solution.py:151
  17.5 1.9 collective-permute-start.9
  19.4 10.7 %collective-permute-start = (bf16[1,256,640]{2,1,0:T(8,128)(2,1)}, bf16[1,256,640]{2,1,0:T(8,128)(2,1)}, u32[]{:S(2)}, u32[]{:S(2)}) collective-permute-start(bf16[1,256,640]{2,1,0:T(8,128)(2,1)} %get-tuple-element.24), channel_id=1, source_target_pairs={{0,448},{16,464},{32,480},{48,496},{64,0},{80,16},{96,32},{112,48}... | collective-permute-start | bytes 983048 | tf_op jit(solution)/shard_map/ppermute | solution.py:198
  30.1 1.9 collective-permute-start.1
  34.3 1.8 multiply_sine_fusion
  36.1 5.5 %collective-permute-start.11 = (bf16[256,256]{1,0:T(8,128)(2,1)S(1)}, bf16[256,256]{1,0:T(8,128)(2,1)S(1)}, u32[]{:S(2)}, u32[]{:S(2)}) collective-permute-start(bf16[256,256]{1,0:T(8,128)(2,1)S(1)} %slice.145), channel_id=1, source_target_pairs={{0,48},{16,0},{32,16},{48,32},{64,112},{80,64},{96,80},{112,96},{1... | collective-permute-start | bytes 393224 | tf_op jit(solution)/shard_map/ppermute | solution.py:159
  41.7 1.9 collective-permute-start.10
  43.7 15.7 %collective-permute-done.10 = bf16[256,384]{1,0:T(8,128)(2,1)S(1)} collective-permute-done((bf16[256,384]{1,0:T(8,128)(2,1)S(1)}, bf16[256,384]{1,0:T(8,128)(2,1)S(1)}, u32[]{:S(2)}, u32[]{:S(2)}) %collective-permute-start.10) | collective-permute-done | bytes 196640 | tf_op jit(solution)/shard_map/ppermute | solution.py:158
  59.7 6.4 %collective-permute-start.12 = (bf16[3,256,640]{2,1,0:T(8,128)(2,1)S(1)}, bf16[3,256,640]{2,1,0:T(8,128)(2,1)S(1)}, u32[]{:S(2)}, u32[]{:S(2)}) collective-permute-start(bf16[3,256,640]{2,1,0:T(8,128)(2,1)S(1)} %pad_maximum_fusion), channel_id=1, source_target_pairs={{0,448},{16,464},{32,480},{48,496},{64,0},{80,16},{96,32},{112,48}... | collective-permute-start | bytes 2949128 | tf_op jit(solution)/shard_map/ppermute | solution.py:198
  66.1 1.9 collective-permute-start.13
  68.1 4.6 %collective-permute-start.2 = (bf16[1,256,640]{2,1,0:T(8,128)(2,1)}, bf16[1,256,640]{2,1,0:T(8,128)(2,1)}, u32[]{:S(2)}, u32[]{:S(2)}) collective-permute-start(bf16[1,256,640]{2,1,0:T(8,128)(2,1)} %collective-permute-done), channel_id=1, source_target_pairs={{0,448},{16,464},{32,480},{48,496},{64,0},{80,16},{96,32},{112,48}... | collective-permute-start | bytes 983048 | tf_op jit(solution)/shard_map/ppermute | solution.py:198
  72.7 1.9 collective-permute-start.3
  74.6 16.5 %collective-permute-done.2 = bf16[1,256,640]{2,1,0:T(8,128)(2,1)} collective-permute-done((bf16[1,256,640]{2,1,0:T(8,128)(2,1)}, bf16[1,256,640]{2,1,0:T(8,128)(2,1)}, u32[]{:S(2)}, u32[]{:S(2)}) %collective-permute-start.2) | collective-permute-done | bytes 327712 | tf_op jit(solution)/shard_map/ppermute | solution.py:198
  91.1 4.2 %collective-permute-start.4 = (bf16[1,256,640]{2,1,0:T(8,128)(2,1)}, bf16[1,256,640]{2,1,0:T(8,128)(2,1)}, u32[]{:S(2)}, u32[]{:S(2)}) collective-permute-start(bf16[1,256,640]{2,1,0:T(8,128)(2,1)} %collective-permute-done.2), channel_id=1, source_target_pairs={{0,448},{16,464},{32,480},{48,496},{64,0},{80,16},{96,32},{112,48}... | collective-permute-start | bytes 983048 | tf_op jit(solution)/shard_map/ppermute | solution.py:198
  95.3 1.9 collective-permute-start.5
  97.6 2.0 %collective-permute-done.4 = bf16[1,256,640]{2,1,0:T(8,128)(2,1)} collective-permute-done((bf16[1,256,640]{2,1,0:T(8,128)(2,1)}, bf16[1,256,640]{2,1,0:T(8,128)(2,1)}, u32[]{:S(2)}, u32[]{:S(2)}) %collective-permute-start.4) | collective-permute-done | bytes 327712 | tf_op jit(solution)/shard_map/ppermute | solution.py:198
  99.6 1.6 slice.143
  101.1 5.0 %collective-permute-start.7 = (bf16[1,256,256]{2,1,0:T(8,128)(2,1)}, bf16[1,256,256]{2,1,0:T(8,128)(2,1)}, u32[]{:S(2)}, u32[]{:S(2)}) collective-permute-start(bf16[1,256,256]{2,1,0:T(8,128)(2,1)} %slice.143), channel_id=1, source_target_pairs={{0,448},{16,464},{32,480},{48,496},{64,0},{80,16},{96,32},{112,48}... | collective-permute-start | bytes 393224 | tf_op jit(solution)/shard_map/ppermute | solution.py:206
  106.2 1.6 slice.142
  107.8 1.9 collective-permute-start.6
  109.7 1.9 collective-permute-start.15
  111.7 4.6 %collective-permute-start.14 = (bf16[3,256,640]{2,1,0:T(8,128)(2,1)S(1)}, bf16[3,256,640]{2,1,0:T(8,128)(2,1)S(1)}, u32[]{:S(2)}, u32[]{:S(2)}) collective-permute-start(bf16[3,256,640]{2,1,0:T(8,128)(2,1)S(1)} %collective-permute-done.12), channel_id=1, source_target_pairs={{0,448},{16,464},{32,480},{48,496},{64,0},{80,16},{96,32},{112,48}... | collective-permute-start | bytes 2949128 | tf_op jit(solution)/shard_map/ppermute | solution.py:198
  116.2 1.5 fusion.41
  117.7 1.7 fusion.33
  119.4 1.3 fusion.34
  120.7 1.3 fusion.31
  122.1 1.3 fusion.32
  123.4 1.4 fusion.43
  125.9 1.4 convolution_add_fusion.12
  127.3 1.4 fusion.46
  128.6 1.3 fusion.35
  129.9 1.4 convolution_add_fusion.11
  131.3 1.4 fusion
  133.1 1.9 collective-permute-start.17
  135.0 4.6 %collective-permute-start.16 = (bf16[3,256,640]{2,1,0:T(8,128)(2,1)S(1)}, bf16[3,256,640]{2,1,0:T(8,128)(2,1)S(1)}, u32[]{:S(2)}, u32[]{:S(2)}) collective-permute-start(bf16[3,256,640]{2,1,0:T(8,128)(2,1)S(1)} %collective-permute-done.14), channel_id=1, source_target_pairs={{0,448},{16,464},{32,480},{48,496},{64,0},{80,16},{96,32},{112,48}... | collective-permute-start | bytes 2949128 | tf_op jit(solution)/shard_map/ppermute | solution.py:198
  142.4 10.1 %collective-permute-done.17 = bf16[3,256,640]{2,1,0:T(8,128)(2,1)S(1)} collective-permute-done((bf16[3,256,640]{2,1,0:T(8,128)(2,1)S(1)}, bf16[3,256,640]{2,1,0:T(8,128)(2,1)S(1)}, u32[]{:S(2)}, u32[]{:S(2)}) %collective-permute-start.17) | collective-permute-done | bytes 983072 | tf_op jit(solution)/shard_map/ppermute | solution.py:200
  152.6 1.9 collective-permute-start.18
  154.5 4.8 %collective-permute-start.19 = (bf16[3,256,256]{2,1,0:T(8,128)(2,1)S(1)}, bf16[3,256,256]{2,1,0:T(8,128)(2,1)S(1)}, u32[]{:S(2)}, u32[]{:S(2)}) collective-permute-start(bf16[3,256,256]{2,1,0:T(8,128)(2,1)S(1)} %slice.165), channel_id=1, source_target_pairs={{0,448},{16,464},{32,480},{48,496},{64,0},{80,16},{96,32},{112,48}... | collective-permute-start | bytes 1179656 | tf_op jit(solution)/shard_map/ppermute | solution.py:206
  161.2 5.0 %collective-permute-done.18 = bf16[3,256,384]{2,1,0:T(8,128)(2,1)S(1)} collective-permute-done((bf16[3,256,384]{2,1,0:T(8,128)(2,1)S(1)}, bf16[3,256,384]{2,1,0:T(8,128)(2,1)S(1)}, u32[]{:S(2)}, u32[]{:S(2)}) %collective-permute-start.18) | collective-permute-done | bytes 589856 | tf_op jit(solution)/shard_map/ppermute | solution.py:205
  167.9 1.4 fusion.17.q_ref
  169.3 11.0 %collective-permute-start.20 = (bf16[512,128]{1,0:T(8,128)(2,1)S(1)}, bf16[512,128]{1,0:T(8,128)(2,1)S(1)}, u32[]{:S(2)}, u32[]{:S(2)}) collective-permute-start(bf16[512,128]{1,0:T(8,128)(2,1)S(1)} %slice.226), channel_id=1, source_target_pairs={{0,1},{1,0},{2,3},{3,2},{4,5},{5,4},{6,7},{7,6},{8,9},{9,8},{10,11... | collective-permute-start | bytes 393224 | tf_op jit(solution)/shard_map/ppermute | solution.py:264
  180.3 0.9 copy.7.row_seg_ref
  181.3 0.7 broadcast_select_fusion
  182.0 6.1 %shard_map.64 = bf16[512,512]{1,0:T(8,128)(2,1)} custom-call(f32[512,640]{1,0:T(8,128)} %copy-done.1, bf16[512,128]{1,0:T(8,128)(2,1)} %get-tuple-element.27.k_ref, bf16[512,128]{1,0:T(8,128)(2,1)} %get-tuple-element.26.v_ref, f32[512,64]{1,0:T(8,128)} %get-tuple-element.17.cos_ref, f32[512,64]{1,0:T(8,128)} %get-tuple-element.18.sin_ref, ...), custom_call_target="tpu_custom_call" | custom-call | flops 538968064 | bytes 2097152 | tf_op jit(solution)/shard_map/pallas_call | solution.py:113
  (70 shorter events, 9.9 us)
Async XLA Ops:
  6.5 4.3 %copy-start.2 = (bf16[256,512]{1,0:T(8,128)(2,1)S(1)}, bf16[256,512]{1,0:T(8,128)(2,1)}, u32[]{:S(2)}) copy-start(bf16[256,512]{1,0:T(8,128)(2,1)} %param.9) | copy-start | bytes 786436
  6.5 103.2 %all-gather.2.cloned.1.call-start = ((), (), s32[]{:S(2)}) async-start(), calls=%async_computation | async-start | bytes 8912896 | tf_op jit(solution)/shard_map/all_gather | solution.py:241
  7.8 24.3 %copy-start.3 = (s32[512]{0:T(512)S(1)}, s32[512]{0:T(512)}, u32[]{:S(2)}) copy-start(s32[512]{0:T(512)} %param.7) | copy-start | bytes 6148
  11.6 24.5 %collective-permute-start.8 = (bf16[256,640]{1,0:T(8,128)(2,1)S(1)}, bf16[256,640]{1,0:T(8,128)(2,1)S(1)}, u32[]{:S(2)}, u32[]{:S(2)}) collective-permute-start(bf16[256,640]{1,0:T(8,128)(2,1)S(1)} %get-tuple-element.25), channel_id=1, source_target_pairs={{0,48},{16,0},{32,16},{48,32},{64,112},{80,64},{96,80},{112,96},{1... | collective-permute-start | bytes 983048 | tf_op jit(solution)/shard_map/ppermute | solution.py:151
  17.5 24.1 %collective-permute-start.9 = (bf16[256,640]{1,0:T(8,128)(2,1)S(1)}, bf16[256,640]{1,0:T(8,128)(2,1)S(1)}, u32[]{:S(2)}, u32[]{:S(2)}) collective-permute-start(bf16[256,640]{1,0:T(8,128)(2,1)S(1)} %get-tuple-element.25), channel_id=1, source_target_pairs={{0,16},{16,32},{32,48},{48,0},{64,80},{80,96},{96,112},{112,64},{1... | collective-permute-start | bytes 983048 | tf_op jit(solution)/shard_map/ppermute | solution.py:153
  19.4 48.6 %collective-permute-start = (bf16[1,256,640]{2,1,0:T(8,128)(2,1)}, bf16[1,256,640]{2,1,0:T(8,128)(2,1)}, u32[]{:S(2)}, u32[]{:S(2)}) collective-permute-start(bf16[1,256,640]{2,1,0:T(8,128)(2,1)} %get-tuple-element.24), channel_id=1, source_target_pairs={{0,448},{16,464},{32,480},{48,496},{64,0},{80,16},{96,32},{112,48}... | collective-permute-start | bytes 983048 | tf_op jit(solution)/shard_map/ppermute | solution.py:198
  30.1 42.6 %collective-permute-start.1 = (bf16[1,256,640]{2,1,0:T(8,128)(2,1)}, bf16[1,256,640]{2,1,0:T(8,128)(2,1)}, u32[]{:S(2)}, u32[]{:S(2)}) collective-permute-start(bf16[1,256,640]{2,1,0:T(8,128)(2,1)} %get-tuple-element.24), channel_id=1, source_target_pairs={{0,64},{16,80},{32,96},{48,112},{64,128},{80,144},{96,160},{112,17... | collective-permute-start | bytes 983048 | tf_op jit(solution)/shard_map/ppermute | solution.py:200
  36.1 7.6 %collective-permute-start.11 = (bf16[256,256]{1,0:T(8,128)(2,1)S(1)}, bf16[256,256]{1,0:T(8,128)(2,1)S(1)}, u32[]{:S(2)}, u32[]{:S(2)}) collective-permute-start(bf16[256,256]{1,0:T(8,128)(2,1)S(1)} %slice.145), channel_id=1, source_target_pairs={{0,48},{16,0},{32,16},{48,32},{64,112},{80,64},{96,80},{112,96},{1... | collective-permute-start | bytes 393224 | tf_op jit(solution)/shard_map/ppermute | solution.py:159
  41.7 17.8 %collective-permute-start.10 = (bf16[256,384]{1,0:T(8,128)(2,1)S(1)}, bf16[256,384]{1,0:T(8,128)(2,1)S(1)}, u32[]{:S(2)}, u32[]{:S(2)}) collective-permute-start(bf16[256,384]{1,0:T(8,128)(2,1)S(1)} %slice.144), channel_id=1, source_target_pairs={{0,16},{16,32},{32,48},{48,0},{64,80},{80,96},{96,112},{112,64},{1... | collective-permute-start | bytes 589832 | tf_op jit(solution)/shard_map/ppermute | solution.py:158
  59.7 49.9 %collective-permute-start.12 = (bf16[3,256,640]{2,1,0:T(8,128)(2,1)S(1)}, bf16[3,256,640]{2,1,0:T(8,128)(2,1)S(1)}, u32[]{:S(2)}, u32[]{:S(2)}) collective-permute-start(bf16[3,256,640]{2,1,0:T(8,128)(2,1)S(1)} %pad_maximum_fusion), channel_id=1, source_target_pairs={{0,448},{16,464},{32,480},{48,496},{64,0},{80,16},{96,32},{112,48}... | collective-permute-start | bytes 2949128 | tf_op jit(solution)/shard_map/ppermute | solution.py:198
  66.1 43.5 %collective-permute-start.13 = (bf16[3,256,640]{2,1,0:T(8,128)(2,1)S(1)}, bf16[3,256,640]{2,1,0:T(8,128)(2,1)S(1)}, u32[]{:S(2)}, u32[]{:S(2)}) collective-permute-start(bf16[3,256,640]{2,1,0:T(8,128)(2,1)S(1)} %pad_maximum_fusion), channel_id=1, source_target_pairs={{0,64},{16,80},{32,96},{48,112},{64,128},{80,144},{96,160},{112,17... | collective-permute-start | bytes 2949128 | tf_op jit(solution)/shard_map/ppermute | solution.py:200
  68.1 23.0 %collective-permute-start.2 = (bf16[1,256,640]{2,1,0:T(8,128)(2,1)}, bf16[1,256,640]{2,1,0:T(8,128)(2,1)}, u32[]{:S(2)}, u32[]{:S(2)}) collective-permute-start(bf16[1,256,640]{2,1,0:T(8,128)(2,1)} %collective-permute-done), channel_id=1, source_target_pairs={{0,448},{16,464},{32,480},{48,496},{64,0},{80,16},{96,32},{112,48}... | collective-permute-start | bytes 983048 | tf_op jit(solution)/shard_map/ppermute | solution.py:198
  72.7 22.6 %collective-permute-start.3 = (bf16[1,256,640]{2,1,0:T(8,128)(2,1)}, bf16[1,256,640]{2,1,0:T(8,128)(2,1)}, u32[]{:S(2)}, u32[]{:S(2)}) collective-permute-start(bf16[1,256,640]{2,1,0:T(8,128)(2,1)} %collective-permute-done.1), channel_id=1, source_target_pairs={{0,64},{16,80},{32,96},{48,112},{64,128},{80,144},{96,160},{112,17... | collective-permute-start | bytes 983048 | tf_op jit(solution)/shard_map/ppermute | solution.py:200
  91.1 8.5 %collective-permute-start.4 = (bf16[1,256,640]{2,1,0:T(8,128)(2,1)}, bf16[1,256,640]{2,1,0:T(8,128)(2,1)}, u32[]{:S(2)}, u32[]{:S(2)}) collective-permute-start(bf16[1,256,640]{2,1,0:T(8,128)(2,1)} %collective-permute-done.2), channel_id=1, source_target_pairs={{0,448},{16,464},{32,480},{48,496},{64,0},{80,16},{96,32},{112,48}... | collective-permute-start | bytes 983048 | tf_op jit(solution)/shard_map/ppermute | solution.py:198
  95.3 10.9 %collective-permute-start.5 = (bf16[1,256,640]{2,1,0:T(8,128)(2,1)}, bf16[1,256,640]{2,1,0:T(8,128)(2,1)}, u32[]{:S(2)}, u32[]{:S(2)}) collective-permute-start(bf16[1,256,640]{2,1,0:T(8,128)(2,1)} %collective-permute-done.3), channel_id=1, source_target_pairs={{0,64},{16,80},{32,96},{48,112},{64,128},{80,144},{96,160},{112,17... | collective-permute-start | bytes 983048 | tf_op jit(solution)/shard_map/ppermute | solution.py:200
  101.1 27.5 %collective-permute-start.7 = (bf16[1,256,256]{2,1,0:T(8,128)(2,1)}, bf16[1,256,256]{2,1,0:T(8,128)(2,1)}, u32[]{:S(2)}, u32[]{:S(2)}) collective-permute-start(bf16[1,256,256]{2,1,0:T(8,128)(2,1)} %slice.143), channel_id=1, source_target_pairs={{0,448},{16,464},{32,480},{48,496},{64,0},{80,16},{96,32},{112,48}... | collective-permute-start | bytes 393224 | tf_op jit(solution)/shard_map/ppermute | solution.py:206
  107.8 20.9 %collective-permute-start.6 = (bf16[1,256,384]{2,1,0:T(8,128)(2,1)}, bf16[1,256,384]{2,1,0:T(8,128)(2,1)S(1)}, u32[]{:S(2)}, u32[]{:S(2)}) collective-permute-start(bf16[1,256,384]{2,1,0:T(8,128)(2,1)} %slice.142), channel_id=1, source_target_pairs={{0,64},{16,80},{32,96},{48,112},{64,128},{80,144},{96,160},{112,17... | collective-permute-start | bytes 589832 | tf_op jit(solution)/shard_map/ppermute | solution.py:205
  109.7 23.3 %collective-permute-start.15 = (bf16[3,256,640]{2,1,0:T(8,128)(2,1)S(1)}, bf16[3,256,640]{2,1,0:T(8,128)(2,1)S(1)}, u32[]{:S(2)}, u32[]{:S(2)}) collective-permute-start(bf16[3,256,640]{2,1,0:T(8,128)(2,1)S(1)} %collective-permute-done.13), channel_id=1, source_target_pairs={{0,64},{16,80},{32,96},{48,112},{64,128},{80,144},{96,160},{112,17... | collective-permute-start | bytes 2949128 | tf_op jit(solution)/shard_map/ppermute | solution.py:200
  111.7 23.3 %collective-permute-start.14 = (bf16[3,256,640]{2,1,0:T(8,128)(2,1)S(1)}, bf16[3,256,640]{2,1,0:T(8,128)(2,1)S(1)}, u32[]{:S(2)}, u32[]{:S(2)}) collective-permute-start(bf16[3,256,640]{2,1,0:T(8,128)(2,1)S(1)} %collective-permute-done.12), channel_id=1, source_target_pairs={{0,448},{16,464},{32,480},{48,496},{64,0},{80,16},{96,32},{112,48}... | collective-permute-start | bytes 2949128 | tf_op jit(solution)/shard_map/ppermute | solution.py:198
  116.2 7.2 %copy-start = (bf16[512,8192]{1,0:T(8,128)(2,1)S(1)}, bf16[512,8192]{1,0:T(8,128)(2,1)}, u32[]{:S(2)}) copy-start(bf16[512,8192]{1,0:T(8,128)(2,1)} %all-gather.2.cloned.1.call-done) | copy-start | bytes 25165828
  133.1 19.4 %collective-permute-start.17 = (bf16[3,256,640]{2,1,0:T(8,128)(2,1)S(1)}, bf16[3,256,640]{2,1,0:T(8,128)(2,1)S(1)}, u32[]{:S(2)}, u32[]{:S(2)}) collective-permute-start(bf16[3,256,640]{2,1,0:T(8,128)(2,1)S(1)} %collective-permute-done.15), channel_id=1, source_target_pairs={{0,64},{16,80},{32,96},{48,112},{64,128},{80,144},{96,160},{112,17... | collective-permute-start | bytes 2949128 | tf_op jit(solution)/shard_map/ppermute | solution.py:200
  135.0 19.5 %collective-permute-start.16 = (bf16[3,256,640]{2,1,0:T(8,128)(2,1)S(1)}, bf16[3,256,640]{2,1,0:T(8,128)(2,1)S(1)}, u32[]{:S(2)}, u32[]{:S(2)}) collective-permute-start(bf16[3,256,640]{2,1,0:T(8,128)(2,1)S(1)} %collective-permute-done.14), channel_id=1, source_target_pairs={{0,448},{16,464},{32,480},{48,496},{64,0},{80,16},{96,32},{112,48}... | collective-permute-start | bytes 2949128 | tf_op jit(solution)/shard_map/ppermute | solution.py:198
  152.6 13.6 %collective-permute-start.18 = (bf16[3,256,384]{2,1,0:T(8,128)(2,1)S(1)}, bf16[3,256,384]{2,1,0:T(8,128)(2,1)S(1)}, u32[]{:S(2)}, u32[]{:S(2)}) collective-permute-start(bf16[3,256,384]{2,1,0:T(8,128)(2,1)S(1)} %slice.164), channel_id=1, source_target_pairs={{0,64},{16,80},{32,96},{48,112},{64,128},{80,144},{96,160},{112,17... | collective-permute-start | bytes 1769480 | tf_op jit(solution)/shard_map/ppermute | solution.py:205
  154.5 11.7 %collective-permute-start.19 = (bf16[3,256,256]{2,1,0:T(8,128)(2,1)S(1)}, bf16[3,256,256]{2,1,0:T(8,128)(2,1)S(1)}, u32[]{:S(2)}, u32[]{:S(2)}) collective-permute-start(bf16[3,256,256]{2,1,0:T(8,128)(2,1)S(1)} %slice.165), channel_id=1, source_target_pairs={{0,448},{16,464},{32,480},{48,496},{64,0},{80,16},{96,32},{112,48}... | collective-permute-start | bytes 1179656 | tf_op jit(solution)/shard_map/ppermute | solution.py:206
  169.3 12.7 %copy-start.1 = (f32[512,640]{1,0:T(8,128)}, f32[512,640]{1,0:T(8,128)S(1)}, u32[]{:S(2)}) copy-start(f32[512,640]{1,0:T(8,128)S(1)} %fusion.17.q_ref) | copy-start | bytes 3932164
  169.3 12.0 %collective-permute-start.20 = (bf16[512,128]{1,0:T(8,128)(2,1)S(1)}, bf16[512,128]{1,0:T(8,128)(2,1)S(1)}, u32[]{:S(2)}, u32[]{:S(2)}) collective-permute-start(bf16[512,128]{1,0:T(8,128)(2,1)S(1)} %slice.226), channel_id=1, source_target_pairs={{0,1},{1,0},{2,3},{3,2},{4,5},{5,4},{6,7},{7,6},{8,9},{9,8},{10,11... | collective-permute-start | bytes 393224 | tf_op jit(solution)/shard_map/ppermute | solution.py:264
Sparse Core Ops, SparseCore 0:
  10.0 73.1 all-gather.1

commit v14 on v13

--- a/solution.py
+++ b/solution.py
@@ -60,7 +60,9 @@
 SEGMENT_MOST = 64
 
 
-def attention_kernel(heads, q_ref, k_ref, v_ref, cos_ref, sin_ref, row_seg_ref, col_seg_ref, o_ref):
+def attention_kernel(
+    heads, q_ref, own_ref, other_ref, core_ref, cos_ref, sin_ref, row_seg_ref, col_seg_ref, o_ref
+):
     half = HEAD_DIM // 2
 
     def rope(x, rows):
@@ -69,7 +71,11 @@
         return jnp.concatenate([a * cosine - b * sine, b * cosine + a * sine], axis=1)
 
     n_rows = q_ref.shape[0]
-    keys = rope(k_ref[...].astype(jnp.float32), slice(0, n_rows)).astype(jnp.bfloat16)
+    key_first = core_ref[0:1, 0:1] == 0
+    own, other = own_ref[...], other_ref[...]
+    key_rows = jnp.where(key_first, own, other)
+    value_rows = jnp.where(key_first, other, own)
+    keys = rope(key_rows.astype(jnp.float32), slice(0, n_rows)).astype(jnp.bfloat16)
     scale = HEAD_DIM ** (-0.5)
     reach = max(ROW_TILE, SEGMENT_MOST)
     for r0 in range(0, n_rows, ROW_TILE):
@@ -78,7 +84,7 @@
         rows = slice(r0, c1)
         places_i = lax.broadcasted_iota(jnp.int32, (ROW_TILE, c1 - c0), 0) + r0
         places_j = lax.broadcasted_iota(jnp.int32, (ROW_TILE, c1 - c0), 1) + c0
-        allowed = (row_seg_ref[rows, :] == col_seg_ref[:, c0:c1]) & (places_j <= places_i)
+        allowed = (row_seg_ref[rows, 0:1] == col_seg_ref[:, c0:c1]) & (places_j <= places_i)
         allowed = jnp.concatenate([allowed] * heads, axis=0)
         query = jnp.concatenate(
             [rope(q_ref[rows, h * HEAD_DIM : (h + 1) * HEAD_DIM], rows) for h in range(heads)],
@@ -90,7 +96,7 @@
         weights = jnp.where(allowed, jnp.exp(scores), 0.0)
         total = jnp.sum(weights, axis=1, keepdims=True)
         probabilities = (weights / total).astype(jnp.bfloat16)
-        mixed = jnp.dot(probabilities, v_ref[c0:c1, :], preferred_element_type=jnp.float32)
+        mixed = jnp.dot(probabilities, value_rows[c0:c1], preferred_element_type=jnp.float32)
         for h in range(heads):
             o_ref[rows, h * HEAD_DIM : (h + 1) * HEAD_DIM] = mixed[
                 h * ROW_TILE : (h + 1) * ROW_TILE
@@ -105,7 +111,7 @@
     return jnp.cos(angles), jnp.sin(angles)
 
 
-def attention_kernel_call(projected, cols, key_rows, value_rows, cosine, sine, row_seg, col_seg):
+def attention_kernel_call(projected, cols, own_rows, other_rows, core, cosine, sine, row_seg, col_seg):
     rows = projected.shape[0]
     half_dim = HEAD_DIM // 2
     vmem = pl.BlockSpec(memory_space=pltpu.VMEM)
@@ -113,7 +119,7 @@
     return pl.pallas_call(
         functools.partial(attention_kernel, heads),
         out_shape=jax.ShapeDtypeStruct((rows, cols), jnp.bfloat16),
-        in_specs=[vmem] * 7,
+        in_specs=[vmem] * 8,
         out_specs=vmem,
         cost_estimate=pl.CostEstimate(
             flops=4 * rows * rows * cols + 8 * rows * cols,
@@ -122,8 +128,9 @@
         ),
     )(
         projected,
-        key_rows,
-        value_rows,
+        own_rows,
+        other_rows,
+        jnp.full((1, 128), core, jnp.int32),
         cosine,
         sine,
         row_seg,
@@ -234,7 +241,8 @@
     near = ring_gather(local_weights, "batch", 1, y_hi)
     others = jnp.stack([near[(yh + r) % y_hi] for r in range(1, y_hi)])
     cosine, sine = rope_tables(positions_in_segment(segment_ids))
-    row_seg, col_seg = segment_ids[:, None], segment_ids[None, :]
+    row_seg = jnp.broadcast_to(segment_ids[:, None], (segment_ids.shape[0], 128))
+    col_seg = segment_ids[None, :]
     others, cosine, sine, row_seg, col_seg = lax.optimization_barrier(
         (others, cosine, sine, row_seg, col_seg)
     )
@@ -262,10 +270,8 @@
     own_rows = projected[:, query_cols:].astype(jnp.bfloat16)
     partner = [(w, w ^ 1) for w in range(n_weight)]
     other_rows = lax.ppermute(own_rows, "weight", perm=partner)
-    key_rows = jnp.where(core == 0, own_rows, other_rows)
-    value_rows = jnp.where(core == 0, other_rows, own_rows)
     return attention_kernel_call(
-        projected, query_cols, key_rows, value_rows, cosine, sine, row_seg, col_seg
+        projected, query_cols, own_rows, other_rows, core, cosine, sine, row_seg, col_seg
     )
 
 

time: 197 us -> 198 us (level)
  no operation moved by 1% of the time
where the time goes in v14:
time: 198 us; the launch traced here: 196 us
  starting transfers between devices  86.3 us (44%)
  waiting for transfers between devices  50.3 us (25%)
  matrix products  24.3 us (12%)
  between operations  15.2 us (8%)
  other arithmetic  7.54 us (4%)
  Pallas kernels  6.08 us (3%)
  local copies, waits for them, and re-layouts  5.97 us (3%)
    ppermute x6, starting transfers between devices, ring_matmul(): from_right = lax.ppermute(from_right, axis, perm=moved(-1))  35 us
    dot_general x32, matrix products, product(): term = jnp.dot(lhs, part[piece], preferred_element_type=jnp.float32)  24.3 us
    ppermute x6, waiting for transfers between devices, ring_matmul(): from_right = lax.ppermute(from_right, axis, perm=moved(-1))  18.4 us
    ppermute x1, waiting for transfers between devices, ring_gather(): lax.ppermute(from_left[..., :cut], axis, perm=moved(1))  15.7 us
    ppermute x6, starting transfers between devices, ring_matmul(): from_left = lax.ppermute(from_left, axis, perm=moved(1))  11.5 us
    ppermute x1, starting transfers between devices, per_device(): other_rows = lax.ppermute(own_rows, 'weight', perm=partner)  11 us
    ppermute x6, waiting for transfers between devices, ring_matmul(): from_left = lax.ppermute(from_left, axis, perm=moved(1))  10.1 us
    ppermute x2, starting transfers between devices, ring_matmul(): lax.ppermute(from_right[..., cut:], axis, perm=moved(-1))  9.77 us
  transfers between devices with their start and end apart: 22, of which 6 were waited for; matrix products, arithmetic and copies ran while one was open for 16% of the time, Pallas kernels for 0%

profile of v14, /device:TPU:7, one launch (start us, length us, event | category | flops | bytes accessed | tf_op | source)
XLA Modules:
  0.0 195.7 jit_solution(16249982643996079548)
XLA Ops:
  6.5 1.3 fusion.18
  7.9 2.0 %fusion.20 = bf16[32,8192]{1,0:T(8,128)(2,1)} fusion(bf16[32,8192]{1,0:T(8,128)(2,1)} %param.6, f32[8192]{0:T(1024)} %param.8, f32[32]{0:T(128)S(1)} %add_rsqrt_fusion), kind=kLoop, calls=%fused_computation.35 | loop fusion | flops 1048576 | bytes 1081472 | tf_op jit(solution)/shard_map/convert_element_type | solution.py:235
  9.9 0.9 dynamic-slice_select_fusion
  10.9 0.8 fusion.121
  11.6 5.9 %collective-permute-start.8 = (bf16[256,640]{1,0:T(8,128)(2,1)S(1)}, bf16[256,640]{1,0:T(8,128)(2,1)S(1)}, u32[]{:S(2)}, u32[]{:S(2)}) collective-permute-start(bf16[256,640]{1,0:T(8,128)(2,1)S(1)} %get-tuple-element.25), channel_id=1, source_target_pairs={{0,48},{16,0},{32,16},{48,32},{64,112},{80,64},{96,80},{112,96},{1... | collective-permute-start | bytes 983048 | tf_op jit(solution)/shard_map/ppermute | solution.py:158
  17.5 1.9 collective-permute-start.9
  19.4 10.7 %collective-permute-start = (bf16[1,256,640]{2,1,0:T(8,128)(2,1)}, bf16[1,256,640]{2,1,0:T(8,128)(2,1)}, u32[]{:S(2)}, u32[]{:S(2)}) collective-permute-start(bf16[1,256,640]{2,1,0:T(8,128)(2,1)} %get-tuple-element.24), channel_id=1, source_target_pairs={{0,448},{16,464},{32,480},{48,496},{64,0},{80,16},{96,32},{112,48}... | collective-permute-start | bytes 983048 | tf_op jit(solution)/shard_map/ppermute | solution.py:205
  30.1 1.9 collective-permute-start.1
  34.3 1.8 multiply_sine_fusion
  36.1 5.5 %collective-permute-start.11 = (bf16[256,256]{1,0:T(8,128)(2,1)S(1)}, bf16[256,256]{1,0:T(8,128)(2,1)S(1)}, u32[]{:S(2)}, u32[]{:S(2)}) collective-permute-start(bf16[256,256]{1,0:T(8,128)(2,1)S(1)} %slice.145), channel_id=1, source_target_pairs={{0,48},{16,0},{32,16},{48,32},{64,112},{80,64},{96,80},{112,96},{1... | collective-permute-start | bytes 393224 | tf_op jit(solution)/shard_map/ppermute | solution.py:166
  41.6 1.9 collective-permute-start.10
  43.7 15.7 %collective-permute-done.10 = bf16[256,384]{1,0:T(8,128)(2,1)S(1)} collective-permute-done((bf16[256,384]{1,0:T(8,128)(2,1)S(1)}, bf16[256,384]{1,0:T(8,128)(2,1)S(1)}, u32[]{:S(2)}, u32[]{:S(2)}) %collective-permute-start.10) | collective-permute-done | bytes 196640 | tf_op jit(solution)/shard_map/ppermute | solution.py:165
  59.7 0.8 broadcast_in_dim.43.row_seg_ref
  60.6 6.4 %collective-permute-start.12 = (bf16[3,256,640]{2,1,0:T(8,128)(2,1)S(1)}, bf16[3,256,640]{2,1,0:T(8,128)(2,1)S(1)}, u32[]{:S(2)}, u32[]{:S(2)}) collective-permute-start(bf16[3,256,640]{2,1,0:T(8,128)(2,1)S(1)} %pad_maximum_fusion), channel_id=1, source_target_pairs={{0,448},{16,464},{32,480},{48,496},{64,0},{80,16},{96,32},{112,48}... | collective-permute-start | bytes 2949128 | tf_op jit(solution)/shard_map/ppermute | solution.py:205
  67.0 1.9 collective-permute-start.13
  68.9 4.6 %collective-permute-start.2 = (bf16[1,256,640]{2,1,0:T(8,128)(2,1)}, bf16[1,256,640]{2,1,0:T(8,128)(2,1)}, u32[]{:S(2)}, u32[]{:S(2)}) collective-permute-start(bf16[1,256,640]{2,1,0:T(8,128)(2,1)} %collective-permute-done), channel_id=1, source_target_pairs={{0,448},{16,464},{32,480},{48,496},{64,0},{80,16},{96,32},{112,48}... | collective-permute-start | bytes 983048 | tf_op jit(solution)/shard_map/ppermute | solution.py:205
  73.5 1.9 collective-permute-start.3
  75.4 16.5 %collective-permute-done.2 = bf16[1,256,640]{2,1,0:T(8,128)(2,1)} collective-permute-done((bf16[1,256,640]{2,1,0:T(8,128)(2,1)}, bf16[1,256,640]{2,1,0:T(8,128)(2,1)}, u32[]{:S(2)}, u32[]{:S(2)}) %collective-permute-start.2) | collective-permute-done | bytes 327712 | tf_op jit(solution)/shard_map/ppermute | solution.py:205
  91.9 4.2 %collective-permute-start.4 = (bf16[1,256,640]{2,1,0:T(8,128)(2,1)}, bf16[1,256,640]{2,1,0:T(8,128)(2,1)}, u32[]{:S(2)}, u32[]{:S(2)}) collective-permute-start(bf16[1,256,640]{2,1,0:T(8,128)(2,1)} %collective-permute-done.2), channel_id=1, source_target_pairs={{0,448},{16,464},{32,480},{48,496},{64,0},{80,16},{96,32},{112,48}... | collective-permute-start | bytes 983048 | tf_op jit(solution)/shard_map/ppermute | solution.py:205
  96.1 1.9 collective-permute-start.5
  98.4 2.0 %collective-permute-done.4 = bf16[1,256,640]{2,1,0:T(8,128)(2,1)} collective-permute-done((bf16[1,256,640]{2,1,0:T(8,128)(2,1)}, bf16[1,256,640]{2,1,0:T(8,128)(2,1)}, u32[]{:S(2)}, u32[]{:S(2)}) %collective-permute-start.4) | collective-permute-done | bytes 327712 | tf_op jit(solution)/shard_map/ppermute | solution.py:205
  100.4 1.6 slice.143
  102.0 5.0 %collective-permute-start.7 = (bf16[1,256,256]{2,1,0:T(8,128)(2,1)}, bf16[1,256,256]{2,1,0:T(8,128)(2,1)}, u32[]{:S(2)}, u32[]{:S(2)}) collective-permute-start(bf16[1,256,256]{2,1,0:T(8,128)(2,1)} %slice.143), channel_id=1, source_target_pairs={{0,448},{16,464},{32,480},{48,496},{64,0},{80,16},{96,32},{112,48}... | collective-permute-start | bytes 393224 | tf_op jit(solution)/shard_map/ppermute | solution.py:213
  107.0 1.6 slice.142
  108.6 1.9 collective-permute-start.6
  110.6 1.9 collective-permute-start.15
  112.5 4.6 %collective-permute-start.14 = (bf16[3,256,640]{2,1,0:T(8,128)(2,1)S(1)}, bf16[3,256,640]{2,1,0:T(8,128)(2,1)S(1)}, u32[]{:S(2)}, u32[]{:S(2)}) collective-permute-start(bf16[3,256,640]{2,1,0:T(8,128)(2,1)S(1)} %collective-permute-done.12), channel_id=1, source_target_pairs={{0,448},{16,464},{32,480},{48,496},{64,0},{80,16},{96,32},{112,48}... | collective-permute-start | bytes 2949128 | tf_op jit(solution)/shard_map/ppermute | solution.py:205
  117.1 1.5 fusion.41
  118.6 1.7 fusion.33
  120.2 1.3 fusion.34
  121.6 1.3 fusion.31
  122.9 1.3 fusion.32
  124.2 1.4 fusion.43
  126.7 1.4 convolution_add_fusion.12
  128.1 1.4 fusion.46
  129.5 1.3 fusion.35
  130.8 1.4 convolution_add_fusion.11
  132.1 1.4 fusion
  133.9 1.9 collective-permute-start.17
  135.8 4.6 %collective-permute-start.16 = (bf16[3,256,640]{2,1,0:T(8,128)(2,1)S(1)}, bf16[3,256,640]{2,1,0:T(8,128)(2,1)S(1)}, u32[]{:S(2)}, u32[]{:S(2)}) collective-permute-start(bf16[3,256,640]{2,1,0:T(8,128)(2,1)S(1)} %collective-permute-done.14), channel_id=1, source_target_pairs={{0,448},{16,464},{32,480},{48,496},{64,0},{80,16},{96,32},{112,48}... | collective-permute-start | bytes 2949128 | tf_op jit(solution)/shard_map/ppermute | solution.py:205
  143.2 10.1 %collective-permute-done.17 = bf16[3,256,640]{2,1,0:T(8,128)(2,1)S(1)} collective-permute-done((bf16[3,256,640]{2,1,0:T(8,128)(2,1)S(1)}, bf16[3,256,640]{2,1,0:T(8,128)(2,1)S(1)}, u32[]{:S(2)}, u32[]{:S(2)}) %collective-permute-start.17) | collective-permute-done | bytes 983072 | tf_op jit(solution)/shard_map/ppermute | solution.py:207
  153.4 1.9 collective-permute-start.18
  155.4 4.8 %collective-permute-start.19 = (bf16[3,256,256]{2,1,0:T(8,128)(2,1)S(1)}, bf16[3,256,256]{2,1,0:T(8,128)(2,1)S(1)}, u32[]{:S(2)}, u32[]{:S(2)}) collective-permute-start(bf16[3,256,256]{2,1,0:T(8,128)(2,1)S(1)} %slice.165), channel_id=1, source_target_pairs={{0,448},{16,464},{32,480},{48,496},{64,0},{80,16},{96,32},{112,48}... | collective-permute-start | bytes 1179656 | tf_op jit(solution)/shard_map/ppermute | solution.py:213
  162.0 5.0 %collective-permute-done.18 = bf16[3,256,384]{2,1,0:T(8,128)(2,1)S(1)} collective-permute-done((bf16[3,256,384]{2,1,0:T(8,128)(2,1)S(1)}, bf16[3,256,384]{2,1,0:T(8,128)(2,1)S(1)}, u32[]{:S(2)}, u32[]{:S(2)}) %collective-permute-start.18) | collective-permute-done | bytes 589856 | tf_op jit(solution)/shard_map/ppermute | solution.py:212
  168.7 1.4 fusion.17.q_ref
  170.1 11.0 %collective-permute-start.20 = (bf16[512,128]{1,0:T(8,128)(2,1)S(1)}, bf16[512,128]{1,0:T(8,128)(2,1)S(1)}, u32[]{:S(2)}, u32[]{:S(2)}) collective-permute-start(bf16[512,128]{1,0:T(8,128)(2,1)S(1)} %slice.226.own_ref), channel_id=1, source_target_pairs={{0,1},{1,0},{2,3},{3,2},{4,5},{5,4},{6,7},{7,6},{8,9},{9,8},{10,11... | collective-permute-start | bytes 393224 | tf_op jit(solution)/shard_map/ppermute | solution.py:272
  181.2 1.0 collective-permute-done.20.other_ref
  182.8 6.1 %shard_map.64 = bf16[512,512]{1,0:T(8,128)(2,1)} custom-call(f32[512,640]{1,0:T(8,128)} %copy-done.1, bf16[512,128]{1,0:T(8,128)(2,1)} %copy-done.3, bf16[512,128]{1,0:T(8,128)(2,1)} %copy-done.4, s32[1,128]{1,0:T(1,128)} %broadcast_in_dim.45.core_ref, f32[512,64]{1,0:T(8,128)} %get-tuple-element.17.cos_ref, f32[512,64]{1,0:T(8,128)} %get-tuple-element.18.sin_ref, ...), custom_call_target="tpu_custom_call" | custom-call | flops 538968064 | bytes 2097152 | tf_op jit(solution)/shard_map/pallas_call | solution.py:119
  (74 shorter events, 10.5 us)
Async XLA Ops:
  6.5 4.3 %copy-start.2 = (bf16[256,512]{1,0:T(8,128)(2,1)S(1)}, bf16[256,512]{1,0:T(8,128)(2,1)}, u32[]{:S(2)}) copy-start(bf16[256,512]{1,0:T(8,128)(2,1)} %param.9) | copy-start | bytes 786436
  6.5 104.0 %all-gather.2.cloned.1.call-start = ((), (), s32[]{:S(2)}) async-start(), calls=%async_computation | async-start | bytes 8912896 | tf_op jit(solution)/shard_map/all_gather | solution.py:249
  7.8 24.3 %copy-start.5 = (s32[512]{0:T(512)S(1)}, s32[512]{0:T(512)}, u32[]{:S(2)}) copy-start(s32[512]{0:T(512)} %param.7) | copy-start | bytes 6148
  11.6 24.5 %collective-permute-start.8 = (bf16[256,640]{1,0:T(8,128)(2,1)S(1)}, bf16[256,640]{1,0:T(8,128)(2,1)S(1)}, u32[]{:S(2)}, u32[]{:S(2)}) collective-permute-start(bf16[256,640]{1,0:T(8,128)(2,1)S(1)} %get-tuple-element.25), channel_id=1, source_target_pairs={{0,48},{16,0},{32,16},{48,32},{64,112},{80,64},{96,80},{112,96},{1... | collective-permute-start | bytes 983048 | tf_op jit(solution)/shard_map/ppermute | solution.py:158
  17.5 24.1 %collective-permute-start.9 = (bf16[256,640]{1,0:T(8,128)(2,1)S(1)}, bf16[256,640]{1,0:T(8,128)(2,1)S(1)}, u32[]{:S(2)}, u32[]{:S(2)}) collective-permute-start(bf16[256,640]{1,0:T(8,128)(2,1)S(1)} %get-tuple-element.25), channel_id=1, source_target_pairs={{0,16},{16,32},{32,48},{48,0},{64,80},{80,96},{96,112},{112,64},{1... | collective-permute-start | bytes 983048 | tf_op jit(solution)/shard_map/ppermute | solution.py:160
  19.4 49.5 %collective-permute-start = (bf16[1,256,640]{2,1,0:T(8,128)(2,1)}, bf16[1,256,640]{2,1,0:T(8,128)(2,1)}, u32[]{:S(2)}, u32[]{:S(2)}) collective-permute-start(bf16[1,256,640]{2,1,0:T(8,128)(2,1)} %get-tuple-element.24), channel_id=1, source_target_pairs={{0,448},{16,464},{32,480},{48,496},{64,0},{80,16},{96,32},{112,48}... | collective-permute-start | bytes 983048 | tf_op jit(solution)/shard_map/ppermute | solution.py:205
  30.1 43.4 %collective-permute-start.1 = (bf16[1,256,640]{2,1,0:T(8,128)(2,1)}, bf16[1,256,640]{2,1,0:T(8,128)(2,1)}, u32[]{:S(2)}, u32[]{:S(2)}) collective-permute-start(bf16[1,256,640]{2,1,0:T(8,128)(2,1)} %get-tuple-element.24), channel_id=1, source_target_pairs={{0,64},{16,80},{32,96},{48,112},{64,128},{80,144},{96,160},{112,17... | collective-permute-start | bytes 983048 | tf_op jit(solution)/shard_map/ppermute | solution.py:207
  36.1 7.6 %collective-permute-start.11 = (bf16[256,256]{1,0:T(8,128)(2,1)S(1)}, bf16[256,256]{1,0:T(8,128)(2,1)S(1)}, u32[]{:S(2)}, u32[]{:S(2)}) collective-permute-start(bf16[256,256]{1,0:T(8,128)(2,1)S(1)} %slice.145), channel_id=1, source_target_pairs={{0,48},{16,0},{32,16},{48,32},{64,112},{80,64},{96,80},{112,96},{1... | collective-permute-start | bytes 393224 | tf_op jit(solution)/shard_map/ppermute | solution.py:166
  41.6 17.8 %collective-permute-start.10 = (bf16[256,384]{1,0:T(8,128)(2,1)S(1)}, bf16[256,384]{1,0:T(8,128)(2,1)S(1)}, u32[]{:S(2)}, u32[]{:S(2)}) collective-permute-start(bf16[256,384]{1,0:T(8,128)(2,1)S(1)} %slice.144), channel_id=1, source_target_pairs={{0,16},{16,32},{32,48},{48,0},{64,80},{80,96},{96,112},{112,64},{1... | collective-permute-start | bytes 589832 | tf_op jit(solution)/shard_map/ppermute | solution.py:165
  60.6 49.9 %collective-permute-start.12 = (bf16[3,256,640]{2,1,0:T(8,128)(2,1)S(1)}, bf16[3,256,640]{2,1,0:T(8,128)(2,1)S(1)}, u32[]{:S(2)}, u32[]{:S(2)}) collective-permute-start(bf16[3,256,640]{2,1,0:T(8,128)(2,1)S(1)} %pad_maximum_fusion), channel_id=1, source_target_pairs={{0,448},{16,464},{32,480},{48,496},{64,0},{80,16},{96,32},{112,48}... | collective-permute-start | bytes 2949128 | tf_op jit(solution)/shard_map/ppermute | solution.py:205
  67.0 43.5 %collective-permute-start.13 = (bf16[3,256,640]{2,1,0:T(8,128)(2,1)S(1)}, bf16[3,256,640]{2,1,0:T(8,128)(2,1)S(1)}, u32[]{:S(2)}, u32[]{:S(2)}) collective-permute-start(bf16[3,256,640]{2,1,0:T(8,128)(2,1)S(1)} %pad_maximum_fusion), channel_id=1, source_target_pairs={{0,64},{16,80},{32,96},{48,112},{64,128},{80,144},{96,160},{112,17... | collective-permute-start | bytes 2949128 | tf_op jit(solution)/shard_map/ppermute | solution.py:207
  68.9 23.0 %collective-permute-start.2 = (bf16[1,256,640]{2,1,0:T(8,128)(2,1)}, bf16[1,256,640]{2,1,0:T(8,128)(2,1)}, u32[]{:S(2)}, u32[]{:S(2)}) collective-permute-start(bf16[1,256,640]{2,1,0:T(8,128)(2,1)} %collective-permute-done), channel_id=1, source_target_pairs={{0,448},{16,464},{32,480},{48,496},{64,0},{80,16},{96,32},{112,48}... | collective-permute-start | bytes 983048 | tf_op jit(solution)/shard_map/ppermute | solution.py:205
  73.5 22.6 %collective-permute-start.3 = (bf16[1,256,640]{2,1,0:T(8,128)(2,1)}, bf16[1,256,640]{2,1,0:T(8,128)(2,1)}, u32[]{:S(2)}, u32[]{:S(2)}) collective-permute-start(bf16[1,256,640]{2,1,0:T(8,128)(2,1)} %collective-permute-done.1), channel_id=1, source_target_pairs={{0,64},{16,80},{32,96},{48,112},{64,128},{80,144},{96,160},{112,17... | collective-permute-start | bytes 983048 | tf_op jit(solution)/shard_map/ppermute | solution.py:207
  91.9 8.5 %collective-permute-start.4 = (bf16[1,256,640]{2,1,0:T(8,128)(2,1)}, bf16[1,256,640]{2,1,0:T(8,128)(2,1)}, u32[]{:S(2)}, u32[]{:S(2)}) collective-permute-start(bf16[1,256,640]{2,1,0:T(8,128)(2,1)} %collective-permute-done.2), channel_id=1, source_target_pairs={{0,448},{16,464},{32,480},{48,496},{64,0},{80,16},{96,32},{112,48}... | collective-permute-start | bytes 983048 | tf_op jit(solution)/shard_map/ppermute | solution.py:205
  96.1 10.9 %collective-permute-start.5 = (bf16[1,256,640]{2,1,0:T(8,128)(2,1)}, bf16[1,256,640]{2,1,0:T(8,128)(2,1)}, u32[]{:S(2)}, u32[]{:S(2)}) collective-permute-start(bf16[1,256,640]{2,1,0:T(8,128)(2,1)} %collective-permute-done.3), channel_id=1, source_target_pairs={{0,64},{16,80},{32,96},{48,112},{64,128},{80,144},{96,160},{112,17... | collective-permute-start | bytes 983048 | tf_op jit(solution)/shard_map/ppermute | solution.py:207
  102.0 27.5 %collective-permute-start.7 = (bf16[1,256,256]{2,1,0:T(8,128)(2,1)}, bf16[1,256,256]{2,1,0:T(8,128)(2,1)}, u32[]{:S(2)}, u32[]{:S(2)}) collective-permute-start(bf16[1,256,256]{2,1,0:T(8,128)(2,1)} %slice.143), channel_id=1, source_target_pairs={{0,448},{16,464},{32,480},{48,496},{64,0},{80,16},{96,32},{112,48}... | collective-permute-start | bytes 393224 | tf_op jit(solution)/shard_map/ppermute | solution.py:213
  108.6 20.9 %collective-permute-start.6 = (bf16[1,256,384]{2,1,0:T(8,128)(2,1)}, bf16[1,256,384]{2,1,0:T(8,128)(2,1)S(1)}, u32[]{:S(2)}, u32[]{:S(2)}) collective-permute-start(bf16[1,256,384]{2,1,0:T(8,128)(2,1)} %slice.142), channel_id=1, source_target_pairs={{0,64},{16,80},{32,96},{48,112},{64,128},{80,144},{96,160},{112,17... | collective-permute-start | bytes 589832 | tf_op jit(solution)/shard_map/ppermute | solution.py:212
  110.6 23.3 %collective-permute-start.15 = (bf16[3,256,640]{2,1,0:T(8,128)(2,1)S(1)}, bf16[3,256,640]{2,1,0:T(8,128)(2,1)S(1)}, u32[]{:S(2)}, u32[]{:S(2)}) collective-permute-start(bf16[3,256,640]{2,1,0:T(8,128)(2,1)S(1)} %collective-permute-done.13), channel_id=1, source_target_pairs={{0,64},{16,80},{32,96},{48,112},{64,128},{80,144},{96,160},{112,17... | collective-permute-start | bytes 2949128 | tf_op jit(solution)/shard_map/ppermute | solution.py:207
  112.5 23.3 %collective-permute-start.14 = (bf16[3,256,640]{2,1,0:T(8,128)(2,1)S(1)}, bf16[3,256,640]{2,1,0:T(8,128)(2,1)S(1)}, u32[]{:S(2)}, u32[]{:S(2)}) collective-permute-start(bf16[3,256,640]{2,1,0:T(8,128)(2,1)S(1)} %collective-permute-done.12), channel_id=1, source_target_pairs={{0,448},{16,464},{32,480},{48,496},{64,0},{80,16},{96,32},{112,48}... | collective-permute-start | bytes 2949128 | tf_op jit(solution)/shard_map/ppermute | solution.py:205
  117.1 7.2 %copy-start = (bf16[512,8192]{1,0:T(8,128)(2,1)S(1)}, bf16[512,8192]{1,0:T(8,128)(2,1)}, u32[]{:S(2)}) copy-start(bf16[512,8192]{1,0:T(8,128)(2,1)} %all-gather.2.cloned.1.call-done) | copy-start | bytes 25165828
  133.9 19.4 %collective-permute-start.17 = (bf16[3,256,640]{2,1,0:T(8,128)(2,1)S(1)}, bf16[3,256,640]{2,1,0:T(8,128)(2,1)S(1)}, u32[]{:S(2)}, u32[]{:S(2)}) collective-permute-start(bf16[3,256,640]{2,1,0:T(8,128)(2,1)S(1)} %collective-permute-done.15), channel_id=1, source_target_pairs={{0,64},{16,80},{32,96},{48,112},{64,128},{80,144},{96,160},{112,17... | collective-permute-start | bytes 2949128 | tf_op jit(solution)/shard_map/ppermute | solution.py:207
  135.8 19.5 %collective-permute-start.16 = (bf16[3,256,640]{2,1,0:T(8,128)(2,1)S(1)}, bf16[3,256,640]{2,1,0:T(8,128)(2,1)S(1)}, u32[]{:S(2)}, u32[]{:S(2)}) collective-permute-start(bf16[3,256,640]{2,1,0:T(8,128)(2,1)S(1)} %collective-permute-done.14), channel_id=1, source_target_pairs={{0,448},{16,464},{32,480},{48,496},{64,0},{80,16},{96,32},{112,48}... | collective-permute-start | bytes 2949128 | tf_op jit(solution)/shard_map/ppermute | solution.py:205
  153.4 13.6 %collective-permute-start.18 = (bf16[3,256,384]{2,1,0:T(8,128)(2,1)S(1)}, bf16[3,256,384]{2,1,0:T(8,128)(2,1)S(1)}, u32[]{:S(2)}, u32[]{:S(2)}) collective-permute-start(bf16[3,256,384]{2,1,0:T(8,128)(2,1)S(1)} %slice.164), channel_id=1, source_target_pairs={{0,64},{16,80},{32,96},{48,112},{64,128},{80,144},{96,160},{112,17... | collective-permute-start | bytes 1769480 | tf_op jit(solution)/shard_map/ppermute | solution.py:212
  155.4 11.7 %collective-permute-start.19 = (bf16[3,256,256]{2,1,0:T(8,128)(2,1)S(1)}, bf16[3,256,256]{2,1,0:T(8,128)(2,1)S(1)}, u32[]{:S(2)}, u32[]{:S(2)}) collective-permute-start(bf16[3,256,256]{2,1,0:T(8,128)(2,1)S(1)} %slice.165), channel_id=1, source_target_pairs={{0,448},{16,464},{32,480},{48,496},{64,0},{80,16},{96,32},{112,48}... | collective-permute-start | bytes 1179656 | tf_op jit(solution)/shard_map/ppermute | solution.py:213
  170.1 12.6 %copy-start.1 = (f32[512,640]{1,0:T(8,128)}, f32[512,640]{1,0:T(8,128)S(1)}, u32[]{:S(2)}) copy-start(f32[512,640]{1,0:T(8,128)S(1)} %fusion.17.q_ref) | copy-start | bytes 3932164
  170.1 12.6 %copy-start.3 = (bf16[512,128]{1,0:T(8,128)(2,1)}, bf16[512,128]{1,0:T(8,128)(2,1)S(1)}, u32[]{:S(2)}) copy-start(bf16[512,128]{1,0:T(8,128)(2,1)S(1)} %slice.226.own_ref) | copy-start | bytes 393220
  170.1 12.0 %collective-permute-start.20 = (bf16[512,128]{1,0:T(8,128)(2,1)S(1)}, bf16[512,128]{1,0:T(8,128)(2,1)S(1)}, u32[]{:S(2)}, u32[]{:S(2)}) collective-permute-start(bf16[512,128]{1,0:T(8,128)(2,1)S(1)} %slice.226.own_ref), channel_id=1, source_target_pairs={{0,1},{1,0},{2,3},{3,2},{4,5},{5,4},{6,7},{7,6},{8,9},{9,8},{10,11... | collective-permute-start | bytes 393224 | tf_op jit(solution)/shard_map/ppermute | solution.py:272
  182.1 0.6 copy-start.4
Sparse Core Ops, SparseCore 0:
  10.0 73.1 all-gather.1

commit v15 on v14

--- a/solution.py
+++ b/solution.py
@@ -61,7 +61,8 @@
 
 
 def attention_kernel(
-    heads, q_ref, own_ref, other_ref, core_ref, cos_ref, sin_ref, row_seg_ref, col_seg_ref, o_ref
+    heads, qa_ref, qb_ref, own_ref, other_ref, core_ref, cos_ref, sin_ref, row_seg_ref, col_seg_ref,
+    o_ref,
 ):
     half = HEAD_DIM // 2
 
@@ -70,7 +71,7 @@
         a, b = x[:, :half], x[:, half:]
         return jnp.concatenate([a * cosine - b * sine, b * cosine + a * sine], axis=1)
 
-    n_rows = q_ref.shape[0]
+    n_rows = qa_ref.shape[0]
     key_first = core_ref[0:1, 0:1] == 0
     own, other = own_ref[...], other_ref[...]
     key_rows = jnp.where(key_first, own, other)
@@ -87,7 +88,14 @@
         allowed = (row_seg_ref[rows, 0:1] == col_seg_ref[:, c0:c1]) & (places_j <= places_i)
         allowed = jnp.concatenate([allowed] * heads, axis=0)
         query = jnp.concatenate(
-            [rope(q_ref[rows, h * HEAD_DIM : (h + 1) * HEAD_DIM], rows) for h in range(heads)],
+            [
+                rope(
+                    qa_ref[rows, h * HEAD_DIM : (h + 1) * HEAD_DIM]
+                    + qb_ref[rows, h * HEAD_DIM : (h + 1) * HEAD_DIM],
+                    rows,
+                )
+                for h in range(heads)
+            ],
             axis=0,
         ).astype(jnp.bfloat16)
         scores = lax.dot_general(
@@ -111,15 +119,17 @@
     return jnp.cos(angles), jnp.sin(angles)
 
 
-def attention_kernel_call(projected, cols, own_rows, other_rows, core, cosine, sine, row_seg, col_seg):
-    rows = projected.shape[0]
+def attention_kernel_call(
+    query_a, query_b, cols, own_rows, other_rows, core_flag, cosine, sine, row_seg, col_seg
+):
+    rows = query_a.shape[0]
     half_dim = HEAD_DIM // 2
     vmem = pl.BlockSpec(memory_space=pltpu.VMEM)
     heads = cols // HEAD_DIM
     return pl.pallas_call(
         functools.partial(attention_kernel, heads),
         out_shape=jax.ShapeDtypeStruct((rows, cols), jnp.bfloat16),
-        in_specs=[vmem] * 8,
+        in_specs=[vmem] * 9,
         out_specs=vmem,
         cost_estimate=pl.CostEstimate(
             flops=4 * rows * rows * cols + 8 * rows * cols,
@@ -127,10 +137,11 @@
             bytes_accessed=rows * cols * 6 + rows * HEAD_DIM * 4 + rows * half_dim * 8,
         ),
     )(
-        projected,
+        query_a,
+        query_b,
         own_rows,
         other_rows,
-        jnp.full((1, 128), core, jnp.int32),
+        core_flag,
         cosine,
         sine,
         row_seg,
@@ -243,8 +254,9 @@
     cosine, sine = rope_tables(positions_in_segment(segment_ids))
     row_seg = jnp.broadcast_to(segment_ids[:, None], (segment_ids.shape[0], 128))
     col_seg = segment_ids[None, :]
-    others, cosine, sine, row_seg, col_seg = lax.optimization_barrier(
-        (others, cosine, sine, row_seg, col_seg)
+    core_flag = jnp.full((1, 128), core, jnp.int32)
+    others, cosine, sine, row_seg, col_seg, core_flag = lax.optimization_barrier(
+        (others, cosine, sine, row_seg, col_seg, core_flag)
     )
     gathered = lax.all_gather(normed, "weight", axis=0, tiled=True)
     pack_rows = gathered.shape[0]
@@ -266,12 +278,20 @@
         lambda z: [(z * y_hi + (yh + r) % y_hi) * shard for r in range(1, y_hi)],
         True,
     )
-    projected = own_part + other_part
-    own_rows = projected[:, query_cols:].astype(jnp.bfloat16)
+    own_rows = (own_part[:, query_cols:] + other_part[:, query_cols:]).astype(jnp.bfloat16)
     partner = [(w, w ^ 1) for w in range(n_weight)]
     other_rows = lax.ppermute(own_rows, "weight", perm=partner)
     return attention_kernel_call(
-        projected, query_cols, own_rows, other_rows, core, cosine, sine, row_seg, col_seg
+        own_part,
+        other_part,
+        query_cols,
+        own_rows,
+        other_rows,
+        core_flag,
+        cosine,
+        sine,
+        row_seg,
+        col_seg,
     )
 
 

time: 198 us -> 215 us (1.086)
  waiting for transfers between devices: 50.3 us -> 76.7 us
  starting transfers between devices: 86.3 us -> 77.9 us
    ppermute x1, waiting for transfers between devices: 0.01 us -> 13.6 us  [ring_gather(): from_left = lax.ppermute(from_left, axis, perm=moved(1))]
    ppermute x6, starting transfers between devices: 35 us -> 29.5 us  [ring_matmul(): from_right = lax.ppermute(from_right, axis, perm=moved(-1))]
    ppermute x6, waiting for transfers between devices: 18.4 us -> 23.7 us  [ring_matmul(): from_right = lax.ppermute(from_right, axis, perm=moved(-1))]
    ppermute x6, waiting for transfers between devices: 10.1 us -> 14.9 us  [ring_matmul(): from_left = lax.ppermute(from_left, axis, perm=moved(1))]
    ppermute x1, starting transfers between devices: 11 us -> 8.23 us  [per_device(): other_rows = lax.ppermute(own_rows, 'weight', perm=partner)]
    ppermute x1, waiting for transfers between devices: 0.01 us -> 2.59 us  [ring_gather(): from_right = lax.ppermute(from_right, axis, perm=moved(-1))]
  transfers between devices with their start and end apart: 22 -> 22, of which waited for: 6 -> 9; matrix products, arithmetic and copies ran while one was open for 16% -> 15% of each run, Pallas kernels for 0% -> 0%
where the time goes in v15:
time: 215 us; the launch traced here: 213 us
  starting transfers between devices  77.9 us (36%)
  waiting for transfers between devices  76.7 us (36%)
  matrix products  22.5 us (10%)
  between operations  15.2 us (7%)
  other arithmetic  7.58 us (4%)
  local copies, waits for them, and re-layouts  6.55 us (3%)
  Pallas kernels  6.44 us (3%)
    ppermute x6, starting transfers between devices, ring_matmul(): from_right = lax.ppermute(from_right, axis, perm=moved(-1))  29.5 us
    ppermute x6, waiting for transfers between devices, ring_matmul(): from_right = lax.ppermute(from_right, axis, perm=moved(-1))  23.7 us
    dot_general x32, matrix products, product(): term = jnp.dot(lhs, part[piece], preferred_element_type=jnp.float32)  22.5 us
    ppermute x1, waiting for transfers between devices, ring_gather(): lax.ppermute(from_left[..., :cut], axis, perm=moved(1))  17 us
    ppermute x6, waiting for transfers between devices, ring_matmul(): from_left = lax.ppermute(from_left, axis, perm=moved(1))  14.9 us
    ppermute x1, waiting for transfers between devices, ring_gather(): from_left = lax.ppermute(from_left, axis, perm=moved(1))  13.6 us
    ppermute x6, starting transfers between devices, ring_matmul(): from_left = lax.ppermute(from_left, axis, perm=moved(1))  12.3 us
    ppermute x2, starting transfers between devices, ring_matmul(): lax.ppermute(from_right[..., cut:], axis, perm=moved(-1))  9.06 us
  transfers between devices with their start and end apart: 22, of which 9 were waited for; matrix products, arithmetic and copies ran while one was open for 15% of the time, Pallas kernels for 0%

profile of v15, /device:TPU:7, one launch (start us, length us, event | category | flops | bytes accessed | tf_op | source)
XLA Modules:
  0.0 212.9 jit_solution(5033106536248202527)
XLA Ops:
  6.5 1.3 fusion.17
  7.9 2.0 fusion.19
  9.9 0.9 dynamic-slice_select_fusion
  11.6 10.7 %collective-permute-start = (bf16[1,256,640]{2,1,0:T(8,128)(2,1)}, bf16[1,256,640]{2,1,0:T(8,128)(2,1)}, u32[]{:S(2)}, u32[]{:S(2)}) collective-permute-start(bf16[1,256,640]{2,1,0:T(8,128)(2,1)} %get-tuple-element.27), channel_id=1, source_target_pairs={{0,448},{16,464},{32,480},{48,496},{64,0},{80,16},{96,32},{112,48}... | collective-permute-start | bytes 983048 | tf_op jit(solution)/shard_map/ppermute | solution.py:216
  22.3 1.9 collective-permute-start.1
  24.2 5.9 %collective-permute-start.8 = (bf16[256,640]{1,0:T(8,128)(2,1)S(1)}, bf16[256,640]{1,0:T(8,128)(2,1)S(1)}, u32[]{:S(2)}, u32[]{:S(2)}) collective-permute-start(bf16[256,640]{1,0:T(8,128)(2,1)S(1)} %get-tuple-element.26), channel_id=1, source_target_pairs={{0,48},{16,0},{32,16},{48,32},{64,112},{80,64},{96,80},{112,96},{1... | collective-permute-start | bytes 983048 | tf_op jit(solution)/shard_map/ppermute | solution.py:169
  30.1 1.9 collective-permute-start.9
  34.2 1.8 multiply_sine_fusion
  36.1 2.6 %collective-permute-done.8 = bf16[256,640]{1,0:T(8,128)(2,1)S(1)} collective-permute-done((bf16[256,640]{1,0:T(8,128)(2,1)S(1)}, bf16[256,640]{1,0:T(8,128)(2,1)S(1)}, u32[]{:S(2)}, u32[]{:S(2)}) %collective-permute-start.8) | collective-permute-done | bytes 327712 | tf_op jit(solution)/shard_map/ppermute | solution.py:169
  38.7 5.2 %collective-permute-start.11 = (bf16[256,256]{1,0:T(8,128)(2,1)S(1)}, bf16[256,256]{1,0:T(8,128)(2,1)S(1)}, u32[]{:S(2)}, u32[]{:S(2)}) collective-permute-start(bf16[256,256]{1,0:T(8,128)(2,1)S(1)} %slice.148), channel_id=1, source_target_pairs={{0,48},{16,0},{32,16},{48,32},{64,112},{80,64},{96,80},{112,96},{1... | collective-permute-start | bytes 393224 | tf_op jit(solution)/shard_map/ppermute | solution.py:177
  43.8 13.6 %collective-permute-done.9 = bf16[256,640]{1,0:T(8,128)(2,1)S(1)} collective-permute-done((bf16[256,640]{1,0:T(8,128)(2,1)S(1)}, bf16[256,640]{1,0:T(8,128)(2,1)S(1)}, u32[]{:S(2)}, u32[]{:S(2)}) %collective-permute-start.9) | collective-permute-done | bytes 327712 | tf_op jit(solution)/shard_map/ppermute | solution.py:171
  57.5 1.9 collective-permute-start.10
  59.5 17.0 %collective-permute-done.10 = bf16[256,384]{1,0:T(8,128)(2,1)S(1)} collective-permute-done((bf16[256,384]{1,0:T(8,128)(2,1)S(1)}, bf16[256,384]{1,0:T(8,128)(2,1)S(1)}, u32[]{:S(2)}, u32[]{:S(2)}) %collective-permute-start.10) | collective-permute-done | bytes 196640 | tf_op jit(solution)/shard_map/ppermute | solution.py:176
  76.8 0.8 broadcast_in_dim.43.row_seg_ref
  78.2 2.5 %collective-permute-start.12 = (bf16[3,256,640]{2,1,0:T(8,128)(2,1)S(1)}, bf16[3,256,640]{2,1,0:T(8,128)(2,1)S(1)}, u32[]{:S(2)}, u32[]{:S(2)}) collective-permute-start(bf16[3,256,640]{2,1,0:T(8,128)(2,1)S(1)} %pad_maximum_fusion), channel_id=1, source_target_pairs={{0,448},{16,464},{32,480},{48,496},{64,0},{80,16},{96,32},{112,48}... | collective-permute-start | bytes 2949128 | tf_op jit(solution)/shard_map/ppermute | solution.py:216
  80.8 2.7 %collective-permute-start.13 = (bf16[3,256,640]{2,1,0:T(8,128)(2,1)S(1)}, bf16[3,256,640]{2,1,0:T(8,128)(2,1)S(1)}, u32[]{:S(2)}, u32[]{:S(2)}) collective-permute-start(bf16[3,256,640]{2,1,0:T(8,128)(2,1)S(1)} %pad_maximum_fusion), channel_id=1, source_target_pairs={{0,64},{16,80},{32,96},{48,112},{64,128},{80,144},{96,160},{112,17... | collective-permute-start | bytes 2949128 | tf_op jit(solution)/shard_map/ppermute | solution.py:218
  83.5 3.8 %collective-permute-start.2 = (bf16[1,256,640]{2,1,0:T(8,128)(2,1)}, bf16[1,256,640]{2,1,0:T(8,128)(2,1)}, u32[]{:S(2)}, u32[]{:S(2)}) collective-permute-start(bf16[1,256,640]{2,1,0:T(8,128)(2,1)} %collective-permute-done), channel_id=1, source_target_pairs={{0,448},{16,464},{32,480},{48,496},{64,0},{80,16},{96,32},{112,48}... | collective-permute-start | bytes 983048 | tf_op jit(solution)/shard_map/ppermute | solution.py:216
  87.3 1.9 collective-permute-start.3
  89.3 20.1 %collective-permute-done.2 = bf16[1,256,640]{2,1,0:T(8,128)(2,1)} collective-permute-done((bf16[1,256,640]{2,1,0:T(8,128)(2,1)}, bf16[1,256,640]{2,1,0:T(8,128)(2,1)}, u32[]{:S(2)}, u32[]{:S(2)}) %collective-permute-start.2) | collective-permute-done | bytes 327712 | tf_op jit(solution)/shard_map/ppermute | solution.py:216
  109.4 3.4 %collective-permute-start.4 = (bf16[1,256,640]{2,1,0:T(8,128)(2,1)}, bf16[1,256,640]{2,1,0:T(8,128)(2,1)}, u32[]{:S(2)}, u32[]{:S(2)}) collective-permute-start(bf16[1,256,640]{2,1,0:T(8,128)(2,1)} %collective-permute-done.2), channel_id=1, source_target_pairs={{0,448},{16,464},{32,480},{48,496},{64,0},{80,16},{96,32},{112,48}... | collective-permute-start | bytes 983048 | tf_op jit(solution)/shard_map/ppermute | solution.py:216
  112.8 1.9 collective-permute-start.5
  115.2 3.6 %collective-permute-done.4 = bf16[1,256,640]{2,1,0:T(8,128)(2,1)} collective-permute-done((bf16[1,256,640]{2,1,0:T(8,128)(2,1)}, bf16[1,256,640]{2,1,0:T(8,128)(2,1)}, u32[]{:S(2)}, u32[]{:S(2)}) %collective-permute-start.4) | collective-permute-done | bytes 327712 | tf_op jit(solution)/shard_map/ppermute | solution.py:216
  118.8 1.6 slice.146
  120.3 4.3 %collective-permute-start.7 = (bf16[1,256,256]{2,1,0:T(8,128)(2,1)}, bf16[1,256,256]{2,1,0:T(8,128)(2,1)}, u32[]{:S(2)}, u32[]{:S(2)}) collective-permute-start(bf16[1,256,256]{2,1,0:T(8,128)(2,1)} %slice.146), channel_id=1, source_target_pairs={{0,448},{16,464},{32,480},{48,496},{64,0},{80,16},{96,32},{112,48}... | collective-permute-start | bytes 393224 | tf_op jit(solution)/shard_map/ppermute | solution.py:224
  124.7 1.6 slice.145
  126.3 1.9 collective-permute-start.6
  128.2 1.9 collective-permute-start.15
  130.2 4.6 %collective-permute-start.14 = (bf16[3,256,640]{2,1,0:T(8,128)(2,1)S(1)}, bf16[3,256,640]{2,1,0:T(8,128)(2,1)S(1)}, u32[]{:S(2)}, u32[]{:S(2)}) collective-permute-start(bf16[3,256,640]{2,1,0:T(8,128)(2,1)S(1)} %collective-permute-done.12), channel_id=1, source_target_pairs={{0,448},{16,464},{32,480},{48,496},{64,0},{80,16},{96,32},{112,48}... | collective-permute-start | bytes 2949128 | tf_op jit(solution)/shard_map/ppermute | solution.py:216
  134.8 1.6 fusion.42
  136.3 1.8 fusion.45
  138.2 1.3 fusion.85
  139.5 1.3 fusion.40
  140.8 1.3 fusion.32
  142.5 1.4 convolution_add_fusion.12
  143.9 1.4 convolution_add_fusion.11
  146.4 1.3 fusion.34
  147.7 1.4 fusion
  149.4 1.4 fusion.16.qa_ref
  151.2 2.3 %collective-permute-done.15 = bf16[3,256,640]{2,1,0:T(8,128)(2,1)S(1)} collective-permute-done((bf16[3,256,640]{2,1,0:T(8,128)(2,1)S(1)}, bf16[3,256,640]{2,1,0:T(8,128)(2,1)S(1)}, u32[]{:S(2)}, u32[]{:S(2)}) %collective-permute-start.15) | collective-permute-done | bytes 983072 | tf_op jit(solution)/shard_map/ppermute | solution.py:218
  153.5 1.9 collective-permute-start.17
  155.4 4.6 %collective-permute-start.16 = (bf16[3,256,640]{2,1,0:T(8,128)(2,1)S(1)}, bf16[3,256,640]{2,1,0:T(8,128)(2,1)S(1)}, u32[]{:S(2)}, u32[]{:S(2)}) collective-permute-start(bf16[3,256,640]{2,1,0:T(8,128)(2,1)S(1)} %collective-permute-done.14), channel_id=1, source_target_pairs={{0,448},{16,464},{32,480},{48,496},{64,0},{80,16},{96,32},{112,48}... | collective-permute-start | bytes 2949128 | tf_op jit(solution)/shard_map/ppermute | solution.py:216
  162.8 12.6 %collective-permute-done.17 = bf16[3,256,640]{2,1,0:T(8,128)(2,1)S(1)} collective-permute-done((bf16[3,256,640]{2,1,0:T(8,128)(2,1)S(1)}, bf16[3,256,640]{2,1,0:T(8,128)(2,1)S(1)}, u32[]{:S(2)}, u32[]{:S(2)}) %collective-permute-start.17) | collective-permute-done | bytes 983072 | tf_op jit(solution)/shard_map/ppermute | solution.py:218
  175.4 1.9 collective-permute-start.18
  177.4 4.8 %collective-permute-start.19 = (bf16[3,256,256]{2,1,0:T(8,128)(2,1)S(1)}, bf16[3,256,256]{2,1,0:T(8,128)(2,1)S(1)}, u32[]{:S(2)}, u32[]{:S(2)}) collective-permute-start(bf16[3,256,256]{2,1,0:T(8,128)(2,1)S(1)} %slice.168), channel_id=1, source_target_pairs={{0,448},{16,464},{32,480},{48,496},{64,0},{80,16},{96,32},{112,48}... | collective-permute-start | bytes 1179656 | tf_op jit(solution)/shard_map/ppermute | solution.py:224
  184.0 3.9 %collective-permute-done.18 = bf16[3,256,384]{2,1,0:T(8,128)(2,1)S(1)} collective-permute-done((bf16[3,256,384]{2,1,0:T(8,128)(2,1)S(1)}, bf16[3,256,384]{2,1,0:T(8,128)(2,1)S(1)}, u32[]{:S(2)}, u32[]{:S(2)}) %collective-permute-start.18) | collective-permute-done | bytes 589856 | tf_op jit(solution)/shard_map/ppermute | solution.py:223
  189.7 8.2 %collective-permute-start.20 = (bf16[512,128]{1,0:T(8,128)(2,1)S(1)}, bf16[512,128]{1,0:T(8,128)(2,1)S(1)}, u32[]{:S(2)}, u32[]{:S(2)}) collective-permute-start(bf16[512,128]{1,0:T(8,128)(2,1)S(1)} %fusion.53.own_ref), channel_id=1, source_target_pairs={{0,1},{1,0},{2,3},{3,2},{4,5},{5,4},{6,7},{7,6},{8,9},{9,8},{10,11... | collective-permute-start | bytes 393224 | tf_op jit(solution)/shard_map/ppermute | solution.py:283
  198.0 1.0 collective-permute-done.20.other_ref
  199.6 6.4 %shard_map.64 = bf16[512,512]{1,0:T(8,128)(2,1)} custom-call(f32[512,640]{1,0:T(8,128)} %copy-done.1, f32[512,640]{1,0:T(8,128)} %copy-done.2, bf16[512,128]{1,0:T(8,128)(2,1)} %copy-done.4, bf16[512,128]{1,0:T(8,128)(2,1)} %copy-done.5, s32[1,128]{1,0:T(1,128)} %broadcast_in_dim.45.core_ref, f32[512,64]{1,0:T(8,128)} %get-tuple-element.19.cos_ref, ...), custom_call_target="tpu_custom_call" | custom-call | flops 538968064 | bytes 2097152 | tf_op jit(solution)/shard_map/pallas_call | solution.py:129
  (76 shorter events, 12.6 us)
Async XLA Ops:
  6.5 4.3 %copy-start.3 = (bf16[256,512]{1,0:T(8,128)(2,1)S(1)}, bf16[256,512]{1,0:T(8,128)(2,1)}, u32[]{:S(2)}) copy-start(bf16[256,512]{1,0:T(8,128)(2,1)} %param.9) | copy-start | bytes 786436
  6.5 121.7 %all-gather.2.cloned.1.call-start = ((), (), s32[]{:S(2)}) async-start(), calls=%async_computation | async-start | bytes 8912896 | tf_op jit(solution)/shard_map/all_gather | solution.py:261
  7.8 24.3 %copy-start.6 = (s32[512]{0:T(512)S(1)}, s32[512]{0:T(512)}, u32[]{:S(2)}) copy-start(s32[512]{0:T(512)} %param.7) | copy-start | bytes 6148
  11.6 71.9 %collective-permute-start = (bf16[1,256,640]{2,1,0:T(8,128)(2,1)}, bf16[1,256,640]{2,1,0:T(8,128)(2,1)}, u32[]{:S(2)}, u32[]{:S(2)}) collective-permute-start(bf16[1,256,640]{2,1,0:T(8,128)(2,1)} %get-tuple-element.27), channel_id=1, source_target_pairs={{0,448},{16,464},{32,480},{48,496},{64,0},{80,16},{96,32},{112,48}... | collective-permute-start | bytes 983048 | tf_op jit(solution)/shard_map/ppermute | solution.py:216
  22.3 65.0 %collective-permute-start.1 = (bf16[1,256,640]{2,1,0:T(8,128)(2,1)}, bf16[1,256,640]{2,1,0:T(8,128)(2,1)}, u32[]{:S(2)}, u32[]{:S(2)}) collective-permute-start(bf16[1,256,640]{2,1,0:T(8,128)(2,1)} %get-tuple-element.27), channel_id=1, source_target_pairs={{0,64},{16,80},{32,96},{48,112},{64,128},{80,144},{96,160},{112,17... | collective-permute-start | bytes 983048 | tf_op jit(solution)/shard_map/ppermute | solution.py:218
  24.2 14.4 %collective-permute-start.8 = (bf16[256,640]{1,0:T(8,128)(2,1)S(1)}, bf16[256,640]{1,0:T(8,128)(2,1)S(1)}, u32[]{:S(2)}, u32[]{:S(2)}) collective-permute-start(bf16[256,640]{1,0:T(8,128)(2,1)S(1)} %get-tuple-element.26), channel_id=1, source_target_pairs={{0,48},{16,0},{32,16},{48,32},{64,112},{80,64},{96,80},{112,96},{1... | collective-permute-start | bytes 983048 | tf_op jit(solution)/shard_map/ppermute | solution.py:169
  30.1 27.3 %collective-permute-start.9 = (bf16[256,640]{1,0:T(8,128)(2,1)S(1)}, bf16[256,640]{1,0:T(8,128)(2,1)S(1)}, u32[]{:S(2)}, u32[]{:S(2)}) collective-permute-start(bf16[256,640]{1,0:T(8,128)(2,1)S(1)} %get-tuple-element.26), channel_id=1, source_target_pairs={{0,16},{16,32},{32,48},{48,0},{64,80},{80,96},{96,112},{112,64},{1... | collective-permute-start | bytes 983048 | tf_op jit(solution)/shard_map/ppermute | solution.py:171
  38.7 20.8 %collective-permute-start.11 = (bf16[256,256]{1,0:T(8,128)(2,1)S(1)}, bf16[256,256]{1,0:T(8,128)(2,1)S(1)}, u32[]{:S(2)}, u32[]{:S(2)}) collective-permute-start(bf16[256,256]{1,0:T(8,128)(2,1)S(1)} %slice.148), channel_id=1, source_target_pairs={{0,48},{16,0},{32,16},{48,32},{64,112},{80,64},{96,80},{112,96},{1... | collective-permute-start | bytes 393224 | tf_op jit(solution)/shard_map/ppermute | solution.py:177
  57.5 19.1 %collective-permute-start.10 = (bf16[256,384]{1,0:T(8,128)(2,1)S(1)}, bf16[256,384]{1,0:T(8,128)(2,1)S(1)}, u32[]{:S(2)}, u32[]{:S(2)}) collective-permute-start(bf16[256,384]{1,0:T(8,128)(2,1)S(1)} %slice.147), channel_id=1, source_target_pairs={{0,16},{16,32},{32,48},{48,0},{64,80},{80,96},{96,112},{112,64},{1... | collective-permute-start | bytes 589832 | tf_op jit(solution)/shard_map/ppermute | solution.py:176
  78.2 50.0 %collective-permute-start.12 = (bf16[3,256,640]{2,1,0:T(8,128)(2,1)S(1)}, bf16[3,256,640]{2,1,0:T(8,128)(2,1)S(1)}, u32[]{:S(2)}, u32[]{:S(2)}) collective-permute-start(bf16[3,256,640]{2,1,0:T(8,128)(2,1)S(1)} %pad_maximum_fusion), channel_id=1, source_target_pairs={{0,448},{16,464},{32,480},{48,496},{64,0},{80,16},{96,32},{112,48}... | collective-permute-start | bytes 2949128 | tf_op jit(solution)/shard_map/ppermute | solution.py:216
  80.8 47.4 %collective-permute-start.13 = (bf16[3,256,640]{2,1,0:T(8,128)(2,1)S(1)}, bf16[3,256,640]{2,1,0:T(8,128)(2,1)S(1)}, u32[]{:S(2)}, u32[]{:S(2)}) collective-permute-start(bf16[3,256,640]{2,1,0:T(8,128)(2,1)S(1)} %pad_maximum_fusion), channel_id=1, source_target_pairs={{0,64},{16,80},{32,96},{48,112},{64,128},{80,144},{96,160},{112,17... | collective-permute-start | bytes 2949128 | tf_op jit(solution)/shard_map/ppermute | solution.py:218
  83.5 25.8 %collective-permute-start.2 = (bf16[1,256,640]{2,1,0:T(8,128)(2,1)}, bf16[1,256,640]{2,1,0:T(8,128)(2,1)}, u32[]{:S(2)}, u32[]{:S(2)}) collective-permute-start(bf16[1,256,640]{2,1,0:T(8,128)(2,1)} %collective-permute-done), channel_id=1, source_target_pairs={{0,448},{16,464},{32,480},{48,496},{64,0},{80,16},{96,32},{112,48}... | collective-permute-start | bytes 983048 | tf_op jit(solution)/shard_map/ppermute | solution.py:216
  87.3 25.5 %collective-permute-start.3 = (bf16[1,256,640]{2,1,0:T(8,128)(2,1)}, bf16[1,256,640]{2,1,0:T(8,128)(2,1)}, u32[]{:S(2)}, u32[]{:S(2)}) collective-permute-start(bf16[1,256,640]{2,1,0:T(8,128)(2,1)} %collective-permute-done.1), channel_id=1, source_target_pairs={{0,64},{16,80},{32,96},{48,112},{64,128},{80,144},{96,160},{112,17... | collective-permute-start | bytes 983048 | tf_op jit(solution)/shard_map/ppermute | solution.py:218
  109.4 9.4 %collective-permute-start.4 = (bf16[1,256,640]{2,1,0:T(8,128)(2,1)}, bf16[1,256,640]{2,1,0:T(8,128)(2,1)}, u32[]{:S(2)}, u32[]{:S(2)}) collective-permute-start(bf16[1,256,640]{2,1,0:T(8,128)(2,1)} %collective-permute-done.2), channel_id=1, source_target_pairs={{0,448},{16,464},{32,480},{48,496},{64,0},{80,16},{96,32},{112,48}... | collective-permute-start | bytes 983048 | tf_op jit(solution)/shard_map/ppermute | solution.py:216
  112.8 11.8 %collective-permute-start.5 = (bf16[1,256,640]{2,1,0:T(8,128)(2,1)}, bf16[1,256,640]{2,1,0:T(8,128)(2,1)}, u32[]{:S(2)}, u32[]{:S(2)}) collective-permute-start(bf16[1,256,640]{2,1,0:T(8,128)(2,1)} %collective-permute-done.3), channel_id=1, source_target_pairs={{0,64},{16,80},{32,96},{48,112},{64,128},{80,144},{96,160},{112,17... | collective-permute-start | bytes 983048 | tf_op jit(solution)/shard_map/ppermute | solution.py:218
  120.3 26.0 %collective-permute-start.7 = (bf16[1,256,256]{2,1,0:T(8,128)(2,1)}, bf16[1,256,256]{2,1,0:T(8,128)(2,1)}, u32[]{:S(2)}, u32[]{:S(2)}) collective-permute-start(bf16[1,256,256]{2,1,0:T(8,128)(2,1)} %slice.146), channel_id=1, source_target_pairs={{0,448},{16,464},{32,480},{48,496},{64,0},{80,16},{96,32},{112,48}... | collective-permute-start | bytes 393224 | tf_op jit(solution)/shard_map/ppermute | solution.py:224
  126.3 20.1 %collective-permute-start.6 = (bf16[1,256,384]{2,1,0:T(8,128)(2,1)}, bf16[1,256,384]{2,1,0:T(8,128)(2,1)S(1)}, u32[]{:S(2)}, u32[]{:S(2)}) collective-permute-start(bf16[1,256,384]{2,1,0:T(8,128)(2,1)} %slice.145), channel_id=1, source_target_pairs={{0,64},{16,80},{32,96},{48,112},{64,128},{80,144},{96,160},{112,17... | collective-permute-start | bytes 589832 | tf_op jit(solution)/shard_map/ppermute | solution.py:223
  128.2 25.2 %collective-permute-start.15 = (bf16[3,256,640]{2,1,0:T(8,128)(2,1)S(1)}, bf16[3,256,640]{2,1,0:T(8,128)(2,1)S(1)}, u32[]{:S(2)}, u32[]{:S(2)}) collective-permute-start(bf16[3,256,640]{2,1,0:T(8,128)(2,1)S(1)} %collective-permute-done.13), channel_id=1, source_target_pairs={{0,64},{16,80},{32,96},{48,112},{64,128},{80,144},{96,160},{112,17... | collective-permute-start | bytes 2949128 | tf_op jit(solution)/shard_map/ppermute | solution.py:218
  130.2 25.2 %collective-permute-start.14 = (bf16[3,256,640]{2,1,0:T(8,128)(2,1)S(1)}, bf16[3,256,640]{2,1,0:T(8,128)(2,1)S(1)}, u32[]{:S(2)}, u32[]{:S(2)}) collective-permute-start(bf16[3,256,640]{2,1,0:T(8,128)(2,1)S(1)} %collective-permute-done.12), channel_id=1, source_target_pairs={{0,448},{16,464},{32,480},{48,496},{64,0},{80,16},{96,32},{112,48}... | collective-permute-start | bytes 2949128 | tf_op jit(solution)/shard_map/ppermute | solution.py:216
  134.8 7.4 %copy-start = (bf16[512,8192]{1,0:T(8,128)(2,1)S(1)}, bf16[512,8192]{1,0:T(8,128)(2,1)}, u32[]{:S(2)}) copy-start(bf16[512,8192]{1,0:T(8,128)(2,1)} %all-gather.2.cloned.1.call-done) | copy-start | bytes 25165828
  150.8 38.9 %copy-start.1 = (f32[512,640]{1,0:T(8,128)}, f32[512,640]{1,0:T(8,128)S(1)}, u32[]{:S(2)}) copy-start(f32[512,640]{1,0:T(8,128)S(1)} %fusion.16.qa_ref) | copy-start | bytes 3932164
  153.5 21.9 %collective-permute-start.17 = (bf16[3,256,640]{2,1,0:T(8,128)(2,1)S(1)}, bf16[3,256,640]{2,1,0:T(8,128)(2,1)S(1)}, u32[]{:S(2)}, u32[]{:S(2)}) collective-permute-start(bf16[3,256,640]{2,1,0:T(8,128)(2,1)S(1)} %collective-permute-done.15), channel_id=1, source_target_pairs={{0,64},{16,80},{32,96},{48,112},{64,128},{80,144},{96,160},{112,17... | collective-permute-start | bytes 2949128 | tf_op jit(solution)/shard_map/ppermute | solution.py:218
  155.4 21.9 %collective-permute-start.16 = (bf16[3,256,640]{2,1,0:T(8,128)(2,1)S(1)}, bf16[3,256,640]{2,1,0:T(8,128)(2,1)S(1)}, u32[]{:S(2)}, u32[]{:S(2)}) collective-permute-start(bf16[3,256,640]{2,1,0:T(8,128)(2,1)S(1)} %collective-permute-done.14), channel_id=1, source_target_pairs={{0,448},{16,464},{32,480},{48,496},{64,0},{80,16},{96,32},{112,48}... | collective-permute-start | bytes 2949128 | tf_op jit(solution)/shard_map/ppermute | solution.py:216
  175.4 12.5 %collective-permute-start.18 = (bf16[3,256,384]{2,1,0:T(8,128)(2,1)S(1)}, bf16[3,256,384]{2,1,0:T(8,128)(2,1)S(1)}, u32[]{:S(2)}, u32[]{:S(2)}) collective-permute-start(bf16[3,256,384]{2,1,0:T(8,128)(2,1)S(1)} %slice.167), channel_id=1, source_target_pairs={{0,64},{16,80},{32,96},{48,112},{64,128},{80,144},{96,160},{112,17... | collective-permute-start | bytes 1769480 | tf_op jit(solution)/shard_map/ppermute | solution.py:223
  177.4 10.6 %collective-permute-start.19 = (bf16[3,256,256]{2,1,0:T(8,128)(2,1)S(1)}, bf16[3,256,256]{2,1,0:T(8,128)(2,1)S(1)}, u32[]{:S(2)}, u32[]{:S(2)}) collective-permute-start(bf16[3,256,256]{2,1,0:T(8,128)(2,1)S(1)} %slice.168), channel_id=1, source_target_pairs={{0,448},{16,464},{32,480},{48,496},{64,0},{80,16},{96,32},{112,48}... | collective-permute-start | bytes 1179656 | tf_op jit(solution)/shard_map/ppermute | solution.py:224
  189.7 9.3 %copy-start.2 = (f32[512,640]{1,0:T(8,128)}, f32[512,640]{1,0:T(8,128)S(1)}, u32[]{:S(2)}) copy-start(f32[512,640]{1,0:T(8,128)S(1)} %fusion.11.qb_ref) | copy-start | bytes 3932164
  189.7 9.2 %copy-start.4 = (bf16[512,128]{1,0:T(8,128)(2,1)}, bf16[512,128]{1,0:T(8,128)(2,1)S(1)}, u32[]{:S(2)}) copy-start(bf16[512,128]{1,0:T(8,128)(2,1)S(1)} %fusion.53.own_ref) | copy-start | bytes 393220
  189.7 9.2 %collective-permute-start.20 = (bf16[512,128]{1,0:T(8,128)(2,1)S(1)}, bf16[512,128]{1,0:T(8,128)(2,1)S(1)}, u32[]{:S(2)}, u32[]{:S(2)}) collective-permute-start(bf16[512,128]{1,0:T(8,128)(2,1)S(1)} %fusion.53.own_ref), channel_id=1, source_target_pairs={{0,1},{1,0},{2,3},{3,2},{4,5},{5,4},{6,7},{7,6},{8,9},{9,8},{10,11... | collective-permute-start | bytes 393224 | tf_op jit(solution)/shard_map/ppermute | solution.py:283
  198.9 0.7 copy-start.5
Sparse Core Ops, SparseCore 0:
  10.0 82.5 all-gather.1

commit v16 on v13

--- a/solution.py
+++ b/solution.py
@@ -152,20 +152,16 @@
             out = lax.dynamic_update_index_in_dim(out, from_right, (here + step) % count, 0)
             from_left = lax.ppermute(from_left, axis, perm=moved(1))
         else:
-            cut = lane_cut(block.shape[-1])
+            cut = block.shape[-2] // 2
             from_left = jnp.concatenate(
                 [
-                    lax.ppermute(from_left[..., :cut], axis, perm=moved(1)),
-                    lax.ppermute(from_right[..., cut:], axis, perm=moved(-1)),
+                    lax.ppermute(from_left[..., :cut, :], axis, perm=moved(1)),
+                    lax.ppermute(from_right[..., cut:, :], axis, perm=moved(-1)),
                 ],
-                axis=-1,
+                axis=-2,
             )
         out = lax.dynamic_update_index_in_dim(out, from_left, (here - step) % count, 0)
     return out
-
-
-def lane_cut(width):
-    return min(width, (width // 2 + 127) // 128 * 128)
 
 
 def ring_matmul(rows, block, axis, stride, count, starts, wait_rows):
@@ -199,13 +195,13 @@
             total = total + product(from_right, (here + step) % count)
             from_left = lax.ppermute(from_left, axis, perm=moved(1))
         else:
-            cut = lane_cut(block.shape[-1])
+            cut = block.shape[-2] // 2
             from_left = jnp.concatenate(
                 [
-                    lax.ppermute(from_left[..., :cut], axis, perm=moved(1)),
-                    lax.ppermute(from_right[..., cut:], axis, perm=moved(-1)),
+                    lax.ppermute(from_left[..., :cut, :], axis, perm=moved(1)),
+                    lax.ppermute(from_right[..., cut:, :], axis, perm=moved(-1)),
                 ],
-                axis=-1,
+                axis=-2,
             )
         total = total + product(from_left, (here - step) % count)
     return total

time: 197 us -> 195 us (0.990)
  waiting for transfers between devices: 49.4 us -> 47.2 us
  transfers between devices with their start and end apart: 22 -> 22, of which waited for: 6 -> 8; matrix products, arithmetic and copies ran while one was open for 16% -> 16% of each run, Pallas kernels for 0% -> 0%
where the time goes in v16:
time: 195 us; the launch traced here: 193 us
  starting transfers between devices  87.2 us (45%)
  waiting for transfers between devices  47.2 us (24%)
  matrix products  24.4 us (13%)
  between operations  15.2 us (8%)
  other arithmetic  8.29 us (4%)
  Pallas kernels  6.06 us (3%)
  local copies, waits for them, and re-layouts  4.69 us (2%)
    ppermute x6, starting transfers between devices, ring_matmul(): from_right = lax.ppermute(from_right, axis, perm=moved(-1))  35.6 us
    dot_general x32, matrix products, product(): term = jnp.dot(lhs, part[piece], preferred_element_type=jnp.float32)  24.4 us
    ppermute x6, waiting for transfers between devices, ring_matmul(): from_right = lax.ppermute(from_right, axis, perm=moved(-1))  18.1 us
    ppermute x1, waiting for transfers between devices, ring_gather(): lax.ppermute(from_left[..., :cut, :], axis, perm=moved(1))  12.5 us
    ppermute x6, starting transfers between devices, ring_matmul(): from_left = lax.ppermute(from_left, axis, perm=moved(1))  11.5 us
    ppermute x1, starting transfers between devices, per_device(): other_rows = lax.ppermute(own_rows, 'weight', perm=partner)  11.2 us
    ppermute x2, starting transfers between devices, ring_matmul(): lax.ppermute(from_right[..., cut:, :], axis, perm=moved(-1))  9.78 us
    ppermute x6, waiting for transfers between devices, ring_matmul(): from_left = lax.ppermute(from_left, axis, perm=moved(1))  9.77 us
  transfers between devices with their start and end apart: 22, of which 8 were waited for; matrix products, arithmetic and copies ran while one was open for 16% of the time, Pallas kernels for 0%

profile of v16, /device:TPU:7, one launch (start us, length us, event | category | flops | bytes accessed | tf_op | source)
XLA Modules:
  0.0 193.0 jit_solution(15468355786718747185)
XLA Ops:
  6.5 1.3 fusion.18
  7.9 2.0 %fusion.20 = bf16[32,8192]{1,0:T(8,128)(2,1)} fusion(bf16[32,8192]{1,0:T(8,128)(2,1)} %param.6, f32[8192]{0:T(1024)} %param.8, f32[32]{0:T(128)S(1)} %add_rsqrt_fusion), kind=kLoop, calls=%fused_computation.35 | loop fusion | flops 1048576 | bytes 1081472 | tf_op jit(solution)/shard_map/convert_element_type | solution.py:224
  9.9 0.9 dynamic-slice_select_fusion
  11.6 5.9 %collective-permute-start.8 = (bf16[256,640]{1,0:T(8,128)(2,1)S(1)}, bf16[256,640]{1,0:T(8,128)(2,1)S(1)}, u32[]{:S(2)}, u32[]{:S(2)}) collective-permute-start(bf16[256,640]{1,0:T(8,128)(2,1)S(1)} %get-tuple-element.25), channel_id=1, source_target_pairs={{0,48},{16,0},{32,16},{48,32},{64,112},{80,64},{96,80},{112,96},{1... | collective-permute-start | bytes 983048 | tf_op jit(solution)/shard_map/ppermute | solution.py:151
  17.5 1.9 collective-permute-start.9
  19.4 10.7 %collective-permute-start = (bf16[1,256,640]{2,1,0:T(8,128)(2,1)}, bf16[1,256,640]{2,1,0:T(8,128)(2,1)}, u32[]{:S(2)}, u32[]{:S(2)}) collective-permute-start(bf16[1,256,640]{2,1,0:T(8,128)(2,1)} %get-tuple-element.24), channel_id=1, source_target_pairs={{0,448},{16,464},{32,480},{48,496},{64,0},{80,16},{96,32},{112,48}... | collective-permute-start | bytes 983048 | tf_op jit(solution)/shard_map/ppermute | solution.py:194
  30.1 1.9 collective-permute-start.1
  34.3 1.8 multiply_sine_fusion
  36.1 5.5 %collective-permute-start.11 = (bf16[128,640]{1,0:T(8,128)(2,1)S(1)}, bf16[128,640]{1,0:T(8,128)(2,1)S(1)}, u32[]{:S(2)}, u32[]{:S(2)}) collective-permute-start(bf16[128,640]{1,0:T(8,128)(2,1)S(1)} %slice.145), channel_id=1, source_target_pairs={{0,48},{16,0},{32,16},{48,32},{64,112},{80,64},{96,80},{112,96},{1... | collective-permute-start | bytes 491528 | tf_op jit(solution)/shard_map/ppermute | solution.py:159
  41.7 1.9 collective-permute-start.10
  43.7 1.1 collective-permute-done.11
  44.8 12.5 %collective-permute-done.10 = bf16[128,640]{1,0:T(8,128)(2,1)S(1)} collective-permute-done((bf16[128,640]{1,0:T(8,128)(2,1)S(1)}, bf16[128,640]{1,0:T(8,128)(2,1)S(1)}, u32[]{:S(2)}, u32[]{:S(2)}) %collective-permute-start.10) | collective-permute-done | bytes 163872 | tf_op jit(solution)/shard_map/ppermute | solution.py:158
  57.6 6.7 %collective-permute-start.12 = (bf16[3,256,640]{2,1,0:T(8,128)(2,1)S(1)}, bf16[3,256,640]{2,1,0:T(8,128)(2,1)S(1)}, u32[]{:S(2)}, u32[]{:S(2)}) collective-permute-start(bf16[3,256,640]{2,1,0:T(8,128)(2,1)S(1)} %pad_maximum_fusion), channel_id=1, source_target_pairs={{0,448},{16,464},{32,480},{48,496},{64,0},{80,16},{96,32},{112,48}... | collective-permute-start | bytes 2949128 | tf_op jit(solution)/shard_map/ppermute | solution.py:194
  64.4 1.9 collective-permute-start.13
  66.3 4.6 %collective-permute-start.2 = (bf16[1,256,640]{2,1,0:T(8,128)(2,1)}, bf16[1,256,640]{2,1,0:T(8,128)(2,1)}, u32[]{:S(2)}, u32[]{:S(2)}) collective-permute-start(bf16[1,256,640]{2,1,0:T(8,128)(2,1)} %collective-permute-done), channel_id=1, source_target_pairs={{0,448},{16,464},{32,480},{48,496},{64,0},{80,16},{96,32},{112,48}... | collective-permute-start | bytes 983048 | tf_op jit(solution)/shard_map/ppermute | solution.py:194
  70.9 1.9 collective-permute-start.3
  72.8 16.1 %collective-permute-done.2 = bf16[1,256,640]{2,1,0:T(8,128)(2,1)} collective-permute-done((bf16[1,256,640]{2,1,0:T(8,128)(2,1)}, bf16[1,256,640]{2,1,0:T(8,128)(2,1)}, u32[]{:S(2)}, u32[]{:S(2)}) %collective-permute-start.2) | collective-permute-done | bytes 327712 | tf_op jit(solution)/shard_map/ppermute | solution.py:194
  89.0 4.5 %collective-permute-start.4 = (bf16[1,256,640]{2,1,0:T(8,128)(2,1)}, bf16[1,256,640]{2,1,0:T(8,128)(2,1)}, u32[]{:S(2)}, u32[]{:S(2)}) collective-permute-start(bf16[1,256,640]{2,1,0:T(8,128)(2,1)} %collective-permute-done.2), channel_id=1, source_target_pairs={{0,448},{16,464},{32,480},{48,496},{64,0},{80,16},{96,32},{112,48}... | collective-permute-start | bytes 983048 | tf_op jit(solution)/shard_map/ppermute | solution.py:194
  93.5 1.9 collective-permute-start.5
  95.8 2.0 %collective-permute-done.4 = bf16[1,256,640]{2,1,0:T(8,128)(2,1)} collective-permute-done((bf16[1,256,640]{2,1,0:T(8,128)(2,1)}, bf16[1,256,640]{2,1,0:T(8,128)(2,1)}, u32[]{:S(2)}, u32[]{:S(2)}) %collective-permute-start.4) | collective-permute-done | bytes 327712 | tf_op jit(solution)/shard_map/ppermute | solution.py:194
  97.8 0.9 slice.143
  98.7 5.0 %collective-permute-start.7 = (bf16[1,128,640]{2,1,0:T(8,128)(2,1)S(1)}, bf16[1,128,640]{2,1,0:T(8,128)(2,1)}, u32[]{:S(2)}, u32[]{:S(2)}) collective-permute-start(bf16[1,128,640]{2,1,0:T(8,128)(2,1)S(1)} %slice.143), channel_id=1, source_target_pairs={{0,448},{16,464},{32,480},{48,496},{64,0},{80,16},{96,32},{112,48}... | collective-permute-start | bytes 491528 | tf_op jit(solution)/shard_map/ppermute | solution.py:202
  103.8 1.6 slice.142
  105.4 1.9 collective-permute-start.6
  107.3 1.9 collective-permute-start.15
  109.3 4.6 %collective-permute-start.14 = (bf16[3,256,640]{2,1,0:T(8,128)(2,1)S(1)}, bf16[3,256,640]{2,1,0:T(8,128)(2,1)S(1)}, u32[]{:S(2)}, u32[]{:S(2)}) collective-permute-start(bf16[3,256,640]{2,1,0:T(8,128)(2,1)S(1)} %collective-permute-done.12), channel_id=1, source_target_pairs={{0,448},{16,464},{32,480},{48,496},{64,0},{80,16},{96,32},{112,48}... | collective-permute-start | bytes 2949128 | tf_op jit(solution)/shard_map/ppermute | solution.py:194
  113.8 1.5 fusion.41
  115.3 1.7 fusion.33
  117.0 1.3 fusion.34
  118.3 1.3 fusion.31
  119.7 1.3 fusion.32
  121.0 1.4 fusion.43
  123.5 1.4 convolution_add_fusion.12
  124.9 1.4 fusion.46
  126.2 1.4 fusion.35
  127.6 1.4 convolution_add_fusion.11
  129.0 1.4 fusion
  130.7 1.9 collective-permute-start.17
  132.7 4.6 %collective-permute-start.16 = (bf16[3,256,640]{2,1,0:T(8,128)(2,1)S(1)}, bf16[3,256,640]{2,1,0:T(8,128)(2,1)S(1)}, u32[]{:S(2)}, u32[]{:S(2)}) collective-permute-start(bf16[3,256,640]{2,1,0:T(8,128)(2,1)S(1)} %collective-permute-done.14), channel_id=1, source_target_pairs={{0,448},{16,464},{32,480},{48,496},{64,0},{80,16},{96,32},{112,48}... | collective-permute-start | bytes 2949128 | tf_op jit(solution)/shard_map/ppermute | solution.py:194
  140.1 9.8 %collective-permute-done.17 = bf16[3,256,640]{2,1,0:T(8,128)(2,1)S(1)} collective-permute-done((bf16[3,256,640]{2,1,0:T(8,128)(2,1)S(1)}, bf16[3,256,640]{2,1,0:T(8,128)(2,1)S(1)}, u32[]{:S(2)}, u32[]{:S(2)}) %collective-permute-start.17) | collective-permute-done | bytes 983072 | tf_op jit(solution)/shard_map/ppermute | solution.py:196
  149.9 1.9 collective-permute-start.18
  151.9 4.8 %collective-permute-start.19 = (bf16[3,128,640]{2,1,0:T(8,128)(2,1)S(1)}, bf16[3,128,640]{2,1,0:T(8,128)(2,1)S(1)}, u32[]{:S(2)}, u32[]{:S(2)}) collective-permute-start(bf16[3,128,640]{2,1,0:T(8,128)(2,1)S(1)} %slice.165), channel_id=1, source_target_pairs={{0,448},{16,464},{32,480},{48,496},{64,0},{80,16},{96,32},{112,48}... | collective-permute-start | bytes 1474568 | tf_op jit(solution)/shard_map/ppermute | solution.py:202
  158.5 4.1 %collective-permute-done.18 = bf16[3,128,640]{2,1,0:T(8,128)(2,1)S(1)} collective-permute-done((bf16[3,128,640]{2,1,0:T(8,128)(2,1)S(1)}, bf16[3,128,640]{2,1,0:T(8,128)(2,1)S(1)}, u32[]{:S(2)}, u32[]{:S(2)}) %collective-permute-start.18) | collective-permute-done | bytes 491552 | tf_op jit(solution)/shard_map/ppermute | solution.py:201
  162.6 1.4 collective-permute-done.19
  165.8 1.4 fusion.17.q_ref
  167.2 11.2 %collective-permute-start.20 = (bf16[512,128]{1,0:T(8,128)(2,1)S(1)}, bf16[512,128]{1,0:T(8,128)(2,1)S(1)}, u32[]{:S(2)}, u32[]{:S(2)}) collective-permute-start(bf16[512,128]{1,0:T(8,128)(2,1)S(1)} %slice.226), channel_id=1, source_target_pairs={{0,1},{1,0},{2,3},{3,2},{4,5},{5,4},{6,7},{7,6},{8,9},{9,8},{10,11... | collective-permute-start | bytes 393224 | tf_op jit(solution)/shard_map/ppermute | solution.py:260
  178.4 0.9 copy.7.row_seg_ref
  180.1 6.1 %shard_map.64 = bf16[512,512]{1,0:T(8,128)(2,1)} custom-call(f32[512,640]{1,0:T(8,128)} %copy-done.1, bf16[512,128]{1,0:T(8,128)(2,1)} %get-tuple-element.27.k_ref, bf16[512,128]{1,0:T(8,128)(2,1)} %get-tuple-element.26.v_ref, f32[512,64]{1,0:T(8,128)} %get-tuple-element.17.cos_ref, f32[512,64]{1,0:T(8,128)} %get-tuple-element.18.sin_ref, ...), custom_call_target="tpu_custom_call" | custom-call | flops 538968064 | bytes 2097152 | tf_op jit(solution)/shard_map/pallas_call | solution.py:113
  (70 shorter events, 11.4 us)
Async XLA Ops:
  6.5 4.3 %copy-start.2 = (bf16[256,512]{1,0:T(8,128)(2,1)S(1)}, bf16[256,512]{1,0:T(8,128)(2,1)}, u32[]{:S(2)}) copy-start(bf16[256,512]{1,0:T(8,128)(2,1)} %param.9) | copy-start | bytes 786436
  6.5 100.8 %all-gather.2.cloned.1.call-start = ((), (), s32[]{:S(2)}) async-start(), calls=%async_computation | async-start | bytes 8912896 | tf_op jit(solution)/shard_map/all_gather | solution.py:237
  7.8 24.3 %copy-start.3 = (s32[512]{0:T(512)S(1)}, s32[512]{0:T(512)}, u32[]{:S(2)}) copy-start(s32[512]{0:T(512)} %param.7) | copy-start | bytes 6148
  11.6 24.5 %collective-permute-start.8 = (bf16[256,640]{1,0:T(8,128)(2,1)S(1)}, bf16[256,640]{1,0:T(8,128)(2,1)S(1)}, u32[]{:S(2)}, u32[]{:S(2)}) collective-permute-start(bf16[256,640]{1,0:T(8,128)(2,1)S(1)} %get-tuple-element.25), channel_id=1, source_target_pairs={{0,48},{16,0},{32,16},{48,32},{64,112},{80,64},{96,80},{112,96},{1... | collective-permute-start | bytes 983048 | tf_op jit(solution)/shard_map/ppermute | solution.py:151
  17.5 24.1 %collective-permute-start.9 = (bf16[256,640]{1,0:T(8,128)(2,1)S(1)}, bf16[256,640]{1,0:T(8,128)(2,1)S(1)}, u32[]{:S(2)}, u32[]{:S(2)}) collective-permute-start(bf16[256,640]{1,0:T(8,128)(2,1)S(1)} %get-tuple-element.25), channel_id=1, source_target_pairs={{0,16},{16,32},{32,48},{48,0},{64,80},{80,96},{96,112},{112,64},{1... | collective-permute-start | bytes 983048 | tf_op jit(solution)/shard_map/ppermute | solution.py:153
  19.4 46.9 %collective-permute-start = (bf16[1,256,640]{2,1,0:T(8,128)(2,1)}, bf16[1,256,640]{2,1,0:T(8,128)(2,1)}, u32[]{:S(2)}, u32[]{:S(2)}) collective-permute-start(bf16[1,256,640]{2,1,0:T(8,128)(2,1)} %get-tuple-element.24), channel_id=1, source_target_pairs={{0,448},{16,464},{32,480},{48,496},{64,0},{80,16},{96,32},{112,48}... | collective-permute-start | bytes 983048 | tf_op jit(solution)/shard_map/ppermute | solution.py:194
  30.1 40.8 %collective-permute-start.1 = (bf16[1,256,640]{2,1,0:T(8,128)(2,1)}, bf16[1,256,640]{2,1,0:T(8,128)(2,1)}, u32[]{:S(2)}, u32[]{:S(2)}) collective-permute-start(bf16[1,256,640]{2,1,0:T(8,128)(2,1)} %get-tuple-element.24), channel_id=1, source_target_pairs={{0,64},{16,80},{32,96},{48,112},{64,128},{80,144},{96,160},{112,17... | collective-permute-start | bytes 983048 | tf_op jit(solution)/shard_map/ppermute | solution.py:196
  36.1 8.7 %collective-permute-start.11 = (bf16[128,640]{1,0:T(8,128)(2,1)S(1)}, bf16[128,640]{1,0:T(8,128)(2,1)S(1)}, u32[]{:S(2)}, u32[]{:S(2)}) collective-permute-start(bf16[128,640]{1,0:T(8,128)(2,1)S(1)} %slice.145), channel_id=1, source_target_pairs={{0,48},{16,0},{32,16},{48,32},{64,112},{80,64},{96,80},{112,96},{1... | collective-permute-start | bytes 491528 | tf_op jit(solution)/shard_map/ppermute | solution.py:159
  41.7 15.7 %collective-permute-start.10 = (bf16[128,640]{1,0:T(8,128)(2,1)S(1)}, bf16[128,640]{1,0:T(8,128)(2,1)S(1)}, u32[]{:S(2)}, u32[]{:S(2)}) collective-permute-start(bf16[128,640]{1,0:T(8,128)(2,1)S(1)} %slice.144), channel_id=1, source_target_pairs={{0,16},{16,32},{32,48},{48,0},{64,80},{80,96},{96,112},{112,64},{1... | collective-permute-start | bytes 491528 | tf_op jit(solution)/shard_map/ppermute | solution.py:158
  57.6 49.6 %collective-permute-start.12 = (bf16[3,256,640]{2,1,0:T(8,128)(2,1)S(1)}, bf16[3,256,640]{2,1,0:T(8,128)(2,1)S(1)}, u32[]{:S(2)}, u32[]{:S(2)}) collective-permute-start(bf16[3,256,640]{2,1,0:T(8,128)(2,1)S(1)} %pad_maximum_fusion), channel_id=1, source_target_pairs={{0,448},{16,464},{32,480},{48,496},{64,0},{80,16},{96,32},{112,48}... | collective-permute-start | bytes 2949128 | tf_op jit(solution)/shard_map/ppermute | solution.py:194
  64.4 42.9 %collective-permute-start.13 = (bf16[3,256,640]{2,1,0:T(8,128)(2,1)S(1)}, bf16[3,256,640]{2,1,0:T(8,128)(2,1)S(1)}, u32[]{:S(2)}, u32[]{:S(2)}) collective-permute-start(bf16[3,256,640]{2,1,0:T(8,128)(2,1)S(1)} %pad_maximum_fusion), channel_id=1, source_target_pairs={{0,64},{16,80},{32,96},{48,112},{64,128},{80,144},{96,160},{112,17... | collective-permute-start | bytes 2949128 | tf_op jit(solution)/shard_map/ppermute | solution.py:196
  66.3 22.6 %collective-permute-start.2 = (bf16[1,256,640]{2,1,0:T(8,128)(2,1)}, bf16[1,256,640]{2,1,0:T(8,128)(2,1)}, u32[]{:S(2)}, u32[]{:S(2)}) collective-permute-start(bf16[1,256,640]{2,1,0:T(8,128)(2,1)} %collective-permute-done), channel_id=1, source_target_pairs={{0,448},{16,464},{32,480},{48,496},{64,0},{80,16},{96,32},{112,48}... | collective-permute-start | bytes 983048 | tf_op jit(solution)/shard_map/ppermute | solution.py:194
  70.9 22.6 %collective-permute-start.3 = (bf16[1,256,640]{2,1,0:T(8,128)(2,1)}, bf16[1,256,640]{2,1,0:T(8,128)(2,1)}, u32[]{:S(2)}, u32[]{:S(2)}) collective-permute-start(bf16[1,256,640]{2,1,0:T(8,128)(2,1)} %collective-permute-done.1), channel_id=1, source_target_pairs={{0,64},{16,80},{32,96},{48,112},{64,128},{80,144},{96,160},{112,17... | collective-permute-start | bytes 983048 | tf_op jit(solution)/shard_map/ppermute | solution.py:196
  89.0 8.8 %collective-permute-start.4 = (bf16[1,256,640]{2,1,0:T(8,128)(2,1)}, bf16[1,256,640]{2,1,0:T(8,128)(2,1)}, u32[]{:S(2)}, u32[]{:S(2)}) collective-permute-start(bf16[1,256,640]{2,1,0:T(8,128)(2,1)} %collective-permute-done.2), channel_id=1, source_target_pairs={{0,448},{16,464},{32,480},{48,496},{64,0},{80,16},{96,32},{112,48}... | collective-permute-start | bytes 983048 | tf_op jit(solution)/shard_map/ppermute | solution.py:194
  93.5 10.3 %collective-permute-start.5 = (bf16[1,256,640]{2,1,0:T(8,128)(2,1)}, bf16[1,256,640]{2,1,0:T(8,128)(2,1)}, u32[]{:S(2)}, u32[]{:S(2)}) collective-permute-start(bf16[1,256,640]{2,1,0:T(8,128)(2,1)} %collective-permute-done.3), channel_id=1, source_target_pairs={{0,64},{16,80},{32,96},{48,112},{64,128},{80,144},{96,160},{112,17... | collective-permute-start | bytes 983048 | tf_op jit(solution)/shard_map/ppermute | solution.py:196
  98.7 27.5 %collective-permute-start.7 = (bf16[1,128,640]{2,1,0:T(8,128)(2,1)S(1)}, bf16[1,128,640]{2,1,0:T(8,128)(2,1)}, u32[]{:S(2)}, u32[]{:S(2)}) collective-permute-start(bf16[1,128,640]{2,1,0:T(8,128)(2,1)S(1)} %slice.143), channel_id=1, source_target_pairs={{0,448},{16,464},{32,480},{48,496},{64,0},{80,16},{96,32},{112,48}... | collective-permute-start | bytes 491528 | tf_op jit(solution)/shard_map/ppermute | solution.py:202
  105.4 20.9 %collective-permute-start.6 = (bf16[1,128,640]{2,1,0:T(8,128)(2,1)}, bf16[1,128,640]{2,1,0:T(8,128)(2,1)}, u32[]{:S(2)}, u32[]{:S(2)}) collective-permute-start(bf16[1,128,640]{2,1,0:T(8,128)(2,1)} %slice.142), channel_id=1, source_target_pairs={{0,64},{16,80},{32,96},{48,112},{64,128},{80,144},{96,160},{112,17... | collective-permute-start | bytes 491528 | tf_op jit(solution)/shard_map/ppermute | solution.py:201
  107.3 23.4 %collective-permute-start.15 = (bf16[3,256,640]{2,1,0:T(8,128)(2,1)S(1)}, bf16[3,256,640]{2,1,0:T(8,128)(2,1)S(1)}, u32[]{:S(2)}, u32[]{:S(2)}) collective-permute-start(bf16[3,256,640]{2,1,0:T(8,128)(2,1)S(1)} %collective-permute-done.13), channel_id=1, source_target_pairs={{0,64},{16,80},{32,96},{48,112},{64,128},{80,144},{96,160},{112,17... | collective-permute-start | bytes 2949128 | tf_op jit(solution)/shard_map/ppermute | solution.py:196
  109.3 23.4 %collective-permute-start.14 = (bf16[3,256,640]{2,1,0:T(8,128)(2,1)S(1)}, bf16[3,256,640]{2,1,0:T(8,128)(2,1)S(1)}, u32[]{:S(2)}, u32[]{:S(2)}) collective-permute-start(bf16[3,256,640]{2,1,0:T(8,128)(2,1)S(1)} %collective-permute-done.12), channel_id=1, source_target_pairs={{0,448},{16,464},{32,480},{48,496},{64,0},{80,16},{96,32},{112,48}... | collective-permute-start | bytes 2949128 | tf_op jit(solution)/shard_map/ppermute | solution.py:194
  113.8 7.2 %copy-start = (bf16[512,8192]{1,0:T(8,128)(2,1)S(1)}, bf16[512,8192]{1,0:T(8,128)(2,1)}, u32[]{:S(2)}) copy-start(bf16[512,8192]{1,0:T(8,128)(2,1)} %all-gather.2.cloned.1.call-done) | copy-start | bytes 25165828
  130.7 19.1 %collective-permute-start.17 = (bf16[3,256,640]{2,1,0:T(8,128)(2,1)S(1)}, bf16[3,256,640]{2,1,0:T(8,128)(2,1)S(1)}, u32[]{:S(2)}, u32[]{:S(2)}) collective-permute-start(bf16[3,256,640]{2,1,0:T(8,128)(2,1)S(1)} %collective-permute-done.15), channel_id=1, source_target_pairs={{0,64},{16,80},{32,96},{48,112},{64,128},{80,144},{96,160},{112,17... | collective-permute-start | bytes 2949128 | tf_op jit(solution)/shard_map/ppermute | solution.py:196
  132.7 19.1 %collective-permute-start.16 = (bf16[3,256,640]{2,1,0:T(8,128)(2,1)S(1)}, bf16[3,256,640]{2,1,0:T(8,128)(2,1)S(1)}, u32[]{:S(2)}, u32[]{:S(2)}) collective-permute-start(bf16[3,256,640]{2,1,0:T(8,128)(2,1)S(1)} %collective-permute-done.14), channel_id=1, source_target_pairs={{0,448},{16,464},{32,480},{48,496},{64,0},{80,16},{96,32},{112,48}... | collective-permute-start | bytes 2949128 | tf_op jit(solution)/shard_map/ppermute | solution.py:194
  149.9 12.7 %collective-permute-start.18 = (bf16[3,128,640]{2,1,0:T(8,128)(2,1)S(1)}, bf16[3,128,640]{2,1,0:T(8,128)(2,1)S(1)}, u32[]{:S(2)}, u32[]{:S(2)}) collective-permute-start(bf16[3,128,640]{2,1,0:T(8,128)(2,1)S(1)} %slice.164), channel_id=1, source_target_pairs={{0,64},{16,80},{32,96},{48,112},{64,128},{80,144},{96,160},{112,17... | collective-permute-start | bytes 1474568 | tf_op jit(solution)/shard_map/ppermute | solution.py:201
  151.9 12.2 %collective-permute-start.19 = (bf16[3,128,640]{2,1,0:T(8,128)(2,1)S(1)}, bf16[3,128,640]{2,1,0:T(8,128)(2,1)S(1)}, u32[]{:S(2)}, u32[]{:S(2)}) collective-permute-start(bf16[3,128,640]{2,1,0:T(8,128)(2,1)S(1)} %slice.165), channel_id=1, source_target_pairs={{0,448},{16,464},{32,480},{48,496},{64,0},{80,16},{96,32},{112,48}... | collective-permute-start | bytes 1474568 | tf_op jit(solution)/shard_map/ppermute | solution.py:202
  167.2 13.0 %copy-start.1 = (f32[512,640]{1,0:T(8,128)}, f32[512,640]{1,0:T(8,128)S(1)}, u32[]{:S(2)}) copy-start(f32[512,640]{1,0:T(8,128)S(1)} %fusion.17.q_ref) | copy-start | bytes 3932164
  167.2 12.2 %collective-permute-start.20 = (bf16[512,128]{1,0:T(8,128)(2,1)S(1)}, bf16[512,128]{1,0:T(8,128)(2,1)S(1)}, u32[]{:S(2)}, u32[]{:S(2)}) collective-permute-start(bf16[512,128]{1,0:T(8,128)(2,1)S(1)} %slice.226), channel_id=1, source_target_pairs={{0,1},{1,0},{2,3},{3,2},{4,5},{5,4},{6,7},{7,6},{8,9},{9,8},{10,11... | collective-permute-start | bytes 393224 | tf_op jit(solution)/shard_map/ppermute | solution.py:260
Sparse Core Ops, SparseCore 0:
  10.0 71.7 all-gather.1

commit v17 on v16

--- a/solution.py
+++ b/solution.py
@@ -131,10 +131,8 @@
     )
 
 
-def ring_gather(block, axis, stride, count):
+def ring_arrivals(block, axis, stride, count):
     n = lax.psum(1, axis)
-    me = lax.axis_index(axis)
-    here = (me // stride) % count
 
     def moved(step):
         pairs = []
@@ -143,14 +141,13 @@
             pairs.append((src, src + (((k + step) % count) - k) * stride))
         return pairs
 
-    out = jnp.zeros((count,) + block.shape, block.dtype)
-    out = lax.dynamic_update_index_in_dim(out, block, here, 0)
+    steps = []
     from_right, from_left = block, block
     for step in range(1, count // 2 + 1):
         if step < count - step:
             from_right = lax.ppermute(from_right, axis, perm=moved(-1))
-            out = lax.dynamic_update_index_in_dim(out, from_right, (here + step) % count, 0)
             from_left = lax.ppermute(from_left, axis, perm=moved(1))
+            steps.append([(from_right, step), (from_left, -step)])
         else:
             cut = block.shape[-2] // 2
             from_left = jnp.concatenate(
@@ -160,8 +157,8 @@
                 ],
                 axis=-2,
             )
-        out = lax.dynamic_update_index_in_dim(out, from_left, (here - step) % count, 0)
-    return out
+            steps.append([(from_left, -step)])
+    return steps
 
 
 def ring_matmul(rows, block, axis, stride, count, starts, wait_rows):
@@ -227,34 +224,31 @@
     y_hi = n_batch // Z_CHIPS
     shard = local_weights.shape[0]
     yh = lax.axis_index("batch") % y_hi
-    near = ring_gather(local_weights, "batch", 1, y_hi)
-    others = jnp.stack([near[(yh + r) % y_hi] for r in range(1, y_hi)])
+    arrivals = ring_arrivals(local_weights, "batch", 1, y_hi)
+    first = jnp.stack([part for part, _ in arrivals[0]])
+    first_offsets = [offset for _, offset in arrivals[0]]
+    rest = jnp.stack([part for step in arrivals[1:] for part, _ in step])
+    rest_offsets = [offset for step in arrivals[1:] for _, offset in step]
     cosine, sine = rope_tables(positions_in_segment(segment_ids))
     row_seg, col_seg = segment_ids[:, None], segment_ids[None, :]
-    others, cosine, sine, row_seg, col_seg = lax.optimization_barrier(
-        (others, cosine, sine, row_seg, col_seg)
+    first, cosine, sine, row_seg, col_seg = lax.optimization_barrier(
+        (first, cosine, sine, row_seg, col_seg)
     )
     gathered = lax.all_gather(normed, "weight", axis=0, tiled=True)
     pack_rows = gathered.shape[0]
-    own_part = ring_matmul(
-        gathered,
-        local_weights[None],
-        "batch",
-        y_hi,
-        Z_CHIPS,
-        lambda z: [(z * y_hi + yh) * shard],
-        False,
-    )
-    other_part = ring_matmul(
-        gathered,
-        others,
-        "batch",
-        y_hi,
-        Z_CHIPS,
-        lambda z: [(z * y_hi + (yh + r) % y_hi) * shard for r in range(1, y_hi)],
-        True,
-    )
-    projected = own_part + other_part
+
+    def starts_of(offsets):
+        return lambda z: [(z * y_hi + (yh + r) % y_hi) * shard for r in offsets]
+
+    projected = ring_matmul(
+        gathered, local_weights[None], "batch", y_hi, Z_CHIPS, starts_of([0]), False
+    )
+    projected = projected + ring_matmul(
+        gathered, first, "batch", y_hi, Z_CHIPS, starts_of(first_offsets), True
+    )
+    projected = projected + ring_matmul(
+        gathered, rest, "batch", y_hi, Z_CHIPS, starts_of(rest_offsets), False
+    )
     own_rows = projected[:, query_cols:].astype(jnp.bfloat16)
     partner = [(w, w ^ 1) for w in range(n_weight)]
     other_rows = lax.ppermute(own_rows, "weight", perm=partner)

time: 195 us -> 206 us (1.056)
  the two profiles are of different devices: /device:TPU:7 before, /device:TPU:15 now
where the time goes in v17:
time: 206 us; the launch traced here: 205 us
  starting transfers between devices  118 us (57%)
  waiting for transfers between devices  30.6 us (15%)
  matrix products  23.2 us (11%)
  between operations  15.3 us (7%)
  other arithmetic  7.42 us (4%)
  Pallas kernels  6.07 us (3%)
  local copies, waits for them, and re-layouts  4.49 us (2%)
    ppermute x9, starting transfers between devices, ring_matmul(): from_right = lax.ppermute(from_right, axis, perm=moved(-1))  52.3 us
    dot_general x32, matrix products, product(): term = jnp.dot(lhs, part[piece], preferred_element_type=jnp.float32)  23.2 us
    ppermute x9, starting transfers between devices, ring_matmul(): from_left = lax.ppermute(from_left, axis, perm=moved(1))  19.9 us
    ppermute x9, waiting for transfers between devices, ring_matmul(): from_left = lax.ppermute(from_left, axis, perm=moved(1))  16.4 us
    ppermute x1, starting transfers between devices, per_device(): other_rows = lax.ppermute(own_rows, 'weight', perm=partner)  13.5 us
    ppermute x3, starting transfers between devices, ring_matmul(): lax.ppermute(from_right[..., cut:, :], axis, perm=moved(-1))  9.96 us
    ppermute x3, starting transfers between devices, ring_matmul(): lax.ppermute(from_left[..., :cut, :], axis, perm=moved(1))  7.69 us
    ppermute x9, waiting for transfers between devices, ring_matmul(): from_right = lax.ppermute(from_right, axis, perm=moved(-1))  6.58 us
  transfers between devices with their start and end apart: 30, of which 8 were waited for; matrix products, arithmetic and copies ran while one was open for 14% of the time, Pallas kernels for 0%

profile of v17, /device:TPU:15, one launch (start us, length us, event | category | flops | bytes accessed | tf_op | source)
XLA Modules:
  0.0 205.1 jit_solution(9382036364233996757)
XLA Ops:
  6.5 1.3 fusion.16
  7.9 2.0 fusion.18
  10.9 4.2 %collective-permute-start.9 = (bf16[256,640]{1,0:T(8,128)(2,1)S(1)}, bf16[256,640]{1,0:T(8,128)(2,1)S(1)}, u32[]{:S(2)}, u32[]{:S(2)}) collective-permute-start(bf16[256,640]{1,0:T(8,128)(2,1)S(1)} %get-tuple-element.22), channel_id=1, source_target_pairs={{0,16},{16,32},{32,48},{48,0},{64,80},{80,96},{96,112},{112,64},{1... | collective-permute-start | bytes 983048 | tf_op jit(solution)/shard_map/ppermute | solution.py:149
  15.1 3.2 %collective-permute-start.8 = (bf16[256,640]{1,0:T(8,128)(2,1)S(1)}, bf16[256,640]{1,0:T(8,128)(2,1)S(1)}, u32[]{:S(2)}, u32[]{:S(2)}) collective-permute-start(bf16[256,640]{1,0:T(8,128)(2,1)S(1)} %get-tuple-element.22), channel_id=1, source_target_pairs={{0,48},{16,0},{32,16},{48,32},{64,112},{80,64},{96,80},{112,96},{1... | collective-permute-start | bytes 983048 | tf_op jit(solution)/shard_map/ppermute | solution.py:148
  18.3 10.7 %collective-permute-start = (bf16[1,256,640]{2,1,0:T(8,128)(2,1)S(1)}, bf16[1,256,640]{2,1,0:T(8,128)(2,1)S(1)}, u32[]{:S(2)}, u32[]{:S(2)}) collective-permute-start(bf16[1,256,640]{2,1,0:T(8,128)(2,1)S(1)} %get-tuple-element.21), channel_id=1, source_target_pairs={{0,448},{16,464},{32,480},{48,496},{64,0},{80,16},{96,32},{112,48}... | collective-permute-start | bytes 983048 | tf_op jit(solution)/shard_map/ppermute | solution.py:191
  29.0 1.9 collective-permute-start.1
  32.8 3.3 %collective-permute-start.18 = (bf16[128,640]{1,0:T(8,128)(2,1)S(1)}, bf16[128,640]{1,0:T(8,128)(2,1)S(1)}, u32[]{:S(2)}, u32[]{:S(2)}) collective-permute-start(bf16[128,640]{1,0:T(8,128)(2,1)S(1)} %slice.136), channel_id=1, source_target_pairs={{0,16},{16,32},{32,48},{48,0},{64,80},{80,96},{96,112},{112,64},{1... | collective-permute-start | bytes 491528 | tf_op jit(solution)/shard_map/ppermute | solution.py:155
  36.1 4.1 %collective-permute-start.19 = (bf16[128,640]{1,0:T(8,128)(2,1)S(1)}, bf16[128,640]{1,0:T(8,128)(2,1)S(1)}, u32[]{:S(2)}, u32[]{:S(2)}) collective-permute-start(bf16[128,640]{1,0:T(8,128)(2,1)S(1)} %slice.137), channel_id=1, source_target_pairs={{0,48},{16,0},{32,16},{48,32},{64,112},{80,64},{96,80},{112,96},{1... | collective-permute-start | bytes 491528 | tf_op jit(solution)/shard_map/ppermute | solution.py:156
  40.3 9.2 %collective-permute-start.2 = (bf16[1,256,640]{2,1,0:T(8,128)(2,1)S(1)}, bf16[1,256,640]{2,1,0:T(8,128)(2,1)S(1)}, u32[]{:S(2)}, u32[]{:S(2)}) collective-permute-start(bf16[1,256,640]{2,1,0:T(8,128)(2,1)S(1)} %collective-permute-done), channel_id=1, source_target_pairs={{0,448},{16,464},{32,480},{48,496},{64,0},{80,16},{96,32},{112,48}... | collective-permute-start | bytes 983048 | tf_op jit(solution)/shard_map/ppermute | solution.py:191
  49.5 1.9 collective-permute-start.3
  52.7 9.8 %collective-permute-start.20 = (bf16[1,256,640]{2,1,0:T(8,128)(2,1)S(1)}, bf16[1,256,640]{2,1,0:T(8,128)(2,1)S(1)}, u32[]{:S(2)}, u32[]{:S(2)}) collective-permute-start(bf16[1,256,640]{2,1,0:T(8,128)(2,1)S(1)} %bitcast.105), channel_id=1, source_target_pairs={{0,448},{16,464},{32,480},{48,496},{64,0},{80,16},{96,32},{112,48}... | collective-permute-start | bytes 983048 | tf_op jit(solution)/shard_map/ppermute | solution.py:191
  62.5 1.9 collective-permute-start.21
  64.4 1.8 multiply_sine_fusion
  66.4 4.6 %collective-permute-start.4 = (bf16[1,256,640]{2,1,0:T(8,128)(2,1)S(1)}, bf16[1,256,640]{2,1,0:T(8,128)(2,1)S(1)}, u32[]{:S(2)}, u32[]{:S(2)}) collective-permute-start(bf16[1,256,640]{2,1,0:T(8,128)(2,1)S(1)} %collective-permute-done.2), channel_id=1, source_target_pairs={{0,448},{16,464},{32,480},{48,496},{64,0},{80,16},{96,32},{112,48}... | collective-permute-start | bytes 983048 | tf_op jit(solution)/shard_map/ppermute | solution.py:191
  71.0 1.9 collective-permute-start.22
  72.9 3.4 %collective-permute-start.23 = (bf16[1,256,640]{2,1,0:T(8,128)(2,1)S(1)}, bf16[1,256,640]{2,1,0:T(8,128)(2,1)}, u32[]{:S(2)}, u32[]{:S(2)}) collective-permute-start(bf16[1,256,640]{2,1,0:T(8,128)(2,1)S(1)} %collective-permute-done.21), channel_id=1, source_target_pairs={{0,64},{16,80},{32,96},{48,112},{64,128},{80,144},{96,160},{112,17... | collective-permute-start | bytes 983048 | tf_op jit(solution)/shard_map/ppermute | solution.py:193
  76.3 3.1 %collective-permute-start.10 = (bf16[2,256,640]{2,1,0:T(8,128)(2,1)S(1)}, bf16[2,256,640]{2,1,0:T(8,128)(2,1)S(1)}, u32[]{:S(2)}, u32[]{:S(2)}) collective-permute-start(bf16[2,256,640]{2,1,0:T(8,128)(2,1)S(1)} %pad_maximum_fusion), channel_id=1, source_target_pairs={{0,448},{16,464},{32,480},{48,496},{64,0},{80,16},{96,32},{112,48}... | collective-permute-start | bytes 1966088 | tf_op jit(solution)/shard_map/ppermute | solution.py:191
  79.4 2.2 %collective-permute-start.11 = (bf16[2,256,640]{2,1,0:T(8,128)(2,1)S(1)}, bf16[2,256,640]{2,1,0:T(8,128)(2,1)}, u32[]{:S(2)}, u32[]{:S(2)}) collective-permute-start(bf16[2,256,640]{2,1,0:T(8,128)(2,1)S(1)} %pad_maximum_fusion), channel_id=1, source_target_pairs={{0,64},{16,80},{32,96},{48,112},{64,128},{80,144},{96,160},{112,17... | collective-permute-start | bytes 1966088 | tf_op jit(solution)/shard_map/ppermute | solution.py:193
  81.6 1.9 collective-permute-start.5
  83.6 4.6 %collective-permute-start.24 = (bf16[1,256,640]{2,1,0:T(8,128)(2,1)}, bf16[1,256,640]{2,1,0:T(8,128)(2,1)S(1)}, u32[]{:S(2)}, u32[]{:S(2)}) collective-permute-start(bf16[1,256,640]{2,1,0:T(8,128)(2,1)} %collective-permute-done.22), channel_id=1, source_target_pairs={{0,448},{16,464},{32,480},{48,496},{64,0},{80,16},{96,32},{112,48}... | collective-permute-start | bytes 983048 | tf_op jit(solution)/shard_map/ppermute | solution.py:191
  88.2 1.9 collective-permute-start.25
  90.6 13.9 %collective-permute-done.5 = bf16[1,256,640]{2,1,0:T(8,128)(2,1)S(1)} collective-permute-done((bf16[1,256,640]{2,1,0:T(8,128)(2,1)}, bf16[1,256,640]{2,1,0:T(8,128)(2,1)S(1)}, u32[]{:S(2)}, u32[]{:S(2)}) %collective-permute-start.5) | collective-permute-done | bytes 327712 | tf_op jit(solution)/shard_map/ppermute | solution.py:193
  104.5 1.9 collective-permute-start.7
  107.1 3.4 %collective-permute-start.6 = (bf16[1,128,640]{2,1,0:T(8,128)(2,1)}, bf16[1,128,640]{2,1,0:T(8,128)(2,1)}, u32[]{:S(2)}, u32[]{:S(2)}) collective-permute-start(bf16[1,128,640]{2,1,0:T(8,128)(2,1)} %slice.118), channel_id=1, source_target_pairs={{0,64},{16,80},{32,96},{48,112},{64,128},{80,144},{96,160},{112,17... | collective-permute-start | bytes 491528 | tf_op jit(solution)/shard_map/ppermute | solution.py:198
  111.4 2.8 %collective-permute-start.27 = (bf16[1,128,640]{2,1,0:T(8,128)(2,1)}, bf16[1,128,640]{2,1,0:T(8,128)(2,1)}, u32[]{:S(2)}, u32[]{:S(2)}) collective-permute-start(bf16[1,128,640]{2,1,0:T(8,128)(2,1)} %slice.139), channel_id=1, source_target_pairs={{0,448},{16,464},{32,480},{48,496},{64,0},{80,16},{96,32},{112,48}... | collective-permute-start | bytes 491528 | tf_op jit(solution)/shard_map/ppermute | solution.py:199
  115.0 2.4 %collective-permute-start.26 = (bf16[1,128,640]{2,1,0:T(8,128)(2,1)}, bf16[1,128,640]{2,1,0:T(8,128)(2,1)}, u32[]{:S(2)}, u32[]{:S(2)}) collective-permute-start(bf16[1,128,640]{2,1,0:T(8,128)(2,1)} %slice.138), channel_id=1, source_target_pairs={{0,64},{16,80},{32,96},{48,112},{64,128},{80,144},{96,160},{112,17... | collective-permute-start | bytes 491528 | tf_op jit(solution)/shard_map/ppermute | solution.py:198
  117.4 2.9 %collective-permute-start.13 = (bf16[2,256,640]{2,1,0:T(8,128)(2,1)}, bf16[2,256,640]{2,1,0:T(8,128)(2,1)S(1)}, u32[]{:S(2)}, u32[]{:S(2)}) collective-permute-start(bf16[2,256,640]{2,1,0:T(8,128)(2,1)} %collective-permute-done.11), channel_id=1, source_target_pairs={{0,64},{16,80},{32,96},{48,112},{64,128},{80,144},{96,160},{112,17... | collective-permute-start | bytes 1966088 | tf_op jit(solution)/shard_map/ppermute | solution.py:193
  120.3 1.5 fusion.32
  121.8 1.8 fusion.35
  123.6 1.4 fusion.38
  125.0 1.4 fusion.40
  126.5 1.4 fusion.24
  129.4 1.4 convolution_add_fusion.8
  132.6 1.4 fusion.5
  134.0 1.4 fusion.48
  135.3 3.6 %collective-permute-start.12 = (bf16[2,256,640]{2,1,0:T(8,128)(2,1)S(1)}, bf16[2,256,640]{2,1,0:T(8,128)(2,1)S(1)}, u32[]{:S(2)}, u32[]{:S(2)}) collective-permute-start(bf16[2,256,640]{2,1,0:T(8,128)(2,1)S(1)} %collective-permute-done.10), channel_id=1, source_target_pairs={{0,448},{16,464},{32,480},{48,496},{64,0},{80,16},{96,32},{112,48}... | collective-permute-start | bytes 1966088 | tf_op jit(solution)/shard_map/ppermute | solution.py:191
  139.0 1.4 fusion.29
  140.4 1.4 fusion.26
  143.1 1.9 collective-permute-start.15
  145.0 1.6 collective-permute-done.12
  146.7 4.8 %collective-permute-start.14 = (bf16[2,256,640]{2,1,0:T(8,128)(2,1)S(1)}, bf16[2,256,640]{2,1,0:T(8,128)(2,1)S(1)}, u32[]{:S(2)}, u32[]{:S(2)}) collective-permute-start(bf16[2,256,640]{2,1,0:T(8,128)(2,1)S(1)} %collective-permute-done.12), channel_id=1, source_target_pairs={{0,448},{16,464},{32,480},{48,496},{64,0},{80,16},{96,32},{112,48}... | collective-permute-start | bytes 1966088 | tf_op jit(solution)/shard_map/ppermute | solution.py:191
  153.5 2.2 %collective-permute-done.15 = bf16[2,256,640]{2,1,0:T(8,128)(2,1)S(1)} collective-permute-done((bf16[2,256,640]{2,1,0:T(8,128)(2,1)S(1)}, bf16[2,256,640]{2,1,0:T(8,128)(2,1)S(1)}, u32[]{:S(2)}, u32[]{:S(2)}) %collective-permute-start.15) | collective-permute-done | bytes 655392 | tf_op jit(solution)/shard_map/ppermute | solution.py:193
  155.7 1.9 collective-permute-start.16
  157.6 4.9 %collective-permute-done.14 = bf16[2,256,640]{2,1,0:T(8,128)(2,1)S(1)} collective-permute-done((bf16[2,256,640]{2,1,0:T(8,128)(2,1)S(1)}, bf16[2,256,640]{2,1,0:T(8,128)(2,1)S(1)}, u32[]{:S(2)}, u32[]{:S(2)}) %collective-permute-start.14) | collective-permute-done | bytes 655392 | tf_op jit(solution)/shard_map/ppermute | solution.py:191
  162.6 5.2 %collective-permute-start.17 = (bf16[2,128,640]{2,1,0:T(8,128)(2,1)S(1)}, bf16[2,128,640]{2,1,0:T(8,128)(2,1)S(1)}, u32[]{:S(2)}, u32[]{:S(2)}) collective-permute-start(bf16[2,128,640]{2,1,0:T(8,128)(2,1)S(1)} %slice.133), channel_id=1, source_target_pairs={{0,448},{16,464},{32,480},{48,496},{64,0},{80,16},{96,32},{112,48}... | collective-permute-start | bytes 983048 | tf_op jit(solution)/shard_map/ppermute | solution.py:199
  169.0 6.2 %collective-permute-done.17 = bf16[2,128,640]{2,1,0:T(8,128)(2,1)S(1)} collective-permute-done((bf16[2,128,640]{2,1,0:T(8,128)(2,1)S(1)}, bf16[2,128,640]{2,1,0:T(8,128)(2,1)S(1)}, u32[]{:S(2)}, u32[]{:S(2)}) %collective-permute-start.17) | collective-permute-done | bytes 327712 | tf_op jit(solution)/shard_map/ppermute | solution.py:199
  177.0 13.5 %collective-permute-start.28 = (bf16[512,128]{1,0:T(8,128)(2,1)S(1)}, bf16[512,128]{1,0:T(8,128)(2,1)S(1)}, u32[]{:S(2)}, u32[]{:S(2)}) collective-permute-start(bf16[512,128]{1,0:T(8,128)(2,1)S(1)} %slice.179), channel_id=1, source_target_pairs={{0,1},{1,0},{2,3},{3,2},{4,5},{5,4},{6,7},{7,6},{8,9},{9,8},{10,11... | collective-permute-start | bytes 393224 | tf_op jit(solution)/shard_map/ppermute | solution.py:254
  192.2 6.1 %shard_map.64 = bf16[512,512]{1,0:T(8,128)(2,1)} custom-call(f32[512,640]{1,0:T(8,128)} %copy-done.1, bf16[512,128]{1,0:T(8,128)(2,1)} %get-tuple-element.24.k_ref, bf16[512,128]{1,0:T(8,128)(2,1)} %get-tuple-element.23.v_ref, f32[512,64]{1,0:T(8,128)} %get-tuple-element.17.cos_ref, f32[512,64]{1,0:T(8,128)} %get-tuple-element.18.sin_ref, ...), custom_call_target="tpu_custom_call" | custom-call | flops 538968064 | bytes 2097152 | tf_op jit(solution)/shard_map/pallas_call | solution.py:113
  (100 shorter events, 17.2 us)
Async XLA Ops:
  6.5 4.3 %copy-start.2 = (bf16[256,512]{1,0:T(8,128)(2,1)S(1)}, bf16[256,512]{1,0:T(8,128)(2,1)}, u32[]{:S(2)}) copy-start(bf16[256,512]{1,0:T(8,128)(2,1)} %param.9) | copy-start | bytes 786436
  6.5 110.9 %all-gather.2.cloned.1.call-start = ((), (), s32[]{:S(2)}) async-start(), calls=%async_computation | async-start | bytes 8912896 | tf_op jit(solution)/shard_map/all_gather | solution.py:237
  7.8 23.1 %copy-start.11 = (s32[512]{0:T(512)S(1)}, s32[512]{0:T(512)}, u32[]{:S(2)}) copy-start(s32[512]{0:T(512)} %param.7) | copy-start | bytes 6148
  10.9 21.8 %collective-permute-start.9 = (bf16[256,640]{1,0:T(8,128)(2,1)S(1)}, bf16[256,640]{1,0:T(8,128)(2,1)S(1)}, u32[]{:S(2)}, u32[]{:S(2)}) collective-permute-start(bf16[256,640]{1,0:T(8,128)(2,1)S(1)} %get-tuple-element.22), channel_id=1, source_target_pairs={{0,16},{16,32},{32,48},{48,0},{64,80},{80,96},{96,112},{112,64},{1... | collective-permute-start | bytes 983048 | tf_op jit(solution)/shard_map/ppermute | solution.py:149
  15.1 21.0 %collective-permute-start.8 = (bf16[256,640]{1,0:T(8,128)(2,1)S(1)}, bf16[256,640]{1,0:T(8,128)(2,1)S(1)}, u32[]{:S(2)}, u32[]{:S(2)}) collective-permute-start(bf16[256,640]{1,0:T(8,128)(2,1)S(1)} %get-tuple-element.22), channel_id=1, source_target_pairs={{0,48},{16,0},{32,16},{48,32},{64,112},{80,64},{96,80},{112,96},{1... | collective-permute-start | bytes 983048 | tf_op jit(solution)/shard_map/ppermute | solution.py:148
  18.3 21.9 %collective-permute-start = (bf16[1,256,640]{2,1,0:T(8,128)(2,1)S(1)}, bf16[1,256,640]{2,1,0:T(8,128)(2,1)S(1)}, u32[]{:S(2)}, u32[]{:S(2)}) collective-permute-start(bf16[1,256,640]{2,1,0:T(8,128)(2,1)S(1)} %get-tuple-element.21), channel_id=1, source_target_pairs={{0,448},{16,464},{32,480},{48,496},{64,0},{80,16},{96,32},{112,48}... | collective-permute-start | bytes 983048 | tf_op jit(solution)/shard_map/ppermute | solution.py:191
  29.0 20.5 %collective-permute-start.1 = (bf16[1,256,640]{2,1,0:T(8,128)(2,1)S(1)}, bf16[1,256,640]{2,1,0:T(8,128)(2,1)S(1)}, u32[]{:S(2)}, u32[]{:S(2)}) collective-permute-start(bf16[1,256,640]{2,1,0:T(8,128)(2,1)S(1)} %get-tuple-element.21), channel_id=1, source_target_pairs={{0,64},{16,80},{32,96},{48,112},{64,128},{80,144},{96,160},{112,17... | collective-permute-start | bytes 983048 | tf_op jit(solution)/shard_map/ppermute | solution.py:193
  32.8 18.7 %collective-permute-start.18 = (bf16[128,640]{1,0:T(8,128)(2,1)S(1)}, bf16[128,640]{1,0:T(8,128)(2,1)S(1)}, u32[]{:S(2)}, u32[]{:S(2)}) collective-permute-start(bf16[128,640]{1,0:T(8,128)(2,1)S(1)} %slice.136), channel_id=1, source_target_pairs={{0,16},{16,32},{32,48},{48,0},{64,80},{80,96},{96,112},{112,64},{1... | collective-permute-start | bytes 491528 | tf_op jit(solution)/shard_map/ppermute | solution.py:155
  36.1 16.5 %collective-permute-start.19 = (bf16[128,640]{1,0:T(8,128)(2,1)S(1)}, bf16[128,640]{1,0:T(8,128)(2,1)S(1)}, u32[]{:S(2)}, u32[]{:S(2)}) collective-permute-start(bf16[128,640]{1,0:T(8,128)(2,1)S(1)} %slice.137), channel_id=1, source_target_pairs={{0,48},{16,0},{32,16},{48,32},{64,112},{80,64},{96,80},{112,96},{1... | collective-permute-start | bytes 491528 | tf_op jit(solution)/shard_map/ppermute | solution.py:156
  40.3 36.0 %copy-start.7 = (bf16[1,256,640]{2,1,0:T(8,128)(2,1)}, bf16[1,256,640]{2,1,0:T(8,128)(2,1)S(1)}, u32[]{:S(2)}) copy-start(bf16[1,256,640]{2,1,0:T(8,128)(2,1)S(1)} %collective-permute-done) | copy-start | bytes 983044
  40.3 26.0 %collective-permute-start.2 = (bf16[1,256,640]{2,1,0:T(8,128)(2,1)S(1)}, bf16[1,256,640]{2,1,0:T(8,128)(2,1)S(1)}, u32[]{:S(2)}, u32[]{:S(2)}) collective-permute-start(bf16[1,256,640]{2,1,0:T(8,128)(2,1)S(1)} %collective-permute-done), channel_id=1, source_target_pairs={{0,448},{16,464},{32,480},{48,496},{64,0},{80,16},{96,32},{112,48}... | collective-permute-start | bytes 983048 | tf_op jit(solution)/shard_map/ppermute | solution.py:191
  49.5 32.1 %copy-start.9 = (bf16[1,256,640]{2,1,0:T(8,128)(2,1)}, bf16[1,256,640]{2,1,0:T(8,128)(2,1)S(1)}, u32[]{:S(2)}) copy-start(bf16[1,256,640]{2,1,0:T(8,128)(2,1)S(1)} %collective-permute-done.1) | copy-start | bytes 983044
  49.5 30.0 %collective-permute-start.3 = (bf16[1,256,640]{2,1,0:T(8,128)(2,1)S(1)}, bf16[1,256,640]{2,1,0:T(8,128)(2,1)}, u32[]{:S(2)}, u32[]{:S(2)}) collective-permute-start(bf16[1,256,640]{2,1,0:T(8,128)(2,1)S(1)} %collective-permute-done.1), channel_id=1, source_target_pairs={{0,64},{16,80},{32,96},{48,112},{64,128},{80,144},{96,160},{112,17... | collective-permute-start | bytes 983048 | tf_op jit(solution)/shard_map/ppermute | solution.py:193
  52.7 18.2 %collective-permute-start.20 = (bf16[1,256,640]{2,1,0:T(8,128)(2,1)S(1)}, bf16[1,256,640]{2,1,0:T(8,128)(2,1)S(1)}, u32[]{:S(2)}, u32[]{:S(2)}) collective-permute-start(bf16[1,256,640]{2,1,0:T(8,128)(2,1)S(1)} %bitcast.105), channel_id=1, source_target_pairs={{0,448},{16,464},{32,480},{48,496},{64,0},{80,16},{96,32},{112,48}... | collective-permute-start | bytes 983048 | tf_op jit(solution)/shard_map/ppermute | solution.py:191
  62.5 10.4 %collective-permute-start.21 = (bf16[1,256,640]{2,1,0:T(8,128)(2,1)S(1)}, bf16[1,256,640]{2,1,0:T(8,128)(2,1)S(1)}, u32[]{:S(2)}, u32[]{:S(2)}) collective-permute-start(bf16[1,256,640]{2,1,0:T(8,128)(2,1)S(1)} %bitcast.106), channel_id=1, source_target_pairs={{0,64},{16,80},{32,96},{48,112},{64,128},{80,144},{96,160},{112,17... | collective-permute-start | bytes 983048 | tf_op jit(solution)/shard_map/ppermute | solution.py:193
  66.3 15.3 %copy-start.3 = (bf16[1,256,640]{2,1,0:T(8,128)(2,1)}, bf16[1,256,640]{2,1,0:T(8,128)(2,1)S(1)}, u32[]{:S(2)}) copy-start(bf16[1,256,640]{2,1,0:T(8,128)(2,1)S(1)} %collective-permute-done.2) | copy-start | bytes 983044
  66.4 15.3 %collective-permute-start.4 = (bf16[1,256,640]{2,1,0:T(8,128)(2,1)S(1)}, bf16[1,256,640]{2,1,0:T(8,128)(2,1)S(1)}, u32[]{:S(2)}, u32[]{:S(2)}) collective-permute-start(bf16[1,256,640]{2,1,0:T(8,128)(2,1)S(1)} %collective-permute-done.2), channel_id=1, source_target_pairs={{0,448},{16,464},{32,480},{48,496},{64,0},{80,16},{96,32},{112,48}... | collective-permute-start | bytes 983048 | tf_op jit(solution)/shard_map/ppermute | solution.py:191
  70.9 17.2 %copy-start.5 = (bf16[1,256,640]{2,1,0:T(8,128)(2,1)}, bf16[1,256,640]{2,1,0:T(8,128)(2,1)S(1)}, u32[]{:S(2)}) copy-start(bf16[1,256,640]{2,1,0:T(8,128)(2,1)S(1)} %collective-permute-done.20) | copy-start | bytes 983044
  71.0 12.6 %collective-permute-start.22 = (bf16[1,256,640]{2,1,0:T(8,128)(2,1)S(1)}, bf16[1,256,640]{2,1,0:T(8,128)(2,1)}, u32[]{:S(2)}, u32[]{:S(2)}) collective-permute-start(bf16[1,256,640]{2,1,0:T(8,128)(2,1)S(1)} %collective-permute-done.20), channel_id=1, source_target_pairs={{0,448},{16,464},{32,480},{48,496},{64,0},{80,16},{96,32},{112,48}... | collective-permute-start | bytes 983048 | tf_op jit(solution)/shard_map/ppermute | solution.py:191
  72.9 15.3 %copy-start.6 = (bf16[1,256,640]{2,1,0:T(8,128)(2,1)}, bf16[1,256,640]{2,1,0:T(8,128)(2,1)S(1)}, u32[]{:S(2)}) copy-start(bf16[1,256,640]{2,1,0:T(8,128)(2,1)S(1)} %collective-permute-done.21) | copy-start | bytes 983044
  72.9 15.3 %collective-permute-start.23 = (bf16[1,256,640]{2,1,0:T(8,128)(2,1)S(1)}, bf16[1,256,640]{2,1,0:T(8,128)(2,1)}, u32[]{:S(2)}, u32[]{:S(2)}) collective-permute-start(bf16[1,256,640]{2,1,0:T(8,128)(2,1)S(1)} %collective-permute-done.21), channel_id=1, source_target_pairs={{0,64},{16,80},{32,96},{48,112},{64,128},{80,144},{96,160},{112,17... | collective-permute-start | bytes 983048 | tf_op jit(solution)/shard_map/ppermute | solution.py:193
  76.3 38.7 %collective-permute-start.10 = (bf16[2,256,640]{2,1,0:T(8,128)(2,1)S(1)}, bf16[2,256,640]{2,1,0:T(8,128)(2,1)S(1)}, u32[]{:S(2)}, u32[]{:S(2)}) collective-permute-start(bf16[2,256,640]{2,1,0:T(8,128)(2,1)S(1)} %pad_maximum_fusion), channel_id=1, source_target_pairs={{0,448},{16,464},{32,480},{48,496},{64,0},{80,16},{96,32},{112,48}... | collective-permute-start | bytes 1966088 | tf_op jit(solution)/shard_map/ppermute | solution.py:191
  79.4 38.0 %collective-permute-start.11 = (bf16[2,256,640]{2,1,0:T(8,128)(2,1)S(1)}, bf16[2,256,640]{2,1,0:T(8,128)(2,1)}, u32[]{:S(2)}, u32[]{:S(2)}) collective-permute-start(bf16[2,256,640]{2,1,0:T(8,128)(2,1)S(1)} %pad_maximum_fusion), channel_id=1, source_target_pairs={{0,64},{16,80},{32,96},{48,112},{64,128},{80,144},{96,160},{112,17... | collective-permute-start | bytes 1966088 | tf_op jit(solution)/shard_map/ppermute | solution.py:193
  81.6 22.9 %collective-permute-start.5 = (bf16[1,256,640]{2,1,0:T(8,128)(2,1)}, bf16[1,256,640]{2,1,0:T(8,128)(2,1)S(1)}, u32[]{:S(2)}, u32[]{:S(2)}) collective-permute-start(bf16[1,256,640]{2,1,0:T(8,128)(2,1)} %collective-permute-done.3), channel_id=1, source_target_pairs={{0,64},{16,80},{32,96},{48,112},{64,128},{80,144},{96,160},{112,17... | collective-permute-start | bytes 983048 | tf_op jit(solution)/shard_map/ppermute | solution.py:193
  83.6 23.5 %collective-permute-start.24 = (bf16[1,256,640]{2,1,0:T(8,128)(2,1)}, bf16[1,256,640]{2,1,0:T(8,128)(2,1)S(1)}, u32[]{:S(2)}, u32[]{:S(2)}) collective-permute-start(bf16[1,256,640]{2,1,0:T(8,128)(2,1)} %collective-permute-done.22), channel_id=1, source_target_pairs={{0,448},{16,464},{32,480},{48,496},{64,0},{80,16},{96,32},{112,48}... | collective-permute-start | bytes 983048 | tf_op jit(solution)/shard_map/ppermute | solution.py:191
  88.2 23.2 %collective-permute-start.25 = (bf16[1,256,640]{2,1,0:T(8,128)(2,1)}, bf16[1,256,640]{2,1,0:T(8,128)(2,1)S(1)}, u32[]{:S(2)}, u32[]{:S(2)}) collective-permute-start(bf16[1,256,640]{2,1,0:T(8,128)(2,1)} %collective-permute-done.23), channel_id=1, source_target_pairs={{0,64},{16,80},{32,96},{48,112},{64,128},{80,144},{96,160},{112,17... | collective-permute-start | bytes 983048 | tf_op jit(solution)/shard_map/ppermute | solution.py:193
  104.5 35.9 %collective-permute-start.7 = (bf16[1,128,640]{2,1,0:T(8,128)(2,1)S(1)}, bf16[1,128,640]{2,1,0:T(8,128)(2,1)}, u32[]{:S(2)}, u32[]{:S(2)}) collective-permute-start(bf16[1,128,640]{2,1,0:T(8,128)(2,1)S(1)} %slice.119), channel_id=1, source_target_pairs={{0,448},{16,464},{32,480},{48,496},{64,0},{80,16},{96,32},{112,48}... | collective-permute-start | bytes 491528 | tf_op jit(solution)/shard_map/ppermute | solution.py:199
  107.1 33.3 %collective-permute-start.6 = (bf16[1,128,640]{2,1,0:T(8,128)(2,1)}, bf16[1,128,640]{2,1,0:T(8,128)(2,1)}, u32[]{:S(2)}, u32[]{:S(2)}) collective-permute-start(bf16[1,128,640]{2,1,0:T(8,128)(2,1)} %slice.118), channel_id=1, source_target_pairs={{0,64},{16,80},{32,96},{48,112},{64,128},{80,144},{96,160},{112,17... | collective-permute-start | bytes 491528 | tf_op jit(solution)/shard_map/ppermute | solution.py:198
  111.4 23.9 %collective-permute-start.27 = (bf16[1,128,640]{2,1,0:T(8,128)(2,1)}, bf16[1,128,640]{2,1,0:T(8,128)(2,1)}, u32[]{:S(2)}, u32[]{:S(2)}) collective-permute-start(bf16[1,128,640]{2,1,0:T(8,128)(2,1)} %slice.139), channel_id=1, source_target_pairs={{0,448},{16,464},{32,480},{48,496},{64,0},{80,16},{96,32},{112,48}... | collective-permute-start | bytes 491528 | tf_op jit(solution)/shard_map/ppermute | solution.py:199
  115.0 24.0 %collective-permute-start.26 = (bf16[1,128,640]{2,1,0:T(8,128)(2,1)}, bf16[1,128,640]{2,1,0:T(8,128)(2,1)}, u32[]{:S(2)}, u32[]{:S(2)}) collective-permute-start(bf16[1,128,640]{2,1,0:T(8,128)(2,1)} %slice.138), channel_id=1, source_target_pairs={{0,64},{16,80},{32,96},{48,112},{64,128},{80,144},{96,160},{112,17... | collective-permute-start | bytes 491528 | tf_op jit(solution)/shard_map/ppermute | solution.py:198
  117.4 25.7 %collective-permute-start.13 = (bf16[2,256,640]{2,1,0:T(8,128)(2,1)}, bf16[2,256,640]{2,1,0:T(8,128)(2,1)S(1)}, u32[]{:S(2)}, u32[]{:S(2)}) collective-permute-start(bf16[2,256,640]{2,1,0:T(8,128)(2,1)} %collective-permute-done.11), channel_id=1, source_target_pairs={{0,64},{16,80},{32,96},{48,112},{64,128},{80,144},{96,160},{112,17... | collective-permute-start | bytes 1966088 | tf_op jit(solution)/shard_map/ppermute | solution.py:193
  120.3 7.6 %copy-start = (bf16[512,8192]{1,0:T(8,128)(2,1)S(1)}, bf16[512,8192]{1,0:T(8,128)(2,1)}, u32[]{:S(2)}) copy-start(bf16[512,8192]{1,0:T(8,128)(2,1)} %all-gather.2.cloned.1.call-done) | copy-start | bytes 25165828
  129.4 1.4 copy-start.8
  130.8 1.0 copy-start.10
  135.3 11.3 %collective-permute-start.12 = (bf16[2,256,640]{2,1,0:T(8,128)(2,1)S(1)}, bf16[2,256,640]{2,1,0:T(8,128)(2,1)S(1)}, u32[]{:S(2)}, u32[]{:S(2)}) collective-permute-start(bf16[2,256,640]{2,1,0:T(8,128)(2,1)S(1)} %collective-permute-done.10), channel_id=1, source_target_pairs={{0,448},{16,464},{32,480},{48,496},{64,0},{80,16},{96,32},{112,48}... | collective-permute-start | bytes 1966088 | tf_op jit(solution)/shard_map/ppermute | solution.py:191
  140.4 1.5 copy-start.4
  143.1 12.5 %collective-permute-start.15 = (bf16[2,256,640]{2,1,0:T(8,128)(2,1)S(1)}, bf16[2,256,640]{2,1,0:T(8,128)(2,1)S(1)}, u32[]{:S(2)}, u32[]{:S(2)}) collective-permute-start(bf16[2,256,640]{2,1,0:T(8,128)(2,1)S(1)} %collective-permute-done.13), channel_id=1, source_target_pairs={{0,64},{16,80},{32,96},{48,112},{64,128},{80,144},{96,160},{112,17... | collective-permute-start | bytes 1966088 | tf_op jit(solution)/shard_map/ppermute | solution.py:193
  146.7 15.9 %collective-permute-start.14 = (bf16[2,256,640]{2,1,0:T(8,128)(2,1)S(1)}, bf16[2,256,640]{2,1,0:T(8,128)(2,1)S(1)}, u32[]{:S(2)}, u32[]{:S(2)}) collective-permute-start(bf16[2,256,640]{2,1,0:T(8,128)(2,1)S(1)} %collective-permute-done.12), channel_id=1, source_target_pairs={{0,448},{16,464},{32,480},{48,496},{64,0},{80,16},{96,32},{112,48}... | collective-permute-start | bytes 1966088 | tf_op jit(solution)/shard_map/ppermute | solution.py:191
  155.7 13.2 %collective-permute-start.16 = (bf16[2,128,640]{2,1,0:T(8,128)(2,1)S(1)}, bf16[2,128,640]{2,1,0:T(8,128)(2,1)S(1)}, u32[]{:S(2)}, u32[]{:S(2)}) collective-permute-start(bf16[2,128,640]{2,1,0:T(8,128)(2,1)S(1)} %slice.132), channel_id=1, source_target_pairs={{0,64},{16,80},{32,96},{48,112},{64,128},{80,144},{96,160},{112,17... | collective-permute-start | bytes 983048 | tf_op jit(solution)/shard_map/ppermute | solution.py:198
  162.6 12.6 %collective-permute-start.17 = (bf16[2,128,640]{2,1,0:T(8,128)(2,1)S(1)}, bf16[2,128,640]{2,1,0:T(8,128)(2,1)S(1)}, u32[]{:S(2)}, u32[]{:S(2)}) collective-permute-start(bf16[2,128,640]{2,1,0:T(8,128)(2,1)S(1)} %slice.133), channel_id=1, source_target_pairs={{0,448},{16,464},{32,480},{48,496},{64,0},{80,16},{96,32},{112,48}... | collective-permute-start | bytes 983048 | tf_op jit(solution)/shard_map/ppermute | solution.py:199
  177.0 15.3 %copy-start.1 = (f32[512,640]{1,0:T(8,128)}, f32[512,640]{1,0:T(8,128)S(1)}, u32[]{:S(2)}) copy-start(f32[512,640]{1,0:T(8,128)S(1)} %fusion.15.q_ref) | copy-start | bytes 3932164
  177.0 14.5 %collective-permute-start.28 = (bf16[512,128]{1,0:T(8,128)(2,1)S(1)}, bf16[512,128]{1,0:T(8,128)(2,1)S(1)}, u32[]{:S(2)}, u32[]{:S(2)}) collective-permute-start(bf16[512,128]{1,0:T(8,128)(2,1)S(1)} %slice.179), channel_id=1, source_target_pairs={{0,1},{1,0},{2,3},{3,2},{4,5},{5,4},{6,7},{7,6},{8,9},{9,8},{10,11... | collective-permute-start | bytes 393224 | tf_op jit(solution)/shard_map/ppermute | solution.py:254
Sparse Core Ops, SparseCore 0:
  10.0 70.1 all-gather.1

commit v18 on v16

--- a/solution.py
+++ b/solution.py
@@ -56,7 +56,7 @@
     return mixed.astype(jnp.bfloat16)
 
 
-ROW_TILE = 64
+ROW_TILE = 128
 SEGMENT_MOST = 64
 
 

time: 195 us -> 195 us (level)
  no operation moved by 1% of the time
where the time goes in v18:
time: 195 us; the launch traced here: 193 us
  starting transfers between devices  87.2 us (45%)
  waiting for transfers between devices  47.2 us (24%)
  matrix products  24.4 us (13%)
  between operations  15.2 us (8%)
  other arithmetic  8.29 us (4%)
  Pallas kernels  5.95 us (3%)
  local copies, waits for them, and re-layouts  4.69 us (2%)
    ppermute x6, starting transfers between devices, ring_matmul(): from_right = lax.ppermute(from_right, axis, perm=moved(-1))  35.6 us
    dot_general x32, matrix products, product(): term = jnp.dot(lhs, part[piece], preferred_element_type=jnp.float32)  24.4 us
    ppermute x6, waiting for transfers between devices, ring_matmul(): from_right = lax.ppermute(from_right, axis, perm=moved(-1))  18.1 us
    ppermute x1, waiting for transfers between devices, ring_gather(): lax.ppermute(from_left[..., :cut, :], axis, perm=moved(1))  12.5 us
    ppermute x6, starting transfers between devices, ring_matmul(): from_left = lax.ppermute(from_left, axis, perm=moved(1))  11.5 us
    ppermute x1, starting transfers between devices, per_device(): other_rows = lax.ppermute(own_rows, 'weight', perm=partner)  11.2 us
    ppermute x2, starting transfers between devices, ring_matmul(): lax.ppermute(from_right[..., cut:, :], axis, perm=moved(-1))  9.78 us
    ppermute x6, waiting for transfers between devices, ring_matmul(): from_left = lax.ppermute(from_left, axis, perm=moved(1))  9.77 us
  transfers between devices with their start and end apart: 22, of which 8 were waited for; matrix products, arithmetic and copies ran while one was open for 16% of the time, Pallas kernels for 0%

profile of v18, /device:TPU:7, one launch (start us, length us, event | category | flops | bytes accessed | tf_op | source)
XLA Modules:
  0.0 192.9 jit_solution(16676435241814006337)
XLA Ops:
  6.5 1.3 fusion.18
  7.9 2.0 %fusion.20 = bf16[32,8192]{1,0:T(8,128)(2,1)} fusion(bf16[32,8192]{1,0:T(8,128)(2,1)} %param.6, f32[8192]{0:T(1024)} %param.8, f32[32]{0:T(128)S(1)} %add_rsqrt_fusion), kind=kLoop, calls=%fused_computation.35 | loop fusion | flops 1048576 | bytes 1081472 | tf_op jit(solution)/shard_map/convert_element_type | solution.py:224
  9.9 0.9 dynamic-slice_select_fusion
  11.6 5.9 %collective-permute-start.8 = (bf16[256,640]{1,0:T(8,128)(2,1)S(1)}, bf16[256,640]{1,0:T(8,128)(2,1)S(1)}, u32[]{:S(2)}, u32[]{:S(2)}) collective-permute-start(bf16[256,640]{1,0:T(8,128)(2,1)S(1)} %get-tuple-element.25), channel_id=1, source_target_pairs={{0,48},{16,0},{32,16},{48,32},{64,112},{80,64},{96,80},{112,96},{1... | collective-permute-start | bytes 983048 | tf_op jit(solution)/shard_map/ppermute | solution.py:151
  17.5 1.9 collective-permute-start.9
  19.4 10.7 %collective-permute-start = (bf16[1,256,640]{2,1,0:T(8,128)(2,1)}, bf16[1,256,640]{2,1,0:T(8,128)(2,1)}, u32[]{:S(2)}, u32[]{:S(2)}) collective-permute-start(bf16[1,256,640]{2,1,0:T(8,128)(2,1)} %get-tuple-element.24), channel_id=1, source_target_pairs={{0,448},{16,464},{32,480},{48,496},{64,0},{80,16},{96,32},{112,48}... | collective-permute-start | bytes 983048 | tf_op jit(solution)/shard_map/ppermute | solution.py:194
  30.1 1.9 collective-permute-start.1
  34.3 1.8 multiply_sine_fusion
  36.1 5.5 %collective-permute-start.11 = (bf16[128,640]{1,0:T(8,128)(2,1)S(1)}, bf16[128,640]{1,0:T(8,128)(2,1)S(1)}, u32[]{:S(2)}, u32[]{:S(2)}) collective-permute-start(bf16[128,640]{1,0:T(8,128)(2,1)S(1)} %slice.145), channel_id=1, source_target_pairs={{0,48},{16,0},{32,16},{48,32},{64,112},{80,64},{96,80},{112,96},{1... | collective-permute-start | bytes 491528 | tf_op jit(solution)/shard_map/ppermute | solution.py:159
  41.7 1.9 collective-permute-start.10
  43.7 1.1 collective-permute-done.11
  44.8 12.5 %collective-permute-done.10 = bf16[128,640]{1,0:T(8,128)(2,1)S(1)} collective-permute-done((bf16[128,640]{1,0:T(8,128)(2,1)S(1)}, bf16[128,640]{1,0:T(8,128)(2,1)S(1)}, u32[]{:S(2)}, u32[]{:S(2)}) %collective-permute-start.10) | collective-permute-done | bytes 163872 | tf_op jit(solution)/shard_map/ppermute | solution.py:158
  57.6 6.7 %collective-permute-start.12 = (bf16[3,256,640]{2,1,0:T(8,128)(2,1)S(1)}, bf16[3,256,640]{2,1,0:T(8,128)(2,1)S(1)}, u32[]{:S(2)}, u32[]{:S(2)}) collective-permute-start(bf16[3,256,640]{2,1,0:T(8,128)(2,1)S(1)} %pad_maximum_fusion), channel_id=1, source_target_pairs={{0,448},{16,464},{32,480},{48,496},{64,0},{80,16},{96,32},{112,48}... | collective-permute-start | bytes 2949128 | tf_op jit(solution)/shard_map/ppermute | solution.py:194
  64.4 1.9 collective-permute-start.13
  66.3 4.6 %collective-permute-start.2 = (bf16[1,256,640]{2,1,0:T(8,128)(2,1)}, bf16[1,256,640]{2,1,0:T(8,128)(2,1)}, u32[]{:S(2)}, u32[]{:S(2)}) collective-permute-start(bf16[1,256,640]{2,1,0:T(8,128)(2,1)} %collective-permute-done), channel_id=1, source_target_pairs={{0,448},{16,464},{32,480},{48,496},{64,0},{80,16},{96,32},{112,48}... | collective-permute-start | bytes 983048 | tf_op jit(solution)/shard_map/ppermute | solution.py:194
  70.9 1.9 collective-permute-start.3
  72.8 16.1 %collective-permute-done.2 = bf16[1,256,640]{2,1,0:T(8,128)(2,1)} collective-permute-done((bf16[1,256,640]{2,1,0:T(8,128)(2,1)}, bf16[1,256,640]{2,1,0:T(8,128)(2,1)}, u32[]{:S(2)}, u32[]{:S(2)}) %collective-permute-start.2) | collective-permute-done | bytes 327712 | tf_op jit(solution)/shard_map/ppermute | solution.py:194
  89.0 4.5 %collective-permute-start.4 = (bf16[1,256,640]{2,1,0:T(8,128)(2,1)}, bf16[1,256,640]{2,1,0:T(8,128)(2,1)}, u32[]{:S(2)}, u32[]{:S(2)}) collective-permute-start(bf16[1,256,640]{2,1,0:T(8,128)(2,1)} %collective-permute-done.2), channel_id=1, source_target_pairs={{0,448},{16,464},{32,480},{48,496},{64,0},{80,16},{96,32},{112,48}... | collective-permute-start | bytes 983048 | tf_op jit(solution)/shard_map/ppermute | solution.py:194
  93.5 1.9 collective-permute-start.5
  95.8 2.0 %collective-permute-done.4 = bf16[1,256,640]{2,1,0:T(8,128)(2,1)} collective-permute-done((bf16[1,256,640]{2,1,0:T(8,128)(2,1)}, bf16[1,256,640]{2,1,0:T(8,128)(2,1)}, u32[]{:S(2)}, u32[]{:S(2)}) %collective-permute-start.4) | collective-permute-done | bytes 327712 | tf_op jit(solution)/shard_map/ppermute | solution.py:194
  97.8 0.9 slice.143
  98.7 5.0 %collective-permute-start.7 = (bf16[1,128,640]{2,1,0:T(8,128)(2,1)S(1)}, bf16[1,128,640]{2,1,0:T(8,128)(2,1)}, u32[]{:S(2)}, u32[]{:S(2)}) collective-permute-start(bf16[1,128,640]{2,1,0:T(8,128)(2,1)S(1)} %slice.143), channel_id=1, source_target_pairs={{0,448},{16,464},{32,480},{48,496},{64,0},{80,16},{96,32},{112,48}... | collective-permute-start | bytes 491528 | tf_op jit(solution)/shard_map/ppermute | solution.py:202
  103.8 1.6 slice.142
  105.4 1.9 collective-permute-start.6
  107.3 1.9 collective-permute-start.15
  109.3 4.6 %collective-permute-start.14 = (bf16[3,256,640]{2,1,0:T(8,128)(2,1)S(1)}, bf16[3,256,640]{2,1,0:T(8,128)(2,1)S(1)}, u32[]{:S(2)}, u32[]{:S(2)}) collective-permute-start(bf16[3,256,640]{2,1,0:T(8,128)(2,1)S(1)} %collective-permute-done.12), channel_id=1, source_target_pairs={{0,448},{16,464},{32,480},{48,496},{64,0},{80,16},{96,32},{112,48}... | collective-permute-start | bytes 2949128 | tf_op jit(solution)/shard_map/ppermute | solution.py:194
  113.8 1.5 fusion.41
  115.3 1.7 fusion.33
  117.0 1.3 fusion.34
  118.3 1.3 fusion.31
  119.7 1.3 fusion.32
  121.0 1.4 fusion.43
  123.5 1.4 convolution_add_fusion.12
  124.9 1.4 fusion.46
  126.2 1.4 fusion.35
  127.6 1.4 convolution_add_fusion.11
  129.0 1.4 fusion
  130.7 1.9 collective-permute-start.17
  132.7 4.6 %collective-permute-start.16 = (bf16[3,256,640]{2,1,0:T(8,128)(2,1)S(1)}, bf16[3,256,640]{2,1,0:T(8,128)(2,1)S(1)}, u32[]{:S(2)}, u32[]{:S(2)}) collective-permute-start(bf16[3,256,640]{2,1,0:T(8,128)(2,1)S(1)} %collective-permute-done.14), channel_id=1, source_target_pairs={{0,448},{16,464},{32,480},{48,496},{64,0},{80,16},{96,32},{112,48}... | collective-permute-start | bytes 2949128 | tf_op jit(solution)/shard_map/ppermute | solution.py:194
  140.1 9.8 %collective-permute-done.17 = bf16[3,256,640]{2,1,0:T(8,128)(2,1)S(1)} collective-permute-done((bf16[3,256,640]{2,1,0:T(8,128)(2,1)S(1)}, bf16[3,256,640]{2,1,0:T(8,128)(2,1)S(1)}, u32[]{:S(2)}, u32[]{:S(2)}) %collective-permute-start.17) | collective-permute-done | bytes 983072 | tf_op jit(solution)/shard_map/ppermute | solution.py:196
  149.9 1.9 collective-permute-start.18
  151.9 4.8 %collective-permute-start.19 = (bf16[3,128,640]{2,1,0:T(8,128)(2,1)S(1)}, bf16[3,128,640]{2,1,0:T(8,128)(2,1)S(1)}, u32[]{:S(2)}, u32[]{:S(2)}) collective-permute-start(bf16[3,128,640]{2,1,0:T(8,128)(2,1)S(1)} %slice.165), channel_id=1, source_target_pairs={{0,448},{16,464},{32,480},{48,496},{64,0},{80,16},{96,32},{112,48}... | collective-permute-start | bytes 1474568 | tf_op jit(solution)/shard_map/ppermute | solution.py:202
  158.5 4.1 %collective-permute-done.18 = bf16[3,128,640]{2,1,0:T(8,128)(2,1)S(1)} collective-permute-done((bf16[3,128,640]{2,1,0:T(8,128)(2,1)S(1)}, bf16[3,128,640]{2,1,0:T(8,128)(2,1)S(1)}, u32[]{:S(2)}, u32[]{:S(2)}) %collective-permute-start.18) | collective-permute-done | bytes 491552 | tf_op jit(solution)/shard_map/ppermute | solution.py:201
  162.6 1.4 collective-permute-done.19
  165.8 1.4 fusion.17.q_ref
  167.2 11.2 %collective-permute-start.20 = (bf16[512,128]{1,0:T(8,128)(2,1)S(1)}, bf16[512,128]{1,0:T(8,128)(2,1)S(1)}, u32[]{:S(2)}, u32[]{:S(2)}) collective-permute-start(bf16[512,128]{1,0:T(8,128)(2,1)S(1)} %slice.226), channel_id=1, source_target_pairs={{0,1},{1,0},{2,3},{3,2},{4,5},{5,4},{6,7},{7,6},{8,9},{9,8},{10,11... | collective-permute-start | bytes 393224 | tf_op jit(solution)/shard_map/ppermute | solution.py:260
  178.4 0.9 copy.7.row_seg_ref
  180.1 6.0 %shard_map.64 = bf16[512,512]{1,0:T(8,128)(2,1)} custom-call(f32[512,640]{1,0:T(8,128)} %copy-done.1, bf16[512,128]{1,0:T(8,128)(2,1)} %get-tuple-element.27.k_ref, bf16[512,128]{1,0:T(8,128)(2,1)} %get-tuple-element.26.v_ref, f32[512,64]{1,0:T(8,128)} %get-tuple-element.17.cos_ref, f32[512,64]{1,0:T(8,128)} %get-tuple-element.18.sin_ref, ...), custom_call_target="tpu_custom_call" | custom-call | flops 538968064 | bytes 2097152 | tf_op jit(solution)/shard_map/pallas_call | solution.py:113
  (70 shorter events, 11.4 us)
Async XLA Ops:
  6.5 4.3 %copy-start.2 = (bf16[256,512]{1,0:T(8,128)(2,1)S(1)}, bf16[256,512]{1,0:T(8,128)(2,1)}, u32[]{:S(2)}) copy-start(bf16[256,512]{1,0:T(8,128)(2,1)} %param.9) | copy-start | bytes 786436
  6.5 100.8 %all-gather.2.cloned.1.call-start = ((), (), s32[]{:S(2)}) async-start(), calls=%async_computation | async-start | bytes 8912896 | tf_op jit(solution)/shard_map/all_gather | solution.py:237
  7.8 24.3 %copy-start.3 = (s32[512]{0:T(512)S(1)}, s32[512]{0:T(512)}, u32[]{:S(2)}) copy-start(s32[512]{0:T(512)} %param.7) | copy-start | bytes 6148
  11.6 24.5 %collective-permute-start.8 = (bf16[256,640]{1,0:T(8,128)(2,1)S(1)}, bf16[256,640]{1,0:T(8,128)(2,1)S(1)}, u32[]{:S(2)}, u32[]{:S(2)}) collective-permute-start(bf16[256,640]{1,0:T(8,128)(2,1)S(1)} %get-tuple-element.25), channel_id=1, source_target_pairs={{0,48},{16,0},{32,16},{48,32},{64,112},{80,64},{96,80},{112,96},{1... | collective-permute-start | bytes 983048 | tf_op jit(solution)/shard_map/ppermute | solution.py:151
  17.5 24.1 %collective-permute-start.9 = (bf16[256,640]{1,0:T(8,128)(2,1)S(1)}, bf16[256,640]{1,0:T(8,128)(2,1)S(1)}, u32[]{:S(2)}, u32[]{:S(2)}) collective-permute-start(bf16[256,640]{1,0:T(8,128)(2,1)S(1)} %get-tuple-element.25), channel_id=1, source_target_pairs={{0,16},{16,32},{32,48},{48,0},{64,80},{80,96},{96,112},{112,64},{1... | collective-permute-start | bytes 983048 | tf_op jit(solution)/shard_map/ppermute | solution.py:153
  19.4 46.9 %collective-permute-start = (bf16[1,256,640]{2,1,0:T(8,128)(2,1)}, bf16[1,256,640]{2,1,0:T(8,128)(2,1)}, u32[]{:S(2)}, u32[]{:S(2)}) collective-permute-start(bf16[1,256,640]{2,1,0:T(8,128)(2,1)} %get-tuple-element.24), channel_id=1, source_target_pairs={{0,448},{16,464},{32,480},{48,496},{64,0},{80,16},{96,32},{112,48}... | collective-permute-start | bytes 983048 | tf_op jit(solution)/shard_map/ppermute | solution.py:194
  30.1 40.8 %collective-permute-start.1 = (bf16[1,256,640]{2,1,0:T(8,128)(2,1)}, bf16[1,256,640]{2,1,0:T(8,128)(2,1)}, u32[]{:S(2)}, u32[]{:S(2)}) collective-permute-start(bf16[1,256,640]{2,1,0:T(8,128)(2,1)} %get-tuple-element.24), channel_id=1, source_target_pairs={{0,64},{16,80},{32,96},{48,112},{64,128},{80,144},{96,160},{112,17... | collective-permute-start | bytes 983048 | tf_op jit(solution)/shard_map/ppermute | solution.py:196
  36.1 8.7 %collective-permute-start.11 = (bf16[128,640]{1,0:T(8,128)(2,1)S(1)}, bf16[128,640]{1,0:T(8,128)(2,1)S(1)}, u32[]{:S(2)}, u32[]{:S(2)}) collective-permute-start(bf16[128,640]{1,0:T(8,128)(2,1)S(1)} %slice.145), channel_id=1, source_target_pairs={{0,48},{16,0},{32,16},{48,32},{64,112},{80,64},{96,80},{112,96},{1... | collective-permute-start | bytes 491528 | tf_op jit(solution)/shard_map/ppermute | solution.py:159
  41.7 15.7 %collective-permute-start.10 = (bf16[128,640]{1,0:T(8,128)(2,1)S(1)}, bf16[128,640]{1,0:T(8,128)(2,1)S(1)}, u32[]{:S(2)}, u32[]{:S(2)}) collective-permute-start(bf16[128,640]{1,0:T(8,128)(2,1)S(1)} %slice.144), channel_id=1, source_target_pairs={{0,16},{16,32},{32,48},{48,0},{64,80},{80,96},{96,112},{112,64},{1... | collective-permute-start | bytes 491528 | tf_op jit(solution)/shard_map/ppermute | solution.py:158
  57.6 49.6 %collective-permute-start.12 = (bf16[3,256,640]{2,1,0:T(8,128)(2,1)S(1)}, bf16[3,256,640]{2,1,0:T(8,128)(2,1)S(1)}, u32[]{:S(2)}, u32[]{:S(2)}) collective-permute-start(bf16[3,256,640]{2,1,0:T(8,128)(2,1)S(1)} %pad_maximum_fusion), channel_id=1, source_target_pairs={{0,448},{16,464},{32,480},{48,496},{64,0},{80,16},{96,32},{112,48}... | collective-permute-start | bytes 2949128 | tf_op jit(solution)/shard_map/ppermute | solution.py:194
  64.4 42.9 %collective-permute-start.13 = (bf16[3,256,640]{2,1,0:T(8,128)(2,1)S(1)}, bf16[3,256,640]{2,1,0:T(8,128)(2,1)S(1)}, u32[]{:S(2)}, u32[]{:S(2)}) collective-permute-start(bf16[3,256,640]{2,1,0:T(8,128)(2,1)S(1)} %pad_maximum_fusion), channel_id=1, source_target_pairs={{0,64},{16,80},{32,96},{48,112},{64,128},{80,144},{96,160},{112,17... | collective-permute-start | bytes 2949128 | tf_op jit(solution)/shard_map/ppermute | solution.py:196
  66.3 22.6 %collective-permute-start.2 = (bf16[1,256,640]{2,1,0:T(8,128)(2,1)}, bf16[1,256,640]{2,1,0:T(8,128)(2,1)}, u32[]{:S(2)}, u32[]{:S(2)}) collective-permute-start(bf16[1,256,640]{2,1,0:T(8,128)(2,1)} %collective-permute-done), channel_id=1, source_target_pairs={{0,448},{16,464},{32,480},{48,496},{64,0},{80,16},{96,32},{112,48}... | collective-permute-start | bytes 983048 | tf_op jit(solution)/shard_map/ppermute | solution.py:194
  70.9 22.6 %collective-permute-start.3 = (bf16[1,256,640]{2,1,0:T(8,128)(2,1)}, bf16[1,256,640]{2,1,0:T(8,128)(2,1)}, u32[]{:S(2)}, u32[]{:S(2)}) collective-permute-start(bf16[1,256,640]{2,1,0:T(8,128)(2,1)} %collective-permute-done.1), channel_id=1, source_target_pairs={{0,64},{16,80},{32,96},{48,112},{64,128},{80,144},{96,160},{112,17... | collective-permute-start | bytes 983048 | tf_op jit(solution)/shard_map/ppermute | solution.py:196
  89.0 8.8 %collective-permute-start.4 = (bf16[1,256,640]{2,1,0:T(8,128)(2,1)}, bf16[1,256,640]{2,1,0:T(8,128)(2,1)}, u32[]{:S(2)}, u32[]{:S(2)}) collective-permute-start(bf16[1,256,640]{2,1,0:T(8,128)(2,1)} %collective-permute-done.2), channel_id=1, source_target_pairs={{0,448},{16,464},{32,480},{48,496},{64,0},{80,16},{96,32},{112,48}... | collective-permute-start | bytes 983048 | tf_op jit(solution)/shard_map/ppermute | solution.py:194
  93.5 10.3 %collective-permute-start.5 = (bf16[1,256,640]{2,1,0:T(8,128)(2,1)}, bf16[1,256,640]{2,1,0:T(8,128)(2,1)}, u32[]{:S(2)}, u32[]{:S(2)}) collective-permute-start(bf16[1,256,640]{2,1,0:T(8,128)(2,1)} %collective-permute-done.3), channel_id=1, source_target_pairs={{0,64},{16,80},{32,96},{48,112},{64,128},{80,144},{96,160},{112,17... | collective-permute-start | bytes 983048 | tf_op jit(solution)/shard_map/ppermute | solution.py:196
  98.7 27.5 %collective-permute-start.7 = (bf16[1,128,640]{2,1,0:T(8,128)(2,1)S(1)}, bf16[1,128,640]{2,1,0:T(8,128)(2,1)}, u32[]{:S(2)}, u32[]{:S(2)}) collective-permute-start(bf16[1,128,640]{2,1,0:T(8,128)(2,1)S(1)} %slice.143), channel_id=1, source_target_pairs={{0,448},{16,464},{32,480},{48,496},{64,0},{80,16},{96,32},{112,48}... | collective-permute-start | bytes 491528 | tf_op jit(solution)/shard_map/ppermute | solution.py:202
  105.4 20.9 %collective-permute-start.6 = (bf16[1,128,640]{2,1,0:T(8,128)(2,1)}, bf16[1,128,640]{2,1,0:T(8,128)(2,1)}, u32[]{:S(2)}, u32[]{:S(2)}) collective-permute-start(bf16[1,128,640]{2,1,0:T(8,128)(2,1)} %slice.142), channel_id=1, source_target_pairs={{0,64},{16,80},{32,96},{48,112},{64,128},{80,144},{96,160},{112,17... | collective-permute-start | bytes 491528 | tf_op jit(solution)/shard_map/ppermute | solution.py:201
  107.3 23.4 %collective-permute-start.15 = (bf16[3,256,640]{2,1,0:T(8,128)(2,1)S(1)}, bf16[3,256,640]{2,1,0:T(8,128)(2,1)S(1)}, u32[]{:S(2)}, u32[]{:S(2)}) collective-permute-start(bf16[3,256,640]{2,1,0:T(8,128)(2,1)S(1)} %collective-permute-done.13), channel_id=1, source_target_pairs={{0,64},{16,80},{32,96},{48,112},{64,128},{80,144},{96,160},{112,17... | collective-permute-start | bytes 2949128 | tf_op jit(solution)/shard_map/ppermute | solution.py:196
  109.3 23.4 %collective-permute-start.14 = (bf16[3,256,640]{2,1,0:T(8,128)(2,1)S(1)}, bf16[3,256,640]{2,1,0:T(8,128)(2,1)S(1)}, u32[]{:S(2)}, u32[]{:S(2)}) collective-permute-start(bf16[3,256,640]{2,1,0:T(8,128)(2,1)S(1)} %collective-permute-done.12), channel_id=1, source_target_pairs={{0,448},{16,464},{32,480},{48,496},{64,0},{80,16},{96,32},{112,48}... | collective-permute-start | bytes 2949128 | tf_op jit(solution)/shard_map/ppermute | solution.py:194
  113.8 7.2 %copy-start = (bf16[512,8192]{1,0:T(8,128)(2,1)S(1)}, bf16[512,8192]{1,0:T(8,128)(2,1)}, u32[]{:S(2)}) copy-start(bf16[512,8192]{1,0:T(8,128)(2,1)} %all-gather.2.cloned.1.call-done) | copy-start | bytes 25165828
  130.7 19.1 %collective-permute-start.17 = (bf16[3,256,640]{2,1,0:T(8,128)(2,1)S(1)}, bf16[3,256,640]{2,1,0:T(8,128)(2,1)S(1)}, u32[]{:S(2)}, u32[]{:S(2)}) collective-permute-start(bf16[3,256,640]{2,1,0:T(8,128)(2,1)S(1)} %collective-permute-done.15), channel_id=1, source_target_pairs={{0,64},{16,80},{32,96},{48,112},{64,128},{80,144},{96,160},{112,17... | collective-permute-start | bytes 2949128 | tf_op jit(solution)/shard_map/ppermute | solution.py:196
  132.7 19.1 %collective-permute-start.16 = (bf16[3,256,640]{2,1,0:T(8,128)(2,1)S(1)}, bf16[3,256,640]{2,1,0:T(8,128)(2,1)S(1)}, u32[]{:S(2)}, u32[]{:S(2)}) collective-permute-start(bf16[3,256,640]{2,1,0:T(8,128)(2,1)S(1)} %collective-permute-done.14), channel_id=1, source_target_pairs={{0,448},{16,464},{32,480},{48,496},{64,0},{80,16},{96,32},{112,48}... | collective-permute-start | bytes 2949128 | tf_op jit(solution)/shard_map/ppermute | solution.py:194
  149.9 12.7 %collective-permute-start.18 = (bf16[3,128,640]{2,1,0:T(8,128)(2,1)S(1)}, bf16[3,128,640]{2,1,0:T(8,128)(2,1)S(1)}, u32[]{:S(2)}, u32[]{:S(2)}) collective-permute-start(bf16[3,128,640]{2,1,0:T(8,128)(2,1)S(1)} %slice.164), channel_id=1, source_target_pairs={{0,64},{16,80},{32,96},{48,112},{64,128},{80,144},{96,160},{112,17... | collective-permute-start | bytes 1474568 | tf_op jit(solution)/shard_map/ppermute | solution.py:201
  151.9 12.2 %collective-permute-start.19 = (bf16[3,128,640]{2,1,0:T(8,128)(2,1)S(1)}, bf16[3,128,640]{2,1,0:T(8,128)(2,1)S(1)}, u32[]{:S(2)}, u32[]{:S(2)}) collective-permute-start(bf16[3,128,640]{2,1,0:T(8,128)(2,1)S(1)} %slice.165), channel_id=1, source_target_pairs={{0,448},{16,464},{32,480},{48,496},{64,0},{80,16},{96,32},{112,48}... | collective-permute-start | bytes 1474568 | tf_op jit(solution)/shard_map/ppermute | solution.py:202
  167.2 13.0 %copy-start.1 = (f32[512,640]{1,0:T(8,128)}, f32[512,640]{1,0:T(8,128)S(1)}, u32[]{:S(2)}) copy-start(f32[512,640]{1,0:T(8,128)S(1)} %fusion.17.q_ref) | copy-start | bytes 3932164
  167.2 12.2 %collective-permute-start.20 = (bf16[512,128]{1,0:T(8,128)(2,1)S(1)}, bf16[512,128]{1,0:T(8,128)(2,1)S(1)}, u32[]{:S(2)}, u32[]{:S(2)}) collective-permute-start(bf16[512,128]{1,0:T(8,128)(2,1)S(1)} %slice.226), channel_id=1, source_target_pairs={{0,1},{1,0},{2,3},{3,2},{4,5},{5,4},{6,7},{7,6},{8,9},{9,8},{10,11... | collective-permute-start | bytes 393224 | tf_op jit(solution)/shard_map/ppermute | solution.py:260
Sparse Core Ops, SparseCore 0:
  10.0 71.7 all-gather.1

commit v19 on v18

--- a/solution.py
+++ b/solution.py
@@ -231,20 +231,12 @@
     others = jnp.stack([near[(yh + r) % y_hi] for r in range(1, y_hi)])
     cosine, sine = rope_tables(positions_in_segment(segment_ids))
     row_seg, col_seg = segment_ids[:, None], segment_ids[None, :]
-    others, cosine, sine, row_seg, col_seg = lax.optimization_barrier(
-        (others, cosine, sine, row_seg, col_seg)
+    own_blocks = ring_gather(local_weights, "batch", y_hi, Z_CHIPS)
+    others, own_blocks, cosine, sine, row_seg, col_seg = lax.optimization_barrier(
+        (others, own_blocks, cosine, sine, row_seg, col_seg)
     )
     gathered = lax.all_gather(normed, "weight", axis=0, tiled=True)
     pack_rows = gathered.shape[0]
-    own_part = ring_matmul(
-        gathered,
-        local_weights[None],
-        "batch",
-        y_hi,
-        Z_CHIPS,
-        lambda z: [(z * y_hi + yh) * shard],
-        False,
-    )
     other_part = ring_matmul(
         gathered,
         others,
@@ -254,6 +246,12 @@
         lambda z: [(z * y_hi + (yh + r) % y_hi) * shard for r in range(1, y_hi)],
         True,
     )
+    own_rows_of_z = lax.dynamic_index_in_dim(
+        gathered.reshape(pack_rows, Z_CHIPS, y_hi, shard), yh, axis=2, keepdims=False
+    )
+    own_part = jnp.einsum(
+        "tzr,zrc->tc", own_rows_of_z, own_blocks, preferred_element_type=jnp.float32
+    )
     projected = own_part + other_part
     own_rows = projected[:, query_cols:].astype(jnp.bfloat16)
     partner = [(w, w ^ 1) for w in range(n_weight)]

time: 195 us -> 221 us (1.13)
  local copies, waits for them, and re-layouts: 4.69 us -> 32.9 us
  matrix products: 24.4 us -> 40.3 us
  waiting for transfers between devices: 47.2 us -> 32.1 us
  starting transfers between devices: 87.2 us -> 83.4 us
    ppermute x6 -> x3, starting transfers between devices: 35.6 us -> 11.2 us  [ring_matmul(): from_right = lax.ppermute(from_right, axis, perm=moved(-1))]
    ppermute x1 -> x4, starting transfers between devices: 5.87 us -> 26.5 us  [ring_gather(): from_right = lax.ppermute(from_right, axis, perm=moved(-1))]
    reshape x0 -> x1, local copies, waits for them, and re-layouts: none -> 14.6 us  [per_device(): gathered.reshape(pack_rows, Z_CHIPS, y_hi, shard)]
    dot_general x32 -> x24, matrix products: 24.4 us -> 34.8 us  [product(): term = jnp.dot(lhs, part[piece], preferred_element_type=jnp.float32)]
    dynamic_slice x0 -> x1, local copies, waits for them, and re-layouts: none -> 9.75 us  [per_device(): lax.dynamic_index_in_dim(gathered.reshape(pack_rows, Z_CHIPS, y_hi, shard...]
    ppermute x1 -> x4, starting transfers between devices: 1.92 us -> 7.68 us  [ring_gather(): from_left = lax.ppermute(from_left, axis, perm=moved(1))]
    dot_general x0 -> x1, matrix products: none -> 5.49 us  [per_device(): jnp.einsum('tzr,zrc->tc', own_rows_of_z, own_blocks, preferred_element_ty...]
    ppermute x2 -> x1, starting transfers between devices: 9.78 us -> 4.79 us  [ring_matmul(): lax.ppermute(from_right[..., cut:, :], axis, perm=moved(-1))]
  transfers between devices with their start and end apart: 22 -> 22, of which waited for: 8 -> 7; matrix products, arithmetic and copies ran while one was open for 16% -> 33% of each run, Pallas kernels for 0% -> 0%
where the time goes in v19:
time: 221 us; the launch traced here: 219 us
  starting transfers between devices  83.4 us (38%)
  matrix products  40.3 us (18%)
  local copies, waits for them, and re-layouts  32.9 us (15%)
  waiting for transfers between devices  32.1 us (15%)
  between operations  15.2 us (7%)
  other arithmetic  9.05 us (4%)
  Pallas kernels  5.95 us (3%)
    dot_general x24, matrix products, product(): term = jnp.dot(lhs, part[piece], preferred_element_type=jnp.float32)  34.8 us
    ppermute x4, starting transfers between devices, ring_gather(): from_right = lax.ppermute(from_right, axis, perm=moved(-1))  26.5 us
    ppermute x3, waiting for transfers between devices, ring_matmul(): from_right = lax.ppermute(from_right, axis, perm=moved(-1))  14.9 us
    reshape x1, local copies, waits for them, and re-layouts, per_device(): gathered.reshape(pack_rows, Z_CHIPS, y_hi, shard)  14.6 us
    ppermute x3, starting transfers between devices, ring_matmul(): from_right = lax.ppermute(from_right, axis, perm=moved(-1))  11.2 us
    ppermute x1, starting transfers between devices, per_device(): other_rows = lax.ppermute(own_rows, 'weight', perm=partner)  10.7 us
    dynamic_slice x1, local copies, waits for them, and re-layouts, per_device(): lax.dynamic_index_in_dim(gathered.reshape(pack_rows, Z_CHIPS, y_hi, shard...  9.75 us
    ppermute x2, starting transfers between devices, ring_gather(): lax.ppermute(from_right[..., cut:, :], axis, perm=moved(-1))  9.5 us
  transfers between devices with their start and end apart: 22, of which 7 were waited for; matrix products, arithmetic and copies ran while one was open for 33% of the time, Pallas kernels for 0%

profile of v19, /device:TPU:7, one launch (start us, length us, event | category | flops | bytes accessed | tf_op | source)
XLA Modules:
  0.0 218.8 jit_solution(7534490276423599465)
XLA Ops:
  7.9 2.0 fusion.19
  10.9 5.9 %collective-permute-start = (bf16[256,640]{1,0:T(8,128)(2,1)S(1)}, bf16[256,640]{1,0:T(8,128)(2,1)S(1)}, u32[]{:S(2)}, u32[]{:S(2)}) collective-permute-start(bf16[256,640]{1,0:T(8,128)(2,1)S(1)} %pad_maximum_fusion.1), channel_id=1, source_target_pairs={{0,48},{16,0},{32,16},{48,32},{64,112},{80,64},{96,80},{112,96},{1... | collective-permute-start | bytes 983048 | tf_op jit(solution)/shard_map/ppermute | solution.py:151
  16.8 1.9 collective-permute-start.1
  18.7 10.7 %collective-permute-start.4 = (bf16[256,640]{1,0:T(8,128)(2,1)S(1)}, bf16[256,640]{1,0:T(8,128)(2,1)S(1)}, u32[]{:S(2)}, u32[]{:S(2)}) collective-permute-start(bf16[256,640]{1,0:T(8,128)(2,1)S(1)} %pad_maximum_fusion.1), channel_id=1, source_target_pairs={{0,448},{16,464},{32,480},{48,496},{64,0},{80,16},{96,32},{112,48}... | collective-permute-start | bytes 983048 | tf_op jit(solution)/shard_map/ppermute | solution.py:151
  29.4 1.9 collective-permute-start.5
  33.5 1.7 broadcast_in_dim.61
  36.2 1.8 multiply_sine_fusion
  38.0 5.5 %collective-permute-start.3 = (bf16[128,640]{1,0:T(8,128)(2,1)S(1)}, bf16[128,640]{1,0:T(8,128)(2,1)S(1)}, u32[]{:S(2)}, u32[]{:S(2)}) collective-permute-start(bf16[128,640]{1,0:T(8,128)(2,1)S(1)} %slice.143), channel_id=1, source_target_pairs={{0,48},{16,0},{32,16},{48,32},{64,112},{80,64},{96,80},{112,96},{1... | collective-permute-start | bytes 491528 | tf_op jit(solution)/shard_map/ppermute | solution.py:159
  43.6 1.9 collective-permute-start.2
  45.5 5.5 %collective-permute-start.6 = (bf16[256,640]{1,0:T(8,128)(2,1)S(1)}, bf16[256,640]{1,0:T(8,128)(2,1)S(1)}, u32[]{:S(2)}, u32[]{:S(2)}) collective-permute-start(bf16[256,640]{1,0:T(8,128)(2,1)S(1)} %collective-permute-done.4), channel_id=1, source_target_pairs={{0,448},{16,464},{32,480},{48,496},{64,0},{80,16},{96,32},{112,48}... | collective-permute-start | bytes 983048 | tf_op jit(solution)/shard_map/ppermute | solution.py:151
  51.0 1.9 collective-permute-start.7
  54.6 4.7 %collective-permute-done.2 = bf16[128,640]{1,0:T(8,128)(2,1)S(1)} collective-permute-done((bf16[128,640]{1,0:T(8,128)(2,1)S(1)}, bf16[128,640]{1,0:T(8,128)(2,1)S(1)}, u32[]{:S(2)}, u32[]{:S(2)}) %collective-permute-start.2) | collective-permute-done | bytes 163872 | tf_op jit(solution)/shard_map/ppermute | solution.py:158
  59.5 4.5 %collective-permute-start.8 = (bf16[256,640]{1,0:T(8,128)(2,1)S(1)}, bf16[256,640]{1,0:T(8,128)(2,1)S(1)}, u32[]{:S(2)}, u32[]{:S(2)}) collective-permute-start(bf16[256,640]{1,0:T(8,128)(2,1)S(1)} %collective-permute-done.6), channel_id=1, source_target_pairs={{0,448},{16,464},{32,480},{48,496},{64,0},{80,16},{96,32},{112,48}... | collective-permute-start | bytes 983048 | tf_op jit(solution)/shard_map/ppermute | solution.py:151
  64.1 1.9 collective-permute-start.9
  67.5 2.3 %collective-permute-done.8 = bf16[256,640]{1,0:T(8,128)(2,1)S(1)} collective-permute-done((bf16[256,640]{1,0:T(8,128)(2,1)S(1)}, bf16[256,640]{1,0:T(8,128)(2,1)S(1)}, u32[]{:S(2)}, u32[]{:S(2)}) %collective-permute-start.8) | collective-permute-done | bytes 327712 | tf_op jit(solution)/shard_map/ppermute | solution.py:151
  69.8 4.0 %collective-permute-start.11 = (bf16[128,640]{1,0:T(8,128)(2,1)S(1)}, bf16[128,640]{1,0:T(8,128)(2,1)S(1)}, u32[]{:S(2)}, u32[]{:S(2)}) collective-permute-start(bf16[128,640]{1,0:T(8,128)(2,1)S(1)} %slice.145), channel_id=1, source_target_pairs={{0,448},{16,464},{32,480},{48,496},{64,0},{80,16},{96,32},{112,48}... | collective-permute-start | bytes 491528 | tf_op jit(solution)/shard_map/ppermute | solution.py:159
  73.9 1.9 collective-permute-start.10
  77.4 3.8 %collective-permute-done.10 = bf16[128,640]{1,0:T(8,128)(2,1)S(1)} collective-permute-done((bf16[128,640]{1,0:T(8,128)(2,1)S(1)}, bf16[128,640]{1,0:T(8,128)(2,1)S(1)}, u32[]{:S(2)}, u32[]{:S(2)}) %collective-permute-start.10) | collective-permute-done | bytes 163872 | tf_op jit(solution)/shard_map/ppermute | solution.py:158
  81.9 1.9 collective-permute-start.12
  83.8 3.4 %collective-permute-start.13 = (bf16[3,256,640]{2,1,0:T(8,128)(2,1)S(1)}, bf16[3,256,640]{2,1,0:T(8,128)(2,1)}, u32[]{:S(2)}, u32[]{:S(2)}) collective-permute-start(bf16[3,256,640]{2,1,0:T(8,128)(2,1)S(1)} %pad_maximum_fusion), channel_id=1, source_target_pairs={{0,64},{16,80},{32,96},{48,112},{64,128},{80,144},{96,160},{112,17... | collective-permute-start | bytes 2949128 | tf_op jit(solution)/shard_map/ppermute | solution.py:196
  87.4 14.9 %collective-permute-done.12 = bf16[3,256,640]{2,1,0:T(8,128)(2,1)} collective-permute-done((bf16[3,256,640]{2,1,0:T(8,128)(2,1)S(1)}, bf16[3,256,640]{2,1,0:T(8,128)(2,1)}, u32[]{:S(2)}, u32[]{:S(2)}) %collective-permute-start.12) | collective-permute-done | bytes 983072 | tf_op jit(solution)/shard_map/ppermute | solution.py:194
  102.3 3.1 %collective-permute-done.13 = bf16[3,256,640]{2,1,0:T(8,128)(2,1)} collective-permute-done((bf16[3,256,640]{2,1,0:T(8,128)(2,1)S(1)}, bf16[3,256,640]{2,1,0:T(8,128)(2,1)}, u32[]{:S(2)}, u32[]{:S(2)}) %collective-permute-start.13) | collective-permute-done | bytes 983072 | tf_op jit(solution)/shard_map/ppermute | solution.py:196
  105.4 1.9 collective-permute-start.15
  107.3 4.8 %collective-permute-start.14 = (bf16[3,256,640]{2,1,0:T(8,128)(2,1)}, bf16[3,256,640]{2,1,0:T(8,128)(2,1)}, u32[]{:S(2)}, u32[]{:S(2)}) collective-permute-start(bf16[3,256,640]{2,1,0:T(8,128)(2,1)} %collective-permute-done.12), channel_id=1, source_target_pairs={{0,448},{16,464},{32,480},{48,496},{64,0},{80,16},{96,32},{112,48}... | collective-permute-start | bytes 2949128 | tf_op jit(solution)/shard_map/ppermute | solution.py:194
  113.4 1.4 fusion.32
  114.9 1.4 fusion.33
  116.3 1.4 fusion.30
  120.4 2.5 %fusion.16 = f32[512,640]{1,0:T(8,128)} fusion(f32[512,640]{1,0:T(8,128)S(1)} %convolution_add_fusion.7, f32[512,640]{1,0:T(8,128)S(1)} %fusion.32, f32[512,640]{1,0:T(8,128)S(1)} %fusion.33, bf16[3,256,640]{2,1,0:T(8,128)(2,1)} %collective-permute-done.12, bf16[512,8192]{1,0:T(8,128)(2,1)} %all-gather.2.cloned.1.call-done, s32[]{:T(128)S(6)} %select_n.325), kind=kOutput, calls=%fused_computation.26 | convolution fusion | flops 168755200 | bytes 5832708 | tf_op jit(solution)/shard_map/dot_general | solution.py:184
  122.9 1.4 fusion.31
  124.3 14.6 %reshape.45 = bf16[512,8,4,256]{3,2,1,0:T(4,128)(2,1)} reshape(bf16[512,8192]{1,0:T(8,128)(2,1)} %all-gather.2.cloned.1.call-done) | data formatting | bytes 16777216 | tf_op jit(solution)/shard_map/reshape | solution.py:250
  138.9 9.7 %constant_dynamic-slice_fusion.3 = bf16[512,8,1,256]{3,2,1,0:T(2,128)(2,1)} fusion(bf16[512,8,4,256]{3,2,1,0:T(4,128)(2,1)} %reshape.45, s32[]{:T(128)S(6)} %select_n.288), kind=kLoop, calls=%fused_computation.147 | loop fusion | bytes 4194308 | tf_op jit(solution)/shard_map/jit(dynamic_index_in_dim)/dynamic_slice | solution.py:249
  148.7 5.5 %fusion.1 = f32[512,640]{1,0:T(8,128)S(1)} fusion(bf16[8,256,640]{2,1,0:T(8,128)(2,1)} %fusion.35, bf16[512,8,1,256]{3,2,1,0:T(2,128)(2,1)} %constant_dynamic-slice_fusion.3), kind=kOutput, calls=%fused_computation.2 | convolution fusion | flops 1342177280 | bytes 6029312 | tf_op jit(solution)/shard_map/tzr,zrc->tc/dot_general | solution.py:252
  154.2 1.9 collective-permute-start.17
  156.1 4.6 %collective-permute-start.16 = (bf16[3,256,640]{2,1,0:T(8,128)(2,1)}, bf16[3,256,640]{2,1,0:T(8,128)(2,1)S(1)}, u32[]{:S(2)}, u32[]{:S(2)}) collective-permute-start(bf16[3,256,640]{2,1,0:T(8,128)(2,1)} %collective-permute-done.14), channel_id=1, source_target_pairs={{0,448},{16,464},{32,480},{48,496},{64,0},{80,16},{96,32},{112,48}... | collective-permute-start | bytes 2949128 | tf_op jit(solution)/shard_map/ppermute | solution.py:194
  160.7 1.4 fusion.26
  162.2 1.4 fusion.27
  163.6 1.4 fusion.28
  165.0 1.5 fusion.5
  166.5 1.4 fusion.29
  168.0 1.5 fusion.4
  169.5 1.7 fusion.15
  171.2 3.2 %collective-permute-done.17 = bf16[3,256,640]{2,1,0:T(8,128)(2,1)S(1)} collective-permute-done((bf16[3,256,640]{2,1,0:T(8,128)(2,1)}, bf16[3,256,640]{2,1,0:T(8,128)(2,1)S(1)}, u32[]{:S(2)}, u32[]{:S(2)}) %collective-permute-start.17) | collective-permute-done | bytes 983072 | tf_op jit(solution)/shard_map/ppermute | solution.py:196
  174.4 1.9 collective-permute-start.18
  176.4 4.8 %collective-permute-start.19 = (bf16[3,128,640]{2,1,0:T(8,128)(2,1)S(1)}, bf16[3,128,640]{2,1,0:T(8,128)(2,1)S(1)}, u32[]{:S(2)}, u32[]{:S(2)}) collective-permute-start(bf16[3,128,640]{2,1,0:T(8,128)(2,1)S(1)} %slice.165), channel_id=1, source_target_pairs={{0,448},{16,464},{32,480},{48,496},{64,0},{80,16},{96,32},{112,48}... | collective-permute-start | bytes 1474568 | tf_op jit(solution)/shard_map/ppermute | solution.py:202
  186.5 1.3 fusion.7
  192.0 1.6 fusion.12.q_ref
  193.6 10.7 %collective-permute-start.20 = (bf16[512,128]{1,0:T(8,128)(2,1)S(1)}, bf16[512,128]{1,0:T(8,128)(2,1)S(1)}, u32[]{:S(2)}, u32[]{:S(2)}) collective-permute-start(bf16[512,128]{1,0:T(8,128)(2,1)S(1)} %slice.226), channel_id=1, source_target_pairs={{0,1},{1,0},{2,3},{3,2},{4,5},{5,4},{6,7},{7,6},{8,9},{9,8},{10,11... | collective-permute-start | bytes 393224 | tf_op jit(solution)/shard_map/ppermute | solution.py:258
  206.0 6.0 %shard_map.64 = bf16[512,512]{1,0:T(8,128)(2,1)} custom-call(f32[512,640]{1,0:T(8,128)} %copy-done, bf16[512,128]{1,0:T(8,128)(2,1)} %get-tuple-element.29.k_ref, bf16[512,128]{1,0:T(8,128)(2,1)} %get-tuple-element.28.v_ref, f32[512,64]{1,0:T(8,128)} %get-tuple-element.19.cos_ref, f32[512,64]{1,0:T(8,128)} %get-tuple-element.20.sin_ref, ...), custom_call_target="tpu_custom_call" | custom-call | flops 538968064 | bytes 2097152 | tf_op jit(solution)/shard_map/pallas_call | solution.py:113
  (73 shorter events, 25.4 us)
Async XLA Ops:
  6.5 4.3 %copy-start.2 = (bf16[256,512]{1,0:T(8,128)(2,1)S(1)}, bf16[256,512]{1,0:T(8,128)(2,1)}, u32[]{:S(2)}) copy-start(bf16[256,512]{1,0:T(8,128)(2,1)} %param.9) | copy-start | bytes 786436
  6.5 98.9 %all-gather.2.cloned.1.call-start = ((), (), s32[]{:S(2)}) async-start(), calls=%async_computation | async-start | bytes 8912896 | tf_op jit(solution)/shard_map/all_gather | solution.py:238
  7.8 23.7 %copy-start.3 = (s32[512]{0:T(512)S(1)}, s32[512]{0:T(512)}, u32[]{:S(2)}) copy-start(s32[512]{0:T(512)} %param.7) | copy-start | bytes 6148
  10.9 27.1 %collective-permute-start = (bf16[256,640]{1,0:T(8,128)(2,1)S(1)}, bf16[256,640]{1,0:T(8,128)(2,1)S(1)}, u32[]{:S(2)}, u32[]{:S(2)}) collective-permute-start(bf16[256,640]{1,0:T(8,128)(2,1)S(1)} %pad_maximum_fusion.1), channel_id=1, source_target_pairs={{0,48},{16,0},{32,16},{48,32},{64,112},{80,64},{96,80},{112,96},{1... | collective-permute-start | bytes 983048 | tf_op jit(solution)/shard_map/ppermute | solution.py:151
  16.8 26.7 %collective-permute-start.1 = (bf16[256,640]{1,0:T(8,128)(2,1)S(1)}, bf16[256,640]{1,0:T(8,128)(2,1)S(1)}, u32[]{:S(2)}, u32[]{:S(2)}) collective-permute-start(bf16[256,640]{1,0:T(8,128)(2,1)S(1)} %pad_maximum_fusion.1), channel_id=1, source_target_pairs={{0,16},{16,32},{32,48},{48,0},{64,80},{80,96},{96,112},{112,64},{1... | collective-permute-start | bytes 983048 | tf_op jit(solution)/shard_map/ppermute | solution.py:153
  18.7 26.8 %collective-permute-start.4 = (bf16[256,640]{1,0:T(8,128)(2,1)S(1)}, bf16[256,640]{1,0:T(8,128)(2,1)S(1)}, u32[]{:S(2)}, u32[]{:S(2)}) collective-permute-start(bf16[256,640]{1,0:T(8,128)(2,1)S(1)} %pad_maximum_fusion.1), channel_id=1, source_target_pairs={{0,448},{16,464},{32,480},{48,496},{64,0},{80,16},{96,32},{112,48}... | collective-permute-start | bytes 983048 | tf_op jit(solution)/shard_map/ppermute | solution.py:151
  29.4 21.6 %collective-permute-start.5 = (bf16[256,640]{1,0:T(8,128)(2,1)S(1)}, bf16[256,640]{1,0:T(8,128)(2,1)S(1)}, u32[]{:S(2)}, u32[]{:S(2)}) collective-permute-start(bf16[256,640]{1,0:T(8,128)(2,1)S(1)} %pad_maximum_fusion.1), channel_id=1, source_target_pairs={{0,64},{16,80},{32,96},{48,112},{64,128},{80,144},{96,160},{112,17... | collective-permute-start | bytes 983048 | tf_op jit(solution)/shard_map/ppermute | solution.py:153
  38.0 16.5 %collective-permute-start.3 = (bf16[128,640]{1,0:T(8,128)(2,1)S(1)}, bf16[128,640]{1,0:T(8,128)(2,1)S(1)}, u32[]{:S(2)}, u32[]{:S(2)}) collective-permute-start(bf16[128,640]{1,0:T(8,128)(2,1)S(1)} %slice.143), channel_id=1, source_target_pairs={{0,48},{16,0},{32,16},{48,32},{64,112},{80,64},{96,80},{112,96},{1... | collective-permute-start | bytes 491528 | tf_op jit(solution)/shard_map/ppermute | solution.py:159
  43.6 15.7 %collective-permute-start.2 = (bf16[128,640]{1,0:T(8,128)(2,1)S(1)}, bf16[128,640]{1,0:T(8,128)(2,1)S(1)}, u32[]{:S(2)}, u32[]{:S(2)}) collective-permute-start(bf16[128,640]{1,0:T(8,128)(2,1)S(1)} %slice.142), channel_id=1, source_target_pairs={{0,16},{16,32},{32,48},{48,0},{64,80},{80,96},{96,112},{112,64},{1... | collective-permute-start | bytes 491528 | tf_op jit(solution)/shard_map/ppermute | solution.py:158
  45.5 14.0 %collective-permute-start.6 = (bf16[256,640]{1,0:T(8,128)(2,1)S(1)}, bf16[256,640]{1,0:T(8,128)(2,1)S(1)}, u32[]{:S(2)}, u32[]{:S(2)}) collective-permute-start(bf16[256,640]{1,0:T(8,128)(2,1)S(1)} %collective-permute-done.4), channel_id=1, source_target_pairs={{0,448},{16,464},{32,480},{48,496},{64,0},{80,16},{96,32},{112,48}... | collective-permute-start | bytes 983048 | tf_op jit(solution)/shard_map/ppermute | solution.py:151
  51.0 13.1 %collective-permute-start.7 = (bf16[256,640]{1,0:T(8,128)(2,1)S(1)}, bf16[256,640]{1,0:T(8,128)(2,1)S(1)}, u32[]{:S(2)}, u32[]{:S(2)}) collective-permute-start(bf16[256,640]{1,0:T(8,128)(2,1)S(1)} %collective-permute-done.5), channel_id=1, source_target_pairs={{0,64},{16,80},{32,96},{48,112},{64,128},{80,144},{96,160},{112,17... | collective-permute-start | bytes 983048 | tf_op jit(solution)/shard_map/ppermute | solution.py:153
  59.5 10.3 %collective-permute-start.8 = (bf16[256,640]{1,0:T(8,128)(2,1)S(1)}, bf16[256,640]{1,0:T(8,128)(2,1)S(1)}, u32[]{:S(2)}, u32[]{:S(2)}) collective-permute-start(bf16[256,640]{1,0:T(8,128)(2,1)S(1)} %collective-permute-done.6), channel_id=1, source_target_pairs={{0,448},{16,464},{32,480},{48,496},{64,0},{80,16},{96,32},{112,48}... | collective-permute-start | bytes 983048 | tf_op jit(solution)/shard_map/ppermute | solution.py:151
  64.1 9.8 %collective-permute-start.9 = (bf16[256,640]{1,0:T(8,128)(2,1)S(1)}, bf16[256,640]{1,0:T(8,128)(2,1)S(1)}, u32[]{:S(2)}, u32[]{:S(2)}) collective-permute-start(bf16[256,640]{1,0:T(8,128)(2,1)S(1)} %collective-permute-done.7), channel_id=1, source_target_pairs={{0,64},{16,80},{32,96},{48,112},{64,128},{80,144},{96,160},{112,17... | collective-permute-start | bytes 983048 | tf_op jit(solution)/shard_map/ppermute | solution.py:153
  69.8 7.5 %collective-permute-start.11 = (bf16[128,640]{1,0:T(8,128)(2,1)S(1)}, bf16[128,640]{1,0:T(8,128)(2,1)S(1)}, u32[]{:S(2)}, u32[]{:S(2)}) collective-permute-start(bf16[128,640]{1,0:T(8,128)(2,1)S(1)} %slice.145), channel_id=1, source_target_pairs={{0,448},{16,464},{32,480},{48,496},{64,0},{80,16},{96,32},{112,48}... | collective-permute-start | bytes 491528 | tf_op jit(solution)/shard_map/ppermute | solution.py:159
  73.9 7.3 %collective-permute-start.10 = (bf16[128,640]{1,0:T(8,128)(2,1)S(1)}, bf16[128,640]{1,0:T(8,128)(2,1)S(1)}, u32[]{:S(2)}, u32[]{:S(2)}) collective-permute-start(bf16[128,640]{1,0:T(8,128)(2,1)S(1)} %slice.144), channel_id=1, source_target_pairs={{0,64},{16,80},{32,96},{48,112},{64,128},{80,144},{96,160},{112,17... | collective-permute-start | bytes 491528 | tf_op jit(solution)/shard_map/ppermute | solution.py:158
  81.9 20.4 %collective-permute-start.12 = (bf16[3,256,640]{2,1,0:T(8,128)(2,1)S(1)}, bf16[3,256,640]{2,1,0:T(8,128)(2,1)}, u32[]{:S(2)}, u32[]{:S(2)}) collective-permute-start(bf16[3,256,640]{2,1,0:T(8,128)(2,1)S(1)} %pad_maximum_fusion), channel_id=1, source_target_pairs={{0,448},{16,464},{32,480},{48,496},{64,0},{80,16},{96,32},{112,48}... | collective-permute-start | bytes 2949128 | tf_op jit(solution)/shard_map/ppermute | solution.py:194
  83.8 21.6 %collective-permute-start.13 = (bf16[3,256,640]{2,1,0:T(8,128)(2,1)S(1)}, bf16[3,256,640]{2,1,0:T(8,128)(2,1)}, u32[]{:S(2)}, u32[]{:S(2)}) collective-permute-start(bf16[3,256,640]{2,1,0:T(8,128)(2,1)S(1)} %pad_maximum_fusion), channel_id=1, source_target_pairs={{0,64},{16,80},{32,96},{48,112},{64,128},{80,144},{96,160},{112,17... | collective-permute-start | bytes 2949128 | tf_op jit(solution)/shard_map/ppermute | solution.py:196
  105.4 48.8 %collective-permute-start.15 = (bf16[3,256,640]{2,1,0:T(8,128)(2,1)}, bf16[3,256,640]{2,1,0:T(8,128)(2,1)}, u32[]{:S(2)}, u32[]{:S(2)}) collective-permute-start(bf16[3,256,640]{2,1,0:T(8,128)(2,1)} %collective-permute-done.13), channel_id=1, source_target_pairs={{0,64},{16,80},{32,96},{48,112},{64,128},{80,144},{96,160},{112,17... | collective-permute-start | bytes 2949128 | tf_op jit(solution)/shard_map/ppermute | solution.py:196
  107.3 48.8 %collective-permute-start.14 = (bf16[3,256,640]{2,1,0:T(8,128)(2,1)}, bf16[3,256,640]{2,1,0:T(8,128)(2,1)}, u32[]{:S(2)}, u32[]{:S(2)}) collective-permute-start(bf16[3,256,640]{2,1,0:T(8,128)(2,1)} %collective-permute-done.12), channel_id=1, source_target_pairs={{0,448},{16,464},{32,480},{48,496},{64,0},{80,16},{96,32},{112,48}... | collective-permute-start | bytes 2949128 | tf_op jit(solution)/shard_map/ppermute | solution.py:194
  154.2 20.2 %collective-permute-start.17 = (bf16[3,256,640]{2,1,0:T(8,128)(2,1)}, bf16[3,256,640]{2,1,0:T(8,128)(2,1)S(1)}, u32[]{:S(2)}, u32[]{:S(2)}) collective-permute-start(bf16[3,256,640]{2,1,0:T(8,128)(2,1)} %collective-permute-done.15), channel_id=1, source_target_pairs={{0,64},{16,80},{32,96},{48,112},{64,128},{80,144},{96,160},{112,17... | collective-permute-start | bytes 2949128 | tf_op jit(solution)/shard_map/ppermute | solution.py:196
  156.1 20.2 %collective-permute-start.16 = (bf16[3,256,640]{2,1,0:T(8,128)(2,1)}, bf16[3,256,640]{2,1,0:T(8,128)(2,1)S(1)}, u32[]{:S(2)}, u32[]{:S(2)}) collective-permute-start(bf16[3,256,640]{2,1,0:T(8,128)(2,1)} %collective-permute-done.14), channel_id=1, source_target_pairs={{0,448},{16,464},{32,480},{48,496},{64,0},{80,16},{96,32},{112,48}... | collective-permute-start | bytes 2949128 | tf_op jit(solution)/shard_map/ppermute | solution.py:194
  167.9 1.6 copy-start.1
  174.4 13.4 %collective-permute-start.18 = (bf16[3,128,640]{2,1,0:T(8,128)(2,1)S(1)}, bf16[3,128,640]{2,1,0:T(8,128)(2,1)S(1)}, u32[]{:S(2)}, u32[]{:S(2)}) collective-permute-start(bf16[3,128,640]{2,1,0:T(8,128)(2,1)S(1)} %slice.164), channel_id=1, source_target_pairs={{0,64},{16,80},{32,96},{48,112},{64,128},{80,144},{96,160},{112,17... | collective-permute-start | bytes 1474568 | tf_op jit(solution)/shard_map/ppermute | solution.py:201
  176.4 11.5 %collective-permute-start.19 = (bf16[3,128,640]{2,1,0:T(8,128)(2,1)S(1)}, bf16[3,128,640]{2,1,0:T(8,128)(2,1)S(1)}, u32[]{:S(2)}, u32[]{:S(2)}) collective-permute-start(bf16[3,128,640]{2,1,0:T(8,128)(2,1)S(1)} %slice.165), channel_id=1, source_target_pairs={{0,448},{16,464},{32,480},{48,496},{64,0},{80,16},{96,32},{112,48}... | collective-permute-start | bytes 1474568 | tf_op jit(solution)/shard_map/ppermute | solution.py:202
  193.6 12.4 %copy-start = (f32[512,640]{1,0:T(8,128)}, f32[512,640]{1,0:T(8,128)S(1)}, u32[]{:S(2)}) copy-start(f32[512,640]{1,0:T(8,128)S(1)} %fusion.12.q_ref) | copy-start | bytes 3932164
  193.6 11.7 %collective-permute-start.20 = (bf16[512,128]{1,0:T(8,128)(2,1)S(1)}, bf16[512,128]{1,0:T(8,128)(2,1)S(1)}, u32[]{:S(2)}, u32[]{:S(2)}) collective-permute-start(bf16[512,128]{1,0:T(8,128)(2,1)S(1)} %slice.226), channel_id=1, source_target_pairs={{0,1},{1,0},{2,3},{3,2},{4,5},{5,4},{6,7},{7,6},{8,9},{9,8},{10,11... | collective-permute-start | bytes 393224 | tf_op jit(solution)/shard_map/ppermute | solution.py:258
Sparse Core Ops, SparseCore 0:
  10.0 71.1 all-gather.1

commit v20 on v18

--- a/solution.py
+++ b/solution.py
@@ -164,6 +164,35 @@
     return out
 
 
+def ring_others(block, axis, stride, count):
+    n = lax.psum(1, axis)
+
+    def moved(step):
+        pairs = []
+        for src in range(n):
+            k = (src // stride) % count
+            pairs.append((src, src + (((k + step) % count) - k) * stride))
+        return pairs
+
+    by_offset = {}
+    from_right, from_left = block, block
+    for step in range(1, count // 2 + 1):
+        if step < count - step:
+            from_right = lax.ppermute(from_right, axis, perm=moved(-1))
+            from_left = lax.ppermute(from_left, axis, perm=moved(1))
+            by_offset[step], by_offset[count - step] = from_right, from_left
+        else:
+            cut = block.shape[-2] // 2
+            by_offset[step] = jnp.concatenate(
+                [
+                    lax.ppermute(from_left[..., :cut, :], axis, perm=moved(1)),
+                    lax.ppermute(from_right[..., cut:, :], axis, perm=moved(-1)),
+                ],
+                axis=-2,
+            )
+    return jnp.stack([by_offset[r] for r in range(1, count)])
+
+
 def ring_matmul(rows, block, axis, stride, count, starts, wait_rows):
     n = lax.psum(1, axis)
     me = lax.axis_index(axis)
@@ -227,8 +256,7 @@
     y_hi = n_batch // Z_CHIPS
     shard = local_weights.shape[0]
     yh = lax.axis_index("batch") % y_hi
-    near = ring_gather(local_weights, "batch", 1, y_hi)
-    others = jnp.stack([near[(yh + r) % y_hi] for r in range(1, y_hi)])
+    others = ring_others(local_weights, "batch", 1, y_hi)
     cosine, sine = rope_tables(positions_in_segment(segment_ids))
     row_seg, col_seg = segment_ids[:, None], segment_ids[None, :]
     others, cosine, sine, row_seg, col_seg = lax.optimization_barrier(

time: 195 us -> 195 us (level)
  the two profiles are of different devices: /device:TPU:7 before, /device:TPU:59 now
where the time goes in v20:
time: 195 us; the launch traced here: 194 us
  starting transfers between devices  86.8 us (45%)
  waiting for transfers between devices  51.1 us (26%)
  matrix products  23.4 us (12%)
  between operations  15 us (8%)
  other arithmetic  7.48 us (4%)
  Pallas kernels  5.95 us (3%)
  local copies, waits for them, and re-layouts  4.61 us (2%)
    ppermute x6, starting transfers between devices, ring_matmul(): from_right = lax.ppermute(from_right, axis, perm=moved(-1))  40.4 us
    dot_general x32, matrix products, product(): term = jnp.dot(lhs, part[piece], preferred_element_type=jnp.float32)  23.4 us
    ppermute x6, waiting for transfers between devices, ring_matmul(): from_right = lax.ppermute(from_right, axis, perm=moved(-1))  22.6 us
    ppermute x6, waiting for transfers between devices, ring_matmul(): from_left = lax.ppermute(from_left, axis, perm=moved(1))  15.5 us
    ppermute x6, starting transfers between devices, ring_matmul(): from_left = lax.ppermute(from_left, axis, perm=moved(1))  11.5 us
    ppermute x2, starting transfers between devices, ring_matmul(): lax.ppermute(from_right[..., cut:, :], axis, perm=moved(-1))  9.96 us
    ppermute x1, waiting for transfers between devices, ring_others(): lax.ppermute(from_left[..., :cut, :], axis, perm=moved(1))  9.2 us
    ppermute x1, starting transfers between devices, per_device(): other_rows = lax.ppermute(own_rows, 'weight', perm=partner)  7.57 us
  transfers between devices with their start and end apart: 22, of which 8 were waited for; matrix products, arithmetic and copies ran while one was open for 15% of the time, Pallas kernels for 0%

profile of v20, /device:TPU:59, one launch (start us, length us, event | category | flops | bytes accessed | tf_op | source)
XLA Modules:
  0.0 194.3 jit_solution(8748798114132906223)
XLA Ops:
  6.5 1.3 fusion.18
  7.9 2.0 %fusion.20 = bf16[32,8192]{1,0:T(8,128)(2,1)} fusion(bf16[32,8192]{1,0:T(8,128)(2,1)} %param.6, f32[8192]{0:T(1024)} %param.8, f32[32]{0:T(128)S(1)} %add_rsqrt_fusion), kind=kLoop, calls=%fused_computation.35 | loop fusion | flops 1048576 | bytes 1081472 | tf_op jit(solution)/shard_map/convert_element_type | solution.py:253
  9.9 0.9 dynamic-slice_select_fusion
  11.5 2.4 %collective-permute-start.9 = (bf16[256,640]{1,0:T(8,128)(2,1)S(1)}, bf16[256,640]{1,0:T(8,128)(2,1)S(1)}, u32[]{:S(2)}, u32[]{:S(2)}) collective-permute-start(bf16[256,640]{1,0:T(8,128)(2,1)S(1)} %get-tuple-element.22), channel_id=1, source_target_pairs={{0,16},{16,32},{32,48},{48,0},{64,80},{80,96},{96,112},{112,64},{1... | collective-permute-start | bytes 983048 | tf_op jit(solution)/shard_map/ppermute | solution.py:182
  13.9 3.8 %collective-permute-start.8 = (bf16[256,640]{1,0:T(8,128)(2,1)S(1)}, bf16[256,640]{1,0:T(8,128)(2,1)S(1)}, u32[]{:S(2)}, u32[]{:S(2)}) collective-permute-start(bf16[256,640]{1,0:T(8,128)(2,1)S(1)} %get-tuple-element.22), channel_id=1, source_target_pairs={{0,48},{16,0},{32,16},{48,32},{64,112},{80,64},{96,80},{112,96},{1... | collective-permute-start | bytes 983048 | tf_op jit(solution)/shard_map/ppermute | solution.py:181
  17.7 10.7 %collective-permute-start = (bf16[1,256,640]{2,1,0:T(8,128)(2,1)S(1)}, bf16[1,256,640]{2,1,0:T(8,128)(2,1)}, u32[]{:S(2)}, u32[]{:S(2)}) collective-permute-start(bf16[1,256,640]{2,1,0:T(8,128)(2,1)S(1)} %get-tuple-element.21), channel_id=1, source_target_pairs={{0,448},{16,464},{32,480},{48,496},{64,0},{80,16},{96,32},{112,48}... | collective-permute-start | bytes 983048 | tf_op jit(solution)/shard_map/ppermute | solution.py:223
  28.3 1.9 collective-permute-start.1
  32.0 5.0 %collective-permute-start.11 = (bf16[128,640]{1,0:T(8,128)(2,1)S(1)}, bf16[128,640]{1,0:T(8,128)(2,1)S(1)}, u32[]{:S(2)}, u32[]{:S(2)}) collective-permute-start(bf16[128,640]{1,0:T(8,128)(2,1)S(1)} %slice.145), channel_id=1, source_target_pairs={{0,48},{16,0},{32,16},{48,32},{64,112},{80,64},{96,80},{112,96},{1... | collective-permute-start | bytes 491528 | tf_op jit(solution)/shard_map/ppermute | solution.py:189
  37.0 2.4 %collective-permute-start.10 = (bf16[128,640]{1,0:T(8,128)(2,1)S(1)}, bf16[128,640]{1,0:T(8,128)(2,1)S(1)}, u32[]{:S(2)}, u32[]{:S(2)}) collective-permute-start(bf16[128,640]{1,0:T(8,128)(2,1)S(1)} %slice.144), channel_id=1, source_target_pairs={{0,16},{16,32},{32,48},{48,0},{64,80},{80,96},{96,112},{112,64},{1... | collective-permute-start | bytes 491528 | tf_op jit(solution)/shard_map/ppermute | solution.py:188
  39.5 1.8 multiply_sine_fusion
  41.3 9.2 %collective-permute-done.10 = bf16[128,640]{1,0:T(8,128)(2,1)S(1)} collective-permute-done((bf16[128,640]{1,0:T(8,128)(2,1)S(1)}, bf16[128,640]{1,0:T(8,128)(2,1)S(1)}, u32[]{:S(2)}, u32[]{:S(2)}) %collective-permute-start.10) | collective-permute-done | bytes 163872 | tf_op jit(solution)/shard_map/ppermute | solution.py:188
  50.7 10.7 %collective-permute-start.12 = (bf16[3,256,640]{2,1,0:T(8,128)(2,1)S(1)}, bf16[3,256,640]{2,1,0:T(8,128)(2,1)S(1)}, u32[]{:S(2)}, u32[]{:S(2)}) collective-permute-start(bf16[3,256,640]{2,1,0:T(8,128)(2,1)S(1)} %pad_maximum_fusion), channel_id=1, source_target_pairs={{0,448},{16,464},{32,480},{48,496},{64,0},{80,16},{96,32},{112,48}... | collective-permute-start | bytes 2949128 | tf_op jit(solution)/shard_map/ppermute | solution.py:223
  61.3 1.9 collective-permute-start.13
  63.3 4.6 %collective-permute-start.2 = (bf16[1,256,640]{2,1,0:T(8,128)(2,1)}, bf16[1,256,640]{2,1,0:T(8,128)(2,1)}, u32[]{:S(2)}, u32[]{:S(2)}) collective-permute-start(bf16[1,256,640]{2,1,0:T(8,128)(2,1)} %collective-permute-done), channel_id=1, source_target_pairs={{0,448},{16,464},{32,480},{48,496},{64,0},{80,16},{96,32},{112,48}... | collective-permute-start | bytes 983048 | tf_op jit(solution)/shard_map/ppermute | solution.py:223
  67.9 1.9 collective-permute-start.3
  69.8 19.1 %collective-permute-done.2 = bf16[1,256,640]{2,1,0:T(8,128)(2,1)} collective-permute-done((bf16[1,256,640]{2,1,0:T(8,128)(2,1)}, bf16[1,256,640]{2,1,0:T(8,128)(2,1)}, u32[]{:S(2)}, u32[]{:S(2)}) %collective-permute-start.2) | collective-permute-done | bytes 327712 | tf_op jit(solution)/shard_map/ppermute | solution.py:223
  88.9 5.3 %collective-permute-start.4 = (bf16[1,256,640]{2,1,0:T(8,128)(2,1)}, bf16[1,256,640]{2,1,0:T(8,128)(2,1)S(1)}, u32[]{:S(2)}, u32[]{:S(2)}) collective-permute-start(bf16[1,256,640]{2,1,0:T(8,128)(2,1)} %collective-permute-done.2), channel_id=1, source_target_pairs={{0,448},{16,464},{32,480},{48,496},{64,0},{80,16},{96,32},{112,48}... | collective-permute-start | bytes 983048 | tf_op jit(solution)/shard_map/ppermute | solution.py:223
  94.3 1.9 collective-permute-start.5
  96.6 3.4 %collective-permute-done.4 = bf16[1,256,640]{2,1,0:T(8,128)(2,1)S(1)} collective-permute-done((bf16[1,256,640]{2,1,0:T(8,128)(2,1)}, bf16[1,256,640]{2,1,0:T(8,128)(2,1)S(1)}, u32[]{:S(2)}, u32[]{:S(2)}) %collective-permute-start.4) | collective-permute-done | bytes 327712 | tf_op jit(solution)/shard_map/ppermute | solution.py:223
  100.1 0.7 slice.143
  100.8 5.2 %collective-permute-start.7 = (bf16[1,128,640]{2,1,0:T(8,128)(2,1)}, bf16[1,128,640]{2,1,0:T(8,128)(2,1)}, u32[]{:S(2)}, u32[]{:S(2)}) collective-permute-start(bf16[1,128,640]{2,1,0:T(8,128)(2,1)} %slice.143), channel_id=1, source_target_pairs={{0,448},{16,464},{32,480},{48,496},{64,0},{80,16},{96,32},{112,48}... | collective-permute-start | bytes 491528 | tf_op jit(solution)/shard_map/ppermute | solution.py:231
  106.0 1.6 slice.142
  107.6 1.9 collective-permute-start.6
  109.5 1.9 collective-permute-start.15
  111.5 4.6 %collective-permute-start.14 = (bf16[3,256,640]{2,1,0:T(8,128)(2,1)S(1)}, bf16[3,256,640]{2,1,0:T(8,128)(2,1)S(1)}, u32[]{:S(2)}, u32[]{:S(2)}) collective-permute-start(bf16[3,256,640]{2,1,0:T(8,128)(2,1)S(1)} %collective-permute-done.12), channel_id=1, source_target_pairs={{0,448},{16,464},{32,480},{48,496},{64,0},{80,16},{96,32},{112,48}... | collective-permute-start | bytes 2949128 | tf_op jit(solution)/shard_map/ppermute | solution.py:223
  116.1 1.5 fusion.40
  117.5 1.7 fusion.33
  119.2 1.3 fusion.34
  120.5 1.3 fusion.31
  121.9 1.3 fusion.32
  123.2 1.4 fusion.42
  125.8 1.4 convolution_add_fusion.12
  127.1 1.4 fusion.45
  128.5 1.4 fusion.35
  129.9 1.4 convolution_add_fusion.11
  131.2 1.4 fusion
  133.0 2.0 %collective-permute-done.15 = bf16[3,256,640]{2,1,0:T(8,128)(2,1)S(1)} collective-permute-done((bf16[3,256,640]{2,1,0:T(8,128)(2,1)S(1)}, bf16[3,256,640]{2,1,0:T(8,128)(2,1)S(1)}, u32[]{:S(2)}, u32[]{:S(2)}) %collective-permute-start.15) | collective-permute-done | bytes 983072 | tf_op jit(solution)/shard_map/ppermute | solution.py:225
  135.0 1.9 collective-permute-start.17
  136.9 4.6 %collective-permute-start.16 = (bf16[3,256,640]{2,1,0:T(8,128)(2,1)S(1)}, bf16[3,256,640]{2,1,0:T(8,128)(2,1)S(1)}, u32[]{:S(2)}, u32[]{:S(2)}) collective-permute-start(bf16[3,256,640]{2,1,0:T(8,128)(2,1)S(1)} %collective-permute-done.14), channel_id=1, source_target_pairs={{0,448},{16,464},{32,480},{48,496},{64,0},{80,16},{96,32},{112,48}... | collective-permute-start | bytes 2949128 | tf_op jit(solution)/shard_map/ppermute | solution.py:223
  144.3 13.5 %collective-permute-done.17 = bf16[3,256,640]{2,1,0:T(8,128)(2,1)S(1)} collective-permute-done((bf16[3,256,640]{2,1,0:T(8,128)(2,1)S(1)}, bf16[3,256,640]{2,1,0:T(8,128)(2,1)S(1)}, u32[]{:S(2)}, u32[]{:S(2)}) %collective-permute-start.17) | collective-permute-done | bytes 983072 | tf_op jit(solution)/shard_map/ppermute | solution.py:225
  157.8 1.9 collective-permute-start.18
  159.8 4.8 %collective-permute-start.19 = (bf16[3,128,640]{2,1,0:T(8,128)(2,1)S(1)}, bf16[3,128,640]{2,1,0:T(8,128)(2,1)S(1)}, u32[]{:S(2)}, u32[]{:S(2)}) collective-permute-start(bf16[3,128,640]{2,1,0:T(8,128)(2,1)S(1)} %slice.165), channel_id=1, source_target_pairs={{0,448},{16,464},{32,480},{48,496},{64,0},{80,16},{96,32},{112,48}... | collective-permute-start | bytes 1474568 | tf_op jit(solution)/shard_map/ppermute | solution.py:231
  166.5 2.7 %collective-permute-done.18 = bf16[3,128,640]{2,1,0:T(8,128)(2,1)S(1)} collective-permute-done((bf16[3,128,640]{2,1,0:T(8,128)(2,1)S(1)}, bf16[3,128,640]{2,1,0:T(8,128)(2,1)S(1)}, u32[]{:S(2)}, u32[]{:S(2)}) %collective-permute-start.18) | collective-permute-done | bytes 491552 | tf_op jit(solution)/shard_map/ppermute | solution.py:230
  169.2 0.9 collective-permute-done.19
  172.3 7.6 %collective-permute-start.20 = (bf16[512,128]{1,0:T(8,128)(2,1)S(1)}, bf16[512,128]{1,0:T(8,128)(2,1)S(1)}, u32[]{:S(2)}, u32[]{:S(2)}) collective-permute-start(bf16[512,128]{1,0:T(8,128)(2,1)S(1)} %slice.226), channel_id=1, source_target_pairs={{0,1},{1,0},{2,3},{3,2},{4,5},{5,4},{6,7},{7,6},{8,9},{9,8},{10,11... | collective-permute-start | bytes 393224 | tf_op jit(solution)/shard_map/ppermute | solution.py:288
  179.8 0.9 copy.7.row_seg_ref
  180.8 0.7 broadcast_select_fusion
  181.5 6.0 %shard_map.64 = bf16[512,512]{1,0:T(8,128)(2,1)} custom-call(f32[512,640]{1,0:T(8,128)} %copy-done.1, bf16[512,128]{1,0:T(8,128)(2,1)} %get-tuple-element.24.k_ref, bf16[512,128]{1,0:T(8,128)(2,1)} %get-tuple-element.23.v_ref, f32[512,64]{1,0:T(8,128)} %get-tuple-element.17.cos_ref, f32[512,64]{1,0:T(8,128)} %get-tuple-element.18.sin_ref, ...), custom_call_target="tpu_custom_call" | custom-call | flops 538968064 | bytes 2097152 | tf_op jit(solution)/shard_map/pallas_call | solution.py:113
  (69 shorter events, 10.5 us)
Async XLA Ops:
  6.5 4.3 %copy-start.2 = (bf16[256,512]{1,0:T(8,128)(2,1)S(1)}, bf16[256,512]{1,0:T(8,128)(2,1)}, u32[]{:S(2)}) copy-start(bf16[256,512]{1,0:T(8,128)(2,1)} %param.9) | copy-start | bytes 786436
  6.5 103.0 %all-gather.2.cloned.1.call-start = ((), (), s32[]{:S(2)}) async-start(), calls=%async_computation | async-start | bytes 8912896 | tf_op jit(solution)/shard_map/all_gather | solution.py:265
  7.8 22.4 %copy-start.5 = (s32[512]{0:T(512)S(1)}, s32[512]{0:T(512)}, u32[]{:S(2)}) copy-start(s32[512]{0:T(512)} %param.7) | copy-start | bytes 6148
  10.9 0.6 copy-start.3
  11.5 25.5 %collective-permute-start.9 = (bf16[256,640]{1,0:T(8,128)(2,1)S(1)}, bf16[256,640]{1,0:T(8,128)(2,1)S(1)}, u32[]{:S(2)}, u32[]{:S(2)}) collective-permute-start(bf16[256,640]{1,0:T(8,128)(2,1)S(1)} %get-tuple-element.22), channel_id=1, source_target_pairs={{0,16},{16,32},{32,48},{48,0},{64,80},{80,96},{96,112},{112,64},{1... | collective-permute-start | bytes 983048 | tf_op jit(solution)/shard_map/ppermute | solution.py:182
  13.9 18.1 %collective-permute-start.8 = (bf16[256,640]{1,0:T(8,128)(2,1)S(1)}, bf16[256,640]{1,0:T(8,128)(2,1)S(1)}, u32[]{:S(2)}, u32[]{:S(2)}) collective-permute-start(bf16[256,640]{1,0:T(8,128)(2,1)S(1)} %get-tuple-element.22), channel_id=1, source_target_pairs={{0,48},{16,0},{32,16},{48,32},{64,112},{80,64},{96,80},{112,96},{1... | collective-permute-start | bytes 983048 | tf_op jit(solution)/shard_map/ppermute | solution.py:181
  17.7 45.6 %collective-permute-start = (bf16[1,256,640]{2,1,0:T(8,128)(2,1)S(1)}, bf16[1,256,640]{2,1,0:T(8,128)(2,1)}, u32[]{:S(2)}, u32[]{:S(2)}) collective-permute-start(bf16[1,256,640]{2,1,0:T(8,128)(2,1)S(1)} %get-tuple-element.21), channel_id=1, source_target_pairs={{0,448},{16,464},{32,480},{48,496},{64,0},{80,16},{96,32},{112,48}... | collective-permute-start | bytes 983048 | tf_op jit(solution)/shard_map/ppermute | solution.py:223
  28.3 39.5 %collective-permute-start.1 = (bf16[1,256,640]{2,1,0:T(8,128)(2,1)S(1)}, bf16[1,256,640]{2,1,0:T(8,128)(2,1)}, u32[]{:S(2)}, u32[]{:S(2)}) collective-permute-start(bf16[1,256,640]{2,1,0:T(8,128)(2,1)S(1)} %get-tuple-element.21), channel_id=1, source_target_pairs={{0,64},{16,80},{32,96},{48,112},{64,128},{80,144},{96,160},{112,17... | collective-permute-start | bytes 983048 | tf_op jit(solution)/shard_map/ppermute | solution.py:225
  32.0 9.3 %collective-permute-start.11 = (bf16[128,640]{1,0:T(8,128)(2,1)S(1)}, bf16[128,640]{1,0:T(8,128)(2,1)S(1)}, u32[]{:S(2)}, u32[]{:S(2)}) collective-permute-start(bf16[128,640]{1,0:T(8,128)(2,1)S(1)} %slice.145), channel_id=1, source_target_pairs={{0,48},{16,0},{32,16},{48,32},{64,112},{80,64},{96,80},{112,96},{1... | collective-permute-start | bytes 491528 | tf_op jit(solution)/shard_map/ppermute | solution.py:189
  37.0 13.5 %collective-permute-start.10 = (bf16[128,640]{1,0:T(8,128)(2,1)S(1)}, bf16[128,640]{1,0:T(8,128)(2,1)S(1)}, u32[]{:S(2)}, u32[]{:S(2)}) collective-permute-start(bf16[128,640]{1,0:T(8,128)(2,1)S(1)} %slice.144), channel_id=1, source_target_pairs={{0,16},{16,32},{32,48},{48,0},{64,80},{80,96},{96,112},{112,64},{1... | collective-permute-start | bytes 491528 | tf_op jit(solution)/shard_map/ppermute | solution.py:188
  50.7 58.8 %collective-permute-start.12 = (bf16[3,256,640]{2,1,0:T(8,128)(2,1)S(1)}, bf16[3,256,640]{2,1,0:T(8,128)(2,1)S(1)}, u32[]{:S(2)}, u32[]{:S(2)}) collective-permute-start(bf16[3,256,640]{2,1,0:T(8,128)(2,1)S(1)} %pad_maximum_fusion), channel_id=1, source_target_pairs={{0,448},{16,464},{32,480},{48,496},{64,0},{80,16},{96,32},{112,48}... | collective-permute-start | bytes 2949128 | tf_op jit(solution)/shard_map/ppermute | solution.py:223
  61.3 48.2 %collective-permute-start.13 = (bf16[3,256,640]{2,1,0:T(8,128)(2,1)S(1)}, bf16[3,256,640]{2,1,0:T(8,128)(2,1)S(1)}, u32[]{:S(2)}, u32[]{:S(2)}) collective-permute-start(bf16[3,256,640]{2,1,0:T(8,128)(2,1)S(1)} %pad_maximum_fusion), channel_id=1, source_target_pairs={{0,64},{16,80},{32,96},{48,112},{64,128},{80,144},{96,160},{112,17... | collective-permute-start | bytes 2949128 | tf_op jit(solution)/shard_map/ppermute | solution.py:225
  63.3 25.7 %collective-permute-start.2 = (bf16[1,256,640]{2,1,0:T(8,128)(2,1)}, bf16[1,256,640]{2,1,0:T(8,128)(2,1)}, u32[]{:S(2)}, u32[]{:S(2)}) collective-permute-start(bf16[1,256,640]{2,1,0:T(8,128)(2,1)} %collective-permute-done), channel_id=1, source_target_pairs={{0,448},{16,464},{32,480},{48,496},{64,0},{80,16},{96,32},{112,48}... | collective-permute-start | bytes 983048 | tf_op jit(solution)/shard_map/ppermute | solution.py:223
  67.9 26.4 %collective-permute-start.3 = (bf16[1,256,640]{2,1,0:T(8,128)(2,1)}, bf16[1,256,640]{2,1,0:T(8,128)(2,1)}, u32[]{:S(2)}, u32[]{:S(2)}) collective-permute-start(bf16[1,256,640]{2,1,0:T(8,128)(2,1)} %collective-permute-done.1), channel_id=1, source_target_pairs={{0,64},{16,80},{32,96},{48,112},{64,128},{80,144},{96,160},{112,17... | collective-permute-start | bytes 983048 | tf_op jit(solution)/shard_map/ppermute | solution.py:225
  88.9 11.1 %collective-permute-start.4 = (bf16[1,256,640]{2,1,0:T(8,128)(2,1)}, bf16[1,256,640]{2,1,0:T(8,128)(2,1)S(1)}, u32[]{:S(2)}, u32[]{:S(2)}) collective-permute-start(bf16[1,256,640]{2,1,0:T(8,128)(2,1)} %collective-permute-done.2), channel_id=1, source_target_pairs={{0,448},{16,464},{32,480},{48,496},{64,0},{80,16},{96,32},{112,48}... | collective-permute-start | bytes 983048 | tf_op jit(solution)/shard_map/ppermute | solution.py:223
  94.3 11.7 %collective-permute-start.5 = (bf16[1,256,640]{2,1,0:T(8,128)(2,1)}, bf16[1,256,640]{2,1,0:T(8,128)(2,1)}, u32[]{:S(2)}, u32[]{:S(2)}) collective-permute-start(bf16[1,256,640]{2,1,0:T(8,128)(2,1)} %collective-permute-done.3), channel_id=1, source_target_pairs={{0,64},{16,80},{32,96},{48,112},{64,128},{80,144},{96,160},{112,17... | collective-permute-start | bytes 983048 | tf_op jit(solution)/shard_map/ppermute | solution.py:225
  100.8 27.7 %collective-permute-start.7 = (bf16[1,128,640]{2,1,0:T(8,128)(2,1)}, bf16[1,128,640]{2,1,0:T(8,128)(2,1)}, u32[]{:S(2)}, u32[]{:S(2)}) collective-permute-start(bf16[1,128,640]{2,1,0:T(8,128)(2,1)} %slice.143), channel_id=1, source_target_pairs={{0,448},{16,464},{32,480},{48,496},{64,0},{80,16},{96,32},{112,48}... | collective-permute-start | bytes 491528 | tf_op jit(solution)/shard_map/ppermute | solution.py:231
  107.6 20.9 %collective-permute-start.6 = (bf16[1,128,640]{2,1,0:T(8,128)(2,1)}, bf16[1,128,640]{2,1,0:T(8,128)(2,1)}, u32[]{:S(2)}, u32[]{:S(2)}) collective-permute-start(bf16[1,128,640]{2,1,0:T(8,128)(2,1)} %slice.142), channel_id=1, source_target_pairs={{0,64},{16,80},{32,96},{48,112},{64,128},{80,144},{96,160},{112,17... | collective-permute-start | bytes 491528 | tf_op jit(solution)/shard_map/ppermute | solution.py:230
  109.5 25.5 %collective-permute-start.15 = (bf16[3,256,640]{2,1,0:T(8,128)(2,1)S(1)}, bf16[3,256,640]{2,1,0:T(8,128)(2,1)S(1)}, u32[]{:S(2)}, u32[]{:S(2)}) collective-permute-start(bf16[3,256,640]{2,1,0:T(8,128)(2,1)S(1)} %collective-permute-done.13), channel_id=1, source_target_pairs={{0,64},{16,80},{32,96},{48,112},{64,128},{80,144},{96,160},{112,17... | collective-permute-start | bytes 2949128 | tf_op jit(solution)/shard_map/ppermute | solution.py:225
  111.5 25.4 %collective-permute-start.14 = (bf16[3,256,640]{2,1,0:T(8,128)(2,1)S(1)}, bf16[3,256,640]{2,1,0:T(8,128)(2,1)S(1)}, u32[]{:S(2)}, u32[]{:S(2)}) collective-permute-start(bf16[3,256,640]{2,1,0:T(8,128)(2,1)S(1)} %collective-permute-done.12), channel_id=1, source_target_pairs={{0,448},{16,464},{32,480},{48,496},{64,0},{80,16},{96,32},{112,48}... | collective-permute-start | bytes 2949128 | tf_op jit(solution)/shard_map/ppermute | solution.py:223
  116.0 7.2 %copy-start = (bf16[512,8192]{1,0:T(8,128)(2,1)S(1)}, bf16[512,8192]{1,0:T(8,128)(2,1)}, u32[]{:S(2)}) copy-start(bf16[512,8192]{1,0:T(8,128)(2,1)} %all-gather.2.cloned.1.call-done) | copy-start | bytes 25165828
  123.2 1.4 copy-start.4
  135.0 22.8 %collective-permute-start.17 = (bf16[3,256,640]{2,1,0:T(8,128)(2,1)S(1)}, bf16[3,256,640]{2,1,0:T(8,128)(2,1)S(1)}, u32[]{:S(2)}, u32[]{:S(2)}) collective-permute-start(bf16[3,256,640]{2,1,0:T(8,128)(2,1)S(1)} %collective-permute-done.15), channel_id=1, source_target_pairs={{0,64},{16,80},{32,96},{48,112},{64,128},{80,144},{96,160},{112,17... | collective-permute-start | bytes 2949128 | tf_op jit(solution)/shard_map/ppermute | solution.py:225
  136.9 22.8 %collective-permute-start.16 = (bf16[3,256,640]{2,1,0:T(8,128)(2,1)S(1)}, bf16[3,256,640]{2,1,0:T(8,128)(2,1)S(1)}, u32[]{:S(2)}, u32[]{:S(2)}) collective-permute-start(bf16[3,256,640]{2,1,0:T(8,128)(2,1)S(1)} %collective-permute-done.14), channel_id=1, source_target_pairs={{0,448},{16,464},{32,480},{48,496},{64,0},{80,16},{96,32},{112,48}... | collective-permute-start | bytes 2949128 | tf_op jit(solution)/shard_map/ppermute | solution.py:223
  157.8 11.3 %collective-permute-start.18 = (bf16[3,128,640]{2,1,0:T(8,128)(2,1)S(1)}, bf16[3,128,640]{2,1,0:T(8,128)(2,1)S(1)}, u32[]{:S(2)}, u32[]{:S(2)}) collective-permute-start(bf16[3,128,640]{2,1,0:T(8,128)(2,1)S(1)} %slice.164), channel_id=1, source_target_pairs={{0,64},{16,80},{32,96},{48,112},{64,128},{80,144},{96,160},{112,17... | collective-permute-start | bytes 1474568 | tf_op jit(solution)/shard_map/ppermute | solution.py:230
  159.8 10.3 %collective-permute-start.19 = (bf16[3,128,640]{2,1,0:T(8,128)(2,1)S(1)}, bf16[3,128,640]{2,1,0:T(8,128)(2,1)S(1)}, u32[]{:S(2)}, u32[]{:S(2)}) collective-permute-start(bf16[3,128,640]{2,1,0:T(8,128)(2,1)S(1)} %slice.165), channel_id=1, source_target_pairs={{0,448},{16,464},{32,480},{48,496},{64,0},{80,16},{96,32},{112,48}... | collective-permute-start | bytes 1474568 | tf_op jit(solution)/shard_map/ppermute | solution.py:231
  172.2 9.3 %copy-start.1 = (f32[512,640]{1,0:T(8,128)}, f32[512,640]{1,0:T(8,128)S(1)}, u32[]{:S(2)}) copy-start(f32[512,640]{1,0:T(8,128)S(1)} %fusion.17.q_ref) | copy-start | bytes 3932164
  172.3 8.5 %collective-permute-start.20 = (bf16[512,128]{1,0:T(8,128)(2,1)S(1)}, bf16[512,128]{1,0:T(8,128)(2,1)S(1)}, u32[]{:S(2)}, u32[]{:S(2)}) collective-permute-start(bf16[512,128]{1,0:T(8,128)(2,1)S(1)} %slice.226), channel_id=1, source_target_pairs={{0,1},{1,0},{2,3},{3,2},{4,5},{5,4},{6,7},{7,6},{8,9},{9,8},{10,11... | collective-permute-start | bytes 393224 | tf_op jit(solution)/shard_map/ppermute | solution.py:288
Sparse Core Ops, SparseCore 0:
  10.0 68.7 all-gather.1

commit v21 on v18

--- a/solution.py
+++ b/solution.py
@@ -164,7 +164,7 @@
     return out
 
 
-def ring_matmul(rows, block, axis, stride, count, starts, wait_rows):
+def ring_matmul(rows, block, axis, stride, count, starts, wait_rows, early=None):
     n = lax.psum(1, axis)
     me = lax.axis_index(axis)
     here = (me // stride) % count
@@ -176,6 +176,14 @@
             k = (src // stride) % count
             pairs.append((src, src + (((k + step) % count) - k) * stride))
         return pairs
+
+    def early_product(part, piece_starts, owner):
+        result = None
+        for piece, start in enumerate(piece_starts(owner)):
+            lhs = lax.dynamic_slice_in_dim(rows, start, depth, 1)
+            term = jnp.dot(lhs, part[piece], preferred_element_type=jnp.float32)
+            result = term if result is None else result + term
+        return result
 
     def product(part, owner):
         result = None
@@ -187,7 +195,24 @@
 
     total = product(block, here)
     from_right, from_left = block, block
-    for step in range(1, count // 2 + 1):
+    first = 1
+    if early is not None:
+        early_block, early_starts = early
+        total = total + early_product(early_block, early_starts, here)
+        early_right = lax.ppermute(early_block, axis, perm=moved(-1))
+        early_left = lax.ppermute(early_block, axis, perm=moved(1))
+        from_right = lax.ppermute(block, axis, perm=moved(-1))
+        from_left = lax.ppermute(block, axis, perm=moved(1))
+        total = total + early_product(early_right, early_starts, (here + 1) % count)
+        total = total + product(from_right, (here + 1) % count)
+        total = total + early_product(early_left, early_starts, (here - 1) % count)
+        total = total + product(from_left, (here - 1) % count)
+        from_right = jnp.concatenate([early_right, from_right], axis=0)
+        from_left = jnp.concatenate([early_left, from_left], axis=0)
+        block_starts = starts
+        starts = lambda owner: early_starts(owner) + block_starts(owner)
+        first = 2
+    for step in range(first, count // 2 + 1):
         if step == 2 and wait_rows:
             rows, from_right, from_left = lax.optimization_barrier((rows, from_right, from_left))
         if step < count - step:
@@ -236,16 +261,7 @@
     )
     gathered = lax.all_gather(normed, "weight", axis=0, tiled=True)
     pack_rows = gathered.shape[0]
-    own_part = ring_matmul(
-        gathered,
-        local_weights[None],
-        "batch",
-        y_hi,
-        Z_CHIPS,
-        lambda z: [(z * y_hi + yh) * shard],
-        False,
-    )
-    other_part = ring_matmul(
+    projected = ring_matmul(
         gathered,
         others,
         "batch",
@@ -253,8 +269,8 @@
         Z_CHIPS,
         lambda z: [(z * y_hi + (yh + r) % y_hi) * shard for r in range(1, y_hi)],
         True,
-    )
-    projected = own_part + other_part
+        early=(local_weights[None], lambda z: [(z * y_hi + yh) * shard]),
+    )
     own_rows = projected[:, query_cols:].astype(jnp.bfloat16)
     partner = [(w, w ^ 1) for w in range(n_weight)]
     other_rows = lax.ppermute(own_rows, "weight", perm=partner)

time: 195 us -> 198 us (1.015)
  the two profiles are of different devices: /device:TPU:7 before, /device:TPU:45 now
where the time goes in v21:
time: 198 us; the launch traced here: 197 us
  waiting for transfers between devices  86.2 us (44%)
  starting transfers between devices  57.6 us (29%)
  matrix products  18.1 us (9%)
  between operations  15 us (8%)
  other arithmetic  11.7 us (6%)
  Pallas kernels  5.95 us (3%)
  local copies, waits for them, and re-layouts  2.63 us (1%)
    ppermute x2, waiting for transfers between devices, ring_matmul(): from_left = lax.ppermute(from_left, axis, perm=moved(1))  35.8 us
    ppermute x1, waiting for transfers between devices, ring_matmul(): early_right = lax.ppermute(early_block, axis, perm=moved(-1))  18.8 us
    dot_general x29, matrix products, product(): term = jnp.dot(lhs, part[piece], preferred_element_type=jnp.float32)  15.7 us
    ppermute x1, waiting for transfers between devices, ring_gather(): lax.ppermute(from_left[..., :cut, :], axis, perm=moved(1))  11.5 us
    ppermute x1, starting transfers between devices, ring_matmul(): from_right = lax.ppermute(block, axis, perm=moved(-1))  10.7 us
    ppermute x2, starting transfers between devices, ring_matmul(): from_right = lax.ppermute(from_right, axis, perm=moved(-1))  9.14 us
    ppermute x1, starting transfers between devices, per_device(): other_rows = lax.ppermute(own_rows, 'weight', perm=partner)  6.67 us
    ppermute x1, waiting for transfers between devices, ring_matmul(): lax.ppermute(from_left[..., :cut, :], axis, perm=moved(1))  6.29 us
  transfers between devices with their start and end apart: 16, of which 10 were waited for; matrix products, arithmetic and copies ran while one was open for 13% of the time, Pallas kernels for 0%

profile of v21, /device:TPU:45, one launch (start us, length us, event | category | flops | bytes accessed | tf_op | source)
XLA Modules:
  0.0 197.2 jit_solution(5823130076402333265)
XLA Ops:
  6.5 1.3 fusion.20
  7.9 2.0 %fusion.22 = bf16[32,8192]{1,0:T(8,128)(2,1)} fusion(bf16[32,8192]{1,0:T(8,128)(2,1)} %param.6, f32[8192]{0:T(1024)} %param.8, f32[32]{0:T(128)S(1)} %add_rsqrt_fusion), kind=kLoop, calls=%fused_computation.37 | loop fusion | flops 1048576 | bytes 1081472 | tf_op jit(solution)/shard_map/convert_element_type | solution.py:249
  9.9 0.9 dynamic-slice_select_fusion
  10.9 0.8 fusion.118
  11.6 2.9 %collective-permute-start = (bf16[256,640]{1,0:T(8,128)(2,1)S(1)}, bf16[256,640]{1,0:T(8,128)(2,1)S(1)}, u32[]{:S(2)}, u32[]{:S(2)}) collective-permute-start(bf16[256,640]{1,0:T(8,128)(2,1)S(1)} %get-tuple-element.25), channel_id=1, source_target_pairs={{0,48},{16,0},{32,16},{48,32},{64,112},{80,64},{96,80},{112,96},{1... | collective-permute-start | bytes 983048 | tf_op jit(solution)/shard_map/ppermute | solution.py:151
  14.5 3.3 %collective-permute-start.1 = (bf16[256,640]{1,0:T(8,128)(2,1)S(1)}, bf16[256,640]{1,0:T(8,128)(2,1)S(1)}, u32[]{:S(2)}, u32[]{:S(2)}) collective-permute-start(bf16[256,640]{1,0:T(8,128)(2,1)S(1)} %get-tuple-element.25), channel_id=1, source_target_pairs={{0,16},{16,32},{32,48},{48,0},{64,80},{80,96},{96,112},{112,64},{1... | collective-permute-start | bytes 983048 | tf_op jit(solution)/shard_map/ppermute | solution.py:153
  17.9 0.5 slice.118
  19.9 1.8 multiply_sine_fusion
  21.7 2.9 %collective-permute-done = bf16[256,640]{1,0:T(8,128)(2,1)S(1)} collective-permute-done((bf16[256,640]{1,0:T(8,128)(2,1)S(1)}, bf16[256,640]{1,0:T(8,128)(2,1)S(1)}, u32[]{:S(2)}, u32[]{:S(2)}) %collective-permute-start) | collective-permute-done | bytes 327712 | tf_op jit(solution)/shard_map/ppermute | solution.py:151
  24.7 4.2 %collective-permute-start.3 = (bf16[128,640]{1,0:T(8,128)(2,1)S(1)}, bf16[128,640]{1,0:T(8,128)(2,1)S(1)}, u32[]{:S(2)}, u32[]{:S(2)}) collective-permute-start(bf16[128,640]{1,0:T(8,128)(2,1)S(1)} %slice.155), channel_id=1, source_target_pairs={{0,48},{16,0},{32,16},{48,32},{64,112},{80,64},{96,80},{112,96},{1... | collective-permute-start | bytes 491528 | tf_op jit(solution)/shard_map/ppermute | solution.py:159
  28.9 6.1 %collective-permute-done.1 = bf16[256,640]{1,0:T(8,128)(2,1)S(1)} collective-permute-done((bf16[256,640]{1,0:T(8,128)(2,1)S(1)}, bf16[256,640]{1,0:T(8,128)(2,1)S(1)}, u32[]{:S(2)}, u32[]{:S(2)}) %collective-permute-start.1) | collective-permute-done | bytes 327712 | tf_op jit(solution)/shard_map/ppermute | solution.py:153
  35.0 1.9 collective-permute-start.2
  37.0 11.5 %collective-permute-done.2 = bf16[128,640]{1,0:T(8,128)(2,1)S(1)} collective-permute-done((bf16[128,640]{1,0:T(8,128)(2,1)S(1)}, bf16[128,640]{1,0:T(8,128)(2,1)S(1)}, u32[]{:S(2)}, u32[]{:S(2)}) %collective-permute-start.2) | collective-permute-done | bytes 163872 | tf_op jit(solution)/shard_map/ppermute | solution.py:158
  48.8 10.7 %collective-permute-start.5 = (bf16[3,256,640]{2,1,0:T(8,128)(2,1)S(1)}, bf16[3,256,640]{2,1,0:T(8,128)(2,1)S(1)}, u32[]{:S(2)}, u32[]{:S(2)}) collective-permute-start(bf16[3,256,640]{2,1,0:T(8,128)(2,1)S(1)} %pad_maximum_fusion.2), channel_id=1, source_target_pairs={{0,448},{16,464},{32,480},{48,496},{64,0},{80,16},{96,32},{112,48}... | collective-permute-start | bytes 2949128 | tf_op jit(solution)/shard_map/ppermute | solution.py:204
  59.5 1.9 collective-permute-start.7
  61.4 4.6 %collective-permute-start.4 = (bf16[1,256,640]{2,1,0:T(8,128)(2,1)}, bf16[1,256,640]{2,1,0:T(8,128)(2,1)S(1)}, u32[]{:S(2)}, u32[]{:S(2)}) collective-permute-start(bf16[1,256,640]{2,1,0:T(8,128)(2,1)} %get-tuple-element.24), channel_id=1, source_target_pairs={{0,448},{16,464},{32,480},{48,496},{64,0},{80,16},{96,32},{112,48}... | collective-permute-start | bytes 983048 | tf_op jit(solution)/shard_map/ppermute | solution.py:202
  66.0 1.9 collective-permute-start.6
  68.3 18.8 %collective-permute-done.4 = bf16[1,256,640]{2,1,0:T(8,128)(2,1)S(1)} collective-permute-done((bf16[1,256,640]{2,1,0:T(8,128)(2,1)}, bf16[1,256,640]{2,1,0:T(8,128)(2,1)S(1)}, u32[]{:S(2)}, u32[]{:S(2)}) %collective-permute-start.4) | collective-permute-done | bytes 327712 | tf_op jit(solution)/shard_map/ppermute | solution.py:202
  87.1 1.3 pad_maximum_fusion
  88.4 3.7 %collective-permute-done.6 = bf16[1,256,640]{2,1,0:T(8,128)(2,1)} collective-permute-done((bf16[1,256,640]{2,1,0:T(8,128)(2,1)}, bf16[1,256,640]{2,1,0:T(8,128)(2,1)}, u32[]{:S(2)}, u32[]{:S(2)}) %collective-permute-start.6) | collective-permute-done | bytes 327712 | tf_op jit(solution)/shard_map/ppermute | solution.py:203
  92.1 2.2 %pad_maximum_fusion.1 = bf16[4,256,640]{2,1,0:T(8,128)(2,1)} fusion(bf16[3,256,640]{2,1,0:T(8,128)(2,1)S(1)} %collective-permute-done.7, bf16[1,256,640]{2,1,0:T(8,128)(2,1)} %collective-permute-done.6), kind=kLoop, calls=%fused_computation.34 | loop fusion | flops 655360 | bytes 2621440 | tf_op jit(solution)/shard_map/concatenate | solution.py:211
  94.3 1.9 collective-permute-start.9
  96.2 4.6 %collective-permute-start.8 = (bf16[4,256,640]{2,1,0:T(8,128)(2,1)}, bf16[4,256,640]{2,1,0:T(8,128)(2,1)S(1)}, u32[]{:S(2)}, u32[]{:S(2)}) collective-permute-start(bf16[4,256,640]{2,1,0:T(8,128)(2,1)} %pad_maximum_fusion), channel_id=1, source_target_pairs={{0,448},{16,464},{32,480},{48,496},{64,0},{80,16},{96,32},{112,48}... | collective-permute-start | bytes 3932168 | tf_op jit(solution)/shard_map/ppermute | solution.py:219
  100.8 1.5 fusion.38
  102.3 1.7 fusion.39
  104.0 1.4 fusion.43
  105.4 1.3 fusion.40
  106.7 1.3 fusion.48
  109.2 0.4 copy-done.4
  110.1 0.4 fusion.2
  110.8 15.3 %collective-permute-done.9 = bf16[4,256,640]{2,1,0:T(8,128)(2,1)S(1)} collective-permute-done((bf16[4,256,640]{2,1,0:T(8,128)(2,1)}, bf16[4,256,640]{2,1,0:T(8,128)(2,1)S(1)}, u32[]{:S(2)}, u32[]{:S(2)}) %collective-permute-start.9) | collective-permute-done | bytes 1310752 | tf_op jit(solution)/shard_map/ppermute | solution.py:221
  126.2 1.9 collective-permute-start.11
  128.1 4.6 %collective-permute-start.10 = (bf16[4,256,640]{2,1,0:T(8,128)(2,1)S(1)}, bf16[4,256,640]{2,1,0:T(8,128)(2,1)S(1)}, u32[]{:S(2)}, u32[]{:S(2)}) collective-permute-start(bf16[4,256,640]{2,1,0:T(8,128)(2,1)S(1)} %collective-permute-done.8), channel_id=1, source_target_pairs={{0,448},{16,464},{32,480},{48,496},{64,0},{80,16},{96,32},{112,48}... | collective-permute-start | bytes 3932168 | tf_op jit(solution)/shard_map/ppermute | solution.py:219
  134.9 0.5 fusion.14
  135.4 0.5 fusion.15
  135.9 0.6 fusion.19
  136.5 20.4 %collective-permute-done.11 = bf16[4,256,640]{2,1,0:T(8,128)(2,1)S(1)} collective-permute-done((bf16[4,256,640]{2,1,0:T(8,128)(2,1)S(1)}, bf16[4,256,640]{2,1,0:T(8,128)(2,1)S(1)}, u32[]{:S(2)}, u32[]{:S(2)}) %collective-permute-start.11) | collective-permute-done | bytes 1310752 | tf_op jit(solution)/shard_map/ppermute | solution.py:221
  157.0 1.9 collective-permute-start.12
  159.0 4.8 %collective-permute-start.13 = (bf16[4,128,640]{2,1,0:T(8,128)(2,1)S(1)}, bf16[4,128,640]{2,1,0:T(8,128)(2,1)S(1)}, u32[]{:S(2)}, u32[]{:S(2)}) collective-permute-start(bf16[4,128,640]{2,1,0:T(8,128)(2,1)S(1)} %slice.179), channel_id=1, source_target_pairs={{0,448},{16,464},{32,480},{48,496},{64,0},{80,16},{96,32},{112,48}... | collective-permute-start | bytes 1966088 | tf_op jit(solution)/shard_map/ppermute | solution.py:227
  166.0 0.5 fusion.9
  166.5 6.3 %collective-permute-done.12 = bf16[4,128,640]{2,1,0:T(8,128)(2,1)S(1)} collective-permute-done((bf16[4,128,640]{2,1,0:T(8,128)(2,1)S(1)}, bf16[4,128,640]{2,1,0:T(8,128)(2,1)S(1)}, u32[]{:S(2)}, u32[]{:S(2)}) %collective-permute-start.12) | collective-permute-done | bytes 655392 | tf_op jit(solution)/shard_map/ppermute | solution.py:226
  172.8 0.9 collective-permute-done.13
  174.9 0.5 fusion.8
  175.4 0.6 fusion.13.q_ref
  176.0 6.7 %collective-permute-start.14 = (bf16[512,128]{1,0:T(8,128)(2,1)S(1)}, bf16[512,128]{1,0:T(8,128)(2,1)S(1)}, u32[]{:S(2)}, u32[]{:S(2)}) collective-permute-start(bf16[512,128]{1,0:T(8,128)(2,1)S(1)} %slice.251), channel_id=1, source_target_pairs={{0,1},{1,0},{2,3},{3,2},{4,5},{5,4},{6,7},{7,6},{8,9},{9,8},{10,11... | collective-permute-start | bytes 393224 | tf_op jit(solution)/shard_map/ppermute | solution.py:276
  182.7 0.9 copy.7.row_seg_ref
  183.7 0.7 broadcast_select_fusion
  184.4 6.0 %shard_map.64 = bf16[512,512]{1,0:T(8,128)(2,1)} custom-call(f32[512,640]{1,0:T(8,128)} %copy-done.1, bf16[512,128]{1,0:T(8,128)(2,1)} %get-tuple-element.27.k_ref, bf16[512,128]{1,0:T(8,128)(2,1)} %get-tuple-element.26.v_ref, f32[512,64]{1,0:T(8,128)} %get-tuple-element.17.cos_ref, f32[512,64]{1,0:T(8,128)} %get-tuple-element.18.sin_ref, ...), custom_call_target="tpu_custom_call" | custom-call | flops 538968064 | bytes 2097152 | tf_op jit(solution)/shard_map/pallas_call | solution.py:113
  (62 shorter events, 9.1 us)
Async XLA Ops:
  6.5 4.3 %copy-start.2 = (bf16[256,512]{1,0:T(8,128)(2,1)S(1)}, bf16[256,512]{1,0:T(8,128)(2,1)}, u32[]{:S(2)}) copy-start(bf16[256,512]{1,0:T(8,128)(2,1)} %param.9) | copy-start | bytes 786436
  6.5 87.8 %all-gather.2.cloned.1.call-start = ((), (), s32[]{:S(2)}) async-start(), calls=%async_computation | async-start | bytes 8912896 | tf_op jit(solution)/shard_map/all_gather | solution.py:262
  7.8 10.1 %copy-start.5 = (s32[512]{0:T(512)S(1)}, s32[512]{0:T(512)}, u32[]{:S(2)}) copy-start(s32[512]{0:T(512)} %param.7) | copy-start | bytes 6148
  10.9 9.0 %copy-start.3 = (bf16[256,128]{1,0:T(8,128)(2,1)}, bf16[256,128]{1,0:T(8,128)(2,1)S(1)}, u32[]{:S(2)}) copy-start(bf16[256,128]{1,0:T(8,128)(2,1)S(1)} %dynamic-slice_select_fusion) | copy-start | bytes 196612
  11.6 13.0 %collective-permute-start = (bf16[256,640]{1,0:T(8,128)(2,1)S(1)}, bf16[256,640]{1,0:T(8,128)(2,1)S(1)}, u32[]{:S(2)}, u32[]{:S(2)}) collective-permute-start(bf16[256,640]{1,0:T(8,128)(2,1)S(1)} %get-tuple-element.25), channel_id=1, source_target_pairs={{0,48},{16,0},{32,16},{48,32},{64,112},{80,64},{96,80},{112,96},{1... | collective-permute-start | bytes 983048 | tf_op jit(solution)/shard_map/ppermute | solution.py:151
  14.5 20.5 %collective-permute-start.1 = (bf16[256,640]{1,0:T(8,128)(2,1)S(1)}, bf16[256,640]{1,0:T(8,128)(2,1)S(1)}, u32[]{:S(2)}, u32[]{:S(2)}) collective-permute-start(bf16[256,640]{1,0:T(8,128)(2,1)S(1)} %get-tuple-element.25), channel_id=1, source_target_pairs={{0,16},{16,32},{32,48},{48,0},{64,80},{80,96},{96,112},{112,64},{1... | collective-permute-start | bytes 983048 | tf_op jit(solution)/shard_map/ppermute | solution.py:153
  24.7 12.3 %collective-permute-start.3 = (bf16[128,640]{1,0:T(8,128)(2,1)S(1)}, bf16[128,640]{1,0:T(8,128)(2,1)S(1)}, u32[]{:S(2)}, u32[]{:S(2)}) collective-permute-start(bf16[128,640]{1,0:T(8,128)(2,1)S(1)} %slice.155), channel_id=1, source_target_pairs={{0,48},{16,0},{32,16},{48,32},{64,112},{80,64},{96,80},{112,96},{1... | collective-permute-start | bytes 491528 | tf_op jit(solution)/shard_map/ppermute | solution.py:159
  35.0 13.5 %collective-permute-start.2 = (bf16[128,640]{1,0:T(8,128)(2,1)S(1)}, bf16[128,640]{1,0:T(8,128)(2,1)S(1)}, u32[]{:S(2)}, u32[]{:S(2)}) collective-permute-start(bf16[128,640]{1,0:T(8,128)(2,1)S(1)} %slice.154), channel_id=1, source_target_pairs={{0,16},{16,32},{32,48},{48,0},{64,80},{80,96},{96,112},{112,64},{1... | collective-permute-start | bytes 491528 | tf_op jit(solution)/shard_map/ppermute | solution.py:158
  48.8 38.4 %collective-permute-start.5 = (bf16[3,256,640]{2,1,0:T(8,128)(2,1)S(1)}, bf16[3,256,640]{2,1,0:T(8,128)(2,1)S(1)}, u32[]{:S(2)}, u32[]{:S(2)}) collective-permute-start(bf16[3,256,640]{2,1,0:T(8,128)(2,1)S(1)} %pad_maximum_fusion.2), channel_id=1, source_target_pairs={{0,448},{16,464},{32,480},{48,496},{64,0},{80,16},{96,32},{112,48}... | collective-permute-start | bytes 2949128 | tf_op jit(solution)/shard_map/ppermute | solution.py:204
  59.5 32.7 %collective-permute-start.7 = (bf16[3,256,640]{2,1,0:T(8,128)(2,1)S(1)}, bf16[3,256,640]{2,1,0:T(8,128)(2,1)S(1)}, u32[]{:S(2)}, u32[]{:S(2)}) collective-permute-start(bf16[3,256,640]{2,1,0:T(8,128)(2,1)S(1)} %pad_maximum_fusion.2), channel_id=1, source_target_pairs={{0,64},{16,80},{32,96},{48,112},{64,128},{80,144},{96,160},{112,17... | collective-permute-start | bytes 2949128 | tf_op jit(solution)/shard_map/ppermute | solution.py:205
  61.4 25.8 %collective-permute-start.4 = (bf16[1,256,640]{2,1,0:T(8,128)(2,1)}, bf16[1,256,640]{2,1,0:T(8,128)(2,1)S(1)}, u32[]{:S(2)}, u32[]{:S(2)}) collective-permute-start(bf16[1,256,640]{2,1,0:T(8,128)(2,1)} %get-tuple-element.24), channel_id=1, source_target_pairs={{0,448},{16,464},{32,480},{48,496},{64,0},{80,16},{96,32},{112,48}... | collective-permute-start | bytes 983048 | tf_op jit(solution)/shard_map/ppermute | solution.py:202
  66.0 26.2 %collective-permute-start.6 = (bf16[1,256,640]{2,1,0:T(8,128)(2,1)}, bf16[1,256,640]{2,1,0:T(8,128)(2,1)}, u32[]{:S(2)}, u32[]{:S(2)}) collective-permute-start(bf16[1,256,640]{2,1,0:T(8,128)(2,1)} %get-tuple-element.24), channel_id=1, source_target_pairs={{0,64},{16,80},{32,96},{48,112},{64,128},{80,144},{96,160},{112,17... | collective-permute-start | bytes 983048 | tf_op jit(solution)/shard_map/ppermute | solution.py:203
  94.3 31.9 %collective-permute-start.9 = (bf16[4,256,640]{2,1,0:T(8,128)(2,1)}, bf16[4,256,640]{2,1,0:T(8,128)(2,1)S(1)}, u32[]{:S(2)}, u32[]{:S(2)}) collective-permute-start(bf16[4,256,640]{2,1,0:T(8,128)(2,1)} %pad_maximum_fusion.1), channel_id=1, source_target_pairs={{0,64},{16,80},{32,96},{48,112},{64,128},{80,144},{96,160},{112,17... | collective-permute-start | bytes 3932168 | tf_op jit(solution)/shard_map/ppermute | solution.py:221
  96.2 31.9 %collective-permute-start.8 = (bf16[4,256,640]{2,1,0:T(8,128)(2,1)}, bf16[4,256,640]{2,1,0:T(8,128)(2,1)S(1)}, u32[]{:S(2)}, u32[]{:S(2)}) collective-permute-start(bf16[4,256,640]{2,1,0:T(8,128)(2,1)} %pad_maximum_fusion), channel_id=1, source_target_pairs={{0,448},{16,464},{32,480},{48,496},{64,0},{80,16},{96,32},{112,48}... | collective-permute-start | bytes 3932168 | tf_op jit(solution)/shard_map/ppermute | solution.py:219
  100.8 7.3 %copy-start = (bf16[512,8192]{1,0:T(8,128)(2,1)S(1)}, bf16[512,8192]{1,0:T(8,128)(2,1)}, u32[]{:S(2)}) copy-start(bf16[512,8192]{1,0:T(8,128)(2,1)} %all-gather.2.cloned.1.call-done) | copy-start | bytes 25165828
  108.8 0.8 copy-start.4
  126.2 30.7 %collective-permute-start.11 = (bf16[4,256,640]{2,1,0:T(8,128)(2,1)S(1)}, bf16[4,256,640]{2,1,0:T(8,128)(2,1)S(1)}, u32[]{:S(2)}, u32[]{:S(2)}) collective-permute-start(bf16[4,256,640]{2,1,0:T(8,128)(2,1)S(1)} %collective-permute-done.9), channel_id=1, source_target_pairs={{0,64},{16,80},{32,96},{48,112},{64,128},{80,144},{96,160},{112,17... | collective-permute-start | bytes 3932168 | tf_op jit(solution)/shard_map/ppermute | solution.py:221
  128.1 30.8 %collective-permute-start.10 = (bf16[4,256,640]{2,1,0:T(8,128)(2,1)S(1)}, bf16[4,256,640]{2,1,0:T(8,128)(2,1)S(1)}, u32[]{:S(2)}, u32[]{:S(2)}) collective-permute-start(bf16[4,256,640]{2,1,0:T(8,128)(2,1)S(1)} %collective-permute-done.8), channel_id=1, source_target_pairs={{0,448},{16,464},{32,480},{48,496},{64,0},{80,16},{96,32},{112,48}... | collective-permute-start | bytes 3932168 | tf_op jit(solution)/shard_map/ppermute | solution.py:219
  157.0 15.8 %collective-permute-start.12 = (bf16[4,128,640]{2,1,0:T(8,128)(2,1)S(1)}, bf16[4,128,640]{2,1,0:T(8,128)(2,1)S(1)}, u32[]{:S(2)}, u32[]{:S(2)}) collective-permute-start(bf16[4,128,640]{2,1,0:T(8,128)(2,1)S(1)} %slice.178), channel_id=1, source_target_pairs={{0,64},{16,80},{32,96},{48,112},{64,128},{80,144},{96,160},{112,17... | collective-permute-start | bytes 1966088 | tf_op jit(solution)/shard_map/ppermute | solution.py:226
  159.0 14.7 %collective-permute-start.13 = (bf16[4,128,640]{2,1,0:T(8,128)(2,1)S(1)}, bf16[4,128,640]{2,1,0:T(8,128)(2,1)S(1)}, u32[]{:S(2)}, u32[]{:S(2)}) collective-permute-start(bf16[4,128,640]{2,1,0:T(8,128)(2,1)S(1)} %slice.179), channel_id=1, source_target_pairs={{0,448},{16,464},{32,480},{48,496},{64,0},{80,16},{96,32},{112,48}... | collective-permute-start | bytes 1966088 | tf_op jit(solution)/shard_map/ppermute | solution.py:227
  176.0 8.4 %copy-start.1 = (f32[512,640]{1,0:T(8,128)}, f32[512,640]{1,0:T(8,128)S(1)}, u32[]{:S(2)}) copy-start(f32[512,640]{1,0:T(8,128)S(1)} %fusion.13.q_ref) | copy-start | bytes 3932164
  176.0 7.6 %collective-permute-start.14 = (bf16[512,128]{1,0:T(8,128)(2,1)S(1)}, bf16[512,128]{1,0:T(8,128)(2,1)S(1)}, u32[]{:S(2)}, u32[]{:S(2)}) collective-permute-start(bf16[512,128]{1,0:T(8,128)(2,1)S(1)} %slice.251), channel_id=1, source_target_pairs={{0,1},{1,0},{2,3},{3,2},{4,5},{5,4},{6,7},{7,6},{8,9},{9,8},{10,11... | collective-permute-start | bytes 393224 | tf_op jit(solution)/shard_map/ppermute | solution.py:276
Sparse Core Ops, SparseCore 0:
  10.0 71.0 all-gather.1

commit v22 on v18

--- a/solution.py
+++ b/solution.py
@@ -188,7 +188,7 @@
     total = product(block, here)
     from_right, from_left = block, block
     for step in range(1, count // 2 + 1):
-        if step == 2 and wait_rows:
+        if step == 3 and wait_rows:
             rows, from_right, from_left = lax.optimization_barrier((rows, from_right, from_left))
         if step < count - step:
             from_right = lax.ppermute(from_right, axis, perm=moved(-1))

time: 195 us -> 205 us (1.051)
  waiting for transfers between devices: 47.2 us -> 54.8 us
    ppermute x6, waiting for transfers between devices: 18.1 us -> 30.3 us  [ring_matmul(): from_right = lax.ppermute(from_right, axis, perm=moved(-1))]
    ppermute x6, waiting for transfers between devices: 9.77 us -> 0.02 us  [ring_matmul(): from_left = lax.ppermute(from_left, axis, perm=moved(1))]
    ppermute x1, waiting for transfers between devices: 0.01 us -> 7.79 us  [ring_gather(): from_right = lax.ppermute(from_right, axis, perm=moved(-1))]
    ppermute x2, waiting for transfers between devices: 4.1 us -> 1.77 us  [ring_matmul(): lax.ppermute(from_left[..., :cut, :], axis, perm=moved(1))]
  transfers between devices with their start and end apart: 22 -> 22, of which waited for: 8 -> 9; matrix products, arithmetic and copies ran while one was open for 16% -> 15% of each run, Pallas kernels for 0% -> 0%
where the time goes in v22:
time: 205 us; the launch traced here: 203 us
  starting transfers between devices  87.7 us (43%)
  waiting for transfers between devices  54.8 us (27%)
  matrix products  25 us (12%)
  between operations  15.1 us (7%)
  other arithmetic  8.3 us (4%)
  local copies, waits for them, and re-layouts  6.52 us (3%)
  Pallas kernels  5.95 us (3%)
    ppermute x6, starting transfers between devices, ring_matmul(): from_right = lax.ppermute(from_right, axis, perm=moved(-1))  36 us
    ppermute x6, waiting for transfers between devices, ring_matmul(): from_right = lax.ppermute(from_right, axis, perm=moved(-1))  30.3 us
    dot_general x32, matrix products, product(): term = jnp.dot(lhs, part[piece], preferred_element_type=jnp.float32)  25 us
    ppermute x1, waiting for transfers between devices, ring_gather(): lax.ppermute(from_left[..., :cut, :], axis, perm=moved(1))  12.3 us
    ppermute x6, starting transfers between devices, ring_matmul(): from_left = lax.ppermute(from_left, axis, perm=moved(1))  11.5 us
    ppermute x1, starting transfers between devices, per_device(): other_rows = lax.ppermute(own_rows, 'weight', perm=partner)  10.3 us
    ppermute x2, starting transfers between devices, ring_matmul(): lax.ppermute(from_right[..., cut:, :], axis, perm=moved(-1))  9.78 us
    ppermute x1, waiting for transfers between devices, ring_gather(): from_right = lax.ppermute(from_right, axis, perm=moved(-1))  7.79 us
  transfers between devices with their start and end apart: 22, of which 9 were waited for; matrix products, arithmetic and copies ran while one was open for 15% of the time, Pallas kernels for 0%

profile of v22, /device:TPU:7, one launch (start us, length us, event | category | flops | bytes accessed | tf_op | source)
XLA Modules:
  0.0 203.3 jit_solution(3983626835461494261)
XLA Ops:
  6.5 1.3 fusion.18
  7.9 2.0 %fusion.20 = bf16[32,8192]{1,0:T(8,128)(2,1)} fusion(bf16[32,8192]{1,0:T(8,128)(2,1)} %param.6, f32[8192]{0:T(1024)} %param.8, f32[32]{0:T(128)S(1)} %add_rsqrt_fusion), kind=kLoop, calls=%fused_computation.35 | loop fusion | flops 1048576 | bytes 1081472 | tf_op jit(solution)/shard_map/convert_element_type | solution.py:224
  9.9 0.9 dynamic-slice_select_fusion
  11.6 5.9 %collective-permute-start.8 = (bf16[256,640]{1,0:T(8,128)(2,1)S(1)}, bf16[256,640]{1,0:T(8,128)(2,1)S(1)}, u32[]{:S(2)}, u32[]{:S(2)}) collective-permute-start(bf16[256,640]{1,0:T(8,128)(2,1)S(1)} %get-tuple-element.25), channel_id=1, source_target_pairs={{0,48},{16,0},{32,16},{48,32},{64,112},{80,64},{96,80},{112,96},{1... | collective-permute-start | bytes 983048 | tf_op jit(solution)/shard_map/ppermute | solution.py:151
  17.5 1.9 collective-permute-start.9
  21.5 1.8 multiply_sine_fusion
  23.3 7.8 %collective-permute-done.8 = bf16[256,640]{1,0:T(8,128)(2,1)S(1)} collective-permute-done((bf16[256,640]{1,0:T(8,128)(2,1)S(1)}, bf16[256,640]{1,0:T(8,128)(2,1)S(1)}, u32[]{:S(2)}, u32[]{:S(2)}) %collective-permute-start.8) | collective-permute-done | bytes 327712 | tf_op jit(solution)/shard_map/ppermute | solution.py:151
  31.1 6.5 %collective-permute-start.11 = (bf16[128,640]{1,0:T(8,128)(2,1)S(1)}, bf16[128,640]{1,0:T(8,128)(2,1)S(1)}, u32[]{:S(2)}, u32[]{:S(2)}) collective-permute-start(bf16[128,640]{1,0:T(8,128)(2,1)S(1)} %slice.145), channel_id=1, source_target_pairs={{0,48},{16,0},{32,16},{48,32},{64,112},{80,64},{96,80},{112,96},{1... | collective-permute-start | bytes 491528 | tf_op jit(solution)/shard_map/ppermute | solution.py:159
  37.7 1.9 collective-permute-start.10
  39.8 0.9 collective-permute-done.11
  40.7 12.3 %collective-permute-done.10 = bf16[128,640]{1,0:T(8,128)(2,1)S(1)} collective-permute-done((bf16[128,640]{1,0:T(8,128)(2,1)S(1)}, bf16[128,640]{1,0:T(8,128)(2,1)S(1)}, u32[]{:S(2)}, u32[]{:S(2)}) %collective-permute-start.10) | collective-permute-done | bytes 163872 | tf_op jit(solution)/shard_map/ppermute | solution.py:158
  53.3 11.1 %collective-permute-start.12 = (bf16[3,256,640]{2,1,0:T(8,128)(2,1)S(1)}, bf16[3,256,640]{2,1,0:T(8,128)(2,1)}, u32[]{:S(2)}, u32[]{:S(2)}) collective-permute-start(bf16[3,256,640]{2,1,0:T(8,128)(2,1)S(1)} %pad_maximum_fusion), channel_id=1, source_target_pairs={{0,448},{16,464},{32,480},{48,496},{64,0},{80,16},{96,32},{112,48}... | collective-permute-start | bytes 2949128 | tf_op jit(solution)/shard_map/ppermute | solution.py:194
  64.4 1.9 collective-permute-start.13
  66.3 4.6 %collective-permute-start = (bf16[1,256,640]{2,1,0:T(8,128)(2,1)}, bf16[1,256,640]{2,1,0:T(8,128)(2,1)S(1)}, u32[]{:S(2)}, u32[]{:S(2)}) collective-permute-start(bf16[1,256,640]{2,1,0:T(8,128)(2,1)} %get-tuple-element.24), channel_id=1, source_target_pairs={{0,448},{16,464},{32,480},{48,496},{64,0},{80,16},{96,32},{112,48}... | collective-permute-start | bytes 983048 | tf_op jit(solution)/shard_map/ppermute | solution.py:194
  70.9 1.9 collective-permute-start.1
  72.8 8.3 %collective-permute-done.12 = bf16[3,256,640]{2,1,0:T(8,128)(2,1)} collective-permute-done((bf16[3,256,640]{2,1,0:T(8,128)(2,1)S(1)}, bf16[3,256,640]{2,1,0:T(8,128)(2,1)}, u32[]{:S(2)}, u32[]{:S(2)}) %collective-permute-start.12) | collective-permute-done | bytes 983072 | tf_op jit(solution)/shard_map/ppermute | solution.py:194
  81.1 5.4 %collective-permute-start.14 = (bf16[3,256,640]{2,1,0:T(8,128)(2,1)}, bf16[3,256,640]{2,1,0:T(8,128)(2,1)S(1)}, u32[]{:S(2)}, u32[]{:S(2)}) collective-permute-start(bf16[3,256,640]{2,1,0:T(8,128)(2,1)} %collective-permute-done.12), channel_id=1, source_target_pairs={{0,448},{16,464},{32,480},{48,496},{64,0},{80,16},{96,32},{112,48}... | collective-permute-start | bytes 2949128 | tf_op jit(solution)/shard_map/ppermute | solution.py:194
  86.6 1.9 collective-permute-start.15
  89.2 5.1 %collective-permute-start.2 = (bf16[1,256,640]{2,1,0:T(8,128)(2,1)S(1)}, bf16[1,256,640]{2,1,0:T(8,128)(2,1)}, u32[]{:S(2)}, u32[]{:S(2)}) collective-permute-start(bf16[1,256,640]{2,1,0:T(8,128)(2,1)S(1)} %collective-permute-done), channel_id=1, source_target_pairs={{0,448},{16,464},{32,480},{48,496},{64,0},{80,16},{96,32},{112,48}... | collective-permute-start | bytes 983048 | tf_op jit(solution)/shard_map/ppermute | solution.py:194
  94.3 1.9 collective-permute-start.3
  96.3 20.0 %collective-permute-done.2 = bf16[1,256,640]{2,1,0:T(8,128)(2,1)} collective-permute-done((bf16[1,256,640]{2,1,0:T(8,128)(2,1)S(1)}, bf16[1,256,640]{2,1,0:T(8,128)(2,1)}, u32[]{:S(2)}, u32[]{:S(2)}) %collective-permute-start.2) | collective-permute-done | bytes 327712 | tf_op jit(solution)/shard_map/ppermute | solution.py:194
  116.2 5.3 %collective-permute-start.4 = (bf16[1,256,640]{2,1,0:T(8,128)(2,1)}, bf16[1,256,640]{2,1,0:T(8,128)(2,1)}, u32[]{:S(2)}, u32[]{:S(2)}) collective-permute-start(bf16[1,256,640]{2,1,0:T(8,128)(2,1)} %collective-permute-done.2), channel_id=1, source_target_pairs={{0,448},{16,464},{32,480},{48,496},{64,0},{80,16},{96,32},{112,48}... | collective-permute-start | bytes 983048 | tf_op jit(solution)/shard_map/ppermute | solution.py:194
  121.6 1.9 collective-permute-start.5
  123.9 2.0 collective-permute-done.4
  125.9 0.9 slice.143
  126.8 5.0 %collective-permute-start.7 = (bf16[1,128,640]{2,1,0:T(8,128)(2,1)S(1)}, bf16[1,128,640]{2,1,0:T(8,128)(2,1)}, u32[]{:S(2)}, u32[]{:S(2)}) collective-permute-start(bf16[1,128,640]{2,1,0:T(8,128)(2,1)S(1)} %slice.143), channel_id=1, source_target_pairs={{0,448},{16,464},{32,480},{48,496},{64,0},{80,16},{96,32},{112,48}... | collective-permute-start | bytes 491528 | tf_op jit(solution)/shard_map/ppermute | solution.py:202
  131.9 1.6 slice.142
  133.4 1.9 collective-permute-start.6
  135.4 1.9 collective-permute-start.17
  137.3 4.6 %collective-permute-start.16 = (bf16[3,256,640]{2,1,0:T(8,128)(2,1)S(1)}, bf16[3,256,640]{2,1,0:T(8,128)(2,1)S(1)}, u32[]{:S(2)}, u32[]{:S(2)}) collective-permute-start(bf16[3,256,640]{2,1,0:T(8,128)(2,1)S(1)} %collective-permute-done.14), channel_id=1, source_target_pairs={{0,448},{16,464},{32,480},{48,496},{64,0},{80,16},{96,32},{112,48}... | collective-permute-start | bytes 2949128 | tf_op jit(solution)/shard_map/ppermute | solution.py:194
  141.9 1.6 fusion.27
  143.5 1.8 fusion.28
  145.3 1.3 fusion.41
  146.6 1.4 fusion.33
  148.1 1.4 fusion.34
  154.1 1.4 fusion.5
  155.5 1.4 fusion.46
  156.8 1.4 fusion.35
  158.2 1.4 fusion
  159.6 1.4 fusion.43
  160.9 1.4 fusion.15
  162.8 1.9 collective-permute-start.18
  164.8 4.8 %collective-permute-start.19 = (bf16[3,128,640]{2,1,0:T(8,128)(2,1)S(1)}, bf16[3,128,640]{2,1,0:T(8,128)(2,1)S(1)}, u32[]{:S(2)}, u32[]{:S(2)}) collective-permute-start(bf16[3,128,640]{2,1,0:T(8,128)(2,1)S(1)} %slice.165), channel_id=1, source_target_pairs={{0,448},{16,464},{32,480},{48,496},{64,0},{80,16},{96,32},{112,48}... | collective-permute-start | bytes 1474568 | tf_op jit(solution)/shard_map/ppermute | solution.py:202
  171.9 1.8 collective-permute-done.18
  173.7 1.5 collective-permute-done.19
  177.0 1.4 fusion.17.q_ref
  178.5 10.3 %collective-permute-start.20 = (bf16[512,128]{1,0:T(8,128)(2,1)S(1)}, bf16[512,128]{1,0:T(8,128)(2,1)S(1)}, u32[]{:S(2)}, u32[]{:S(2)}) collective-permute-start(bf16[512,128]{1,0:T(8,128)(2,1)S(1)} %slice.226), channel_id=1, source_target_pairs={{0,1},{1,0},{2,3},{3,2},{4,5},{5,4},{6,7},{7,6},{8,9},{9,8},{10,11... | collective-permute-start | bytes 393224 | tf_op jit(solution)/shard_map/ppermute | solution.py:260
  190.5 6.0 %shard_map.64 = bf16[512,512]{1,0:T(8,128)(2,1)} custom-call(f32[512,640]{1,0:T(8,128)} %copy-done.1, bf16[512,128]{1,0:T(8,128)(2,1)} %get-tuple-element.27.k_ref, bf16[512,128]{1,0:T(8,128)(2,1)} %get-tuple-element.26.v_ref, f32[512,64]{1,0:T(8,128)} %get-tuple-element.17.cos_ref, f32[512,64]{1,0:T(8,128)} %get-tuple-element.18.sin_ref, ...), custom_call_target="tpu_custom_call" | custom-call | flops 538968064 | bytes 2097152 | tf_op jit(solution)/shard_map/pallas_call | solution.py:113
  (78 shorter events, 14.3 us)
Async XLA Ops:
  6.5 4.3 %copy-start.2 = (bf16[256,512]{1,0:T(8,128)(2,1)S(1)}, bf16[256,512]{1,0:T(8,128)(2,1)}, u32[]{:S(2)}) copy-start(bf16[256,512]{1,0:T(8,128)(2,1)} %param.9) | copy-start | bytes 786436
  6.5 128.9 %all-gather.2.cloned.1.call-start = ((), (), s32[]{:S(2)}) async-start(), calls=%async_computation | async-start | bytes 8912896 | tf_op jit(solution)/shard_map/all_gather | solution.py:237
  7.8 11.7 %copy-start.7 = (s32[512]{0:T(512)S(1)}, s32[512]{0:T(512)}, u32[]{:S(2)}) copy-start(s32[512]{0:T(512)} %param.7) | copy-start | bytes 6148
  11.6 19.5 %collective-permute-start.8 = (bf16[256,640]{1,0:T(8,128)(2,1)S(1)}, bf16[256,640]{1,0:T(8,128)(2,1)S(1)}, u32[]{:S(2)}, u32[]{:S(2)}) collective-permute-start(bf16[256,640]{1,0:T(8,128)(2,1)S(1)} %get-tuple-element.25), channel_id=1, source_target_pairs={{0,48},{16,0},{32,16},{48,32},{64,112},{80,64},{96,80},{112,96},{1... | collective-permute-start | bytes 983048 | tf_op jit(solution)/shard_map/ppermute | solution.py:151
  17.5 20.2 %collective-permute-start.9 = (bf16[256,640]{1,0:T(8,128)(2,1)S(1)}, bf16[256,640]{1,0:T(8,128)(2,1)S(1)}, u32[]{:S(2)}, u32[]{:S(2)}) collective-permute-start(bf16[256,640]{1,0:T(8,128)(2,1)S(1)} %get-tuple-element.25), channel_id=1, source_target_pairs={{0,16},{16,32},{32,48},{48,0},{64,80},{80,96},{96,112},{112,64},{1... | collective-permute-start | bytes 983048 | tf_op jit(solution)/shard_map/ppermute | solution.py:153
  31.1 9.6 %collective-permute-start.11 = (bf16[128,640]{1,0:T(8,128)(2,1)S(1)}, bf16[128,640]{1,0:T(8,128)(2,1)S(1)}, u32[]{:S(2)}, u32[]{:S(2)}) collective-permute-start(bf16[128,640]{1,0:T(8,128)(2,1)S(1)} %slice.145), channel_id=1, source_target_pairs={{0,48},{16,0},{32,16},{48,32},{64,112},{80,64},{96,80},{112,96},{1... | collective-permute-start | bytes 491528 | tf_op jit(solution)/shard_map/ppermute | solution.py:159
  37.7 15.3 %collective-permute-start.10 = (bf16[128,640]{1,0:T(8,128)(2,1)S(1)}, bf16[128,640]{1,0:T(8,128)(2,1)S(1)}, u32[]{:S(2)}, u32[]{:S(2)}) collective-permute-start(bf16[128,640]{1,0:T(8,128)(2,1)S(1)} %slice.144), channel_id=1, source_target_pairs={{0,16},{16,32},{32,48},{48,0},{64,80},{80,96},{96,112},{112,64},{1... | collective-permute-start | bytes 491528 | tf_op jit(solution)/shard_map/ppermute | solution.py:158
  53.3 27.8 %collective-permute-start.12 = (bf16[3,256,640]{2,1,0:T(8,128)(2,1)S(1)}, bf16[3,256,640]{2,1,0:T(8,128)(2,1)}, u32[]{:S(2)}, u32[]{:S(2)}) collective-permute-start(bf16[3,256,640]{2,1,0:T(8,128)(2,1)S(1)} %pad_maximum_fusion), channel_id=1, source_target_pairs={{0,448},{16,464},{32,480},{48,496},{64,0},{80,16},{96,32},{112,48}... | collective-permute-start | bytes 2949128 | tf_op jit(solution)/shard_map/ppermute | solution.py:194
  64.4 22.2 %collective-permute-start.13 = (bf16[3,256,640]{2,1,0:T(8,128)(2,1)S(1)}, bf16[3,256,640]{2,1,0:T(8,128)(2,1)S(1)}, u32[]{:S(2)}, u32[]{:S(2)}) collective-permute-start(bf16[3,256,640]{2,1,0:T(8,128)(2,1)S(1)} %pad_maximum_fusion), channel_id=1, source_target_pairs={{0,64},{16,80},{32,96},{48,112},{64,128},{80,144},{96,160},{112,17... | collective-permute-start | bytes 2949128 | tf_op jit(solution)/shard_map/ppermute | solution.py:196
  66.3 22.2 %collective-permute-start = (bf16[1,256,640]{2,1,0:T(8,128)(2,1)}, bf16[1,256,640]{2,1,0:T(8,128)(2,1)S(1)}, u32[]{:S(2)}, u32[]{:S(2)}) collective-permute-start(bf16[1,256,640]{2,1,0:T(8,128)(2,1)} %get-tuple-element.24), channel_id=1, source_target_pairs={{0,448},{16,464},{32,480},{48,496},{64,0},{80,16},{96,32},{112,48}... | collective-permute-start | bytes 983048 | tf_op jit(solution)/shard_map/ppermute | solution.py:194
  70.9 23.4 %collective-permute-start.1 = (bf16[1,256,640]{2,1,0:T(8,128)(2,1)}, bf16[1,256,640]{2,1,0:T(8,128)(2,1)S(1)}, u32[]{:S(2)}, u32[]{:S(2)}) collective-permute-start(bf16[1,256,640]{2,1,0:T(8,128)(2,1)} %get-tuple-element.24), channel_id=1, source_target_pairs={{0,64},{16,80},{32,96},{48,112},{64,128},{80,144},{96,160},{112,17... | collective-permute-start | bytes 983048 | tf_op jit(solution)/shard_map/ppermute | solution.py:196
  81.1 54.2 %collective-permute-start.14 = (bf16[3,256,640]{2,1,0:T(8,128)(2,1)}, bf16[3,256,640]{2,1,0:T(8,128)(2,1)S(1)}, u32[]{:S(2)}, u32[]{:S(2)}) collective-permute-start(bf16[3,256,640]{2,1,0:T(8,128)(2,1)} %collective-permute-done.12), channel_id=1, source_target_pairs={{0,448},{16,464},{32,480},{48,496},{64,0},{80,16},{96,32},{112,48}... | collective-permute-start | bytes 2949128 | tf_op jit(solution)/shard_map/ppermute | solution.py:194
  86.6 48.8 %collective-permute-start.15 = (bf16[3,256,640]{2,1,0:T(8,128)(2,1)S(1)}, bf16[3,256,640]{2,1,0:T(8,128)(2,1)}, u32[]{:S(2)}, u32[]{:S(2)}) collective-permute-start(bf16[3,256,640]{2,1,0:T(8,128)(2,1)S(1)} %collective-permute-done.13), channel_id=1, source_target_pairs={{0,64},{16,80},{32,96},{48,112},{64,128},{80,144},{96,160},{112,17... | collective-permute-start | bytes 2949128 | tf_op jit(solution)/shard_map/ppermute | solution.py:196
  88.5 0.7 copy-start.3
  89.2 27.0 %collective-permute-start.2 = (bf16[1,256,640]{2,1,0:T(8,128)(2,1)S(1)}, bf16[1,256,640]{2,1,0:T(8,128)(2,1)}, u32[]{:S(2)}, u32[]{:S(2)}) collective-permute-start(bf16[1,256,640]{2,1,0:T(8,128)(2,1)S(1)} %collective-permute-done), channel_id=1, source_target_pairs={{0,448},{16,464},{32,480},{48,496},{64,0},{80,16},{96,32},{112,48}... | collective-permute-start | bytes 983048 | tf_op jit(solution)/shard_map/ppermute | solution.py:194
  94.3 21.9 %copy-start.5 = (bf16[1,256,640]{2,1,0:T(8,128)(2,1)}, bf16[1,256,640]{2,1,0:T(8,128)(2,1)S(1)}, u32[]{:S(2)}) copy-start(bf16[1,256,640]{2,1,0:T(8,128)(2,1)S(1)} %collective-permute-done.1) | copy-start | bytes 983044
  94.3 27.2 %collective-permute-start.3 = (bf16[1,256,640]{2,1,0:T(8,128)(2,1)S(1)}, bf16[1,256,640]{2,1,0:T(8,128)(2,1)}, u32[]{:S(2)}, u32[]{:S(2)}) collective-permute-start(bf16[1,256,640]{2,1,0:T(8,128)(2,1)S(1)} %collective-permute-done.1), channel_id=1, source_target_pairs={{0,64},{16,80},{32,96},{48,112},{64,128},{80,144},{96,160},{112,17... | collective-permute-start | bytes 983048 | tf_op jit(solution)/shard_map/ppermute | solution.py:196
  116.2 9.6 %collective-permute-start.4 = (bf16[1,256,640]{2,1,0:T(8,128)(2,1)}, bf16[1,256,640]{2,1,0:T(8,128)(2,1)}, u32[]{:S(2)}, u32[]{:S(2)}) collective-permute-start(bf16[1,256,640]{2,1,0:T(8,128)(2,1)} %collective-permute-done.2), channel_id=1, source_target_pairs={{0,448},{16,464},{32,480},{48,496},{64,0},{80,16},{96,32},{112,48}... | collective-permute-start | bytes 983048 | tf_op jit(solution)/shard_map/ppermute | solution.py:194
  121.6 10.3 %collective-permute-start.5 = (bf16[1,256,640]{2,1,0:T(8,128)(2,1)}, bf16[1,256,640]{2,1,0:T(8,128)(2,1)}, u32[]{:S(2)}, u32[]{:S(2)}) collective-permute-start(bf16[1,256,640]{2,1,0:T(8,128)(2,1)} %collective-permute-done.3), channel_id=1, source_target_pairs={{0,64},{16,80},{32,96},{48,112},{64,128},{80,144},{96,160},{112,17... | collective-permute-start | bytes 983048 | tf_op jit(solution)/shard_map/ppermute | solution.py:196
  126.8 30.0 %collective-permute-start.7 = (bf16[1,128,640]{2,1,0:T(8,128)(2,1)S(1)}, bf16[1,128,640]{2,1,0:T(8,128)(2,1)}, u32[]{:S(2)}, u32[]{:S(2)}) collective-permute-start(bf16[1,128,640]{2,1,0:T(8,128)(2,1)S(1)} %slice.143), channel_id=1, source_target_pairs={{0,448},{16,464},{32,480},{48,496},{64,0},{80,16},{96,32},{112,48}... | collective-permute-start | bytes 491528 | tf_op jit(solution)/shard_map/ppermute | solution.py:202
  133.4 23.4 %collective-permute-start.6 = (bf16[1,128,640]{2,1,0:T(8,128)(2,1)}, bf16[1,128,640]{2,1,0:T(8,128)(2,1)}, u32[]{:S(2)}, u32[]{:S(2)}) collective-permute-start(bf16[1,128,640]{2,1,0:T(8,128)(2,1)} %slice.142), channel_id=1, source_target_pairs={{0,64},{16,80},{32,96},{48,112},{64,128},{80,144},{96,160},{112,17... | collective-permute-start | bytes 491528 | tf_op jit(solution)/shard_map/ppermute | solution.py:201
  135.4 27.4 %collective-permute-start.17 = (bf16[3,256,640]{2,1,0:T(8,128)(2,1)}, bf16[3,256,640]{2,1,0:T(8,128)(2,1)S(1)}, u32[]{:S(2)}, u32[]{:S(2)}) collective-permute-start(bf16[3,256,640]{2,1,0:T(8,128)(2,1)} %collective-permute-done.15), channel_id=1, source_target_pairs={{0,64},{16,80},{32,96},{48,112},{64,128},{80,144},{96,160},{112,17... | collective-permute-start | bytes 2949128 | tf_op jit(solution)/shard_map/ppermute | solution.py:196
  137.3 27.4 %collective-permute-start.16 = (bf16[3,256,640]{2,1,0:T(8,128)(2,1)S(1)}, bf16[3,256,640]{2,1,0:T(8,128)(2,1)S(1)}, u32[]{:S(2)}, u32[]{:S(2)}) collective-permute-start(bf16[3,256,640]{2,1,0:T(8,128)(2,1)S(1)} %collective-permute-done.14), channel_id=1, source_target_pairs={{0,448},{16,464},{32,480},{48,496},{64,0},{80,16},{96,32},{112,48}... | collective-permute-start | bytes 2949128 | tf_op jit(solution)/shard_map/ppermute | solution.py:194
  141.9 7.6 %copy-start = (bf16[512,8192]{1,0:T(8,128)(2,1)S(1)}, bf16[512,8192]{1,0:T(8,128)(2,1)}, u32[]{:S(2)}) copy-start(bf16[512,8192]{1,0:T(8,128)(2,1)} %all-gather.2.cloned.1.call-done) | copy-start | bytes 25165828
  151.8 1.0 copy-start.4
  152.7 1.0 copy-start.6
  162.8 10.8 %collective-permute-start.18 = (bf16[3,128,640]{2,1,0:T(8,128)(2,1)S(1)}, bf16[3,128,640]{2,1,0:T(8,128)(2,1)S(1)}, u32[]{:S(2)}, u32[]{:S(2)}) collective-permute-start(bf16[3,128,640]{2,1,0:T(8,128)(2,1)S(1)} %slice.164), channel_id=1, source_target_pairs={{0,64},{16,80},{32,96},{48,112},{64,128},{80,144},{96,160},{112,17... | collective-permute-start | bytes 1474568 | tf_op jit(solution)/shard_map/ppermute | solution.py:201
  164.8 10.3 %collective-permute-start.19 = (bf16[3,128,640]{2,1,0:T(8,128)(2,1)S(1)}, bf16[3,128,640]{2,1,0:T(8,128)(2,1)S(1)}, u32[]{:S(2)}, u32[]{:S(2)}) collective-permute-start(bf16[3,128,640]{2,1,0:T(8,128)(2,1)S(1)} %slice.165), channel_id=1, source_target_pairs={{0,448},{16,464},{32,480},{48,496},{64,0},{80,16},{96,32},{112,48}... | collective-permute-start | bytes 1474568 | tf_op jit(solution)/shard_map/ppermute | solution.py:202
  178.4 12.1 %copy-start.1 = (f32[512,640]{1,0:T(8,128)}, f32[512,640]{1,0:T(8,128)S(1)}, u32[]{:S(2)}) copy-start(f32[512,640]{1,0:T(8,128)S(1)} %fusion.17.q_ref) | copy-start | bytes 3932164
  178.5 11.3 %collective-permute-start.20 = (bf16[512,128]{1,0:T(8,128)(2,1)S(1)}, bf16[512,128]{1,0:T(8,128)(2,1)S(1)}, u32[]{:S(2)}, u32[]{:S(2)}) collective-permute-start(bf16[512,128]{1,0:T(8,128)(2,1)S(1)} %slice.226), channel_id=1, source_target_pairs={{0,1},{1,0},{2,3},{3,2},{4,5},{5,4},{6,7},{7,6},{8,9},{9,8},{10,11... | collective-permute-start | bytes 393224 | tf_op jit(solution)/shard_map/ppermute | solution.py:260
Sparse Core Ops, SparseCore 0:
  10.0 71.7 all-gather.1

commit v23 on v18

--- a/solution.py
+++ b/solution.py
@@ -116,8 +116,8 @@
         in_specs=[vmem] * 7,
         out_specs=vmem,
         cost_estimate=pl.CostEstimate(
-            flops=4 * rows * rows * cols + 8 * rows * cols,
-            transcendentals=heads * rows * rows,
+            flops=4 * rows * 2 * ROW_TILE * cols + 8 * rows * cols,
+            transcendentals=heads * rows * 2 * ROW_TILE,
             bytes_accessed=rows * cols * 6 + rows * HEAD_DIM * 4 + rows * half_dim * 8,
         ),
     )(

time: 195 us -> 195 us (level)
  no operation moved by 1% of the time
where the time goes in v23:
time: 195 us; the launch traced here: 193 us
  starting transfers between devices  87.2 us (45%)
  waiting for transfers between devices  47.2 us (24%)
  matrix products  24.4 us (13%)
  between operations  15.2 us (8%)
  other arithmetic  8.29 us (4%)
  Pallas kernels  5.95 us (3%)
  local copies, waits for them, and re-layouts  4.69 us (2%)
    ppermute x6, starting transfers between devices, ring_matmul(): from_right = lax.ppermute(from_right, axis, perm=moved(-1))  35.6 us
    dot_general x32, matrix products, product(): term = jnp.dot(lhs, part[piece], preferred_element_type=jnp.float32)  24.4 us
    ppermute x6, waiting for transfers between devices, ring_matmul(): from_right = lax.ppermute(from_right, axis, perm=moved(-1))  18.1 us
    ppermute x1, waiting for transfers between devices, ring_gather(): lax.ppermute(from_left[..., :cut, :], axis, perm=moved(1))  12.5 us
    ppermute x6, starting transfers between devices, ring_matmul(): from_left = lax.ppermute(from_left, axis, perm=moved(1))  11.5 us
    ppermute x1, starting transfers between devices, per_device(): other_rows = lax.ppermute(own_rows, 'weight', perm=partner)  11.2 us
    ppermute x2, starting transfers between devices, ring_matmul(): lax.ppermute(from_right[..., cut:, :], axis, perm=moved(-1))  9.78 us
    ppermute x6, waiting for transfers between devices, ring_matmul(): from_left = lax.ppermute(from_left, axis, perm=moved(1))  9.77 us
  transfers between devices with their start and end apart: 22, of which 8 were waited for; matrix products, arithmetic and copies ran while one was open for 16% of the time, Pallas kernels for 0%

profile of v23, /device:TPU:7, one launch (start us, length us, event | category | flops | bytes accessed | tf_op | source)
XLA Modules:
  0.0 192.9 jit_solution(16676435241814006337)
XLA Ops:
  6.5 1.3 fusion.18
  7.9 2.0 %fusion.20 = bf16[32,8192]{1,0:T(8,128)(2,1)} fusion(bf16[32,8192]{1,0:T(8,128)(2,1)} %param.6, f32[8192]{0:T(1024)} %param.8, f32[32]{0:T(128)S(1)} %add_rsqrt_fusion), kind=kLoop, calls=%fused_computation.35 | loop fusion | flops 1048576 | bytes 1081472 | tf_op jit(solution)/shard_map/convert_element_type | solution.py:224
  9.9 0.9 dynamic-slice_select_fusion
  11.6 5.9 %collective-permute-start.8 = (bf16[256,640]{1,0:T(8,128)(2,1)S(1)}, bf16[256,640]{1,0:T(8,128)(2,1)S(1)}, u32[]{:S(2)}, u32[]{:S(2)}) collective-permute-start(bf16[256,640]{1,0:T(8,128)(2,1)S(1)} %get-tuple-element.25), channel_id=1, source_target_pairs={{0,48},{16,0},{32,16},{48,32},{64,112},{80,64},{96,80},{112,96},{1... | collective-permute-start | bytes 983048 | tf_op jit(solution)/shard_map/ppermute | solution.py:151
  17.5 1.9 collective-permute-start.9
  19.4 10.7 %collective-permute-start = (bf16[1,256,640]{2,1,0:T(8,128)(2,1)}, bf16[1,256,640]{2,1,0:T(8,128)(2,1)}, u32[]{:S(2)}, u32[]{:S(2)}) collective-permute-start(bf16[1,256,640]{2,1,0:T(8,128)(2,1)} %get-tuple-element.24), channel_id=1, source_target_pairs={{0,448},{16,464},{32,480},{48,496},{64,0},{80,16},{96,32},{112,48}... | collective-permute-start | bytes 983048 | tf_op jit(solution)/shard_map/ppermute | solution.py:194
  30.1 1.9 collective-permute-start.1
  34.3 1.8 multiply_sine_fusion
  36.1 5.5 %collective-permute-start.11 = (bf16[128,640]{1,0:T(8,128)(2,1)S(1)}, bf16[128,640]{1,0:T(8,128)(2,1)S(1)}, u32[]{:S(2)}, u32[]{:S(2)}) collective-permute-start(bf16[128,640]{1,0:T(8,128)(2,1)S(1)} %slice.145), channel_id=1, source_target_pairs={{0,48},{16,0},{32,16},{48,32},{64,112},{80,64},{96,80},{112,96},{1... | collective-permute-start | bytes 491528 | tf_op jit(solution)/shard_map/ppermute | solution.py:159
  41.7 1.9 collective-permute-start.10
  43.7 1.1 collective-permute-done.11
  44.8 12.5 %collective-permute-done.10 = bf16[128,640]{1,0:T(8,128)(2,1)S(1)} collective-permute-done((bf16[128,640]{1,0:T(8,128)(2,1)S(1)}, bf16[128,640]{1,0:T(8,128)(2,1)S(1)}, u32[]{:S(2)}, u32[]{:S(2)}) %collective-permute-start.10) | collective-permute-done | bytes 163872 | tf_op jit(solution)/shard_map/ppermute | solution.py:158
  57.6 6.7 %collective-permute-start.12 = (bf16[3,256,640]{2,1,0:T(8,128)(2,1)S(1)}, bf16[3,256,640]{2,1,0:T(8,128)(2,1)S(1)}, u32[]{:S(2)}, u32[]{:S(2)}) collective-permute-start(bf16[3,256,640]{2,1,0:T(8,128)(2,1)S(1)} %pad_maximum_fusion), channel_id=1, source_target_pairs={{0,448},{16,464},{32,480},{48,496},{64,0},{80,16},{96,32},{112,48}... | collective-permute-start | bytes 2949128 | tf_op jit(solution)/shard_map/ppermute | solution.py:194
  64.4 1.9 collective-permute-start.13
  66.3 4.6 %collective-permute-start.2 = (bf16[1,256,640]{2,1,0:T(8,128)(2,1)}, bf16[1,256,640]{2,1,0:T(8,128)(2,1)}, u32[]{:S(2)}, u32[]{:S(2)}) collective-permute-start(bf16[1,256,640]{2,1,0:T(8,128)(2,1)} %collective-permute-done), channel_id=1, source_target_pairs={{0,448},{16,464},{32,480},{48,496},{64,0},{80,16},{96,32},{112,48}... | collective-permute-start | bytes 983048 | tf_op jit(solution)/shard_map/ppermute | solution.py:194
  70.9 1.9 collective-permute-start.3
  72.8 16.1 %collective-permute-done.2 = bf16[1,256,640]{2,1,0:T(8,128)(2,1)} collective-permute-done((bf16[1,256,640]{2,1,0:T(8,128)(2,1)}, bf16[1,256,640]{2,1,0:T(8,128)(2,1)}, u32[]{:S(2)}, u32[]{:S(2)}) %collective-permute-start.2) | collective-permute-done | bytes 327712 | tf_op jit(solution)/shard_map/ppermute | solution.py:194
  89.0 4.5 %collective-permute-start.4 = (bf16[1,256,640]{2,1,0:T(8,128)(2,1)}, bf16[1,256,640]{2,1,0:T(8,128)(2,1)}, u32[]{:S(2)}, u32[]{:S(2)}) collective-permute-start(bf16[1,256,640]{2,1,0:T(8,128)(2,1)} %collective-permute-done.2), channel_id=1, source_target_pairs={{0,448},{16,464},{32,480},{48,496},{64,0},{80,16},{96,32},{112,48}... | collective-permute-start | bytes 983048 | tf_op jit(solution)/shard_map/ppermute | solution.py:194
  93.5 1.9 collective-permute-start.5
  95.8 2.0 %collective-permute-done.4 = bf16[1,256,640]{2,1,0:T(8,128)(2,1)} collective-permute-done((bf16[1,256,640]{2,1,0:T(8,128)(2,1)}, bf16[1,256,640]{2,1,0:T(8,128)(2,1)}, u32[]{:S(2)}, u32[]{:S(2)}) %collective-permute-start.4) | collective-permute-done | bytes 327712 | tf_op jit(solution)/shard_map/ppermute | solution.py:194
  97.8 0.9 slice.143
  98.7 5.0 %collective-permute-start.7 = (bf16[1,128,640]{2,1,0:T(8,128)(2,1)S(1)}, bf16[1,128,640]{2,1,0:T(8,128)(2,1)}, u32[]{:S(2)}, u32[]{:S(2)}) collective-permute-start(bf16[1,128,640]{2,1,0:T(8,128)(2,1)S(1)} %slice.143), channel_id=1, source_target_pairs={{0,448},{16,464},{32,480},{48,496},{64,0},{80,16},{96,32},{112,48}... | collective-permute-start | bytes 491528 | tf_op jit(solution)/shard_map/ppermute | solution.py:202
  103.8 1.6 slice.142
  105.4 1.9 collective-permute-start.6
  107.3 1.9 collective-permute-start.15
  109.3 4.6 %collective-permute-start.14 = (bf16[3,256,640]{2,1,0:T(8,128)(2,1)S(1)}, bf16[3,256,640]{2,1,0:T(8,128)(2,1)S(1)}, u32[]{:S(2)}, u32[]{:S(2)}) collective-permute-start(bf16[3,256,640]{2,1,0:T(8,128)(2,1)S(1)} %collective-permute-done.12), channel_id=1, source_target_pairs={{0,448},{16,464},{32,480},{48,496},{64,0},{80,16},{96,32},{112,48}... | collective-permute-start | bytes 2949128 | tf_op jit(solution)/shard_map/ppermute | solution.py:194
  113.8 1.5 fusion.41
  115.3 1.7 fusion.33
  117.0 1.3 fusion.34
  118.3 1.3 fusion.31
  119.7 1.3 fusion.32
  121.0 1.4 fusion.43
  123.5 1.4 convolution_add_fusion.12
  124.9 1.4 fusion.46
  126.2 1.4 fusion.35
  127.6 1.4 convolution_add_fusion.11
  129.0 1.4 fusion
  130.7 1.9 collective-permute-start.17
  132.7 4.6 %collective-permute-start.16 = (bf16[3,256,640]{2,1,0:T(8,128)(2,1)S(1)}, bf16[3,256,640]{2,1,0:T(8,128)(2,1)S(1)}, u32[]{:S(2)}, u32[]{:S(2)}) collective-permute-start(bf16[3,256,640]{2,1,0:T(8,128)(2,1)S(1)} %collective-permute-done.14), channel_id=1, source_target_pairs={{0,448},{16,464},{32,480},{48,496},{64,0},{80,16},{96,32},{112,48}... | collective-permute-start | bytes 2949128 | tf_op jit(solution)/shard_map/ppermute | solution.py:194
  140.1 9.8 %collective-permute-done.17 = bf16[3,256,640]{2,1,0:T(8,128)(2,1)S(1)} collective-permute-done((bf16[3,256,640]{2,1,0:T(8,128)(2,1)S(1)}, bf16[3,256,640]{2,1,0:T(8,128)(2,1)S(1)}, u32[]{:S(2)}, u32[]{:S(2)}) %collective-permute-start.17) | collective-permute-done | bytes 983072 | tf_op jit(solution)/shard_map/ppermute | solution.py:196
  149.9 1.9 collective-permute-start.18
  151.9 4.8 %collective-permute-start.19 = (bf16[3,128,640]{2,1,0:T(8,128)(2,1)S(1)}, bf16[3,128,640]{2,1,0:T(8,128)(2,1)S(1)}, u32[]{:S(2)}, u32[]{:S(2)}) collective-permute-start(bf16[3,128,640]{2,1,0:T(8,128)(2,1)S(1)} %slice.165), channel_id=1, source_target_pairs={{0,448},{16,464},{32,480},{48,496},{64,0},{80,16},{96,32},{112,48}... | collective-permute-start | bytes 1474568 | tf_op jit(solution)/shard_map/ppermute | solution.py:202
  158.5 4.1 %collective-permute-done.18 = bf16[3,128,640]{2,1,0:T(8,128)(2,1)S(1)} collective-permute-done((bf16[3,128,640]{2,1,0:T(8,128)(2,1)S(1)}, bf16[3,128,640]{2,1,0:T(8,128)(2,1)S(1)}, u32[]{:S(2)}, u32[]{:S(2)}) %collective-permute-start.18) | collective-permute-done | bytes 491552 | tf_op jit(solution)/shard_map/ppermute | solution.py:201
  162.6 1.4 collective-permute-done.19
  165.8 1.4 fusion.17.q_ref
  167.2 11.2 %collective-permute-start.20 = (bf16[512,128]{1,0:T(8,128)(2,1)S(1)}, bf16[512,128]{1,0:T(8,128)(2,1)S(1)}, u32[]{:S(2)}, u32[]{:S(2)}) collective-permute-start(bf16[512,128]{1,0:T(8,128)(2,1)S(1)} %slice.226), channel_id=1, source_target_pairs={{0,1},{1,0},{2,3},{3,2},{4,5},{5,4},{6,7},{7,6},{8,9},{9,8},{10,11... | collective-permute-start | bytes 393224 | tf_op jit(solution)/shard_map/ppermute | solution.py:260
  178.4 0.9 copy.7.row_seg_ref
  180.1 6.0 %shard_map.64 = bf16[512,512]{1,0:T(8,128)(2,1)} custom-call(f32[512,640]{1,0:T(8,128)} %copy-done.1, bf16[512,128]{1,0:T(8,128)(2,1)} %get-tuple-element.27.k_ref, bf16[512,128]{1,0:T(8,128)(2,1)} %get-tuple-element.26.v_ref, f32[512,64]{1,0:T(8,128)} %get-tuple-element.17.cos_ref, f32[512,64]{1,0:T(8,128)} %get-tuple-element.18.sin_ref, ...), custom_call_target="tpu_custom_call" | custom-call | flops 270532608 | bytes 2097152 | tf_op jit(solution)/shard_map/pallas_call | solution.py:113
  (70 shorter events, 11.4 us)
Async XLA Ops:
  6.5 4.3 %copy-start.2 = (bf16[256,512]{1,0:T(8,128)(2,1)S(1)}, bf16[256,512]{1,0:T(8,128)(2,1)}, u32[]{:S(2)}) copy-start(bf16[256,512]{1,0:T(8,128)(2,1)} %param.9) | copy-start | bytes 786436
  6.5 100.8 %all-gather.2.cloned.1.call-start = ((), (), s32[]{:S(2)}) async-start(), calls=%async_computation | async-start | bytes 8912896 | tf_op jit(solution)/shard_map/all_gather | solution.py:237
  7.8 24.3 %copy-start.3 = (s32[512]{0:T(512)S(1)}, s32[512]{0:T(512)}, u32[]{:S(2)}) copy-start(s32[512]{0:T(512)} %param.7) | copy-start | bytes 6148
  11.6 24.5 %collective-permute-start.8 = (bf16[256,640]{1,0:T(8,128)(2,1)S(1)}, bf16[256,640]{1,0:T(8,128)(2,1)S(1)}, u32[]{:S(2)}, u32[]{:S(2)}) collective-permute-start(bf16[256,640]{1,0:T(8,128)(2,1)S(1)} %get-tuple-element.25), channel_id=1, source_target_pairs={{0,48},{16,0},{32,16},{48,32},{64,112},{80,64},{96,80},{112,96},{1... | collective-permute-start | bytes 983048 | tf_op jit(solution)/shard_map/ppermute | solution.py:151
  17.5 24.1 %collective-permute-start.9 = (bf16[256,640]{1,0:T(8,128)(2,1)S(1)}, bf16[256,640]{1,0:T(8,128)(2,1)S(1)}, u32[]{:S(2)}, u32[]{:S(2)}) collective-permute-start(bf16[256,640]{1,0:T(8,128)(2,1)S(1)} %get-tuple-element.25), channel_id=1, source_target_pairs={{0,16},{16,32},{32,48},{48,0},{64,80},{80,96},{96,112},{112,64},{1... | collective-permute-start | bytes 983048 | tf_op jit(solution)/shard_map/ppermute | solution.py:153
  19.4 46.9 %collective-permute-start = (bf16[1,256,640]{2,1,0:T(8,128)(2,1)}, bf16[1,256,640]{2,1,0:T(8,128)(2,1)}, u32[]{:S(2)}, u32[]{:S(2)}) collective-permute-start(bf16[1,256,640]{2,1,0:T(8,128)(2,1)} %get-tuple-element.24), channel_id=1, source_target_pairs={{0,448},{16,464},{32,480},{48,496},{64,0},{80,16},{96,32},{112,48}... | collective-permute-start | bytes 983048 | tf_op jit(solution)/shard_map/ppermute | solution.py:194
  30.1 40.8 %collective-permute-start.1 = (bf16[1,256,640]{2,1,0:T(8,128)(2,1)}, bf16[1,256,640]{2,1,0:T(8,128)(2,1)}, u32[]{:S(2)}, u32[]{:S(2)}) collective-permute-start(bf16[1,256,640]{2,1,0:T(8,128)(2,1)} %get-tuple-element.24), channel_id=1, source_target_pairs={{0,64},{16,80},{32,96},{48,112},{64,128},{80,144},{96,160},{112,17... | collective-permute-start | bytes 983048 | tf_op jit(solution)/shard_map/ppermute | solution.py:196
  36.1 8.7 %collective-permute-start.11 = (bf16[128,640]{1,0:T(8,128)(2,1)S(1)}, bf16[128,640]{1,0:T(8,128)(2,1)S(1)}, u32[]{:S(2)}, u32[]{:S(2)}) collective-permute-start(bf16[128,640]{1,0:T(8,128)(2,1)S(1)} %slice.145), channel_id=1, source_target_pairs={{0,48},{16,0},{32,16},{48,32},{64,112},{80,64},{96,80},{112,96},{1... | collective-permute-start | bytes 491528 | tf_op jit(solution)/shard_map/ppermute | solution.py:159
  41.7 15.7 %collective-permute-start.10 = (bf16[128,640]{1,0:T(8,128)(2,1)S(1)}, bf16[128,640]{1,0:T(8,128)(2,1)S(1)}, u32[]{:S(2)}, u32[]{:S(2)}) collective-permute-start(bf16[128,640]{1,0:T(8,128)(2,1)S(1)} %slice.144), channel_id=1, source_target_pairs={{0,16},{16,32},{32,48},{48,0},{64,80},{80,96},{96,112},{112,64},{1... | collective-permute-start | bytes 491528 | tf_op jit(solution)/shard_map/ppermute | solution.py:158
  57.6 49.6 %collective-permute-start.12 = (bf16[3,256,640]{2,1,0:T(8,128)(2,1)S(1)}, bf16[3,256,640]{2,1,0:T(8,128)(2,1)S(1)}, u32[]{:S(2)}, u32[]{:S(2)}) collective-permute-start(bf16[3,256,640]{2,1,0:T(8,128)(2,1)S(1)} %pad_maximum_fusion), channel_id=1, source_target_pairs={{0,448},{16,464},{32,480},{48,496},{64,0},{80,16},{96,32},{112,48}... | collective-permute-start | bytes 2949128 | tf_op jit(solution)/shard_map/ppermute | solution.py:194
  64.4 42.9 %collective-permute-start.13 = (bf16[3,256,640]{2,1,0:T(8,128)(2,1)S(1)}, bf16[3,256,640]{2,1,0:T(8,128)(2,1)S(1)}, u32[]{:S(2)}, u32[]{:S(2)}) collective-permute-start(bf16[3,256,640]{2,1,0:T(8,128)(2,1)S(1)} %pad_maximum_fusion), channel_id=1, source_target_pairs={{0,64},{16,80},{32,96},{48,112},{64,128},{80,144},{96,160},{112,17... | collective-permute-start | bytes 2949128 | tf_op jit(solution)/shard_map/ppermute | solution.py:196
  66.3 22.6 %collective-permute-start.2 = (bf16[1,256,640]{2,1,0:T(8,128)(2,1)}, bf16[1,256,640]{2,1,0:T(8,128)(2,1)}, u32[]{:S(2)}, u32[]{:S(2)}) collective-permute-start(bf16[1,256,640]{2,1,0:T(8,128)(2,1)} %collective-permute-done), channel_id=1, source_target_pairs={{0,448},{16,464},{32,480},{48,496},{64,0},{80,16},{96,32},{112,48}... | collective-permute-start | bytes 983048 | tf_op jit(solution)/shard_map/ppermute | solution.py:194
  70.9 22.6 %collective-permute-start.3 = (bf16[1,256,640]{2,1,0:T(8,128)(2,1)}, bf16[1,256,640]{2,1,0:T(8,128)(2,1)}, u32[]{:S(2)}, u32[]{:S(2)}) collective-permute-start(bf16[1,256,640]{2,1,0:T(8,128)(2,1)} %collective-permute-done.1), channel_id=1, source_target_pairs={{0,64},{16,80},{32,96},{48,112},{64,128},{80,144},{96,160},{112,17... | collective-permute-start | bytes 983048 | tf_op jit(solution)/shard_map/ppermute | solution.py:196
  89.0 8.8 %collective-permute-start.4 = (bf16[1,256,640]{2,1,0:T(8,128)(2,1)}, bf16[1,256,640]{2,1,0:T(8,128)(2,1)}, u32[]{:S(2)}, u32[]{:S(2)}) collective-permute-start(bf16[1,256,640]{2,1,0:T(8,128)(2,1)} %collective-permute-done.2), channel_id=1, source_target_pairs={{0,448},{16,464},{32,480},{48,496},{64,0},{80,16},{96,32},{112,48}... | collective-permute-start | bytes 983048 | tf_op jit(solution)/shard_map/ppermute | solution.py:194
  93.5 10.3 %collective-permute-start.5 = (bf16[1,256,640]{2,1,0:T(8,128)(2,1)}, bf16[1,256,640]{2,1,0:T(8,128)(2,1)}, u32[]{:S(2)}, u32[]{:S(2)}) collective-permute-start(bf16[1,256,640]{2,1,0:T(8,128)(2,1)} %collective-permute-done.3), channel_id=1, source_target_pairs={{0,64},{16,80},{32,96},{48,112},{64,128},{80,144},{96,160},{112,17... | collective-permute-start | bytes 983048 | tf_op jit(solution)/shard_map/ppermute | solution.py:196
  98.7 27.5 %collective-permute-start.7 = (bf16[1,128,640]{2,1,0:T(8,128)(2,1)S(1)}, bf16[1,128,640]{2,1,0:T(8,128)(2,1)}, u32[]{:S(2)}, u32[]{:S(2)}) collective-permute-start(bf16[1,128,640]{2,1,0:T(8,128)(2,1)S(1)} %slice.143), channel_id=1, source_target_pairs={{0,448},{16,464},{32,480},{48,496},{64,0},{80,16},{96,32},{112,48}... | collective-permute-start | bytes 491528 | tf_op jit(solution)/shard_map/ppermute | solution.py:202
  105.4 20.9 %collective-permute-start.6 = (bf16[1,128,640]{2,1,0:T(8,128)(2,1)}, bf16[1,128,640]{2,1,0:T(8,128)(2,1)}, u32[]{:S(2)}, u32[]{:S(2)}) collective-permute-start(bf16[1,128,640]{2,1,0:T(8,128)(2,1)} %slice.142), channel_id=1, source_target_pairs={{0,64},{16,80},{32,96},{48,112},{64,128},{80,144},{96,160},{112,17... | collective-permute-start | bytes 491528 | tf_op jit(solution)/shard_map/ppermute | solution.py:201
  107.3 23.4 %collective-permute-start.15 = (bf16[3,256,640]{2,1,0:T(8,128)(2,1)S(1)}, bf16[3,256,640]{2,1,0:T(8,128)(2,1)S(1)}, u32[]{:S(2)}, u32[]{:S(2)}) collective-permute-start(bf16[3,256,640]{2,1,0:T(8,128)(2,1)S(1)} %collective-permute-done.13), channel_id=1, source_target_pairs={{0,64},{16,80},{32,96},{48,112},{64,128},{80,144},{96,160},{112,17... | collective-permute-start | bytes 2949128 | tf_op jit(solution)/shard_map/ppermute | solution.py:196
  109.3 23.4 %collective-permute-start.14 = (bf16[3,256,640]{2,1,0:T(8,128)(2,1)S(1)}, bf16[3,256,640]{2,1,0:T(8,128)(2,1)S(1)}, u32[]{:S(2)}, u32[]{:S(2)}) collective-permute-start(bf16[3,256,640]{2,1,0:T(8,128)(2,1)S(1)} %collective-permute-done.12), channel_id=1, source_target_pairs={{0,448},{16,464},{32,480},{48,496},{64,0},{80,16},{96,32},{112,48}... | collective-permute-start | bytes 2949128 | tf_op jit(solution)/shard_map/ppermute | solution.py:194
  113.8 7.2 %copy-start = (bf16[512,8192]{1,0:T(8,128)(2,1)S(1)}, bf16[512,8192]{1,0:T(8,128)(2,1)}, u32[]{:S(2)}) copy-start(bf16[512,8192]{1,0:T(8,128)(2,1)} %all-gather.2.cloned.1.call-done) | copy-start | bytes 25165828
  130.7 19.1 %collective-permute-start.17 = (bf16[3,256,640]{2,1,0:T(8,128)(2,1)S(1)}, bf16[3,256,640]{2,1,0:T(8,128)(2,1)S(1)}, u32[]{:S(2)}, u32[]{:S(2)}) collective-permute-start(bf16[3,256,640]{2,1,0:T(8,128)(2,1)S(1)} %collective-permute-done.15), channel_id=1, source_target_pairs={{0,64},{16,80},{32,96},{48,112},{64,128},{80,144},{96,160},{112,17... | collective-permute-start | bytes 2949128 | tf_op jit(solution)/shard_map/ppermute | solution.py:196
  132.7 19.1 %collective-permute-start.16 = (bf16[3,256,640]{2,1,0:T(8,128)(2,1)S(1)}, bf16[3,256,640]{2,1,0:T(8,128)(2,1)S(1)}, u32[]{:S(2)}, u32[]{:S(2)}) collective-permute-start(bf16[3,256,640]{2,1,0:T(8,128)(2,1)S(1)} %collective-permute-done.14), channel_id=1, source_target_pairs={{0,448},{16,464},{32,480},{48,496},{64,0},{80,16},{96,32},{112,48}... | collective-permute-start | bytes 2949128 | tf_op jit(solution)/shard_map/ppermute | solution.py:194
  149.9 12.7 %collective-permute-start.18 = (bf16[3,128,640]{2,1,0:T(8,128)(2,1)S(1)}, bf16[3,128,640]{2,1,0:T(8,128)(2,1)S(1)}, u32[]{:S(2)}, u32[]{:S(2)}) collective-permute-start(bf16[3,128,640]{2,1,0:T(8,128)(2,1)S(1)} %slice.164), channel_id=1, source_target_pairs={{0,64},{16,80},{32,96},{48,112},{64,128},{80,144},{96,160},{112,17... | collective-permute-start | bytes 1474568 | tf_op jit(solution)/shard_map/ppermute | solution.py:201
  151.9 12.2 %collective-permute-start.19 = (bf16[3,128,640]{2,1,0:T(8,128)(2,1)S(1)}, bf16[3,128,640]{2,1,0:T(8,128)(2,1)S(1)}, u32[]{:S(2)}, u32[]{:S(2)}) collective-permute-start(bf16[3,128,640]{2,1,0:T(8,128)(2,1)S(1)} %slice.165), channel_id=1, source_target_pairs={{0,448},{16,464},{32,480},{48,496},{64,0},{80,16},{96,32},{112,48}... | collective-permute-start | bytes 1474568 | tf_op jit(solution)/shard_map/ppermute | solution.py:202
  167.2 13.0 %copy-start.1 = (f32[512,640]{1,0:T(8,128)}, f32[512,640]{1,0:T(8,128)S(1)}, u32[]{:S(2)}) copy-start(f32[512,640]{1,0:T(8,128)S(1)} %fusion.17.q_ref) | copy-start | bytes 3932164
  167.2 12.2 %collective-permute-start.20 = (bf16[512,128]{1,0:T(8,128)(2,1)S(1)}, bf16[512,128]{1,0:T(8,128)(2,1)S(1)}, u32[]{:S(2)}, u32[]{:S(2)}) collective-permute-start(bf16[512,128]{1,0:T(8,128)(2,1)S(1)} %slice.226), channel_id=1, source_target_pairs={{0,1},{1,0},{2,3},{3,2},{4,5},{5,4},{6,7},{7,6},{8,9},{9,8},{10,11... | collective-permute-start | bytes 393224 | tf_op jit(solution)/shard_map/ppermute | solution.py:260
Sparse Core Ops, SparseCore 0:
  10.0 71.7 all-gather.1
